TPU v7x, 256 devices: a whole 4x4x8 slice. The times are simulated.
256 devices in a mesh: req: 2 (over core), blk: 128 (over z, x, y).
Axes of the slice: x: 4, y: 4, z: 8, core: 2. Of those that a mesh axis runs over, the one named last changes fastest.
Arguments:
- query: bfloat16 [2, 8192, 2048], P('req', 'blk'), may hold values from -64 to 64
- rotated_key_value: bfloat16 [2, 2, 8192, 512], P('req', None, 'blk'), may hold values from -64 to 64
- lengths: int32 [2], P('req'), may hold values from 6144 to 8192, as said below
- block_map: int32 [256], replicated, may hold values from 0 to 255, as said below
- segment_head: int32 [4], replicated, may hold values from 0 to 3, each once
Outputs:
- attended: bfloat16 [2, 8192, 2048], P('req', 'blk')
- cache: bfloat16 [2, 2, 128, 256, 128], P('req', None, 'blk')
Inputs may be any that keep to these rules, and one draw needn't show every extreme that they name: `lengths`: one of the two prompts has exactly 8192 tokens. `block_map`: each prompt block appears once; storage blocks 2d and 2d+1 hold blocks b and 255 - b for some b < 128.
All inputs are finite; a program needn't handle non-finite values.
Results may differ from a plain program's by a relative error of at most 0.007.
Values may be sent and summed in bfloat16 or wider, within the bound.
No kernel may reach another device: no remote copies, remote signals or barrier semaphores. Data moves between devices by JAX's collectives and lax.ppermute only.
A program may use at most 128 MiB of HBM per device.

v0:
```python
import jax
import jax.numpy as jnp
from jax import lax
from jax.sharding import PartitionSpec as P

QUERY_HEADS = 16
KEY_VALUE_HEADS = 4
HEAD_DIMENSION = 128
WINDOW = 4096


def body(query, rotated_key_value, lengths, block_map, segment_head):
    token_index = query.shape[1]
    half_width = token_index // 2
    query_groups = QUERY_HEADS // KEY_VALUE_HEADS
    token_count = lax.axis_size("blk")
    place = lax.axis_index("blk")
    segment_list = token_count // KEY_VALUE_HEADS
    group_repeats = half_width // segment_list
    prompt_blocks = 2 * token_count
    length = lengths[0]
    scale = HEAD_DIMENSION ** (-0.5)
    my_blocks = lax.dynamic_slice_in_dim(block_map, 2 * place, 2)
    qpos = (
        my_blocks[:, None] * half_width + jnp.arange(half_width, dtype=jnp.int32)[None, :]
    ).reshape(token_index)
    query_rows = query[0].reshape(token_index, KEY_VALUE_HEADS, query_groups, HEAD_DIMENSION)
    slot_seg = place % segment_list
    segment_piece = lax.all_gather(rotated_key_value, "blk", axis=2, tiled=True)
    upper_limit = jnp.full((KEY_VALUE_HEADS, query_groups, token_index), -1e30, jnp.float32)
    held = jnp.zeros((2, prompt_blocks, group_repeats, HEAD_DIMENSION), jnp.bfloat16)
    row_indices = segment_piece.shape[2]
    nblock = row_indices // half_width
    owned = jnp.take(block_map, jnp.arange(nblock, dtype=jnp.int32))
    kpos = (owned[:, None] * half_width + jnp.arange(half_width, dtype=jnp.int32)[None, :]).reshape(
        row_indices
    )
    key_rows = segment_piece[0, 0].reshape(row_indices, KEY_VALUE_HEADS, HEAD_DIMENSION)
    value_rows = segment_piece[0, 1].reshape(row_indices, KEY_VALUE_HEADS, HEAD_DIMENSION)
    scores = (
        jnp.einsum("qhgd,khd->hgqk", query_rows, key_rows, preferred_element_type=jnp.float32)
        * scale
    )
    allowed = (kpos[None, :] <= qpos[:, None]) & (kpos[None, :] > qpos[:, None] - WINDOW)
    allowed = allowed & ((kpos[None, :] < length) | (kpos[None, :] == qpos[:, None]))
    allowed = allowed[None, None]
    fresh = jnp.maximum(upper_limit, jnp.max(jnp.where(allowed, scores, -1e30), axis=-1))
    prob = jnp.where(allowed, jnp.exp(scores - fresh[..., None]), 0.0)
    total = jnp.sum(prob, axis=-1)
    summed = jnp.einsum(
        "hgqk,khd->hgqd", prob.astype(jnp.bfloat16), value_rows, preferred_element_type=jnp.float32
    )
    final = (fresh, total, summed, held)
    upper_limit, total, summed, held = final
    result = summed / total[..., None]
    result = jnp.where((qpos < length)[None, None, :, None], result, 0.0)
    attended = (
        result.transpose(2, 0, 1, 3)
        .reshape(1, token_index, QUERY_HEADS * HEAD_DIMENSION)
        .astype(jnp.bfloat16)
    )
    launch_lattice = rotated_key_value[0].reshape(
        2, 2, group_repeats, segment_list, KEY_VALUE_HEADS, HEAD_DIMENSION
    )
    launch_lattice = jnp.take(launch_lattice, segment_head, axis=4)
    outgoing = launch_lattice.transpose(0, 4, 3, 1, 2, 5).reshape(
        2, token_count, 2, group_repeats, HEAD_DIMENSION
    )
    arrived = lax.all_to_all(outgoing, "blk", split_axis=1, concat_axis=1, tiled=True)
    arrived = arrived.reshape(2, prompt_blocks, group_repeats, HEAD_DIMENSION)
    held = (
        jnp.zeros((2, prompt_blocks, group_repeats, HEAD_DIMENSION), jnp.bfloat16)
        .at[:, block_map]
        .set(arrived)
    )
    position = (
        jnp.arange(prompt_blocks, dtype=jnp.int32)[:, None] * group_repeats
        + jnp.arange(group_repeats, dtype=jnp.int32)[None, :]
    ) * segment_list + slot_seg
    held = jnp.where((position < length)[None, :, :, None], held, jnp.zeros((), jnp.bfloat16))
    cache = held.reshape(2, prompt_blocks * group_repeats, HEAD_DIMENSION)[None, :, None]
    return (attended, cache)


def solution(mesh):
    return jax.shard_map(
        body,
        mesh=mesh,
        in_specs=(P("req", "blk", None), P("req", None, "blk", None), P("req"), P(), P()),
        out_specs=(P("req", "blk", None), P("req", None, "blk", None, None)),
        check_vma=False,
    )
```

profile of v0, /device:TPU:8, one launch (start us, length us, event | category | flops | bytes accessed | tf_op | source)
XLA Modules:
  0.0 320.0 jit_solution(6120186794051382634)
XLA Ops:
  7.2 1.7 copy.26
  8.9 0.9 reshape.238
  9.9 0.7 compare_select_fusion.1
  10.6 0.6 gather_fusion.1
  11.1 0.7 compare_and_fusion
  11.8 0.1 fusion.22
  11.9 0.8 copy.35
  12.7 15.4 %all-to-all-start = ((bf16[2,128,2,1,128]{4,2,0,3,1:T(2,128)(2,1)}), bf16[2,128,2,1,128]{4,2,0,3,1:T(2,128)(2,1)S(1)}, u32[]{:S(2)}, u32[]{:S(2)}) async-start(bf16[2,128,2,1,128]{4,2,0,3,1:T(2,128)(2,1)} %copy.35), calls=%async_computation | async-start | bytes 262144 | tf_op jit(solution)/shard_map/all_to_all | solution.py:69
  28.1 2.0 gather_fusion
  30.1 0.1 iota_add_fusion
  30.2 0.1 add.100
  30.3 0.8 dynamic-slice_multiply_fusion
  31.1 0.1 iota_add_fusion.1
  31.1 0.1 add.96
  31.9 0.8 or_and_fusion
  32.7 1.1 reshape_squeeze.13
  33.8 0.7 compare_select_fusion
  34.5 5.9 %all-to-all-done = bf16[2,128,2,1,128]{4,2,0,3,1:T(2,128)(2,1)S(1)} async-done(((bf16[2,128,2,1,128]{4,2,0,3,1:T(2,128)(2,1)}), bf16[2,128,2,1,128]{4,2,0,3,1:T(2,128)(2,1)S(1)}, u32[]{:S(2)}, u32[]{:S(2)}) %all-to-all-start) | async-done | bytes 131104 | tf_op jit(solution)/shard_map/all_to_all | solution.py:69
  40.4 0.1 copy.36
  40.5 0.1 copy.37
  40.7 7.2 %scatter_fusion = bf16[2,256,128]{2,0,1:T(2,128)(2,1)S(1)} fusion(bf16[2,256,128]{2,0,1:T(2,128)(2,1)S(1)} %broadcast.181, s32[256]{0:T(256)S(1)} %compare_select_fusion, bf16[256,2,128]{2,1,0:T(2,128)(2,1)S(1)} %copy.37), kind=kCustom, calls=%fused_computation.2 | custom fusion | bytes 394240 | tf_op jit(solution)/shard_map/scatter | solution.py:74
  47.9 0.3 fusion.23
  48.2 0.7 copy.38
  48.9 116.6 %all-gather.2.cloned.1.call-done = bf16[1,2,8192,512]{3,1,0,2:T(2,128)(2,1)} async-done(((bf16[1,2,64,512]{3,1,0,2:T(2,128)(2,1)}), bf16[1,2,8192,512]{3,1,0,2:T(2,128)(2,1)}) %all-gather.2.cloned.1.call-update) | async-done | bytes 16777232 | tf_op jit(solution)/shard_map/all_gather | solution.py:29
  165.5 32.7 %fusion.27 = (bf16[1,1,8192,512]{3,1,0,2:T(2,128)(2,1)}, bf16[1,1,8192,512]{3,1,0,2:T(2,128)(2,1)}) fusion(bf16[1,2,8192,512]{3,1,0,2:T(2,128)(2,1)} %all-gather.2.cloned.1.call-done), kind=kLoop, calls=%fused_computation.40 | loop fusion | bytes 33554432 | tf_op jit(solution)/shard_map/slice | solution.py:38
  198.2 33.4 %copy.46 = bf16[1,1,8192,512]{2,3,1,0:T(8,128)(2,1)} copy(bf16[1,1,8192,512]{3,1,0,2:T(2,128)(2,1)} %get-tuple-element.11) | data formatting | bytes 16777216
  231.5 33.3 %copy.45 = bf16[1,1,8192,512]{2,3,1,0:T(8,128)(2,1)} copy(bf16[1,1,8192,512]{3,1,0,2:T(2,128)(2,1)} %get-tuple-element.10) | data formatting | bytes 16777216
  264.9 16.0 %fusion = (f32[4,4,64]{2,1,0:T(4,128)S(1)}, f32[4,8192,64,4]{1,2,3,0:T(8,128)}) fusion(pred[64,8192]{1,0:T(8,128)(4,1)S(1)} %or_and_fusion, bf16[8192,4,128,1]{0,2,3,1:T(8,128)(2,1)} %bitcast.67, bf16[64,4,4,128]{3,2,1,0:T(4,128)(2,1)S(1)} %reshape_squeeze.13), kind=kOutput, calls=%fused_computation.5 | convolution fusion | flops 2172648448 | bytes 42733568 | tf_op jit(solution)/shard_map/qhgd,khd->hgqk/dot_general | solution.py:41
  280.9 15.2 %fusion.3 = f32[4,4,64]{2,1,0:T(4,128)S(1)} fusion(f32[4,8192,64,4]{1,2,3,0:T(8,128)} %get-tuple-element.13, f32[4,4,64]{2,1,0:T(4,128)S(1)} %broadcast_maximum_fusion, pred[64,8192]{1,0:T(8,128)(4,1)S(1)} %or_and_fusion), kind=kLoop, calls=%fused_computation.8 | loop fusion | flops 33553408 | bytes 34086912 | tf_op jit(solution)/shard_map/reduce_sum | solution.py:49
  296.1 15.9 %fusion.17 = bf16[64,4,4,128]{3,0,2,1:T(8,128)(2,1)S(1)} fusion(bf16[8192,4,128,1]{0,2,3,1:T(8,128)(2,1)} %bitcast.68, f32[4,8192,64,4]{1,2,3,0:T(8,128)} %get-tuple-element.13, f32[4,4,64]{2,1,0:T(4,128)S(1)} %broadcast_maximum_fusion, pred[64,8192]{1,0:T(8,128)(4,1)S(1)} %or_and_fusion, f32[64,4,4]{0,2,1:T(4,128)S(1)} %bitcast.71, ...), kind=kOutput, calls=%fused_computation.16 | convolution fusion | flops 2181431296 | bytes 42737728 | tf_op jit(solution)/shard_map/hgqk,khd->hgqd/dot_general | solution.py:50
  312.1 0.2 copy.32
  312.3 0.9 convert_element_type.19
  (14 shorter events, 0.2 us)
Async XLA Ops:
  7.2 158.3 %all-gather.2.cloned.1.call-start = ((), (), s32[]{:S(2)}) async-start(), calls=%async_computation.1 | async-start | bytes 16908288 | tf_op jit(solution)/shard_map/all_gather | solution.py:29
  12.7 27.7 %all-to-all-start = ((bf16[2,128,2,1,128]{4,2,0,3,1:T(2,128)(2,1)}), bf16[2,128,2,1,128]{4,2,0,3,1:T(2,128)(2,1)S(1)}, u32[]{:S(2)}, u32[]{:S(2)}) async-start(bf16[2,128,2,1,128]{4,2,0,3,1:T(2,128)(2,1)} %copy.35), calls=%async_computation | async-start | bytes 262144 | tf_op jit(solution)/shard_map/all_to_all | solution.py:69
Sparse Core Ops, SparseCore 0:
  12.0 153.3 all-gather.1
where the time goes:
time: 323 us; the launch traced here: 320 us
  waiting for transfers between devices  122 us (38%)
  local copies, waits for them, and re-layouts  116 us (36%)
  matrix products  31.9 us (10%)
  other arithmetic  19.4 us (6%)
  starting transfers between devices  15.4 us (5%)
  between operations  14.9 us (5%)
    all_gather x1, waiting for transfers between devices, body(): segment_piece = lax.all_gather(rotated_key_value, 'blk', axis=2, tiled=True)  117 us
    unnamed x4, local copies, waits for them, and re-layouts  69.1 us
    slice x1, local copies, waits for them, and re-layouts, body(): segment_piece[0, 0].reshape(row_indices, KEY_VALUE_HEADS, HEAD_DIMENSION)  32.7 us
    dot_general x1, matrix products, body(): jnp.einsum('qhgd,khd->hgqk', query_rows, key_rows, preferred_element_type...  16 us
    dot_general x1, matrix products, body(): jnp.einsum('hgqk,khd->hgqd', prob.astype(jnp.bfloat16), value_rows, prefe...  15.9 us
    all_to_all x1, starting transfers between devices, body(): lax.all_to_all(outgoing, 'blk', split_axis=1, concat_axis=1, tiled=True)  15.4 us
    reduce_sum x1, other arithmetic, body(): total = jnp.sum(prob, axis=-1)  15.2 us
    scatter x1, local copies, waits for them, and re-layouts, body(): held = jnp.zeros((2, prompt_blocks, group_repeats, HEAD_DIMENSION), jnp.b...  7.17 us
  transfers between devices with their start and end apart: 2, of which 2 were waited for; matrix products, arithmetic and copies ran while one was open for 6% of the time, Pallas kernels for 0%

commit v1 on v0

v1 whole, which is shorter than its diff:
```python
import functools
import math

import jax
import jax.numpy as jnp
from jax import lax
from jax.experimental import pallas as pl
from jax.experimental.pallas import tpu as pltpu
from jax.sharding import PartitionSpec as P

QUERY_HEADS = 16
KEY_VALUE_HEADS = 4
GROUP = QUERY_HEADS // KEY_VALUE_HEADS
HEAD_DIMENSION = 128
WINDOW = 4096
BLOCK = 32
WINDOW_BLOCKS = WINDOW // BLOCK
BLOCKS = 256
CHUNK_BLOCKS = 16
CHUNK = CHUNK_BLOCKS * BLOCK
NZ, NX, NY = 8, 4, 4
N_BLK = NZ * NX * NY
ROWS = GROUP * BLOCK
LOG2E = 1.4426950408889634
NEG = -1e30


def attention_kernel(table, q_blocks, length, q_ref, c0, r1, r2, r3, l1, l2, l3, r4, l4, o_ref, kv, s_scr, sems):
    step = 2 * 64 * NY * NX
    half = step // 2
    pieces = [(c0, 0), (r1, 7), (r2, 6), (r3, 5), (l1, 1), (l2, 2), (l3, 3)]
    copies = [
        pltpu.make_async_copy(src, kv.at[pl.ds(slot * step, step)], sems.at[i])
        for i, (src, slot) in enumerate(pieces)
    ]
    copies.append(pltpu.make_async_copy(r4, kv.at[pl.ds(4 * step, half)], sems.at[7]))
    copies.append(pltpu.make_async_copy(l4, kv.at[pl.ds(4 * step + half, half)], sems.at[8]))
    for copy in copies:
        copy.start()
    for copy in copies:
        copy.wait()

    token = lax.broadcasted_iota(jnp.int32, (ROWS, CHUNK), 0) % BLOCK
    key = lax.broadcasted_iota(jnp.int32, (ROWS, CHUNK), 1)
    ahead = token - key
    row_token = lax.broadcasted_iota(jnp.int32, (ROWS, HEAD_DIMENSION), 0) % BLOCK
    scale = HEAD_DIMENSION**-0.5 * LOG2E
    ones = jnp.ones((CHUNK, HEAD_DIMENSION), jnp.bfloat16)

    def load(chunk, offset):
        return jnp.concatenate(
            [
                kv[pl.ds(pl.multiple_of(table[chunk * CHUNK_BLOCKS + u] + offset, BLOCK), BLOCK), :]
                for u in range(CHUNK_BLOCKS)
            ],
            axis=0,
        )

    def one_block(i, carry):
        block = q_blocks[i]
        low = jnp.maximum(block - WINDOW_BLOCKS, 0) // CHUNK_BLOCKS
        high = block // CHUNK_BLOCKS
        q = q_ref[i]

        def scores(chunk, top, masked):
            s = lax.dot_general(q, load(chunk, 0), (((1,), (1,)), ((), ())), preferred_element_type=jnp.float32)
            if masked:
                distance = ahead + (block * BLOCK - chunk * CHUNK)
                s = jnp.where((distance >= 0) & (distance < WINDOW), s, NEG)
            s_scr[chunk - low] = s
            for j in range(CHUNK // 128):
                top = jnp.maximum(top, s[:, j * 128 : (j + 1) * 128])
            return top

        top = jnp.full((ROWS, 128), NEG, jnp.float32)
        top = scores(high, top, True)
        top = lax.cond(low < high, lambda t: scores(low, t, True), lambda t: t, top)
        top = lax.fori_loop(low + 1, high, lambda c, t: scores(c, t, False), top)
        top = jnp.max(top, axis=1, keepdims=True) * scale

        def weigh(chunk, acc):
            p = jnp.exp2(s_scr[chunk - low] * scale - top).astype(jnp.bfloat16)
            v = jnp.concatenate([load(chunk, 64), ones], axis=1)
            return acc + lax.dot_general(p, v, (((1,), (0,)), ((), ())), preferred_element_type=jnp.float32)

        acc = lax.fori_loop(low, high + 1, weigh, jnp.zeros((ROWS, 2 * HEAD_DIMENSION), jnp.float32))
        out = acc[:, :HEAD_DIMENSION] / acc[:, HEAD_DIMENSION:]
        out = jnp.where(block * BLOCK + row_token < length[0], out, 0.0)
        o_ref[i] = out.astype(jnp.bfloat16)
        return carry

    lax.fori_loop(0, 2 * NY, one_block, 0)


def attention(table, q_blocks, length, q, pieces):
    smem = pl.BlockSpec(memory_space=pltpu.SMEM)
    vmem = pl.BlockSpec(memory_space=pltpu.VMEM)
    return pl.pallas_call(
        attention_kernel,
        out_shape=jax.ShapeDtypeStruct((2 * NY, ROWS, HEAD_DIMENSION), jnp.bfloat16),
        in_specs=[smem] * 3 + [vmem] + [pl.BlockSpec(memory_space=pl.ANY)] * 9,
        out_specs=vmem,
        scratch_shapes=[
            pltpu.VMEM((2 * BLOCKS * BLOCK, HEAD_DIMENSION), jnp.bfloat16),
            pltpu.VMEM((WINDOW // CHUNK + 1, ROWS, CHUNK), jnp.float32),
            pltpu.SemaphoreType.DMA((9,)),
        ],
        compiler_params=pltpu.CompilerParams(vmem_limit_bytes=32 * 1024 * 1024),
        cost_estimate=pl.CostEstimate(flops=3_000_000_000, bytes_accessed=5_000_000, transcendentals=4_000_000),
        name="attention",
    )(table, q_blocks, length, q, *pieces)


def body(query, rotated_key_value, lengths, block_map, segment_head):
    place = lax.axis_index("blk")
    z, x, y = place // 16, (place // 4) % 4, place % 4
    y_groups = [[4 * g + i for i in range(4)] for g in range(N_BLK // 4)]

    def move(value, target):
        return lax.ppermute(value, "blk", [(s, target(s // 16, (s // 4) % 4, s % 4)) for s in range(N_BLK)])

    def index(zz, xx, yy):
        return (zz % NZ) * 16 + xx * 4 + yy

    outgoing = jnp.take(rotated_key_value[0].reshape(2, 64, KEY_VALUE_HEADS, HEAD_DIMENSION), segment_head, axis=2)
    outgoing = outgoing.transpose(2, 0, 1, 3)
    own = lax.all_to_all(outgoing, "blk", 0, 0, axis_index_groups=y_groups, tiled=True)
    q = query[0].reshape(2, BLOCK, KEY_VALUE_HEADS, GROUP, HEAD_DIMENSION)
    q = jnp.take(q, segment_head, axis=2).transpose(2, 0, 3, 1, 4)

    x1 = move(own, lambda a, b, c: index(a, b ^ 1, c))
    x3 = move(own, lambda a, b, c: index(a, b ^ 3, c))
    x2 = move(x1, lambda a, b, c: index(a, b ^ 3, c))
    plane = jnp.concatenate([own, x1, x2, x3], axis=0).reshape(4 * 4 * 128, HEAD_DIMENSION)
    right = lambda v: move(v, lambda a, b, c: index(a + 1, b, c))
    left = lambda v: move(v, lambda a, b, c: index(a - 1, b, c))
    r1, l1 = right(plane), left(plane)
    q = lax.all_to_all(q, "blk", 0, 0, axis_index_groups=y_groups, tiled=True)
    r2, l2 = right(r1), left(l1)
    r3, l3 = right(r2), left(l2)
    half = plane.shape[0] // 2
    r4, l4 = right(r3[:half]), left(l3[half:])
    pieces = [plane, r1, r2, r3, l1, l2, l3, r4, l4]

    blocks = jnp.arange(BLOCKS, dtype=jnp.int32)
    hit = block_map[None, :] == blocks[:, None]
    device = blocks // 2
    slot = ((device // 16 - z) % NZ * 4 + ((device // 4) % 4 ^ x)) * 4 + device % 4
    row = slot * 128 + (blocks % 2) * BLOCK
    table = jnp.sum(jnp.where(hit, row[None, :], 0), axis=1, dtype=jnp.int32)
    q_blocks = lax.dynamic_slice_in_dim(block_map, (z * 4 + x) * 8, 8)
    out = attention(table, q_blocks, lengths, q.reshape(2 * NY, ROWS, HEAD_DIMENSION), pieces)
    out = out.reshape(4, 2, GROUP, BLOCK, HEAD_DIMENSION)
    out = lax.all_to_all(out, "blk", 0, 0, axis_index_groups=y_groups, tiled=True)
    heads = jnp.arange(KEY_VALUE_HEADS, dtype=jnp.int32)
    inverse = jnp.sum(jnp.where(segment_head[None, :] == heads[:, None], heads[None, :], 0), axis=1)
    attended = jnp.take(out, inverse, axis=0).transpose(1, 3, 0, 2, 4).reshape(1, 64, QUERY_HEADS * HEAD_DIMENSION)

    offset = (z % 2) * 16 + x * 4 + z // 2
    pick = (jnp.arange(BLOCK, dtype=jnp.int32) == offset)[None, None, None, :, None]

    def rows_of(piece):
        v = piece.reshape(-1, 2, 2, BLOCK, HEAD_DIMENSION)
        v = jnp.sum(jnp.where(pick, v, jnp.zeros((), jnp.bfloat16)), axis=3)
        return v.transpose(0, 2, 1, 3).reshape(-1, 2 * HEAD_DIMENSION)

    ordered = [plane, l1, l2, l3, r4, l4, r3, r2, r1]
    picked = jnp.concatenate([rows_of(v) for v in ordered], axis=0)
    position = blocks * BLOCK + offset
    where = (table // 128) * 2 + (table // BLOCK) % 2
    choose = (where[:, None] == blocks[None, :]) & (position < lengths[0])[:, None]
    cache = jnp.dot(choose.astype(jnp.bfloat16), picked, preferred_element_type=jnp.float32).astype(jnp.bfloat16)
    cache = move(cache, lambda a, b, c: index(2 * c + a % 2, b, a // 2))
    cache = cache.reshape(BLOCKS, 2, HEAD_DIMENSION).transpose(1, 0, 2)[None, :, None]
    return attended, cache


def solution(mesh):
    return jax.shard_map(
        body,
        mesh=mesh,
        in_specs=(P("req", "blk", None), P("req", None, "blk", None), P("req"), P(), P()),
        out_specs=(P("req", "blk", None), P("req", None, "blk", None, None)),
        check_vma=False,
    )
```

time: 323 us -> 123 us (0.38)
  local copies, waits for them, and re-layouts: 116 us -> 8.72 us
  waiting for transfers between devices: 122 us -> 33.3 us
  matrix products: 31.9 us -> 0.91 us
  starting transfers between devices: 15.4 us -> 39.9 us
  Pallas kernels: 0 us -> 23.5 us
  other arithmetic: 19.4 us -> 4.71 us
  between operations: 14.9 us -> 1.65 us
  blocking collectives: 0 us -> 9.23 us
    all_gather x1 -> x0, waiting for transfers between devices: 117 us -> none  [body(): segment_piece = lax.all_gather(rotated_key_value, 'blk', axis=2, tiled=True)]
    unnamed x4 -> x27, local copies, waits for them, and re-layouts: 69.1 us -> 3.83 us
    slice x1 -> x2, local copies, waits for them, and re-layouts: 32.7 us -> 0.04 us  [body(): r4, l4 = (right(r3[:half]), left(l3[half:]))]
    dot_general x2 -> x1, matrix products: 31.9 us -> 0.91 us  [body(): jnp.dot(choose.astype(jnp.bfloat16), picked, preferred_element_type=jnp.f...]
    ppermute x0 -> x12, waiting for transfers between devices: none -> 28.8 us  [move(): lax.ppermute(value, 'blk', [(s, target(s // 16, s // 4 % 4, s % 4)) for s...]
    ppermute x0 -> x12, starting transfers between devices: none -> 26.6 us  [move(): lax.ppermute(value, 'blk', [(s, target(s // 16, s // 4 % 4, s % 4)) for s...]
    pallas_call x0 -> x1, Pallas kernels: none -> 23.5 us  [attention(): pl.pallas_call(attention_kernel, out_shape=jax.ShapeDtypeStruct((2 * NY,...]
    reduce_sum x1 -> x4, other arithmetic: 15.2 us -> 2.93 us  [the longest x2 2.7 us: rows_of(): v = jnp.sum(jnp.where(pick, v, jnp.zeros((), jnp.bfloat16)), axis=3)]
  transfers between devices with their start and end apart: 2 -> 14, of which waited for: 2 -> 7; matrix products, arithmetic and copies ran while one was open for 6% -> 5% of each run, Pallas kernels for 0% -> 19%
where the time goes in v1:
time: 123 us; the launch traced here: 122 us
  starting transfers between devices  39.9 us (32%)
  waiting for transfers between devices  33.3 us (27%)
  Pallas kernels  23.5 us (19%)
  blocking collectives  9.23 us (8%)
  local copies, waits for them, and re-layouts  8.72 us (7%)
  other arithmetic  4.71 us (4%)
  between operations  1.65 us (1%)
    ppermute x12, waiting for transfers between devices, move(): lax.ppermute(value, 'blk', [(s, target(s // 16, s // 4 % 4, s % 4)) for s...  28.8 us
    ppermute x12, starting transfers between devices, move(): lax.ppermute(value, 'blk', [(s, target(s // 16, s // 4 % 4, s % 4)) for s...  26.6 us
    pallas_call x1, Pallas kernels, attention(): pl.pallas_call(attention_kernel, out_shape=jax.ShapeDtypeStruct((2 * NY,...  23.5 us
    all_to_all x1, blocking collectives, body(): lax.all_to_all(outgoing, 'blk', 0, 0, axis_index_groups=y_groups, tiled=T...  9.23 us
    all_to_all x1, starting transfers between devices, body(): lax.all_to_all(out, 'blk', 0, 0, axis_index_groups=y_groups, tiled=True)  7.85 us
    all_to_all x1, starting transfers between devices, body(): q = lax.all_to_all(q, 'blk', 0, 0, axis_index_groups=y_groups, tiled=True)  5.46 us
    all_to_all x1, waiting for transfers between devices, body(): lax.all_to_all(out, 'blk', 0, 0, axis_index_groups=y_groups, tiled=True)  4.55 us
    unnamed x27, local copies, waits for them, and re-layouts  3.83 us
  transfers between devices with their start and end apart: 14, of which 7 were waited for; matrix products, arithmetic and copies ran while one was open for 5% of the time, Pallas kernels for 19%

profile of v1, /device:TPU:8, one launch (start us, length us, event | category | flops | bytes accessed | tf_op | source)
XLA Modules:
  0.0 121.9 jit_solution(5555853090781429123)
XLA Ops:
  0.6 0.7 compare_select_fusion.1
  1.4 0.9 reshape_squeeze.7
  3.0 9.2 %all_to_all.15 = bf16[4,2,64,128]{3,2,1,0:T(8,128)(2,1)S(1)} all-to-all(bf16[4,2,64,128]{3,2,1,0:T(8,128)(2,1)S(1)} %broadcast_select_fusion), channel_id=1, replica_groups={{0,1,2,3},{4,5,6,7},{8,9,10,11},{12,13,14,15},{16,17,18,19},{20,21,22,2..., dimensions={0} | all-to-all | bytes 262144 | tf_op jit(solution)/shard_map/all_to_all | solution.py:127
  12.3 1.5 %collective-permute-start = (bf16[4,2,64,128]{3,2,1,0:T(8,128)(2,1)S(1)}, bf16[4,2,64,128]{3,2,1,0:T(8,128)(2,1)S(1)}, u32[]{:S(2)}, u32[]{:S(2)}) collective-permute-start(bf16[4,2,64,128]{3,2,1,0:T(8,128)(2,1)S(1)} %all_to_all.15), channel_id=1, source_target_pairs={{0,4},{1,5},{2,6},{3,7},{4,0},{5,1},{6,2},{7,3},{8,12},{9,13},{10,... | collective-permute-start | bytes 393224 | tf_op jit(solution)/shard_map/ppermute | solution.py:120
  13.7 3.5 %collective-permute-done = bf16[4,2,64,128]{3,2,1,0:T(8,128)(2,1)S(1)} collective-permute-done((bf16[4,2,64,128]{3,2,1,0:T(8,128)(2,1)S(1)}, bf16[4,2,64,128]{3,2,1,0:T(8,128)(2,1)S(1)}, u32[]{:S(2)}, u32[]{:S(2)}) %collective-permute-start) | collective-permute-done | bytes 131104 | tf_op jit(solution)/shard_map/ppermute | solution.py:120
  17.2 2.8 %collective-permute-start.1 = (bf16[4,2,64,128]{3,2,1,0:T(8,128)(2,1)S(1)}, bf16[4,2,64,128]{3,2,1,0:T(8,128)(2,1)S(1)}, u32[]{:S(2)}, u32[]{:S(2)}) collective-permute-start(bf16[4,2,64,128]{3,2,1,0:T(8,128)(2,1)S(1)} %collective-permute-done), channel_id=1, source_target_pairs={{0,12},{1,13},{2,14},{3,15},{4,8},{5,9},{6,10},{7,11},{8,4},{9,5},... | collective-permute-start | bytes 393224 | tf_op jit(solution)/shard_map/ppermute | solution.py:120
  20.6 3.1 %collective-permute-done.1 = bf16[4,2,64,128]{3,2,1,0:T(8,128)(2,1)S(1)} collective-permute-done((bf16[4,2,64,128]{3,2,1,0:T(8,128)(2,1)S(1)}, bf16[4,2,64,128]{3,2,1,0:T(8,128)(2,1)S(1)}, u32[]{:S(2)}, u32[]{:S(2)}) %collective-permute-start.1) | collective-permute-done | bytes 131104 | tf_op jit(solution)/shard_map/ppermute | solution.py:120
  23.7 2.6 %collective-permute-done.2 = bf16[4,2,64,128]{3,2,1,0:T(8,128)(2,1)S(1)} collective-permute-done((bf16[4,2,64,128]{3,2,1,0:T(8,128)(2,1)S(1)}, bf16[4,2,64,128]{3,2,1,0:T(8,128)(2,1)S(1)}, u32[]{:S(2)}, u32[]{:S(2)}) %collective-permute-start.2) | collective-permute-done | bytes 131104 | tf_op jit(solution)/shard_map/ppermute | solution.py:120
  26.3 2.0 %collective-permute-start.3 = (bf16[2048,128]{1,0:T(8,128)(2,1)S(1)}, bf16[2048,128]{1,0:T(8,128)(2,1)S(1)}, u32[]{:S(2)}, u32[]{:S(2)}) collective-permute-start(bf16[2048,128]{1,0:T(8,128)(2,1)S(1)} %bitcast.88), channel_id=1, source_target_pairs={{0,16},{1,17},{2,18},{3,19},{4,20},{5,21},{6,22},{7,23},{8,24},{9,... | collective-permute-start | bytes 1572872 | tf_op jit(solution)/shard_map/ppermute | solution.py:120
  28.3 4.0 %collective-permute-start.6 = (bf16[2048,128]{1,0:T(8,128)(2,1)S(1)}, bf16[2048,128]{1,0:T(8,128)(2,1)S(1)}, u32[]{:S(2)}, u32[]{:S(2)}) collective-permute-start(bf16[2048,128]{1,0:T(8,128)(2,1)S(1)} %bitcast.89), channel_id=1, source_target_pairs={{0,112},{1,113},{2,114},{3,115},{4,116},{5,117},{6,118},{7,119},{8... | collective-permute-start | bytes 1572872 | tf_op jit(solution)/shard_map/ppermute | solution.py:120
  32.6 0.6 gather_fusion
  33.2 0.8 select_bitcast_fusion
  34.0 5.5 %all-to-all-start = ((bf16[4,2,4,32,128]{4,3,2,1,0:T(8,128)(2,1)}), bf16[4,2,4,32,128]{4,3,2,1,0:T(8,128)(2,1)}, u32[]{:S(2)}, u32[]{:S(2)}) async-start(bf16[4,2,4,32,128]{4,3,2,1,0:T(8,128)(2,1)} %select_bitcast_fusion), calls=%async_computation | async-start | bytes 524288 | tf_op jit(solution)/shard_map/all_to_all | solution.py:138
  40.1 0.7 copy-done.6
  41.1 3.2 %collective-permute-start.7 = (bf16[2048,128]{1,0:T(8,128)(2,1)S(1)}, bf16[2048,128]{1,0:T(8,128)(2,1)S(1)}, u32[]{:S(2)}, u32[]{:S(2)}) collective-permute-start(bf16[2048,128]{1,0:T(8,128)(2,1)S(1)} %collective-permute-done.6.l1), channel_id=1, source_target_pairs={{0,112},{1,113},{2,114},{3,115},{4,116},{5,117},{6,118},{7,119},{8... | collective-permute-start | bytes 1572872 | tf_op jit(solution)/shard_map/ppermute | solution.py:120
  44.4 8.7 %collective-permute-done.4.r2 = bf16[2048,128]{1,0:T(8,128)(2,1)S(1)} collective-permute-done((bf16[2048,128]{1,0:T(8,128)(2,1)S(1)}, bf16[2048,128]{1,0:T(8,128)(2,1)S(1)}, u32[]{:S(2)}, u32[]{:S(2)}) %collective-permute-start.4) | collective-permute-done | bytes 524320 | tf_op jit(solution)/shard_map/ppermute | solution.py:120
  53.2 3.2 %collective-permute-start.8 = (bf16[2048,128]{1,0:T(8,128)(2,1)S(1)}, bf16[2048,128]{1,0:T(8,128)(2,1)S(1)}, u32[]{:S(2)}, u32[]{:S(2)}) collective-permute-start(bf16[2048,128]{1,0:T(8,128)(2,1)S(1)} %collective-permute-done.7.l2), channel_id=1, source_target_pairs={{0,112},{1,113},{2,114},{3,115},{4,116},{5,117},{6,118},{7,119},{8... | collective-permute-start | bytes 1572872 | tf_op jit(solution)/shard_map/ppermute | solution.py:120
  56.4 9.3 %collective-permute-done.5.r3 = bf16[2048,128]{1,0:T(8,128)(2,1)S(1)} collective-permute-done((bf16[2048,128]{1,0:T(8,128)(2,1)S(1)}, bf16[2048,128]{1,0:T(8,128)(2,1)S(1)}, u32[]{:S(2)}, u32[]{:S(2)}) %collective-permute-start.5) | collective-permute-done | bytes 524320 | tf_op jit(solution)/shard_map/ppermute | solution.py:120
  65.9 3.4 %collective-permute-start.10 = (bf16[1024,128]{1,0:T(8,128)(2,1)S(1)}, bf16[1024,128]{1,0:T(8,128)(2,1)S(1)}, u32[]{:S(2)}, u32[]{:S(2)}) collective-permute-start(bf16[1024,128]{1,0:T(8,128)(2,1)S(1)} %slice.15), channel_id=1, source_target_pairs={{0,112},{1,113},{2,114},{3,115},{4,116},{5,117},{6,118},{7,119},{8... | collective-permute-start | bytes 786440 | tf_op jit(solution)/shard_map/ppermute | solution.py:120
  69.3 2.4 %select_reduce_fusion = (bf16[16,2,2,128]{3,2,1,0:T(2,128)(2,1)S(1)}, bf16[16,2,2,128]{3,2,1,0:T(2,128)(2,1)S(1)}, bf16[16,2,2,128]{3,2,1,0:T(2,128)(2,1)S(1)}, ...) fusion(pred[32]{0:T(512)(128)(4,1)S(1)} %iota_compare_fusion.3,, ...), kind=kLoop, calls=%fused_computation.4 | loop fusion | flops 3612672 | bytes 3784736 | tf_op jit(solution)/shard_map/reduce_sum | solution.py:164
  71.9 1.6 %collective-permute-done.9.r4 = bf16[1024,128]{1,0:T(8,128)(2,1)S(1)} collective-permute-done((bf16[1024,128]{1,0:T(8,128)(2,1)S(1)}, bf16[1024,128]{1,0:T(8,128)(2,1)S(1)}, u32[]{:S(2)}, u32[]{:S(2)}) %collective-permute-start.9) | collective-permute-done | bytes 262176 | tf_op jit(solution)/shard_map/ppermute | solution.py:120
  74.2 0.9 convolution_convert_fusion
  75.2 5.7 %collective-permute-start.11 = (bf16[256,256]{1,0:T(8,128)(2,1)}, bf16[256,256]{1,0:T(8,128)(2,1)S(1)}, u32[]{:S(2)}, u32[]{:S(2)}) collective-permute-start(bf16[256,256]{1,0:T(8,128)(2,1)} %convolution_convert_fusion), channel_id=1, source_target_pairs={{0,0},{1,32},{2,64},{3,96},{4,4},{5,36},{6,68},{7,100},{8,8},{9,40... | collective-permute-start | bytes 393224 | tf_op jit(solution)/shard_map/ppermute | solution.py:120
  80.9 1.0 copy-done.1
  82.0 0.9 copy-done.3
  82.9 23.5 %attention.1 = bf16[8,128,128]{2,1,0:T(8,128)(2,1)S(1)} custom-call(s32[256]{0:T(256)S(1)} %select_reduce_fusion.9.table, s32[8]{0:T(128)S(1)} %dynamic_slice.3.q_blocks, s32[1]{0:T(128)} %copy.77.length, bf16[8,128,128]{2,1,0:T(8,128)(2,1)} %bitcast.1.q_ref, bf16[2048,128]{1,0:T(8,128)(2,1)S(1)} %bitcast.90, ...), custom_call_target="tpu_custom_call" | custom-call | flops 3000000000 | bytes 5000000 | tf_op jit(solution)/shard_map/attention/pallas_call | solution.py:98
  106.4 0.7 copy-done.4
  107.1 7.8 %all-to-all-start.2 = ((bf16[4,2,4,32,128]{4,3,2,1,0:T(8,128)(2,1)}), bf16[4,2,4,32,128]{4,3,2,1,0:T(8,128)(2,1)S(1)}, u32[]{:S(2)}, u32[]{:S(2)}) async-start(bf16[4,2,4,32,128]{4,3,2,1,0:T(8,128)(2,1)} %bitcast.91), calls=%async_computation.2 | async-start | bytes 524288 | tf_op jit(solution)/shard_map/all_to_all | solution.py:154
  115.0 0.7 bitcast_bitcast_fusion
  115.6 4.6 %all-to-all-done.2 = bf16[4,2,4,32,128]{4,3,2,1,0:T(8,128)(2,1)S(1)} async-done(((bf16[4,2,4,32,128]{4,3,2,1,0:T(8,128)(2,1)}), bf16[4,2,4,32,128]{4,3,2,1,0:T(8,128)(2,1)S(1)}, u32[]{:S(2)}, u32[]{:S(2)}) %all-to-all-start.2) | async-done | bytes 262176 | tf_op jit(solution)/shard_map/all_to_all | solution.py:154
  120.2 0.6 gather_fusion.2
  121.0 0.9 reshape.235
  (67 shorter events, 3.3 us)
Async XLA Ops:
  0.6 0.7 copy-start.7
  12.3 5.0 %collective-permute-start = (bf16[4,2,64,128]{3,2,1,0:T(8,128)(2,1)S(1)}, bf16[4,2,64,128]{3,2,1,0:T(8,128)(2,1)S(1)}, u32[]{:S(2)}, u32[]{:S(2)}) collective-permute-start(bf16[4,2,64,128]{3,2,1,0:T(8,128)(2,1)S(1)} %all_to_all.15), channel_id=1, source_target_pairs={{0,4},{1,5},{2,6},{3,7},{4,0},{5,1},{6,2},{7,3},{8,12},{9,13},{10,... | collective-permute-start | bytes 393224 | tf_op jit(solution)/shard_map/ppermute | solution.py:120
  17.2 6.4 %collective-permute-start.1 = (bf16[4,2,64,128]{3,2,1,0:T(8,128)(2,1)S(1)}, bf16[4,2,64,128]{3,2,1,0:T(8,128)(2,1)S(1)}, u32[]{:S(2)}, u32[]{:S(2)}) collective-permute-start(bf16[4,2,64,128]{3,2,1,0:T(8,128)(2,1)S(1)} %collective-permute-done), channel_id=1, source_target_pairs={{0,12},{1,13},{2,14},{3,15},{4,8},{5,9},{6,10},{7,11},{8,4},{9,5},... | collective-permute-start | bytes 393224 | tf_op jit(solution)/shard_map/ppermute | solution.py:120
  20.0 6.3 %collective-permute-start.2 = (bf16[4,2,64,128]{3,2,1,0:T(8,128)(2,1)S(1)}, bf16[4,2,64,128]{3,2,1,0:T(8,128)(2,1)S(1)}, u32[]{:S(2)}, u32[]{:S(2)}) collective-permute-start(bf16[4,2,64,128]{3,2,1,0:T(8,128)(2,1)S(1)} %all_to_all.15), channel_id=1, source_target_pairs={{0,12},{1,13},{2,14},{3,15},{4,8},{5,9},{6,10},{7,11},{8,4},{9,5},... | collective-permute-start | bytes 393224 | tf_op jit(solution)/shard_map/ppermute | solution.py:120
  20.6 11.7 %copy-start.5 = (bf16[1,64,2048]{2,1,0:T(8,128)(2,1)S(1)}, bf16[1,64,2048]{2,1,0:T(8,128)(2,1)}, u32[]{:S(2)}) copy-start(bf16[1,64,2048]{2,1,0:T(8,128)(2,1)} %param.5) | copy-start | bytes 786436
  26.3 14.7 %collective-permute-start.3 = (bf16[2048,128]{1,0:T(8,128)(2,1)S(1)}, bf16[2048,128]{1,0:T(8,128)(2,1)S(1)}, u32[]{:S(2)}, u32[]{:S(2)}) collective-permute-start(bf16[2048,128]{1,0:T(8,128)(2,1)S(1)} %bitcast.88), channel_id=1, source_target_pairs={{0,16},{1,17},{2,18},{3,19},{4,20},{5,21},{6,22},{7,23},{8,24},{9,... | collective-permute-start | bytes 1572872 | tf_op jit(solution)/shard_map/ppermute | solution.py:120
  28.3 12.8 %collective-permute-start.6 = (bf16[2048,128]{1,0:T(8,128)(2,1)S(1)}, bf16[2048,128]{1,0:T(8,128)(2,1)S(1)}, u32[]{:S(2)}, u32[]{:S(2)}) collective-permute-start(bf16[2048,128]{1,0:T(8,128)(2,1)S(1)} %bitcast.89), channel_id=1, source_target_pairs={{0,112},{1,113},{2,114},{3,115},{4,116},{5,117},{6,118},{7,119},{8... | collective-permute-start | bytes 1572872 | tf_op jit(solution)/shard_map/ppermute | solution.py:120
  34.0 46.9 %all-to-all-start = ((bf16[4,2,4,32,128]{4,3,2,1,0:T(8,128)(2,1)}), bf16[4,2,4,32,128]{4,3,2,1,0:T(8,128)(2,1)}, u32[]{:S(2)}, u32[]{:S(2)}) async-start(bf16[4,2,4,32,128]{4,3,2,1,0:T(8,128)(2,1)} %select_bitcast_fusion), calls=%async_computation | async-start | bytes 524288 | tf_op jit(solution)/shard_map/all_to_all | solution.py:138
  40.1 0.7 copy-start.6
  41.0 12.2 %collective-permute-start.4 = (bf16[2048,128]{1,0:T(8,128)(2,1)S(1)}, bf16[2048,128]{1,0:T(8,128)(2,1)S(1)}, u32[]{:S(2)}, u32[]{:S(2)}) collective-permute-start(bf16[2048,128]{1,0:T(8,128)(2,1)S(1)} %collective-permute-done.3.r1), channel_id=1, source_target_pairs={{0,16},{1,17},{2,18},{3,19},{4,20},{5,21},{6,22},{7,23},{8,24},{9,... | collective-permute-start | bytes 1572872 | tf_op jit(solution)/shard_map/ppermute | solution.py:120
  41.1 12.1 %collective-permute-start.7 = (bf16[2048,128]{1,0:T(8,128)(2,1)S(1)}, bf16[2048,128]{1,0:T(8,128)(2,1)S(1)}, u32[]{:S(2)}, u32[]{:S(2)}) collective-permute-start(bf16[2048,128]{1,0:T(8,128)(2,1)S(1)} %collective-permute-done.6.l1), channel_id=1, source_target_pairs={{0,112},{1,113},{2,114},{3,115},{4,116},{5,117},{6,118},{7,119},{8... | collective-permute-start | bytes 1572872 | tf_op jit(solution)/shard_map/ppermute | solution.py:120
  53.1 12.6 %collective-permute-start.5 = (bf16[2048,128]{1,0:T(8,128)(2,1)S(1)}, bf16[2048,128]{1,0:T(8,128)(2,1)S(1)}, u32[]{:S(2)}, u32[]{:S(2)}) collective-permute-start(bf16[2048,128]{1,0:T(8,128)(2,1)S(1)} %collective-permute-done.4.r2), channel_id=1, source_target_pairs={{0,16},{1,17},{2,18},{3,19},{4,20},{5,21},{6,22},{7,23},{8,24},{9,... | collective-permute-start | bytes 1572872 | tf_op jit(solution)/shard_map/ppermute | solution.py:120
  53.2 16.1 %copy-start = (bf16[2048,128]{1,0:T(8,128)(2,1)}, bf16[2048,128]{1,0:T(8,128)(2,1)S(1)}, u32[]{:S(2)}) copy-start(bf16[2048,128]{1,0:T(8,128)(2,1)S(1)} %collective-permute-done.7.l2) | copy-start | bytes 1572868
  53.2 12.7 %collective-permute-start.8 = (bf16[2048,128]{1,0:T(8,128)(2,1)S(1)}, bf16[2048,128]{1,0:T(8,128)(2,1)S(1)}, u32[]{:S(2)}, u32[]{:S(2)}) collective-permute-start(bf16[2048,128]{1,0:T(8,128)(2,1)S(1)} %collective-permute-done.7.l2), channel_id=1, source_target_pairs={{0,112},{1,113},{2,114},{3,115},{4,116},{5,117},{6,118},{7,119},{8... | collective-permute-start | bytes 1572872 | tf_op jit(solution)/shard_map/ppermute | solution.py:120
  65.8 7.7 %collective-permute-start.9 = (bf16[1024,128]{1,0:T(8,128)(2,1)S(1)}, bf16[1024,128]{1,0:T(8,128)(2,1)S(1)}, u32[]{:S(2)}, u32[]{:S(2)}) collective-permute-start(bf16[1024,128]{1,0:T(8,128)(2,1)S(1)} %slice.14), channel_id=1, source_target_pairs={{0,16},{1,17},{2,18},{3,19},{4,20},{5,21},{6,22},{7,23},{8,24},{9,... | collective-permute-start | bytes 786440 | tf_op jit(solution)/shard_map/ppermute | solution.py:120
  65.9 7.5 %collective-permute-start.10 = (bf16[1024,128]{1,0:T(8,128)(2,1)S(1)}, bf16[1024,128]{1,0:T(8,128)(2,1)S(1)}, u32[]{:S(2)}, u32[]{:S(2)}) collective-permute-start(bf16[1024,128]{1,0:T(8,128)(2,1)S(1)} %slice.15), channel_id=1, source_target_pairs={{0,112},{1,113},{2,114},{3,115},{4,116},{5,117},{6,118},{7,119},{8... | collective-permute-start | bytes 786440 | tf_op jit(solution)/shard_map/ppermute | solution.py:120
  73.4 0.7 copy-start.2
  75.2 39.8 %collective-permute-start.11 = (bf16[256,256]{1,0:T(8,128)(2,1)}, bf16[256,256]{1,0:T(8,128)(2,1)S(1)}, u32[]{:S(2)}, u32[]{:S(2)}) collective-permute-start(bf16[256,256]{1,0:T(8,128)(2,1)} %convolution_convert_fusion), channel_id=1, source_target_pairs={{0,0},{1,32},{2,64},{3,96},{4,4},{5,36},{6,68},{7,100},{8,8},{9,40... | collective-permute-start | bytes 393224 | tf_op jit(solution)/shard_map/ppermute | solution.py:120
  80.9 1.0 copy-start.1
  82.0 0.9 copy-start.3
  106.4 0.7 copy-start.4
  107.1 13.1 %all-to-all-start.2 = ((bf16[4,2,4,32,128]{4,3,2,1,0:T(8,128)(2,1)}), bf16[4,2,4,32,128]{4,3,2,1,0:T(8,128)(2,1)S(1)}, u32[]{:S(2)}, u32[]{:S(2)}) async-start(bf16[4,2,4,32,128]{4,3,2,1,0:T(8,128)(2,1)} %bitcast.91), calls=%async_computation.2 | async-start | bytes 524288 | tf_op jit(solution)/shard_map/all_to_all | solution.py:154

commit v2 on v0

v2 whole, which is shorter than its diff:
```python
import jax
import jax.numpy as jnp
from jax import lax
from jax.experimental import pallas as pl
from jax.experimental.pallas import tpu as pltpu
from jax.sharding import PartitionSpec as P

QUERY_HEADS = 16
KEY_VALUE_HEADS = 4
GROUP = QUERY_HEADS // KEY_VALUE_HEADS
HEAD = 128
WINDOW = 4096
BLOCK = 32
BLOCKS = 256
NZ, NX, NY = 8, 4, 4
N_BLK = NZ * NX * NY
PLANE = NX * NY
KEY_BLOCKS = 2 * NZ * NY
Q_BLOCKS = 2 * PLANE
ROWS = GROUP * BLOCK
KEYS = KEY_BLOCKS * BLOCK
JOINED = 4
CHUNK_BLOCKS = 8
CHUNK = CHUNK_BLOCKS * BLOCK
MESSAGE = 2 * ROWS + 16
SCALE = HEAD**-0.5 * 1.4426950408889634
NEG = -1e30

SMEM = pl.BlockSpec(memory_space=pltpu.SMEM)
VMEM = pl.BlockSpec(memory_space=pltpu.VMEM)
PARAMS = pltpu.CompilerParams(vmem_limit_bytes=40 * 1024 * 1024)


def split_kv_kernel(heads, kv_ref, o_ref):
    for y in range(NY):
        o_ref[y] = kv_ref[:, pl.ds(pl.multiple_of(heads[y] * HEAD, HEAD), HEAD)]


def split_q_kernel(heads, q_ref, o_ref):
    for y in range(NY):
        for g in range(GROUP):
            column = pl.multiple_of((heads[y] * GROUP + g) * HEAD, HEAD)
            for j in range(2):
                tile = q_ref[j * BLOCK : (j + 1) * BLOCK, pl.ds(column, HEAD)]
                for x in range(NX):
                    o_ref[x * NY + y, j * ROWS + g * BLOCK : j * ROWS + (g + 1) * BLOCK] = tile


def arrange_kernel(rank, offset, c0, r1, r2, r3, l1, l2, l3, r4, l4, k_ref, v_ref, pick_ref):
    v_ref[:, HEAD:] = jnp.ones((KEYS, HEAD), jnp.bfloat16)
    pieces = [(c0, 0), (l1, 1), (l2, 2), (l3, 3), (r4, 4), (l4, 4), (r3, 5), (r2, 6), (r1, 7)]
    for piece, zrel in pieces:
        lines = range(NY)
        if piece is r4:
            lines = range(NY // 2)
        if piece is l4:
            lines = range(NY // 2, NY)
        for at, y in enumerate(lines):
            for j in range(2):
                row = pl.multiple_of(rank[(zrel * NY + y) * 2 + j] * BLOCK, BLOCK)
                k_ref[pl.ds(row, BLOCK), :] = piece[at * 128 + j * BLOCK : at * 128 + (j + 1) * BLOCK, :]
                v_ref[pl.ds(row, BLOCK), :HEAD] = piece[at * 128 + 64 + j * BLOCK : at * 128 + 64 + (j + 1) * BLOCK, :]
    some = 16
    line = lax.broadcasted_iota(jnp.int32, (NX * some, some * BLOCK), 0)
    column = lax.broadcasted_iota(jnp.int32, (NX * some, some * BLOCK), 1)
    wanted = (line % some) * BLOCK + offset[0] + (line // some) * NY
    select = jnp.where(column == wanted, 1.0, 0.0).astype(jnp.bfloat16)
    for c in range(KEY_BLOCKS // some):
        rows = slice(c * some * BLOCK, (c + 1) * some * BLOCK)
        k = jnp.dot(select, k_ref[rows, :], preferred_element_type=jnp.float32).astype(jnp.bfloat16)
        v = jnp.dot(select, v_ref[rows, :HEAD], preferred_element_type=jnp.float32).astype(jnp.bfloat16)
        for x in range(NX):
            pick_ref[x, c * some : (c + 1) * some, :HEAD] = k[x * some : (x + 1) * some]
            pick_ref[x, c * some : (c + 1) * some, HEAD:] = v[x * some : (x + 1) * some]


def attention_kernel(q_order, q_ids, lows, highs, q_ref, k_ref, v_ref, kpos_ref, o_ref, s_scr, top_scr, acc_scr, stat):
    lane = lax.broadcasted_iota(jnp.int32, (ROWS, 128), 1)
    token = lax.broadcasted_iota(jnp.int32, (BLOCK, CHUNK), 0)

    def one_group(i, carry):
        low, high = lows[i], highs[i]
        q = jnp.concatenate([q_ref[q_order[i * JOINED + u]] for u in range(JOINED)], axis=0)
        top_scr[...] = jnp.full((JOINED * ROWS, 128), NEG, jnp.float32)
        acc_scr[...] = jnp.zeros((JOINED * ROWS, 2 * HEAD), jnp.float32)

        def scores(chunk, carry):
            start = pl.multiple_of(chunk * CHUNK, CHUNK)
            k = k_ref[pl.ds(start, CHUNK), :]
            s = lax.dot_general(q, k, (((1,), (1,)), ((), ())), preferred_element_type=jnp.float32)
            kpos = kpos_ref[pl.ds(chunk, 1), :]
            for u in range(JOINED):
                distance = (q_ids[i * JOINED + u] * BLOCK + token) - kpos
                bias = jnp.where((distance >= 0) & (distance < WINDOW), 0.0, NEG)
                for g in range(GROUP):
                    rows = slice(u * ROWS + g * BLOCK, u * ROWS + (g + 1) * BLOCK)
                    part = s[rows] + bias
                    s_scr[chunk - low, rows, :] = part
                    top_scr[rows] = jnp.maximum(top_scr[rows], jnp.maximum(part[:, :128], part[:, 128:]))
            return carry

        lax.fori_loop(low, high, scores, 0)
        top = jnp.max(top_scr[...], axis=1, keepdims=True) * SCALE
        top_scr[...] = jnp.broadcast_to(top, (JOINED * ROWS, 128))

        def weigh(chunk, carry):
            start = pl.multiple_of(chunk * CHUNK, CHUNK)
            top = top_scr[...]
            s = s_scr[chunk - low]
            p = jnp.exp2(s * SCALE - jnp.concatenate([top, top], axis=1)).astype(jnp.bfloat16)
            acc_scr[...] += jnp.dot(p, v_ref[pl.ds(start, CHUNK), :], preferred_element_type=jnp.float32)
            return carry

        lax.fori_loop(low, high, weigh, 0)
        for u in range(JOINED):
            rows = slice(u * ROWS, (u + 1) * ROWS)
            block = q_order[i * JOINED + u]
            total = acc_scr[rows, HEAD:]
            out = acc_scr[rows, :HEAD] / jnp.maximum(total, 1e-30)
            o_ref[block // 2, pl.ds(pl.multiple_of(block % 2 * ROWS, ROWS), ROWS), :] = out.astype(jnp.bfloat16)
            old = jnp.where(lane == block, top_scr[rows], stat[...])
            stat[...] = jnp.where(lane == block + Q_BLOCKS, total, old)
        return carry

    stat[...] = jnp.zeros((ROWS, 128), jnp.float32)
    lax.fori_loop(0, Q_BLOCKS // JOINED, one_group, 0)
    turned = stat[...].T
    for d in range(PLANE):
        value = jnp.concatenate(
            [turned[2 * d : 2 * d + 2], turned[Q_BLOCKS + 2 * d : Q_BLOCKS + 2 * d + 2]], axis=0
        )
        first = value.astype(jnp.bfloat16).astype(jnp.float32)
        second = (value - first).astype(jnp.bfloat16).astype(jnp.float32)
        third = value - first - second
        rows = jnp.concatenate([first, second, third, jnp.zeros_like(first)], axis=0)
        o_ref[d, 2 * ROWS :, :] = rows.astype(jnp.bfloat16)


def combine_kernel(heads, blocks, length, m_ref, o_ref):
    values = []
    for d in range(PLANE):
        rows = m_ref[d, 2 * ROWS :, :].astype(jnp.float32)
        values.append(rows[0:4] + rows[4:8] + rows[8:12])
    weights = [None] * PLANE
    for y in range(NY):
        sources = [x * NY + y for x in range(NX)]
        top = values[sources[0]][0:2]
        for d in sources[1:]:
            top = jnp.maximum(top, values[d][0:2])
        parts = [jnp.exp2(values[d][0:2] - top) * values[d][2:4] for d in sources]
        total = parts[0] + parts[1] + parts[2] + parts[3]
        for d, part in zip(sources, parts):
            weights[d] = part / total
    matrix = jnp.concatenate(weights + [jnp.zeros((128 - Q_BLOCKS, 128), jnp.float32)], axis=0).T
    token = lax.broadcasted_iota(jnp.int32, (ROWS, HEAD), 0) % BLOCK
    for y in range(NY):
        for j in range(2):
            out = jnp.zeros((ROWS, HEAD), jnp.float32)
            for x in range(NX):
                d = x * NY + y
                weight = matrix[:, 2 * d + j : 2 * d + j + 1]
                out += weight * m_ref[d, j * ROWS : (j + 1) * ROWS, :].astype(jnp.float32)
            out = jnp.where(blocks[j] * BLOCK + token < length[0], out, 0.0).astype(jnp.bfloat16)
            for g in range(GROUP):
                column = pl.multiple_of((heads[y] * GROUP + g) * HEAD, HEAD)
                o_ref[j * BLOCK : (j + 1) * BLOCK, pl.ds(column, HEAD)] = out[g * BLOCK : (g + 1) * BLOCK]


def ranks(ids):
    return jnp.sum(ids[..., None, :] < ids[..., :, None], axis=-1, dtype=jnp.int32)


def placed(values, rank):
    places = jnp.arange(values.shape[-1], dtype=jnp.int32)
    return jnp.sum(jnp.where(rank[..., None, :] == places[:, None], values[..., None, :], 0), axis=-1, dtype=jnp.int32)


def body(query, rotated_key_value, lengths, block_map, segment_head):
    place = lax.axis_index("blk")
    z, x, y = place // 16, (place // 4) % 4, place % 4
    y_groups = [[4 * g + i for i in range(4)] for g in range(N_BLK // 4)]
    x_groups = [[16 * a + 4 * i + c for i in range(4)] for a in range(NZ) for c in range(NY)]
    planes = [[16 * a + i for i in range(16)] for a in range(NZ)]

    def move(value, target):
        return lax.ppermute(value, "blk", [(s, target(s // 16, (s // 4) % 4, s % 4)) for s in range(N_BLK)])

    def index(zz, xx, yy):
        return (zz % NZ) * 16 + xx * 4 + yy

    def exchange(value, groups):
        return lax.all_to_all(value, "blk", 0, 0, axis_index_groups=groups, tiled=True)

    kv = pl.pallas_call(
        split_kv_kernel,
        out_shape=jax.ShapeDtypeStruct((NY, 128, HEAD), jnp.bfloat16),
        in_specs=[SMEM, VMEM],
        out_specs=VMEM,
        name="split_kv",
    )(segment_head, rotated_key_value.reshape(128, KEY_VALUE_HEADS * HEAD))
    own = exchange(kv, y_groups).reshape(NY * 128, HEAD)
    right = lambda v: move(v, lambda a, b, c: index(a + 1, b, c))
    left = lambda v: move(v, lambda a, b, c: index(a - 1, b, c))
    r1, l1 = right(own), left(own)
    q = pl.pallas_call(
        split_q_kernel,
        out_shape=jax.ShapeDtypeStruct((PLANE, 2 * ROWS, HEAD), jnp.bfloat16),
        in_specs=[SMEM, VMEM],
        out_specs=VMEM,
        name="split_q",
    )(segment_head, query.reshape(2 * BLOCK, QUERY_HEADS * HEAD))
    q = exchange(q, planes).reshape(Q_BLOCKS, ROWS, HEAD)
    r2, l2 = right(r1), left(l1)
    r3, l3 = right(r2), left(l2)
    half = own.shape[0] // 2
    r4, l4 = right(r3[:half]), left(l3[half:])

    ids = block_map.reshape(NZ, NX, NY, 2).transpose(1, 0, 2, 3).reshape(NX, KEY_BLOCKS)
    rank = ranks(ids)
    ordered = placed(ids, rank)
    mine = lax.dynamic_index_in_dim(ordered, x, 0, keepdims=False)
    my_rank = lax.dynamic_index_in_dim(rank, x, 0, keepdims=False).reshape(NZ, 2 * NY)
    my_rank = lax.dynamic_slice_in_dim(jnp.concatenate([my_rank, my_rank], axis=0), z, NZ, 0).reshape(KEY_BLOCKS)
    q_ids = lax.dynamic_slice_in_dim(block_map, z * Q_BLOCKS, Q_BLOCKS)
    q_rank = ranks(q_ids)
    q_order = placed(jnp.arange(Q_BLOCKS, dtype=jnp.int32), q_rank)
    q_sorted = placed(q_ids, q_rank)
    grouped = q_sorted.reshape(Q_BLOCKS // JOINED, JOINED)
    lows = jnp.sum(mine[None, :] < grouped[:, :1] - WINDOW // BLOCK, axis=1, dtype=jnp.int32) // CHUNK_BLOCKS
    highs = jnp.sum(mine[None, :] <= grouped[:, -1:], axis=1, dtype=jnp.int32)
    highs = (highs + CHUNK_BLOCKS - 1) // CHUNK_BLOCKS
    kpos = mine[:, None] * BLOCK + jnp.arange(BLOCK, dtype=jnp.int32)[None, :]
    kpos = kpos.reshape(KEYS // CHUNK, CHUNK)

    offset = ((z % 2) * 16 + z // 2).reshape(1)
    k, v, pick = pl.pallas_call(
        arrange_kernel,
        out_shape=(
            jax.ShapeDtypeStruct((KEYS, HEAD), jnp.bfloat16),
            jax.ShapeDtypeStruct((KEYS, 2 * HEAD), jnp.bfloat16),
            jax.ShapeDtypeStruct((NX, KEY_BLOCKS, 2 * HEAD), jnp.bfloat16),
        ),
        in_specs=[SMEM] * 2 + [VMEM] * 9,
        out_specs=(VMEM,) * 3,
        name="arrange",
    )(my_rank, offset, own, r1, r2, r3, l1, l2, l3, r4, l4)

    out = pl.pallas_call(
        attention_kernel,
        out_shape=jax.ShapeDtypeStruct((PLANE, MESSAGE, HEAD), jnp.bfloat16),
        in_specs=[SMEM] * 4 + [VMEM] * 4,
        out_specs=VMEM,
        scratch_shapes=[
            pltpu.VMEM((KEYS // CHUNK, JOINED * ROWS, CHUNK), jnp.float32),
            pltpu.VMEM((JOINED * ROWS, 128), jnp.float32),
            pltpu.VMEM((JOINED * ROWS, 2 * HEAD), jnp.float32),
            pltpu.VMEM((ROWS, 128), jnp.float32),
        ],
        compiler_params=PARAMS,
        cost_estimate=pl.CostEstimate(flops=3_000_000_000, bytes_accessed=4_000_000, transcendentals=5_000_000),
        name="attention",
    )(q_order, q_sorted, lows, highs, q, k, v, kpos)

    pick = exchange(pick, x_groups).reshape(BLOCKS, 2 * HEAD)
    blocks = jnp.arange(BLOCKS, dtype=jnp.int32)
    position = blocks * BLOCK + offset + 4 * x
    choose = (ordered.reshape(1, BLOCKS) == blocks[:, None]) & (position < lengths[0])[:, None]
    cache = jnp.dot(choose.astype(jnp.bfloat16), pick, preferred_element_type=jnp.float32).astype(jnp.bfloat16)
    cache = move(cache, lambda a, b, c: index(2 * c + a % 2, b, a // 2))
    cache = cache.reshape(BLOCKS, 2, HEAD).transpose(1, 0, 2)[None, :, None]

    out = exchange(out, planes)
    my_blocks = lax.dynamic_slice_in_dim(block_map, 2 * place, 2)
    attended = pl.pallas_call(
        combine_kernel,
        out_shape=jax.ShapeDtypeStruct((2 * BLOCK, QUERY_HEADS * HEAD), jnp.bfloat16),
        in_specs=[SMEM] * 3 + [VMEM],
        out_specs=VMEM,
        name="combine",
    )(segment_head, my_blocks, lengths, out)
    return attended.reshape(1, 2 * BLOCK, QUERY_HEADS * HEAD), cache


def solution(mesh):
    return jax.shard_map(
        body,
        mesh=mesh,
        in_specs=(P("req", "blk", None), P("req", None, "blk", None), P("req"), P(), P()),
        out_specs=(P("req", "blk", None), P("req", None, "blk", None, None)),
        check_vma=False,
    )
```

time: 323 us -> 107 us (0.33)
  local copies, waits for them, and re-layouts: 116 us -> 8.35 us
  waiting for transfers between devices: 122 us -> 20.9 us
  matrix products: 31.9 us -> 0.23 us
  Pallas kernels: 0 us -> 29.6 us
  starting transfers between devices: 15.4 us -> 43.4 us
  other arithmetic: 19.4 us -> 1.14 us
  between operations: 14.9 us -> 1.49 us
    all_gather x1 -> x0, waiting for transfers between devices: 117 us -> none  [body(): segment_piece = lax.all_gather(rotated_key_value, 'blk', axis=2, tiled=True)]
    unnamed x4 -> x26, local copies, waits for them, and re-layouts: 69.1 us -> 3.85 us
    slice x1 -> x2, local copies, waits for them, and re-layouts: 32.7 us -> 0.01 us  [body(): r4, l4 = (right(r3[:half]), left(l3[half:]))]
    dot_general x2 -> x1, matrix products: 31.9 us -> 0.23 us  [body(): jnp.dot(choose.astype(jnp.bfloat16), pick, preferred_element_type=jnp.flo...]
    pallas_call x0 -> x5, Pallas kernels: none -> 29.6 us  [the longest x1 20.4 us: body(): pl.pallas_call(attention_kernel, out_shape=jax.ShapeDtypeStruct((PLANE, M...]
    ppermute x0 -> x9, waiting for transfers between devices: none -> 20.9 us  [move(): lax.ppermute(value, 'blk', [(s, target(s // 16, s // 4 % 4, s % 4)) for s...]
    ppermute x0 -> x9, starting transfers between devices: none -> 19 us  [move(): lax.ppermute(value, 'blk', [(s, target(s // 16, s // 4 % 4, s % 4)) for s...]
    reduce_sum x1 -> x5, other arithmetic: 15.2 us -> 0.88 us  [the longest x2 0.4 us: ranks(): jnp.sum(ids[..., None, :] < ids[..., :, None], axis=-1, dtype=jnp.int32)]
  transfers between devices with their start and end apart: 2 -> 13, of which waited for: 2 -> 7; matrix products, arithmetic and copies ran while one was open for 6% -> 6% of each run, Pallas kernels for 0% -> 24%
where the time goes in v2:
time: 107 us; the launch traced here: 105 us
  starting transfers between devices  43.4 us (41%)
  Pallas kernels  29.6 us (28%)
  waiting for transfers between devices  20.9 us (20%)
  local copies, waits for them, and re-layouts  8.35 us (8%)
  between operations  1.49 us (1%)
  other arithmetic  1.14 us (1%)
    all_to_all x4, starting transfers between devices, exchange(): lax.all_to_all(value, 'blk', 0, 0, axis_index_groups=groups, tiled=True)  24.4 us
    ppermute x9, waiting for transfers between devices, move(): lax.ppermute(value, 'blk', [(s, target(s // 16, s // 4 % 4, s % 4)) for s...  20.9 us
    pallas_call x1, Pallas kernels, body(): pl.pallas_call(attention_kernel, out_shape=jax.ShapeDtypeStruct((PLANE, M...  20.4 us
    ppermute x9, starting transfers between devices, move(): lax.ppermute(value, 'blk', [(s, target(s // 16, s // 4 % 4, s % 4)) for s...  19 us
    unnamed x26, local copies, waits for them, and re-layouts  3.85 us
    pallas_call x1, Pallas kernels, body(): pl.pallas_call(combine_kernel, out_shape=jax.ShapeDtypeStruct((2 * BLOCK,...  2.79 us
    pallas_call x1, Pallas kernels, body(): pl.pallas_call(arrange_kernel, out_shape=(jax.ShapeDtypeStruct((KEYS, HEA...  2.72 us
  transfers between devices with their start and end apart: 13, of which 7 were waited for; matrix products, arithmetic and copies ran while one was open for 6% of the time, Pallas kernels for 24%

profile of v2, /device:TPU:8, one launch (start us, length us, event | category | flops | bytes accessed | tf_op | source)
XLA Modules:
  0.0 105.1 jit_solution(2961764150990919811)
XLA Ops:
  0.6 1.6 %split_kv.1 = bf16[4,128,128]{2,1,0:T(8,128)(2,1)} custom-call(s32[4]{0:T(128)} %heads.5, bf16[128,512]{1,0:T(8,128)(2,1)} %bitcast.31), custom_call_target="tpu_custom_call" | custom-call | tf_op jit(solution)/shard_map/split_kv/pallas_call | solution.py:194
  2.2 5.5 %all-to-all-start.1 = ((bf16[4,128,128]{2,1,0:T(8,128)(2,1)}), bf16[4,128,128]{2,1,0:T(8,128)(2,1)S(1)}, u32[]{:S(2)}, u32[]{:S(2)}) async-start(bf16[4,128,128]{2,1,0:T(8,128)(2,1)} %split_kv.1), calls=%async_computation.1 | async-start | bytes 262144 | tf_op jit(solution)/shard_map/all_to_all | solution.py:192
  7.7 0.8 reshape.72
  8.6 0.8 dynamic_slice.17
  9.8 0.3 copy.12
  10.2 2.1 %split_q.1 = bf16[16,256,128]{2,1,0:T(8,128)(2,1)} custom-call(s32[4]{0:T(128)} %heads.5, bf16[64,2048]{1,0:T(8,128)(2,1)} %bitcast.27), custom_call_target="tpu_custom_call" | custom-call | tf_op jit(solution)/shard_map/split_q/pallas_call | solution.py:205
  12.3 6.7 %all-to-all-start = ((bf16[16,256,128]{2,1,0:T(8,128)(2,1)}), bf16[16,256,128]{2,1,0:T(8,128)(2,1)S(1)}, u32[]{:S(2)}, u32[]{:S(2)}) async-start(bf16[16,256,128]{2,1,0:T(8,128)(2,1)} %split_q.1), calls=%async_computation | async-start | bytes 2097152 | tf_op jit(solution)/shard_map/all_to_all | solution.py:192
  19.0 0.2 convert_reduce_fusion
  19.6 5.9 %collective-permute-start.3 = (bf16[512,128]{1,0:T(8,128)(2,1)S(1)}, bf16[512,128]{1,0:T(8,128)(2,1)S(1)}, u32[]{:S(2)}, u32[]{:S(2)}) collective-permute-start(bf16[512,128]{1,0:T(8,128)(2,1)S(1)} %bitcast.24), channel_id=1, source_target_pairs={{0,112},{1,113},{2,114},{3,115},{4,116},{5,117},{6,118},{7,119},{8... | collective-permute-start | bytes 393224 | tf_op jit(solution)/shard_map/ppermute | solution.py:186
  25.5 2.5 %collective-permute-done.3.l1 = bf16[512,128]{1,0:T(8,128)(2,1)S(1)} collective-permute-done((bf16[512,128]{1,0:T(8,128)(2,1)S(1)}, bf16[512,128]{1,0:T(8,128)(2,1)S(1)}, u32[]{:S(2)}, u32[]{:S(2)}) %collective-permute-start.3) | collective-permute-done | bytes 131104 | tf_op jit(solution)/shard_map/ppermute | solution.py:186
  28.0 3.7 %collective-permute-start.4 = (bf16[512,128]{1,0:T(8,128)(2,1)S(1)}, bf16[512,128]{1,0:T(8,128)(2,1)S(1)}, u32[]{:S(2)}, u32[]{:S(2)}) collective-permute-start(bf16[512,128]{1,0:T(8,128)(2,1)S(1)} %collective-permute-done.3.l1), channel_id=1, source_target_pairs={{0,112},{1,113},{2,114},{3,115},{4,116},{5,117},{6,118},{7,119},{8... | collective-permute-start | bytes 393224 | tf_op jit(solution)/shard_map/ppermute | solution.py:186
  32.2 1.9 %collective-permute-done.4.l2 = bf16[512,128]{1,0:T(8,128)(2,1)S(1)} collective-permute-done((bf16[512,128]{1,0:T(8,128)(2,1)S(1)}, bf16[512,128]{1,0:T(8,128)(2,1)S(1)}, u32[]{:S(2)}, u32[]{:S(2)}) %collective-permute-start.4) | collective-permute-done | bytes 131104 | tf_op jit(solution)/shard_map/ppermute | solution.py:186
  34.2 3.7 %collective-permute-start.5 = (bf16[512,128]{1,0:T(8,128)(2,1)S(1)}, bf16[512,128]{1,0:T(8,128)(2,1)S(1)}, u32[]{:S(2)}, u32[]{:S(2)}) collective-permute-start(bf16[512,128]{1,0:T(8,128)(2,1)S(1)} %collective-permute-done.4.l2), channel_id=1, source_target_pairs={{0,112},{1,113},{2,114},{3,115},{4,116},{5,117},{6,118},{7,119},{8... | collective-permute-start | bytes 393224 | tf_op jit(solution)/shard_map/ppermute | solution.py:186
  37.9 2.5 %collective-permute-done.5.l3 = bf16[512,128]{1,0:T(8,128)(2,1)S(1)} collective-permute-done((bf16[512,128]{1,0:T(8,128)(2,1)S(1)}, bf16[512,128]{1,0:T(8,128)(2,1)S(1)}, u32[]{:S(2)}, u32[]{:S(2)}) %collective-permute-start.5) | collective-permute-done | bytes 131104 | tf_op jit(solution)/shard_map/ppermute | solution.py:186
  40.4 3.8 %collective-permute-start.7 = (bf16[256,128]{1,0:T(8,128)(2,1)S(1)}, bf16[256,128]{1,0:T(8,128)(2,1)S(1)}, u32[]{:S(2)}, u32[]{:S(2)}) collective-permute-start(bf16[256,128]{1,0:T(8,128)(2,1)S(1)} %slice.17), channel_id=1, source_target_pairs={{0,112},{1,113},{2,114},{3,115},{4,116},{5,117},{6,118},{7,119},{8... | collective-permute-start | bytes 196616 | tf_op jit(solution)/shard_map/ppermute | solution.py:186
  44.5 0.7 reshape.77.rank
  45.1 1.0 collective-permute-done.7.l4
  46.1 3.8 %collective-permute-done.6.r4 = bf16[256,128]{1,0:T(8,128)(2,1)S(1)} collective-permute-done((bf16[256,128]{1,0:T(8,128)(2,1)S(1)}, bf16[256,128]{1,0:T(8,128)(2,1)S(1)}, u32[]{:S(2)}, u32[]{:S(2)}) %collective-permute-start.6) | collective-permute-done | bytes 65568 | tf_op jit(solution)/shard_map/ppermute | solution.py:186
  50.0 0.6 copy-done.11
  50.5 2.7 %arrange.1 = (bf16[2048,128]{1,0:T(8,128)(2,1)}, bf16[2048,256]{1,0:T(8,128)(2,1)}, bf16[4,64,256]{2,1,0:T(8,128)(2,1)}) custom-call(s32[64]{0:T(128)} %reshape.77.rank, s32[1]{0:T(128)} %bitcast.5.offset, bf16[512,128]{1,0:T(8,128)(2,1)} %bitcast.26, bf16[512,128]{1,0:T(8,128)(2,1)} %copy-done.7, bf16[512,128]{1,0:T(8,128)(2,1)} %copy-done.9, ...), custom_call_target="tpu_custom_call" | custom-call | tf_op jit(solution)/shard_map/arrange/pallas_call | solution.py:236
  53.2 4.7 %all-to-all-start.3 = ((bf16[4,64,256]{2,1,0:T(8,128)(2,1)}), bf16[4,64,256]{2,1,0:T(8,128)(2,1)S(1)}, u32[]{:S(2)}, u32[]{:S(2)}) async-start(bf16[4,64,256]{2,1,0:T(8,128)(2,1)} %get-tuple-element.7), calls=%async_computation.3 | async-start | bytes 262144 | tf_op jit(solution)/shard_map/all_to_all | solution.py:192
  58.0 1.2 %copy-done = bf16[2048,256]{1,0:T(8,128)(2,1)S(1)} copy-done((bf16[2048,256]{1,0:T(8,128)(2,1)S(1)}, bf16[2048,256]{1,0:T(8,128)(2,1)}, u32[]{:S(2)}) %copy-start) | copy-done | bytes 1048600
  59.2 1.0 copy-done.1
  60.2 20.4 %attention.1 = bf16[16,272,128]{2,1,0:T(8,128)(2,1)} custom-call(s32[32]{0:T(128)S(1)} %get-tuple-element.13.q_order, s32[32]{0:T(128)S(1)} %get-tuple-element.12.q_ids, s32[8]{0:T(128)S(1)} %get-tuple-element.17.lows, s32[8]{0:T(128)S(1)} %get-tuple-element.16.highs, bf16[32,128,128]{2,1,0:T(8,128)(2,1)S(1)} %bitcast.23, bf16[2048,128]{1,0:T(8,128)(2,1)S(1)} %copy-done.1, ...), custom_call_target="tpu_custom_call" | custom-call | flops 3000000000 | bytes 4000000 | tf_op jit(solution)/shard_map/attention/pallas_call | solution.py:248
  80.7 7.5 %all-to-all-start.2 = ((bf16[16,272,128]{2,1,0:T(8,128)(2,1)}), bf16[16,272,128]{2,1,0:T(8,128)(2,1)S(1)}, u32[]{:S(2)}, u32[]{:S(2)}) async-start(bf16[16,272,128]{2,1,0:T(8,128)(2,1)} %attention.1), calls=%async_computation.2 | async-start | bytes 2228224 | tf_op jit(solution)/shard_map/all_to_all | solution.py:192
  88.9 0.2 convolution_convert_fusion
  89.1 1.9 %collective-permute-start.8 = (bf16[256,256]{1,0:T(8,128)(2,1)S(1)}, bf16[256,256]{1,0:T(8,128)(2,1)S(1)}, u32[]{:S(2)}, u32[]{:S(2)}) collective-permute-start(bf16[256,256]{1,0:T(8,128)(2,1)S(1)} %convolution_convert_fusion), channel_id=1, source_target_pairs={{0,0},{1,32},{2,64},{3,96},{4,4},{5,36},{6,68},{7,100},{8,8},{9,40... | collective-permute-start | bytes 393224 | tf_op jit(solution)/shard_map/ppermute | solution.py:186
  91.1 0.6 dynamic_slice.16.blocks
  91.7 9.0 %collective-permute-done.8 = bf16[256,256]{1,0:T(8,128)(2,1)S(1)} collective-permute-done((bf16[256,256]{1,0:T(8,128)(2,1)S(1)}, bf16[256,256]{1,0:T(8,128)(2,1)S(1)}, u32[]{:S(2)}, u32[]{:S(2)}) %collective-permute-start.8) | collective-permute-done | bytes 131104 | tf_op jit(solution)/shard_map/ppermute | solution.py:186
  100.7 0.7 bitcast_bitcast_fusion
  101.3 1.0 copy-done.2
  102.3 2.8 %combine.1 = bf16[64,2048]{1,0:T(8,128)(2,1)} custom-call(s32[4]{0:T(128)} %heads.5, s32[2]{0:T(128)} %dynamic_slice.16.blocks, s32[1]{0:T(128)} %copy.18.length, bf16[16,272,128]{2,1,0:T(8,128)(2,1)} %copy-done.2), custom_call_target="tpu_custom_call" | custom-call | tf_op jit(solution)/shard_map/combine/pallas_call | solution.py:274
  (55 shorter events, 1.9 us)
Async XLA Ops:
  2.2 10.0 %all-to-all-start.1 = ((bf16[4,128,128]{2,1,0:T(8,128)(2,1)}), bf16[4,128,128]{2,1,0:T(8,128)(2,1)S(1)}, u32[]{:S(2)}, u32[]{:S(2)}) async-start(bf16[4,128,128]{2,1,0:T(8,128)(2,1)} %split_kv.1), calls=%async_computation.1 | async-start | bytes 262144 | tf_op jit(solution)/shard_map/all_to_all | solution.py:192
  12.2 19.6 %copy-start.3 = (bf16[4,128,128]{2,1,0:T(8,128)(2,1)}, bf16[4,128,128]{2,1,0:T(8,128)(2,1)S(1)}, u32[]{:S(2)}) copy-start(bf16[4,128,128]{2,1,0:T(8,128)(2,1)S(1)} %all-to-all-done.1) | copy-start | bytes 393220
  12.3 41.0 %all-to-all-start = ((bf16[16,256,128]{2,1,0:T(8,128)(2,1)}), bf16[16,256,128]{2,1,0:T(8,128)(2,1)S(1)}, u32[]{:S(2)}, u32[]{:S(2)}) async-start(bf16[16,256,128]{2,1,0:T(8,128)(2,1)} %split_q.1), calls=%async_computation | async-start | bytes 2097152 | tf_op jit(solution)/shard_map/all_to_all | solution.py:192
  19.6 8.4 %collective-permute-start.3 = (bf16[512,128]{1,0:T(8,128)(2,1)S(1)}, bf16[512,128]{1,0:T(8,128)(2,1)S(1)}, u32[]{:S(2)}, u32[]{:S(2)}) collective-permute-start(bf16[512,128]{1,0:T(8,128)(2,1)S(1)} %bitcast.24), channel_id=1, source_target_pairs={{0,112},{1,113},{2,114},{3,115},{4,116},{5,117},{6,118},{7,119},{8... | collective-permute-start | bytes 393224 | tf_op jit(solution)/shard_map/ppermute | solution.py:186
  25.5 6.2 %collective-permute-start = (bf16[512,128]{1,0:T(8,128)(2,1)S(1)}, bf16[512,128]{1,0:T(8,128)(2,1)S(1)}, u32[]{:S(2)}, u32[]{:S(2)}) collective-permute-start(bf16[512,128]{1,0:T(8,128)(2,1)S(1)} %bitcast.25), channel_id=1, source_target_pairs={{0,16},{1,17},{2,18},{3,19},{4,20},{5,21},{6,22},{7,23},{8,24},{9,... | collective-permute-start | bytes 393224 | tf_op jit(solution)/shard_map/ppermute | solution.py:186
  28.0 21.9 %copy-start.6 = (bf16[512,128]{1,0:T(8,128)(2,1)}, bf16[512,128]{1,0:T(8,128)(2,1)S(1)}, u32[]{:S(2)}) copy-start(bf16[512,128]{1,0:T(8,128)(2,1)S(1)} %collective-permute-done.3.l1) | copy-start | bytes 393220
  28.0 6.2 %collective-permute-start.4 = (bf16[512,128]{1,0:T(8,128)(2,1)S(1)}, bf16[512,128]{1,0:T(8,128)(2,1)S(1)}, u32[]{:S(2)}, u32[]{:S(2)}) collective-permute-start(bf16[512,128]{1,0:T(8,128)(2,1)S(1)} %collective-permute-done.3.l1), channel_id=1, source_target_pairs={{0,112},{1,113},{2,114},{3,115},{4,116},{5,117},{6,118},{7,119},{8... | collective-permute-start | bytes 393224 | tf_op jit(solution)/shard_map/ppermute | solution.py:186
  31.7 18.2 %copy-start.7 = (bf16[512,128]{1,0:T(8,128)(2,1)}, bf16[512,128]{1,0:T(8,128)(2,1)S(1)}, u32[]{:S(2)}) copy-start(bf16[512,128]{1,0:T(8,128)(2,1)S(1)} %collective-permute-done.r1) | copy-start | bytes 393220
  31.7 6.2 %collective-permute-start.1 = (bf16[512,128]{1,0:T(8,128)(2,1)S(1)}, bf16[512,128]{1,0:T(8,128)(2,1)S(1)}, u32[]{:S(2)}, u32[]{:S(2)}) collective-permute-start(bf16[512,128]{1,0:T(8,128)(2,1)S(1)} %collective-permute-done.r1), channel_id=1, source_target_pairs={{0,16},{1,17},{2,18},{3,19},{4,20},{5,21},{6,22},{7,23},{8,24},{9,... | collective-permute-start | bytes 393224 | tf_op jit(solution)/shard_map/ppermute | solution.py:186
  34.2 15.7 %copy-start.8 = (bf16[512,128]{1,0:T(8,128)(2,1)}, bf16[512,128]{1,0:T(8,128)(2,1)S(1)}, u32[]{:S(2)}) copy-start(bf16[512,128]{1,0:T(8,128)(2,1)S(1)} %collective-permute-done.4.l2) | copy-start | bytes 393220
  34.2 6.2 %collective-permute-start.5 = (bf16[512,128]{1,0:T(8,128)(2,1)S(1)}, bf16[512,128]{1,0:T(8,128)(2,1)S(1)}, u32[]{:S(2)}, u32[]{:S(2)}) collective-permute-start(bf16[512,128]{1,0:T(8,128)(2,1)S(1)} %collective-permute-done.4.l2), channel_id=1, source_target_pairs={{0,112},{1,113},{2,114},{3,115},{4,116},{5,117},{6,118},{7,119},{8... | collective-permute-start | bytes 393224 | tf_op jit(solution)/shard_map/ppermute | solution.py:186
  37.9 12.1 %copy-start.9 = (bf16[512,128]{1,0:T(8,128)(2,1)}, bf16[512,128]{1,0:T(8,128)(2,1)S(1)}, u32[]{:S(2)}) copy-start(bf16[512,128]{1,0:T(8,128)(2,1)S(1)} %collective-permute-done.1.r2) | copy-start | bytes 393220
  37.9 6.5 %collective-permute-start.2 = (bf16[512,128]{1,0:T(8,128)(2,1)S(1)}, bf16[512,128]{1,0:T(8,128)(2,1)S(1)}, u32[]{:S(2)}, u32[]{:S(2)}) collective-permute-start(bf16[512,128]{1,0:T(8,128)(2,1)S(1)} %collective-permute-done.1.r2), channel_id=1, source_target_pairs={{0,16},{1,17},{2,18},{3,19},{4,20},{5,21},{6,22},{7,23},{8,24},{9,... | collective-permute-start | bytes 393224 | tf_op jit(solution)/shard_map/ppermute | solution.py:186
  40.4 9.5 %copy-start.4 = (bf16[512,128]{1,0:T(8,128)(2,1)}, bf16[512,128]{1,0:T(8,128)(2,1)S(1)}, u32[]{:S(2)}) copy-start(bf16[512,128]{1,0:T(8,128)(2,1)S(1)} %collective-permute-done.5.l3) | copy-start | bytes 393220
  40.4 5.7 %collective-permute-start.7 = (bf16[256,128]{1,0:T(8,128)(2,1)S(1)}, bf16[256,128]{1,0:T(8,128)(2,1)S(1)}, u32[]{:S(2)}, u32[]{:S(2)}) collective-permute-start(bf16[256,128]{1,0:T(8,128)(2,1)S(1)} %slice.17), channel_id=1, source_target_pairs={{0,112},{1,113},{2,114},{3,115},{4,116},{5,117},{6,118},{7,119},{8... | collective-permute-start | bytes 196616 | tf_op jit(solution)/shard_map/ppermute | solution.py:186
  44.3 5.6 %copy-start.5 = (bf16[512,128]{1,0:T(8,128)(2,1)}, bf16[512,128]{1,0:T(8,128)(2,1)S(1)}, u32[]{:S(2)}) copy-start(bf16[512,128]{1,0:T(8,128)(2,1)S(1)} %collective-permute-done.2.r3) | copy-start | bytes 393220
  44.3 5.6 %collective-permute-start.6 = (bf16[256,128]{1,0:T(8,128)(2,1)S(1)}, bf16[256,128]{1,0:T(8,128)(2,1)S(1)}, u32[]{:S(2)}, u32[]{:S(2)}) collective-permute-start(bf16[256,128]{1,0:T(8,128)(2,1)S(1)} %slice.16), channel_id=1, source_target_pairs={{0,16},{1,17},{2,18},{3,19},{4,20},{5,21},{6,22},{7,23},{8,24},{9,... | collective-permute-start | bytes 196616 | tf_op jit(solution)/shard_map/ppermute | solution.py:186
  46.1 3.8 %copy-start.10 = (bf16[256,128]{1,0:T(8,128)(2,1)}, bf16[256,128]{1,0:T(8,128)(2,1)S(1)}, u32[]{:S(2)}) copy-start(bf16[256,128]{1,0:T(8,128)(2,1)S(1)} %collective-permute-done.7.l4) | copy-start | bytes 196612
  49.9 0.6 copy-start.11
  53.2 27.4 %all-to-all-start.3 = ((bf16[4,64,256]{2,1,0:T(8,128)(2,1)}), bf16[4,64,256]{2,1,0:T(8,128)(2,1)S(1)}, u32[]{:S(2)}, u32[]{:S(2)}) async-start(bf16[4,64,256]{2,1,0:T(8,128)(2,1)} %get-tuple-element.7), calls=%async_computation.3 | async-start | bytes 262144 | tf_op jit(solution)/shard_map/all_to_all | solution.py:192
  58.0 1.2 %copy-start = (bf16[2048,256]{1,0:T(8,128)(2,1)S(1)}, bf16[2048,256]{1,0:T(8,128)(2,1)}, u32[]{:S(2)}) copy-start(bf16[2048,256]{1,0:T(8,128)(2,1)} %get-tuple-element.6.v_ref) | copy-start | bytes 3145732
  59.2 1.0 copy-start.1
  80.7 10.4 %copy-start.12 = (s32[256]{0:T(256)S(1)}, s32[256]{0:T(256)}, u32[]{:S(2)}) copy-start(s32[256]{0:T(256)} %param.8) | copy-start | bytes 3076
  80.7 20.7 %all-to-all-start.2 = ((bf16[16,272,128]{2,1,0:T(8,128)(2,1)}), bf16[16,272,128]{2,1,0:T(8,128)(2,1)S(1)}, u32[]{:S(2)}, u32[]{:S(2)}) async-start(bf16[16,272,128]{2,1,0:T(8,128)(2,1)} %attention.1), calls=%async_computation.2 | async-start | bytes 2228224 | tf_op jit(solution)/shard_map/all_to_all | solution.py:192
  89.1 11.6 %collective-permute-start.8 = (bf16[256,256]{1,0:T(8,128)(2,1)S(1)}, bf16[256,256]{1,0:T(8,128)(2,1)S(1)}, u32[]{:S(2)}, u32[]{:S(2)}) collective-permute-start(bf16[256,256]{1,0:T(8,128)(2,1)S(1)} %convolution_convert_fusion), channel_id=1, source_target_pairs={{0,0},{1,32},{2,64},{3,96},{4,4},{5,36},{6,68},{7,100},{8,8},{9,40... | collective-permute-start | bytes 393224 | tf_op jit(solution)/shard_map/ppermute | solution.py:186
  101.3 1.0 copy-start.2

commit v3 on v2

--- a/solution.py
+++ b/solution.py
@@ -1,3 +1,5 @@
+import functools
+
 import jax
 import jax.numpy as jnp
 from jax import lax
@@ -25,15 +27,20 @@
 MESSAGE = 2 * ROWS + 16
 SCALE = HEAD**-0.5 * 1.4426950408889634
 NEG = -1e30
+AT_ORDER = KEY_BLOCKS
+AT_ID = AT_ORDER + Q_BLOCKS
+AT_LOW = AT_ID + Q_BLOCKS
+AT_HIGH = AT_LOW + Q_BLOCKS // JOINED
 
 SMEM = pl.BlockSpec(memory_space=pltpu.SMEM)
 VMEM = pl.BlockSpec(memory_space=pltpu.VMEM)
 PARAMS = pltpu.CompilerParams(vmem_limit_bytes=40 * 1024 * 1024)
 
 
-def split_kv_kernel(heads, kv_ref, o_ref):
-    for y in range(NY):
-        o_ref[y] = kv_ref[:, pl.ds(pl.multiple_of(heads[y] * HEAD, HEAD), HEAD)]
+def split_kv_kernel(heads, kv_ref, *o_refs):
+    y = lax.rem(lax.axis_index("blk"), NY)
+    for k in range(NY):
+        o_refs[k][...] = kv_ref[:, pl.ds(pl.multiple_of(heads[y ^ k] * HEAD, HEAD), HEAD)]
 
 
 def split_q_kernel(heads, q_ref, o_ref):
@@ -46,80 +53,98 @@
                     o_ref[x * NY + y, j * ROWS + g * BLOCK : j * ROWS + (g + 1) * BLOCK] = tile
 
 
-def arrange_kernel(rank, offset, c0, r1, r2, r3, l1, l2, l3, r4, l4, k_ref, v_ref, pick_ref):
-    v_ref[:, HEAD:] = jnp.ones((KEYS, HEAD), jnp.bfloat16)
-    pieces = [(c0, 0), (l1, 1), (l2, 2), (l3, 3), (r4, 4), (l4, 4), (r3, 5), (r2, 6), (r1, 7)]
-    for piece, zrel in pieces:
-        lines = range(NY)
-        if piece is r4:
-            lines = range(NY // 2)
-        if piece is l4:
-            lines = range(NY // 2, NY)
-        for at, y in enumerate(lines):
+def arrange(table, pieces, k_scr, kt_scr, v_scr, pick_ref):
+    place = lax.axis_index("blk")
+    z, y = place // PLANE, lax.rem(place, NY)
+    v_scr[:, HEAD:] = jnp.ones((KEYS, HEAD), jnp.bfloat16)
+    for piece, zrel, lines in pieces:
+        for at, line in enumerate(lines):
             for j in range(2):
-                row = pl.multiple_of(rank[(zrel * NY + y) * 2 + j] * BLOCK, BLOCK)
-                k_ref[pl.ds(row, BLOCK), :] = piece[at * 128 + j * BLOCK : at * 128 + (j + 1) * BLOCK, :]
-                v_ref[pl.ds(row, BLOCK), :HEAD] = piece[at * 128 + 64 + j * BLOCK : at * 128 + 64 + (j + 1) * BLOCK, :]
+                source = (lax.rem(z + zrel, NZ) * NY + (y ^ line)) * 2 + j
+                row = pl.multiple_of(table[source] * BLOCK, BLOCK)
+                k_scr[pl.ds(row, BLOCK), :] = piece[at * 128 + j * BLOCK : at * 128 + (j + 1) * BLOCK, :]
+                v_scr[pl.ds(row, BLOCK), :HEAD] = piece[at * 128 + 64 + j * BLOCK : at * 128 + 64 + (j + 1) * BLOCK, :]
+    for t in range(KEYS // 128):
+        kt_scr[:, t * 128 : (t + 1) * 128] = k_scr[t * 128 : (t + 1) * 128, :].T
     some = 16
+    offset = lax.rem(z, 2) * 16 + z // 2
     line = lax.broadcasted_iota(jnp.int32, (NX * some, some * BLOCK), 0)
     column = lax.broadcasted_iota(jnp.int32, (NX * some, some * BLOCK), 1)
-    wanted = (line % some) * BLOCK + offset[0] + (line // some) * NY
+    wanted = (line % some) * BLOCK + offset + (line // some) * NY
     select = jnp.where(column == wanted, 1.0, 0.0).astype(jnp.bfloat16)
     for c in range(KEY_BLOCKS // some):
         rows = slice(c * some * BLOCK, (c + 1) * some * BLOCK)
-        k = jnp.dot(select, k_ref[rows, :], preferred_element_type=jnp.float32).astype(jnp.bfloat16)
-        v = jnp.dot(select, v_ref[rows, :HEAD], preferred_element_type=jnp.float32).astype(jnp.bfloat16)
+        k = jnp.dot(select, k_scr[rows, :], preferred_element_type=jnp.float32).astype(jnp.bfloat16)
+        v = jnp.dot(select, v_scr[rows, :HEAD], preferred_element_type=jnp.float32).astype(jnp.bfloat16)
         for x in range(NX):
             pick_ref[x, c * some : (c + 1) * some, :HEAD] = k[x * some : (x + 1) * some]
             pick_ref[x, c * some : (c + 1) * some, HEAD:] = v[x * some : (x + 1) * some]
 
 
-def attention_kernel(q_order, q_ids, lows, highs, q_ref, k_ref, v_ref, kpos_ref, o_ref, s_scr, top_scr, acc_scr, stat):
+def attention_kernel(table, q_ref, kpos_ref, *refs):
+    pieces, (o_ref, pick_ref, k_scr, kt_scr, v_scr, s_scr, stat) = refs[:9], refs[9:]
+    own, r1, r2, r3, l1, l2, l3, r4, l4 = pieces
+    every, first, last = range(NY), range(NY // 2), range(NY // 2, NY)
+    arrange(
+        table,
+        [(own, 0, every), (l1, 1, every), (l2, 2, every), (l3, 3, every), (r4, 4, first), (l4, 4, last)]
+        + [(r3, 5, every), (r2, 6, every), (r1, 7, every)],
+        k_scr,
+        kt_scr,
+        v_scr,
+        pick_ref,
+    )
     lane = lax.broadcasted_iota(jnp.int32, (ROWS, 128), 1)
     token = lax.broadcasted_iota(jnp.int32, (BLOCK, CHUNK), 0)
 
     def one_group(i, carry):
-        low, high = lows[i], highs[i]
-        q = jnp.concatenate([q_ref[q_order[i * JOINED + u]] for u in range(JOINED)], axis=0)
-        top_scr[...] = jnp.full((JOINED * ROWS, 128), NEG, jnp.float32)
-        acc_scr[...] = jnp.zeros((JOINED * ROWS, 2 * HEAD), jnp.float32)
-
-        def scores(chunk, carry):
-            start = pl.multiple_of(chunk * CHUNK, CHUNK)
-            k = k_ref[pl.ds(start, CHUNK), :]
-            s = lax.dot_general(q, k, (((1,), (1,)), ((), ())), preferred_element_type=jnp.float32)
-            kpos = kpos_ref[pl.ds(chunk, 1), :]
+        low, high = table[AT_LOW + i], table[AT_HIGH + i]
+        blocks = [table[AT_ORDER + i * JOINED + u] for u in range(JOINED)]
+        ids = [table[AT_ID + i * JOINED + u] for u in range(JOINED)]
+
+        def finish(u, out, total, top):
+            place = pl.ds(pl.multiple_of(blocks[u] % 2 * ROWS, ROWS), ROWS)
+            o_ref[blocks[u] // 2, place, :] = out.astype(jnp.bfloat16)
+            old = jnp.where(lane == blocks[u], top, stat[...])
+            stat[...] = jnp.where(lane == blocks[u] + Q_BLOCKS, total, old)
+
+        def work(n):
+            q = jnp.concatenate([q_ref[blocks[u]] for u in range(JOINED)], axis=0)
+            tops = [None] * (JOINED * GROUP)
+            for c in range(n):
+                start = pl.multiple_of((low + c) * CHUNK, CHUNK)
+                s = jnp.dot(q, kt_scr[:, pl.ds(start, CHUNK)], preferred_element_type=jnp.float32)
+                kpos = kpos_ref[pl.ds(low + c, 1), :]
+                for u in range(JOINED):
+                    distance = (ids[u] * BLOCK + token) - kpos
+                    bias = jnp.where((distance >= 0) & (distance < WINDOW), 0.0, NEG)
+                    for g in range(GROUP):
+                        r = u * GROUP + g
+                        part = s[r * BLOCK : (r + 1) * BLOCK] + bias
+                        s_scr[c, r * BLOCK : (r + 1) * BLOCK, :] = part
+                        wide = jnp.maximum(part[:, :128], part[:, 128:])
+                        tops[r] = wide if tops[r] is None else jnp.maximum(tops[r], wide)
+            top = jnp.max(jnp.concatenate(tops, axis=0), axis=1, keepdims=True) * SCALE
+            top = jnp.broadcast_to(top, (JOINED * ROWS, 128))
+            twice = jnp.concatenate([top, top], axis=1)
+            acc = None
+            for c in range(n):
+                start = pl.multiple_of((low + c) * CHUNK, CHUNK)
+                p = jnp.exp2(s_scr[c] * SCALE - twice).astype(jnp.bfloat16)
+                part = jnp.dot(p, v_scr[pl.ds(start, CHUNK), :], preferred_element_type=jnp.float32)
+                acc = part if acc is None else acc + part
             for u in range(JOINED):
-                distance = (q_ids[i * JOINED + u] * BLOCK + token) - kpos
-                bias = jnp.where((distance >= 0) & (distance < WINDOW), 0.0, NEG)
-                for g in range(GROUP):
-                    rows = slice(u * ROWS + g * BLOCK, u * ROWS + (g + 1) * BLOCK)
-                    part = s[rows] + bias
-                    s_scr[chunk - low, rows, :] = part
-                    top_scr[rows] = jnp.maximum(top_scr[rows], jnp.maximum(part[:, :128], part[:, 128:]))
-            return carry
-
-        lax.fori_loop(low, high, scores, 0)
-        top = jnp.max(top_scr[...], axis=1, keepdims=True) * SCALE
-        top_scr[...] = jnp.broadcast_to(top, (JOINED * ROWS, 128))
-
-        def weigh(chunk, carry):
-            start = pl.multiple_of(chunk * CHUNK, CHUNK)
-            top = top_scr[...]
-            s = s_scr[chunk - low]
-            p = jnp.exp2(s * SCALE - jnp.concatenate([top, top], axis=1)).astype(jnp.bfloat16)
-            acc_scr[...] += jnp.dot(p, v_ref[pl.ds(start, CHUNK), :], preferred_element_type=jnp.float32)
-            return carry
-
-        lax.fori_loop(low, high, weigh, 0)
-        for u in range(JOINED):
-            rows = slice(u * ROWS, (u + 1) * ROWS)
-            block = q_order[i * JOINED + u]
-            total = acc_scr[rows, HEAD:]
-            out = acc_scr[rows, :HEAD] / jnp.maximum(total, 1e-30)
-            o_ref[block // 2, pl.ds(pl.multiple_of(block % 2 * ROWS, ROWS), ROWS), :] = out.astype(jnp.bfloat16)
-            old = jnp.where(lane == block, top_scr[rows], stat[...])
-            stat[...] = jnp.where(lane == block + Q_BLOCKS, total, old)
+                rows = slice(u * ROWS, (u + 1) * ROWS)
+                finish(u, acc[rows, :HEAD] / acc[rows, HEAD:], acc[rows, HEAD:], top[rows])
+
+        @pl.when(high <= low)
+        def _():
+            nothing = jnp.zeros((ROWS, 128), jnp.float32)
+            for u in range(JOINED):
+                finish(u, nothing, nothing, nothing + NEG)
+
+        for n in range(1, KEYS // CHUNK + 1):
+            pl.when(high - low == n)(functools.partial(work, n))
         return carry
 
     stat[...] = jnp.zeros((ROWS, 128), jnp.float32)
@@ -193,12 +218,13 @@
 
     kv = pl.pallas_call(
         split_kv_kernel,
-        out_shape=jax.ShapeDtypeStruct((NY, 128, HEAD), jnp.bfloat16),
+        out_shape=(jax.ShapeDtypeStruct((128, HEAD), jnp.bfloat16),) * NY,
         in_specs=[SMEM, VMEM],
-        out_specs=VMEM,
+        out_specs=(VMEM,) * NY,
         name="split_kv",
     )(segment_head, rotated_key_value.reshape(128, KEY_VALUE_HEADS * HEAD))
-    own = exchange(kv, y_groups).reshape(NY * 128, HEAD)
+    line = [kv[0]] + [move(kv[k], lambda a, b, c, k=k: index(a, b, c ^ k)) for k in range(1, NY)]
+    own = jnp.concatenate(line, axis=0)
     right = lambda v: move(v, lambda a, b, c: index(a + 1, b, c))
     left = lambda v: move(v, lambda a, b, c: index(a - 1, b, c))
     r1, l1 = right(own), left(own)
@@ -219,8 +245,7 @@
     rank = ranks(ids)
     ordered = placed(ids, rank)
     mine = lax.dynamic_index_in_dim(ordered, x, 0, keepdims=False)
-    my_rank = lax.dynamic_index_in_dim(rank, x, 0, keepdims=False).reshape(NZ, 2 * NY)
-    my_rank = lax.dynamic_slice_in_dim(jnp.concatenate([my_rank, my_rank], axis=0), z, NZ, 0).reshape(KEY_BLOCKS)
+    my_rank = lax.dynamic_index_in_dim(rank, x, 0, keepdims=False)
     q_ids = lax.dynamic_slice_in_dim(block_map, z * Q_BLOCKS, Q_BLOCKS)
     q_rank = ranks(q_ids)
     q_order = placed(jnp.arange(Q_BLOCKS, dtype=jnp.int32), q_rank)
@@ -229,37 +254,31 @@
     lows = jnp.sum(mine[None, :] < grouped[:, :1] - WINDOW // BLOCK, axis=1, dtype=jnp.int32) // CHUNK_BLOCKS
     highs = jnp.sum(mine[None, :] <= grouped[:, -1:], axis=1, dtype=jnp.int32)
     highs = (highs + CHUNK_BLOCKS - 1) // CHUNK_BLOCKS
+    table = jnp.concatenate([my_rank, q_order, q_sorted, lows, highs])
     kpos = mine[:, None] * BLOCK + jnp.arange(BLOCK, dtype=jnp.int32)[None, :]
     kpos = kpos.reshape(KEYS // CHUNK, CHUNK)
 
-    offset = ((z % 2) * 16 + z // 2).reshape(1)
-    k, v, pick = pl.pallas_call(
-        arrange_kernel,
+    out, pick = pl.pallas_call(
+        attention_kernel,
         out_shape=(
-            jax.ShapeDtypeStruct((KEYS, HEAD), jnp.bfloat16),
-            jax.ShapeDtypeStruct((KEYS, 2 * HEAD), jnp.bfloat16),
+            jax.ShapeDtypeStruct((PLANE, MESSAGE, HEAD), jnp.bfloat16),
             jax.ShapeDtypeStruct((NX, KEY_BLOCKS, 2 * HEAD), jnp.bfloat16),
         ),
-        in_specs=[SMEM] * 2 + [VMEM] * 9,
-        out_specs=(VMEM,) * 3,
-        name="arrange",
-    )(my_rank, offset, own, r1, r2, r3, l1, l2, l3, r4, l4)
-
-    out = pl.pallas_call(
-        attention_kernel,
-        out_shape=jax.ShapeDtypeStruct((PLANE, MESSAGE, HEAD), jnp.bfloat16),
-        in_specs=[SMEM] * 4 + [VMEM] * 4,
-        out_specs=VMEM,
+        in_specs=[SMEM] + [VMEM] * 11,
+        out_specs=(VMEM, VMEM),
         scratch_shapes=[
+            pltpu.VMEM((KEYS, HEAD), jnp.bfloat16),
+            pltpu.VMEM((HEAD, KEYS), jnp.bfloat16),
+            pltpu.VMEM((KEYS, 2 * HEAD), jnp.bfloat16),
             pltpu.VMEM((KEYS // CHUNK, JOINED * ROWS, CHUNK), jnp.float32),
-            pltpu.VMEM((JOINED * ROWS, 128), jnp.float32),
-            pltpu.VMEM((JOINED * ROWS, 2 * HEAD), jnp.float32),
             pltpu.VMEM((ROWS, 128), jnp.float32),
         ],
         compiler_params=PARAMS,
         cost_estimate=pl.CostEstimate(flops=3_000_000_000, bytes_accessed=4_000_000, transcendentals=5_000_000),
         name="attention",
-    )(q_order, q_sorted, lows, highs, q, k, v, kpos)
+    )(table, q, kpos, own, r1, r2, r3, l1, l2, l3, r4, l4)
+    out = exchange(out, planes)
+    offset = (z % 2) * 16 + z // 2
 
     pick = exchange(pick, x_groups).reshape(BLOCKS, 2 * HEAD)
     blocks = jnp.arange(BLOCKS, dtype=jnp.int32)
@@ -269,7 +288,6 @@
     cache = move(cache, lambda a, b, c: index(2 * c + a % 2, b, a // 2))
     cache = cache.reshape(BLOCKS, 2, HEAD).transpose(1, 0, 2)[None, :, None]
 
-    out = exchange(out, planes)
     my_blocks = lax.dynamic_slice_in_dim(block_map, 2 * place, 2)
     attended = pl.pallas_call(
         combine_kernel,

time: 107 us -> 95 us (0.89)
  the two profiles are of different devices: /device:TPU:8 before, /device:TPU:16 now
where the time goes in v3:
time: 95 us; the launch traced here: 95.4 us
  starting transfers between devices  36.7 us (39%)
  waiting for transfers between devices  23.6 us (25%)
  Pallas kernels  18.8 us (20%)
  blocking collectives  9.93 us (10%)
  local copies, waits for them, and re-layouts  3.45 us (4%)
  between operations  1.45 us (2%)
  other arithmetic  1.13 us (1%)
    ppermute x12, waiting for transfers between devices, move(): lax.ppermute(value, 'blk', [(s, target(s // 16, s // 4 % 4, s % 4)) for s...  23.6 us
    ppermute x12, starting transfers between devices, move(): lax.ppermute(value, 'blk', [(s, target(s // 16, s // 4 % 4, s % 4)) for s...  22.8 us
    all_to_all x2, starting transfers between devices, exchange(): lax.all_to_all(value, 'blk', 0, 0, axis_index_groups=groups, tiled=True)  13.9 us
    pallas_call x1, Pallas kernels, body(): pl.pallas_call(attention_kernel, out_shape=(jax.ShapeDtypeStruct((PLANE,...  12.3 us
    all_to_all x1, blocking collectives, exchange(): lax.all_to_all(value, 'blk', 0, 0, axis_index_groups=groups, tiled=True)  9.93 us
    pallas_call x1, Pallas kernels, body(): pl.pallas_call(combine_kernel, out_shape=jax.ShapeDtypeStruct((2 * BLOCK,...  2.79 us
    pallas_call x1, Pallas kernels, body(): pl.pallas_call(split_q_kernel, out_shape=jax.ShapeDtypeStruct((PLANE, 2 *...  2.09 us
  transfers between devices with their start and end apart: 14, of which 6 were waited for; matrix products, arithmetic and copies ran while one was open for 4% of the time, Pallas kernels for 2%

profile of v3, /device:TPU:16, one launch (start us, length us, event | category | flops | bytes accessed | tf_op | source)
XLA Modules:
  0.0 95.4 jit_solution(14811836699159305684)
XLA Ops:
  0.6 1.6 %split_kv.1 = (bf16[128,128]{1,0:T(8,128)(2,1)}, bf16[128,128]{1,0:T(8,128)(2,1)}, bf16[128,128]{1,0:T(8,128)(2,1)}, bf16[128,128]{1,0:T(8,128)(2,1)}) custom-call(s32[4]{0:T(128)} %heads.5, bf16[128,512]{1,0:T(8,128)(2,1)} %bitcast.28), custom_call_target="tpu_custom_call" | custom-call | tf_op jit(solution)/shard_map/split_kv/pallas_call | solution.py:219
  2.2 1.3 %collective-permute-start = (bf16[128,128]{1,0:T(8,128)(2,1)}, bf16[128,128]{1,0:T(8,128)(2,1)S(1)}, u32[]{:S(2)}, u32[]{:S(2)}) collective-permute-start(bf16[128,128]{1,0:T(8,128)(2,1)} %get-tuple-element.9), channel_id=1, source_target_pairs={{0,1},{1,0},{2,3},{3,2},{4,5},{5,4},{6,7},{7,6},{8,9},{9,8},{10,11... | collective-permute-start | bytes 98312 | tf_op jit(solution)/shard_map/ppermute | solution.py:211
  3.5 0.8 collective-permute-start.1
  4.3 1.4 %collective-permute-start.2 = (bf16[128,128]{1,0:T(8,128)(2,1)}, bf16[128,128]{1,0:T(8,128)(2,1)S(1)}, u32[]{:S(2)}, u32[]{:S(2)}) collective-permute-start(bf16[128,128]{1,0:T(8,128)(2,1)} %get-tuple-element.11), channel_id=1, source_target_pairs={{0,3},{1,2},{2,1},{3,0},{4,7},{5,6},{6,5},{7,4},{8,11},{9,10},{10,... | collective-permute-start | bytes 98312 | tf_op jit(solution)/shard_map/ppermute | solution.py:211
  5.7 2.1 %split_q.1 = bf16[16,256,128]{2,1,0:T(8,128)(2,1)} custom-call(s32[4]{0:T(128)} %heads.5, bf16[64,2048]{1,0:T(8,128)(2,1)} %bitcast.24), custom_call_target="tpu_custom_call" | custom-call | tf_op jit(solution)/shard_map/split_q/pallas_call | solution.py:231
  7.8 8.4 %all-to-all-start = ((bf16[16,256,128]{2,1,0:T(8,128)(2,1)}), bf16[16,256,128]{2,1,0:T(8,128)(2,1)S(1)}, u32[]{:S(2)}, u32[]{:S(2)}) async-start(bf16[16,256,128]{2,1,0:T(8,128)(2,1)} %split_q.1), calls=%async_computation | async-start | bytes 2097152 | tf_op jit(solution)/shard_map/all_to_all | solution.py:217
  16.3 0.2 reshape.58
  16.5 0.2 convert_reduce_fusion.1
  16.7 0.3 copy.12
  17.1 0.2 convert_reduce_fusion
  18.1 5.9 %collective-permute-start.6 = (bf16[512,128]{1,0:T(8,128)(2,1)S(1)}, bf16[512,128]{1,0:T(8,128)(2,1)S(1)}, u32[]{:S(2)}, u32[]{:S(2)}) collective-permute-start(bf16[512,128]{1,0:T(8,128)(2,1)S(1)} %constant_dynamic-update-slice_fusion.refs_0_), channel_id=1, source_target_pairs={{0,112},{1,113},{2,114},{3,115},{4,116},{5,117},{6,118},{7,119},{8... | collective-permute-start | bytes 393224 | tf_op jit(solution)/shard_map/ppermute | solution.py:211
  24.1 2.5 %collective-permute-done.6.refs_4_ = bf16[512,128]{1,0:T(8,128)(2,1)S(1)} collective-permute-done((bf16[512,128]{1,0:T(8,128)(2,1)S(1)}, bf16[512,128]{1,0:T(8,128)(2,1)S(1)}, u32[]{:S(2)}, u32[]{:S(2)}) %collective-permute-start.6) | collective-permute-done | bytes 131104 | tf_op jit(solution)/shard_map/ppermute | solution.py:211
  26.6 3.7 %collective-permute-start.7 = (bf16[512,128]{1,0:T(8,128)(2,1)S(1)}, bf16[512,128]{1,0:T(8,128)(2,1)S(1)}, u32[]{:S(2)}, u32[]{:S(2)}) collective-permute-start(bf16[512,128]{1,0:T(8,128)(2,1)S(1)} %collective-permute-done.6.refs_4_), channel_id=1, source_target_pairs={{0,112},{1,113},{2,114},{3,115},{4,116},{5,117},{6,118},{7,119},{8... | collective-permute-start | bytes 393224 | tf_op jit(solution)/shard_map/ppermute | solution.py:211
  30.2 0.2 slice_reduce_fusion
  30.4 0.2 convert_reduce_fusion.2
  30.6 2.1 %collective-permute-done.7.refs_5_ = bf16[512,128]{1,0:T(8,128)(2,1)S(1)} collective-permute-done((bf16[512,128]{1,0:T(8,128)(2,1)S(1)}, bf16[512,128]{1,0:T(8,128)(2,1)S(1)}, u32[]{:S(2)}, u32[]{:S(2)}) %collective-permute-start.7) | collective-permute-done | bytes 131104 | tf_op jit(solution)/shard_map/ppermute | solution.py:211
  32.8 3.7 %collective-permute-start.8 = (bf16[512,128]{1,0:T(8,128)(2,1)S(1)}, bf16[512,128]{1,0:T(8,128)(2,1)S(1)}, u32[]{:S(2)}, u32[]{:S(2)}) collective-permute-start(bf16[512,128]{1,0:T(8,128)(2,1)S(1)} %collective-permute-done.7.refs_5_), channel_id=1, source_target_pairs={{0,112},{1,113},{2,114},{3,115},{4,116},{5,117},{6,118},{7,119},{8... | collective-permute-start | bytes 393224 | tf_op jit(solution)/shard_map/ppermute | solution.py:211
  36.4 3.2 %collective-permute-done.8.refs_6_ = bf16[512,128]{1,0:T(8,128)(2,1)S(1)} collective-permute-done((bf16[512,128]{1,0:T(8,128)(2,1)S(1)}, bf16[512,128]{1,0:T(8,128)(2,1)S(1)}, u32[]{:S(2)}, u32[]{:S(2)}) %collective-permute-start.8) | collective-permute-done | bytes 131104 | tf_op jit(solution)/shard_map/ppermute | solution.py:211
  39.6 3.7 %collective-permute-start.10 = (bf16[256,128]{1,0:T(8,128)(2,1)S(1)}, bf16[256,128]{1,0:T(8,128)(2,1)S(1)}, u32[]{:S(2)}, u32[]{:S(2)}) collective-permute-start(bf16[256,128]{1,0:T(8,128)(2,1)S(1)} %slice.17), channel_id=1, source_target_pairs={{0,112},{1,113},{2,114},{3,115},{4,116},{5,117},{6,118},{7,119},{8... | collective-permute-start | bytes 196616 | tf_op jit(solution)/shard_map/ppermute | solution.py:211
  43.3 0.3 collective-permute-start.9
  43.7 1.5 %collective-permute-done.10.refs_8_ = bf16[256,128]{1,0:T(8,128)(2,1)S(1)} collective-permute-done((bf16[256,128]{1,0:T(8,128)(2,1)S(1)}, bf16[256,128]{1,0:T(8,128)(2,1)S(1)}, u32[]{:S(2)}, u32[]{:S(2)}) %collective-permute-start.10) | collective-permute-done | bytes 65568 | tf_op jit(solution)/shard_map/ppermute | solution.py:211
  45.2 3.8 %collective-permute-done.9.refs_7_ = bf16[256,128]{1,0:T(8,128)(2,1)S(1)} collective-permute-done((bf16[256,128]{1,0:T(8,128)(2,1)S(1)}, bf16[256,128]{1,0:T(8,128)(2,1)S(1)}, u32[]{:S(2)}, u32[]{:S(2)}) %collective-permute-start.9) | collective-permute-done | bytes 65568 | tf_op jit(solution)/shard_map/ppermute | solution.py:211
  49.0 12.3 %attention.1 = (bf16[16,272,128]{2,1,0:T(8,128)(2,1)}, bf16[4,64,256]{2,1,0:T(8,128)(2,1)S(1)}) custom-call(s32[144]{0:T(256)S(1)} %concatenate.6.table, bf16[32,128,128]{2,1,0:T(8,128)(2,1)S(1)} %bitcast.23, s32[8,256]{1,0:T(8,128)S(1)} %broadcast_add_fusion.kpos_ref, bf16[512,128]{1,0:T(8,128)(2,1)S(1)} %constant_dynamic-update-slice_fusion.refs_0_, ...), custom_call_target="tpu_custom_call" | custom-call | flops 3000000000 | bytes 4000000 | tf_op jit(solution)/shard_map/attention/pallas_call | solution.py:261
  61.4 9.9 %all_to_all.15 = bf16[4,64,256]{2,1,0:T(8,128)(2,1)S(1)} all-to-all(bf16[4,64,256]{2,1,0:T(8,128)(2,1)S(1)} %get-tuple-element.13), channel_id=1, replica_groups={{0,4,8,12},{1,5,9,13},{2,6,10,14},{3,7,11,15},{16,20,24,28},{17,21,25,2..., dimensions={0} | all-to-all | bytes 262144 | tf_op jit(solution)/shard_map/all_to_all | solution.py:217
  71.3 5.4 %all-to-all-start.1 = ((bf16[16,272,128]{2,1,0:T(8,128)(2,1)}), bf16[16,272,128]{2,1,0:T(8,128)(2,1)S(1)}, u32[]{:S(2)}, u32[]{:S(2)}) async-start(bf16[16,272,128]{2,1,0:T(8,128)(2,1)} %get-tuple-element.12), calls=%async_computation.1 | async-start | bytes 2228224 | tf_op jit(solution)/shard_map/all_to_all | solution.py:217
  77.5 0.2 convolution_convert_fusion
  77.7 2.1 %collective-permute-start.11 = (bf16[256,256]{1,0:T(8,128)(2,1)S(1)}, bf16[256,256]{1,0:T(8,128)(2,1)S(1)}, u32[]{:S(2)}, u32[]{:S(2)}) collective-permute-start(bf16[256,256]{1,0:T(8,128)(2,1)S(1)} %convolution_convert_fusion), channel_id=1, source_target_pairs={{0,0},{1,32},{2,64},{3,96},{4,4},{5,36},{6,68},{7,100},{8,8},{9,40... | collective-permute-start | bytes 393224 | tf_op jit(solution)/shard_map/ppermute | solution.py:211
  79.9 0.6 dynamic_slice.13.blocks
  80.4 10.5 %collective-permute-done.11 = bf16[256,256]{1,0:T(8,128)(2,1)S(1)} collective-permute-done((bf16[256,256]{1,0:T(8,128)(2,1)S(1)}, bf16[256,256]{1,0:T(8,128)(2,1)S(1)}, u32[]{:S(2)}, u32[]{:S(2)}) %collective-permute-start.11) | collective-permute-done | bytes 131104 | tf_op jit(solution)/shard_map/ppermute | solution.py:211
  90.9 0.7 bitcast_bitcast_fusion
  91.6 1.0 %copy-done = bf16[16,272,128]{2,1,0:T(8,128)(2,1)} copy-done((bf16[16,272,128]{2,1,0:T(8,128)(2,1)}, bf16[16,272,128]{2,1,0:T(8,128)(2,1)S(1)}, u32[]{:S(2)}) %copy-start) | copy-done | bytes 1114136
  92.6 2.8 %combine.1 = bf16[64,2048]{1,0:T(8,128)(2,1)} custom-call(s32[4]{0:T(128)} %heads.5, s32[2]{0:T(128)} %dynamic_slice.13.blocks, s32[1]{0:T(128)} %copy.21.length, bf16[16,272,128]{2,1,0:T(8,128)(2,1)} %copy-done), custom_call_target="tpu_custom_call" | custom-call | tf_op jit(solution)/shard_map/combine/pallas_call | solution.py:292
  (39 shorter events, 1.1 us)
Async XLA Ops:
  2.2 15.8 %collective-permute-start = (bf16[128,128]{1,0:T(8,128)(2,1)}, bf16[128,128]{1,0:T(8,128)(2,1)S(1)}, u32[]{:S(2)}, u32[]{:S(2)}) collective-permute-start(bf16[128,128]{1,0:T(8,128)(2,1)} %get-tuple-element.9), channel_id=1, source_target_pairs={{0,1},{1,0},{2,3},{3,2},{4,5},{5,4},{6,7},{7,6},{8,9},{9,8},{10,11... | collective-permute-start | bytes 98312 | tf_op jit(solution)/shard_map/ppermute | solution.py:211
  3.5 14.6 %collective-permute-start.1 = (bf16[128,128]{1,0:T(8,128)(2,1)}, bf16[128,128]{1,0:T(8,128)(2,1)S(1)}, u32[]{:S(2)}, u32[]{:S(2)}) collective-permute-start(bf16[128,128]{1,0:T(8,128)(2,1)} %get-tuple-element.10), channel_id=1, source_target_pairs={{0,2},{1,3},{2,0},{3,1},{4,6},{5,7},{6,4},{7,5},{8,10},{9,11},{10,... | collective-permute-start | bytes 98312 | tf_op jit(solution)/shard_map/ppermute | solution.py:211
  4.3 13.8 %collective-permute-start.2 = (bf16[128,128]{1,0:T(8,128)(2,1)}, bf16[128,128]{1,0:T(8,128)(2,1)S(1)}, u32[]{:S(2)}, u32[]{:S(2)}) collective-permute-start(bf16[128,128]{1,0:T(8,128)(2,1)} %get-tuple-element.11), channel_id=1, source_target_pairs={{0,3},{1,2},{2,1},{3,0},{4,7},{5,6},{6,5},{7,4},{8,11},{9,10},{10,... | collective-permute-start | bytes 98312 | tf_op jit(solution)/shard_map/ppermute | solution.py:211
  7.8 8.4 %copy-start.2 = (s32[256]{0:T(256)S(1)}, s32[256]{0:T(256)}, u32[]{:S(2)}) copy-start(s32[256]{0:T(256)} %param.8) | copy-start | bytes 3076
  7.8 9.7 %copy-start.1 = (bf16[128,128]{1,0:T(8,128)(2,1)S(1)}, bf16[128,128]{1,0:T(8,128)(2,1)}, u32[]{:S(2)}) copy-start(bf16[128,128]{1,0:T(8,128)(2,1)} %get-tuple-element.8) | copy-start | bytes 98308
  7.8 41.2 %all-to-all-start = ((bf16[16,256,128]{2,1,0:T(8,128)(2,1)}), bf16[16,256,128]{2,1,0:T(8,128)(2,1)S(1)}, u32[]{:S(2)}, u32[]{:S(2)}) async-start(bf16[16,256,128]{2,1,0:T(8,128)(2,1)} %split_q.1), calls=%async_computation | async-start | bytes 2097152 | tf_op jit(solution)/shard_map/all_to_all | solution.py:217
  18.1 8.5 %collective-permute-start.6 = (bf16[512,128]{1,0:T(8,128)(2,1)S(1)}, bf16[512,128]{1,0:T(8,128)(2,1)S(1)}, u32[]{:S(2)}, u32[]{:S(2)}) collective-permute-start(bf16[512,128]{1,0:T(8,128)(2,1)S(1)} %constant_dynamic-update-slice_fusion.refs_0_), channel_id=1, source_target_pairs={{0,112},{1,113},{2,114},{3,115},{4,116},{5,117},{6,118},{7,119},{8... | collective-permute-start | bytes 393224 | tf_op jit(solution)/shard_map/ppermute | solution.py:211
  24.1 6.2 %collective-permute-start.3 = (bf16[512,128]{1,0:T(8,128)(2,1)S(1)}, bf16[512,128]{1,0:T(8,128)(2,1)S(1)}, u32[]{:S(2)}, u32[]{:S(2)}) collective-permute-start(bf16[512,128]{1,0:T(8,128)(2,1)S(1)} %constant_dynamic-update-slice_fusion.refs_0_), channel_id=1, source_target_pairs={{0,16},{1,17},{2,18},{3,19},{4,20},{5,21},{6,22},{7,23},{8,24},{9,... | collective-permute-start | bytes 393224 | tf_op jit(solution)/shard_map/ppermute | solution.py:211
  26.6 6.2 %collective-permute-start.7 = (bf16[512,128]{1,0:T(8,128)(2,1)S(1)}, bf16[512,128]{1,0:T(8,128)(2,1)S(1)}, u32[]{:S(2)}, u32[]{:S(2)}) collective-permute-start(bf16[512,128]{1,0:T(8,128)(2,1)S(1)} %collective-permute-done.6.refs_4_), channel_id=1, source_target_pairs={{0,112},{1,113},{2,114},{3,115},{4,116},{5,117},{6,118},{7,119},{8... | collective-permute-start | bytes 393224 | tf_op jit(solution)/shard_map/ppermute | solution.py:211
  30.2 6.2 %collective-permute-start.4 = (bf16[512,128]{1,0:T(8,128)(2,1)S(1)}, bf16[512,128]{1,0:T(8,128)(2,1)S(1)}, u32[]{:S(2)}, u32[]{:S(2)}) collective-permute-start(bf16[512,128]{1,0:T(8,128)(2,1)S(1)} %collective-permute-done.3.refs_1_), channel_id=1, source_target_pairs={{0,16},{1,17},{2,18},{3,19},{4,20},{5,21},{6,22},{7,23},{8,24},{9,... | collective-permute-start | bytes 393224 | tf_op jit(solution)/shard_map/ppermute | solution.py:211
  32.8 6.8 %collective-permute-start.8 = (bf16[512,128]{1,0:T(8,128)(2,1)S(1)}, bf16[512,128]{1,0:T(8,128)(2,1)S(1)}, u32[]{:S(2)}, u32[]{:S(2)}) collective-permute-start(bf16[512,128]{1,0:T(8,128)(2,1)S(1)} %collective-permute-done.7.refs_5_), channel_id=1, source_target_pairs={{0,112},{1,113},{2,114},{3,115},{4,116},{5,117},{6,118},{7,119},{8... | collective-permute-start | bytes 393224 | tf_op jit(solution)/shard_map/ppermute | solution.py:211
  36.4 6.9 %collective-permute-start.5 = (bf16[512,128]{1,0:T(8,128)(2,1)S(1)}, bf16[512,128]{1,0:T(8,128)(2,1)S(1)}, u32[]{:S(2)}, u32[]{:S(2)}) collective-permute-start(bf16[512,128]{1,0:T(8,128)(2,1)S(1)} %collective-permute-done.4.refs_2_), channel_id=1, source_target_pairs={{0,16},{1,17},{2,18},{3,19},{4,20},{5,21},{6,22},{7,23},{8,24},{9,... | collective-permute-start | bytes 393224 | tf_op jit(solution)/shard_map/ppermute | solution.py:211
  39.6 5.6 %collective-permute-start.10 = (bf16[256,128]{1,0:T(8,128)(2,1)S(1)}, bf16[256,128]{1,0:T(8,128)(2,1)S(1)}, u32[]{:S(2)}, u32[]{:S(2)}) collective-permute-start(bf16[256,128]{1,0:T(8,128)(2,1)S(1)} %slice.17), channel_id=1, source_target_pairs={{0,112},{1,113},{2,114},{3,115},{4,116},{5,117},{6,118},{7,119},{8... | collective-permute-start | bytes 196616 | tf_op jit(solution)/shard_map/ppermute | solution.py:211
  43.3 5.7 %collective-permute-start.9 = (bf16[256,128]{1,0:T(8,128)(2,1)S(1)}, bf16[256,128]{1,0:T(8,128)(2,1)S(1)}, u32[]{:S(2)}, u32[]{:S(2)}) collective-permute-start(bf16[256,128]{1,0:T(8,128)(2,1)S(1)} %slice.16), channel_id=1, source_target_pairs={{0,16},{1,17},{2,18},{3,19},{4,20},{5,21},{6,22},{7,23},{8,24},{9,... | collective-permute-start | bytes 196616 | tf_op jit(solution)/shard_map/ppermute | solution.py:211
  71.3 20.3 %all-to-all-start.1 = ((bf16[16,272,128]{2,1,0:T(8,128)(2,1)}), bf16[16,272,128]{2,1,0:T(8,128)(2,1)S(1)}, u32[]{:S(2)}, u32[]{:S(2)}) async-start(bf16[16,272,128]{2,1,0:T(8,128)(2,1)} %get-tuple-element.12), calls=%async_computation.1 | async-start | bytes 2228224 | tf_op jit(solution)/shard_map/all_to_all | solution.py:217
  77.7 13.2 %collective-permute-start.11 = (bf16[256,256]{1,0:T(8,128)(2,1)S(1)}, bf16[256,256]{1,0:T(8,128)(2,1)S(1)}, u32[]{:S(2)}, u32[]{:S(2)}) collective-permute-start(bf16[256,256]{1,0:T(8,128)(2,1)S(1)} %convolution_convert_fusion), channel_id=1, source_target_pairs={{0,0},{1,32},{2,64},{3,96},{4,4},{5,36},{6,68},{7,100},{8,8},{9,40... | collective-permute-start | bytes 393224 | tf_op jit(solution)/shard_map/ppermute | solution.py:211
  91.6 1.0 %copy-start = (bf16[16,272,128]{2,1,0:T(8,128)(2,1)}, bf16[16,272,128]{2,1,0:T(8,128)(2,1)S(1)}, u32[]{:S(2)}) copy-start(bf16[16,272,128]{2,1,0:T(8,128)(2,1)S(1)} %all-to-all-done.1.m_ref) | copy-start | bytes 3342340

commit v4 on v3

--- a/solution.py
+++ b/solution.py
@@ -53,7 +53,7 @@
                     o_ref[x * NY + y, j * ROWS + g * BLOCK : j * ROWS + (g + 1) * BLOCK] = tile
 
 
-def arrange(table, pieces, k_scr, kt_scr, v_scr, pick_ref):
+def arrange(table, pieces, k_scr, kt_scr, v_scr):
     place = lax.axis_index("blk")
     z, y = place // PLANE, lax.rem(place, NY)
     v_scr[:, HEAD:] = jnp.ones((KEYS, HEAD), jnp.bfloat16)
@@ -66,23 +66,42 @@
                 v_scr[pl.ds(row, BLOCK), :HEAD] = piece[at * 128 + 64 + j * BLOCK : at * 128 + 64 + (j + 1) * BLOCK, :]
     for t in range(KEYS // 128):
         kt_scr[:, t * 128 : (t + 1) * 128] = k_scr[t * 128 : (t + 1) * 128, :].T
-    some = 16
-    offset = lax.rem(z, 2) * 16 + z // 2
-    line = lax.broadcasted_iota(jnp.int32, (NX * some, some * BLOCK), 0)
-    column = lax.broadcasted_iota(jnp.int32, (NX * some, some * BLOCK), 1)
-    wanted = (line % some) * BLOCK + offset + (line // some) * NY
-    select = jnp.where(column == wanted, 1.0, 0.0).astype(jnp.bfloat16)
-    for c in range(KEY_BLOCKS // some):
-        rows = slice(c * some * BLOCK, (c + 1) * some * BLOCK)
-        k = jnp.dot(select, k_scr[rows, :], preferred_element_type=jnp.float32).astype(jnp.bfloat16)
-        v = jnp.dot(select, v_scr[rows, :HEAD], preferred_element_type=jnp.float32).astype(jnp.bfloat16)
-        for x in range(NX):
-            pick_ref[x, c * some : (c + 1) * some, :HEAD] = k[x * some : (x + 1) * some]
-            pick_ref[x, c * some : (c + 1) * some, HEAD:] = v[x * some : (x + 1) * some]
+
+
+def pick_kernel(*refs):
+    own, r1, r2, r3, l1, l2, l3, r4, l4 = refs[:9]
+    o_refs = refs[9:]
+    place = lax.axis_index("blk")
+    z, x = place // PLANE, lax.rem(place // NY, NX)
+
+    def select(lines, rows):
+        count = 2 * NX * lines * 2
+        out = lax.broadcasted_iota(jnp.int32, (count, rows), 0)
+        column = lax.broadcasted_iota(jnp.int32, (count, rows), 1)
+        half, k, line, j = out // (NX * lines * 2), out // (lines * 2) % NX, out // 2 % lines, out % 2
+        offset = lax.rem(z, 2) * 16 + (x ^ k) * NY + z // 2
+        wanted = line * 128 + half * 64 + j * BLOCK + offset
+        return jnp.where(column == wanted, 1.0, 0.0).astype(jnp.bfloat16)
+
+    whole, part = select(NY, 512), select(NY // 2, 256)
+    picked = [jnp.dot(whole, piece[...], preferred_element_type=jnp.float32) for piece in (own, l1, l2, l3)]
+    picked.append([jnp.dot(part, piece[...], preferred_element_type=jnp.float32) for piece in (r4, l4)])
+    picked += [jnp.dot(whole, piece[...], preferred_element_type=jnp.float32) for piece in (r3, r2, r1)]
+    for k in range(NX):
+        for half in range(2):
+            rows = []
+            for piece in picked:
+                if isinstance(piece, list):
+                    at = (half * NX + k) * 4
+                    rows += [piece[0][at : at + 4], piece[1][at : at + 4]]
+                else:
+                    at = (half * NX + k) * 8
+                    rows.append(piece[at : at + 8])
+            o_refs[k][:, half * HEAD : (half + 1) * HEAD] = jnp.concatenate(rows, axis=0).astype(jnp.bfloat16)
 
 
 def attention_kernel(table, q_ref, kpos_ref, *refs):
-    pieces, (o_ref, pick_ref, k_scr, kt_scr, v_scr, s_scr, stat) = refs[:9], refs[9:]
+    pieces, (o_ref, k_scr, kt_scr, v_scr, s_scr, stat) = refs[:9], refs[9:]
     own, r1, r2, r3, l1, l2, l3, r4, l4 = pieces
     every, first, last = range(NY), range(NY // 2), range(NY // 2, NY)
     arrange(
@@ -92,7 +111,6 @@
         k_scr,
         kt_scr,
         v_scr,
-        pick_ref,
     )
     lane = lax.broadcasted_iota(jnp.int32, (ROWS, 128), 1)
     token = lax.broadcasted_iota(jnp.int32, (BLOCK, CHUNK), 0)
@@ -225,9 +243,9 @@
     )(segment_head, rotated_key_value.reshape(128, KEY_VALUE_HEADS * HEAD))
     line = [kv[0]] + [move(kv[k], lambda a, b, c, k=k: index(a, b, c ^ k)) for k in range(1, NY)]
     own = jnp.concatenate(line, axis=0)
-    right = lambda v: move(v, lambda a, b, c: index(a + 1, b, c))
-    left = lambda v: move(v, lambda a, b, c: index(a - 1, b, c))
-    r1, l1 = right(own), left(own)
+    shift = lambda v, d: move(v, lambda a, b, c: index(a + d, b, c))
+    r1, l1 = shift(own, 1), shift(own, -1)
+    r2, l2 = shift(own, 2), shift(own, -2)
     q = pl.pallas_call(
         split_q_kernel,
         out_shape=jax.ShapeDtypeStruct((PLANE, 2 * ROWS, HEAD), jnp.bfloat16),
@@ -235,11 +253,11 @@
         out_specs=VMEM,
         name="split_q",
     )(segment_head, query.reshape(2 * BLOCK, QUERY_HEADS * HEAD))
+    q, _ = lax.optimization_barrier((q, (r1, l1, r2, l2)))
     q = exchange(q, planes).reshape(Q_BLOCKS, ROWS, HEAD)
-    r2, l2 = right(r1), left(l1)
-    r3, l3 = right(r2), left(l2)
+    r3, l3 = shift(r1, 2), shift(l1, -2)
     half = own.shape[0] // 2
-    r4, l4 = right(r3[:half]), left(l3[half:])
+    r4, l4 = shift(r2[:half], 2), shift(l2[half:], -2)
 
     ids = block_map.reshape(NZ, NX, NY, 2).transpose(1, 0, 2, 3).reshape(NX, KEY_BLOCKS)
     rank = ranks(ids)
@@ -258,14 +276,12 @@
     kpos = mine[:, None] * BLOCK + jnp.arange(BLOCK, dtype=jnp.int32)[None, :]
     kpos = kpos.reshape(KEYS // CHUNK, CHUNK)
 
-    out, pick = pl.pallas_call(
+    pieces = (own, r1, r2, r3, l1, l2, l3, r4, l4)
+    partial = pl.pallas_call(
         attention_kernel,
-        out_shape=(
-            jax.ShapeDtypeStruct((PLANE, MESSAGE, HEAD), jnp.bfloat16),
-            jax.ShapeDtypeStruct((NX, KEY_BLOCKS, 2 * HEAD), jnp.bfloat16),
-        ),
+        out_shape=jax.ShapeDtypeStruct((PLANE, MESSAGE, HEAD), jnp.bfloat16),
         in_specs=[SMEM] + [VMEM] * 11,
-        out_specs=(VMEM, VMEM),
+        out_specs=VMEM,
         scratch_shapes=[
             pltpu.VMEM((KEYS, HEAD), jnp.bfloat16),
             pltpu.VMEM((HEAD, KEYS), jnp.bfloat16),
@@ -276,16 +292,29 @@
         compiler_params=PARAMS,
         cost_estimate=pl.CostEstimate(flops=3_000_000_000, bytes_accessed=4_000_000, transcendentals=5_000_000),
         name="attention",
-    )(table, q, kpos, own, r1, r2, r3, l1, l2, l3, r4, l4)
-    out = exchange(out, planes)
-    offset = (z % 2) * 16 + z // 2
-
-    pick = exchange(pick, x_groups).reshape(BLOCKS, 2 * HEAD)
+    )(table, q, kpos, *pieces)
+    out = exchange(partial, planes)
+
+    pieces, _ = lax.optimization_barrier((pieces, partial))
+    picked = pl.pallas_call(
+        pick_kernel,
+        out_shape=(jax.ShapeDtypeStruct((KEY_BLOCKS, 2 * HEAD), jnp.bfloat16),) * NX,
+        in_specs=[VMEM] * 9,
+        out_specs=(VMEM,) * NX,
+        cost_estimate=pl.CostEstimate(flops=20_000_000, bytes_accessed=1_200_000, transcendentals=0),
+        name="pick",
+    )(*pieces)
+    picked = jnp.concatenate(
+        [move(picked[k], lambda a, b, c, k=k: index(2 * c + a % 2, b ^ k, a // 2)) for k in range(NX)], axis=0
+    )
     blocks = jnp.arange(BLOCKS, dtype=jnp.int32)
-    position = blocks * BLOCK + offset + 4 * x
-    choose = (ordered.reshape(1, BLOCKS) == blocks[:, None]) & (position < lengths[0])[:, None]
-    cache = jnp.dot(choose.astype(jnp.bfloat16), pick, preferred_element_type=jnp.float32).astype(jnp.bfloat16)
-    cache = move(cache, lambda a, b, c: index(2 * c + a % 2, b, a // 2))
+    stored = jnp.sum(jnp.where(block_map[None, :] == blocks[:, None], blocks[None, :], 0), axis=1, dtype=jnp.int32)
+    from_z, from_y = 2 * y + z % 2, z // 2
+    row = ((stored // 8 % NX) ^ x) * KEY_BLOCKS + (stored // 32 - from_z) % NZ * 8
+    row = row + ((stored // 2 % NY) ^ from_y) * 2 + stored % 2
+    position = blocks * BLOCK + place % BLOCK
+    choose = (row[:, None] == blocks[None, :]) & (position < lengths[0])[:, None]
+    cache = jnp.dot(choose.astype(jnp.bfloat16), picked, preferred_element_type=jnp.float32).astype(jnp.bfloat16)
     cache = cache.reshape(BLOCKS, 2, HEAD).transpose(1, 0, 2)[None, :, None]
 
     my_blocks = lax.dynamic_slice_in_dim(block_map, 2 * place, 2)

time: 95 us -> 102 us (1.074)
  starting transfers between devices: 36.7 us -> 56.5 us
  blocking collectives: 9.93 us -> 0 us
  waiting for transfers between devices: 23.6 us -> 18.2 us
  local copies, waits for them, and re-layouts: 3.45 us -> 5.66 us
    ppermute x12 -> x15, starting transfers between devices: 22.8 us -> 41.2 us  [move(): lax.ppermute(value, 'blk', [(s, target(s // 16, s // 4 % 4, s % 4)) for s...]
    all_to_all x1 -> x0, blocking collectives: 9.93 us -> none  [exchange(): lax.all_to_all(value, 'blk', 0, 0, axis_index_groups=groups, tiled=True)]
    ppermute x12 -> x15, waiting for transfers between devices: 23.6 us -> 17.7 us  [move(): lax.ppermute(value, 'blk', [(s, target(s // 16, s // 4 % 4, s % 4)) for s...]
    all_to_all x2, starting transfers between devices: 13.9 us -> 15.3 us  [exchange(): lax.all_to_all(value, 'blk', 0, 0, axis_index_groups=groups, tiled=True)]
    pallas_call x1 -> x2, Pallas kernels: 12.3 us -> 12.9 us  [the longest x1 10.6 us: body(): pl.pallas_call(attention_kernel, out_shape=jax.ShapeDtypeStruct((PLANE, M...]
  transfers between devices with their start and end apart: 14 -> 17, of which waited for: 6 -> 8; matrix products, arithmetic and copies ran while one was open for 4% -> 6% of each run, Pallas kernels for 2% -> 4%
where the time goes in v4:
time: 102 us; the launch traced here: 103 us
  starting transfers between devices  56.5 us (55%)
  Pallas kernels  19.4 us (19%)
  waiting for transfers between devices  18.2 us (18%)
  local copies, waits for them, and re-layouts  5.66 us (6%)
  between operations  1.48 us (1%)
  other arithmetic  1.26 us (1%)
    ppermute x15, starting transfers between devices, move(): lax.ppermute(value, 'blk', [(s, target(s // 16, s // 4 % 4, s % 4)) for s...  41.2 us
    ppermute x15, waiting for transfers between devices, move(): lax.ppermute(value, 'blk', [(s, target(s // 16, s // 4 % 4, s % 4)) for s...  17.7 us
    all_to_all x2, starting transfers between devices, exchange(): lax.all_to_all(value, 'blk', 0, 0, axis_index_groups=groups, tiled=True)  15.3 us
    pallas_call x1, Pallas kernels, body(): pl.pallas_call(attention_kernel, out_shape=jax.ShapeDtypeStruct((PLANE, M...  10.6 us
    pallas_call x1, Pallas kernels, body(): pl.pallas_call(combine_kernel, out_shape=jax.ShapeDtypeStruct((2 * BLOCK,...  2.79 us
    pallas_call x1, Pallas kernels, body(): pl.pallas_call(pick_kernel, out_shape=(jax.ShapeDtypeStruct((KEY_BLOCKS,...  2.26 us
    pallas_call x1, Pallas kernels, body(): pl.pallas_call(split_q_kernel, out_shape=jax.ShapeDtypeStruct((PLANE, 2 *...  2.08 us
  transfers between devices with their start and end apart: 17, of which 8 were waited for; matrix products, arithmetic and copies ran while one was open for 6% of the time, Pallas kernels for 4%

profile of v4, /device:TPU:16, one launch (start us, length us, event | category | flops | bytes accessed | tf_op | source)
XLA Modules:
  0.0 102.8 jit_solution(4585419480256096889)
XLA Ops:
  0.6 1.6 %split_kv.1 = (bf16[128,128]{1,0:T(8,128)(2,1)}, bf16[128,128]{1,0:T(8,128)(2,1)}, bf16[128,128]{1,0:T(8,128)(2,1)}, bf16[128,128]{1,0:T(8,128)(2,1)}) custom-call(s32[4]{0:T(128)} %heads.5, bf16[128,512]{1,0:T(8,128)(2,1)} %bitcast.21), custom_call_target="tpu_custom_call" | custom-call | tf_op jit(solution)/shard_map/split_kv/pallas_call | solution.py:237
  2.2 1.3 %collective-permute-start = (bf16[128,128]{1,0:T(8,128)(2,1)}, bf16[128,128]{1,0:T(8,128)(2,1)S(1)}, u32[]{:S(2)}, u32[]{:S(2)}) collective-permute-start(bf16[128,128]{1,0:T(8,128)(2,1)} %get-tuple-element.21), channel_id=1, source_target_pairs={{0,1},{1,0},{2,3},{3,2},{4,5},{5,4},{6,7},{7,6},{8,9},{9,8},{10,11... | collective-permute-start | bytes 98312 | tf_op jit(solution)/shard_map/ppermute | solution.py:229
  3.5 0.8 collective-permute-start.1
  4.3 1.4 %collective-permute-start.2 = (bf16[128,128]{1,0:T(8,128)(2,1)}, bf16[128,128]{1,0:T(8,128)(2,1)S(1)}, u32[]{:S(2)}, u32[]{:S(2)}) collective-permute-start(bf16[128,128]{1,0:T(8,128)(2,1)} %get-tuple-element.23), channel_id=1, source_target_pairs={{0,3},{1,2},{2,1},{3,0},{4,7},{5,6},{6,5},{7,4},{8,11},{9,10},{10,... | collective-permute-start | bytes 98312 | tf_op jit(solution)/shard_map/ppermute | solution.py:229
  5.7 0.8 constant_dynamic-update-slice_fusion.3
  6.5 0.8 dynamic_slice.15
  7.2 1.9 %collective-permute-done.1 = bf16[128,128]{1,0:T(8,128)(2,1)S(1)} collective-permute-done((bf16[128,128]{1,0:T(8,128)(2,1)}, bf16[128,128]{1,0:T(8,128)(2,1)S(1)}, u32[]{:S(2)}, u32[]{:S(2)}) %collective-permute-start.1) | collective-permute-done | bytes 32800 | tf_op jit(solution)/shard_map/ppermute | solution.py:229
  9.2 6.4 %collective-permute-start.6 = (bf16[512,128]{1,0:T(8,128)(2,1)S(1)}, bf16[512,128]{1,0:T(8,128)(2,1)S(1)}, u32[]{:S(2)}, u32[]{:S(2)}) collective-permute-start(bf16[512,128]{1,0:T(8,128)(2,1)S(1)} %constant_dynamic-update-slice_fusion.refs_0_), channel_id=1, source_target_pairs={{0,96},{1,97},{2,98},{3,99},{4,100},{5,101},{6,102},{7,103},{8,104... | collective-permute-start | bytes 393224 | tf_op jit(solution)/shard_map/ppermute | solution.py:229
  15.6 3.7 %collective-permute-start.4 = (bf16[512,128]{1,0:T(8,128)(2,1)S(1)}, bf16[512,128]{1,0:T(8,128)(2,1)S(1)}, u32[]{:S(2)}, u32[]{:S(2)}) collective-permute-start(bf16[512,128]{1,0:T(8,128)(2,1)S(1)} %constant_dynamic-update-slice_fusion.refs_0_), channel_id=1, source_target_pairs={{0,112},{1,113},{2,114},{3,115},{4,116},{5,117},{6,118},{7,119},{8... | collective-permute-start | bytes 393224 | tf_op jit(solution)/shard_map/ppermute | solution.py:229
  19.5 0.8 reshape.143
  21.0 2.1 %split_q.1 = bf16[16,256,128]{2,1,0:T(8,128)(2,1)} custom-call(s32[4]{0:T(128)} %heads.5, bf16[64,2048]{1,0:T(8,128)(2,1)} %bitcast.17), custom_call_target="tpu_custom_call" | custom-call | tf_op jit(solution)/shard_map/split_q/pallas_call | solution.py:249
  23.1 1.8 %collective-permute-done.5.refs_2_ = bf16[512,128]{1,0:T(8,128)(2,1)S(1)} collective-permute-done((bf16[512,128]{1,0:T(8,128)(2,1)S(1)}, bf16[512,128]{1,0:T(8,128)(2,1)S(1)}, u32[]{:S(2)}, u32[]{:S(2)}) %collective-permute-start.5) | collective-permute-done | bytes 131104 | tf_op jit(solution)/shard_map/ppermute | solution.py:229
  24.9 1.5 %collective-permute-done.3.refs_1_ = bf16[512,128]{1,0:T(8,128)(2,1)S(1)} collective-permute-done((bf16[512,128]{1,0:T(8,128)(2,1)S(1)}, bf16[512,128]{1,0:T(8,128)(2,1)S(1)}, u32[]{:S(2)}, u32[]{:S(2)}) %collective-permute-start.3) | collective-permute-done | bytes 131104 | tf_op jit(solution)/shard_map/ppermute | solution.py:229
  26.4 7.3 %all-to-all-start = ((bf16[16,256,128]{2,1,0:T(8,128)(2,1)}), bf16[16,256,128]{2,1,0:T(8,128)(2,1)S(1)}, u32[]{:S(2)}, u32[]{:S(2)}) async-start(bf16[16,256,128]{2,1,0:T(8,128)(2,1)} %split_q.1), calls=%async_computation | async-start | bytes 2097152 | tf_op jit(solution)/shard_map/all_to_all | solution.py:235
  35.0 2.7 %collective-permute-start.7 = (bf16[512,128]{1,0:T(8,128)(2,1)S(1)}, bf16[512,128]{1,0:T(8,128)(2,1)S(1)}, u32[]{:S(2)}, u32[]{:S(2)}) collective-permute-start(bf16[512,128]{1,0:T(8,128)(2,1)S(1)} %collective-permute-done.3.refs_1_), channel_id=1, source_target_pairs={{0,32},{1,33},{2,34},{3,35},{4,36},{5,37},{6,38},{7,39},{8,40},{9,... | collective-permute-start | bytes 393224 | tf_op jit(solution)/shard_map/ppermute | solution.py:229
  37.7 1.5 %collective-permute-start.10 = (bf16[256,128]{1,0:T(8,128)(2,1)S(1)}, bf16[256,128]{1,0:T(8,128)(2,1)S(1)}, u32[]{:S(2)}, u32[]{:S(2)}) collective-permute-start(bf16[256,128]{1,0:T(8,128)(2,1)S(1)} %slice.17), channel_id=1, source_target_pairs={{0,96},{1,97},{2,98},{3,99},{4,100},{5,101},{6,102},{7,103},{8,104... | collective-permute-start | bytes 196616 | tf_op jit(solution)/shard_map/ppermute | solution.py:229
  39.3 1.5 %collective-permute-start.9 = (bf16[256,128]{1,0:T(8,128)(2,1)S(1)}, bf16[256,128]{1,0:T(8,128)(2,1)S(1)}, u32[]{:S(2)}, u32[]{:S(2)}) collective-permute-start(bf16[256,128]{1,0:T(8,128)(2,1)S(1)} %slice.16), channel_id=1, source_target_pairs={{0,32},{1,33},{2,34},{3,35},{4,36},{5,37},{6,38},{7,39},{8,40},{9,... | collective-permute-start | bytes 196616 | tf_op jit(solution)/shard_map/ppermute | solution.py:229
  40.8 3.2 %collective-permute-done.10.refs_8_ = bf16[256,128]{1,0:T(8,128)(2,1)S(1)} collective-permute-done((bf16[256,128]{1,0:T(8,128)(2,1)S(1)}, bf16[256,128]{1,0:T(8,128)(2,1)S(1)}, u32[]{:S(2)}, u32[]{:S(2)}) %collective-permute-start.10) | collective-permute-done | bytes 65568 | tf_op jit(solution)/shard_map/ppermute | solution.py:229
  44.0 2.2 %collective-permute-done.9.refs_7_ = bf16[256,128]{1,0:T(8,128)(2,1)S(1)} collective-permute-done((bf16[256,128]{1,0:T(8,128)(2,1)S(1)}, bf16[256,128]{1,0:T(8,128)(2,1)S(1)}, u32[]{:S(2)}, u32[]{:S(2)}) %collective-permute-start.9) | collective-permute-done | bytes 65568 | tf_op jit(solution)/shard_map/ppermute | solution.py:229
  46.7 10.6 %attention.1 = bf16[16,272,128]{2,1,0:T(8,128)(2,1)} custom-call(s32[144]{0:T(256)S(1)} %concatenate.9.table, bf16[32,128,128]{2,1,0:T(8,128)(2,1)S(1)} %bitcast.16, s32[8,256]{1,0:T(8,128)S(1)} %broadcast_add_fusion.kpos_ref, bf16[512,128]{1,0:T(8,128)(2,1)S(1)} %constant_dynamic-update-slice_fusion.refs_0_, ...), custom_call_target="tpu_custom_call" | custom-call | flops 3000000000 | bytes 4000000 | tf_op jit(solution)/shard_map/attention/pallas_call | solution.py:280
  57.4 8.0 %all-to-all-start.1 = ((bf16[16,272,128]{2,1,0:T(8,128)(2,1)}), bf16[16,272,128]{2,1,0:T(8,128)(2,1)S(1)}, u32[]{:S(2)}, u32[]{:S(2)}) async-start(bf16[16,272,128]{2,1,0:T(8,128)(2,1)} %attention.1), calls=%async_computation.1 | async-start | bytes 2228224 | tf_op jit(solution)/shard_map/all_to_all | solution.py:235
  66.2 2.3 %pick.1 = (bf16[64,256]{1,0:T(8,128)(2,1)}, bf16[64,256]{1,0:T(8,128)(2,1)}, bf16[64,256]{1,0:T(8,128)(2,1)}, bf16[64,256]{1,0:T(8,128)(2,1)}) custom-call(bf16[512,128]{1,0:T(8,128)(2,1)} %copy-done.2, bf16[512,128]{1,0:T(8,128)(2,1)} %copy-done.4, bf16[512,128]{1,0:T(8,128)(2,1)} %copy-done.1, bf16[512,128]{1,0:T(8,128)(2,1)} %copy-done.6, ...), custom_call_target="tpu_custom_call" | custom-call | flops 20000000 | bytes 1200000 | tf_op jit(solution)/shard_map/pick/pallas_call | solution.py:299
  68.5 5.0 %collective-permute-start.11 = (bf16[64,256]{1,0:T(8,128)(2,1)}, bf16[64,256]{1,0:T(8,128)(2,1)S(1)}, u32[]{:S(2)}, u32[]{:S(2)}) collective-permute-start(bf16[64,256]{1,0:T(8,128)(2,1)} %get-tuple-element.34), channel_id=1, source_target_pairs={{0,0},{1,32},{2,64},{3,96},{4,4},{5,36},{6,68},{7,100},{8,8},{9,40... | collective-permute-start | bytes 98312 | tf_op jit(solution)/shard_map/ppermute | solution.py:229
  73.5 6.2 %collective-permute-start.12 = (bf16[64,256]{1,0:T(8,128)(2,1)}, bf16[64,256]{1,0:T(8,128)(2,1)S(1)}, u32[]{:S(2)}, u32[]{:S(2)}) collective-permute-start(bf16[64,256]{1,0:T(8,128)(2,1)} %get-tuple-element.35), channel_id=1, source_target_pairs={{0,4},{1,36},{2,68},{3,100},{4,0},{5,32},{6,64},{7,96},{8,12},{9,4... | collective-permute-start | bytes 98312 | tf_op jit(solution)/shard_map/ppermute | solution.py:229
  79.7 5.6 %collective-permute-start.13 = (bf16[64,256]{1,0:T(8,128)(2,1)}, bf16[64,256]{1,0:T(8,128)(2,1)S(1)}, u32[]{:S(2)}, u32[]{:S(2)}) collective-permute-start(bf16[64,256]{1,0:T(8,128)(2,1)} %get-tuple-element.36), channel_id=1, source_target_pairs={{0,8},{1,40},{2,72},{3,104},{4,12},{5,44},{6,76},{7,108},{8,0},{9,... | collective-permute-start | bytes 98312 | tf_op jit(solution)/shard_map/ppermute | solution.py:229
  85.3 4.8 %collective-permute-start.14 = (bf16[64,256]{1,0:T(8,128)(2,1)}, bf16[64,256]{1,0:T(8,128)(2,1)S(1)}, u32[]{:S(2)}, u32[]{:S(2)}) collective-permute-start(bf16[64,256]{1,0:T(8,128)(2,1)} %get-tuple-element.37), channel_id=1, source_target_pairs={{0,12},{1,44},{2,76},{3,108},{4,8},{5,40},{6,72},{7,104},{8,4},{9,... | collective-permute-start | bytes 98312 | tf_op jit(solution)/shard_map/ppermute | solution.py:229
  90.2 0.6 dynamic_slice.13.blocks
  90.8 1.9 %collective-permute-done.13 = bf16[64,256]{1,0:T(8,128)(2,1)S(1)} collective-permute-done((bf16[64,256]{1,0:T(8,128)(2,1)}, bf16[64,256]{1,0:T(8,128)(2,1)S(1)}, u32[]{:S(2)}, u32[]{:S(2)}) %collective-permute-start.13) | collective-permute-done | bytes 32800 | tf_op jit(solution)/shard_map/ppermute | solution.py:229
  92.7 5.2 %collective-permute-done.14 = bf16[64,256]{1,0:T(8,128)(2,1)S(1)} collective-permute-done((bf16[64,256]{1,0:T(8,128)(2,1)}, bf16[64,256]{1,0:T(8,128)(2,1)S(1)}, u32[]{:S(2)}, u32[]{:S(2)}) %collective-permute-start.14) | collective-permute-done | bytes 32800 | tf_op jit(solution)/shard_map/ppermute | solution.py:229
  98.2 0.8 copy.15
  99.0 1.0 copy-done.9
  100.0 2.8 %combine.1 = bf16[64,2048]{1,0:T(8,128)(2,1)} custom-call(s32[4]{0:T(128)} %heads.5, s32[2]{0:T(128)} %dynamic_slice.13.blocks, s32[1]{0:T(128)} %copy.19.length, bf16[16,272,128]{2,1,0:T(8,128)(2,1)} %copy-done.9), custom_call_target="tpu_custom_call" | custom-call | tf_op jit(solution)/shard_map/combine/pallas_call | solution.py:321
  (62 shorter events, 3.4 us)
Async XLA Ops:
  2.2 5.0 %collective-permute-start = (bf16[128,128]{1,0:T(8,128)(2,1)}, bf16[128,128]{1,0:T(8,128)(2,1)S(1)}, u32[]{:S(2)}, u32[]{:S(2)}) collective-permute-start(bf16[128,128]{1,0:T(8,128)(2,1)} %get-tuple-element.21), channel_id=1, source_target_pairs={{0,1},{1,0},{2,3},{3,2},{4,5},{5,4},{6,7},{7,6},{8,9},{9,8},{10,11... | collective-permute-start | bytes 98312 | tf_op jit(solution)/shard_map/ppermute | solution.py:229
  3.5 5.6 %collective-permute-start.1 = (bf16[128,128]{1,0:T(8,128)(2,1)}, bf16[128,128]{1,0:T(8,128)(2,1)S(1)}, u32[]{:S(2)}, u32[]{:S(2)}) collective-permute-start(bf16[128,128]{1,0:T(8,128)(2,1)} %get-tuple-element.22), channel_id=1, source_target_pairs={{0,2},{1,3},{2,0},{3,1},{4,6},{5,7},{6,4},{7,5},{8,10},{9,11},{10,... | collective-permute-start | bytes 98312 | tf_op jit(solution)/shard_map/ppermute | solution.py:229
  4.3 4.8 %collective-permute-start.2 = (bf16[128,128]{1,0:T(8,128)(2,1)}, bf16[128,128]{1,0:T(8,128)(2,1)S(1)}, u32[]{:S(2)}, u32[]{:S(2)}) collective-permute-start(bf16[128,128]{1,0:T(8,128)(2,1)} %get-tuple-element.23), channel_id=1, source_target_pairs={{0,3},{1,2},{2,1},{3,0},{4,7},{5,6},{6,5},{7,4},{8,11},{9,10},{10,... | collective-permute-start | bytes 98312 | tf_op jit(solution)/shard_map/ppermute | solution.py:229
  9.2 37.5 %copy-start.2 = (bf16[512,128]{1,0:T(8,128)(2,1)}, bf16[512,128]{1,0:T(8,128)(2,1)S(1)}, u32[]{:S(2)}) copy-start(bf16[512,128]{1,0:T(8,128)(2,1)S(1)} %constant_dynamic-update-slice_fusion.refs_0_) | copy-start | bytes 393220
  9.2 13.9 %collective-permute-start.6 = (bf16[512,128]{1,0:T(8,128)(2,1)S(1)}, bf16[512,128]{1,0:T(8,128)(2,1)S(1)}, u32[]{:S(2)}, u32[]{:S(2)}) collective-permute-start(bf16[512,128]{1,0:T(8,128)(2,1)S(1)} %constant_dynamic-update-slice_fusion.refs_0_), channel_id=1, source_target_pairs={{0,96},{1,97},{2,98},{3,99},{4,100},{5,101},{6,102},{7,103},{8,104... | collective-permute-start | bytes 393224 | tf_op jit(solution)/shard_map/ppermute | solution.py:229
  15.6 9.3 %collective-permute-start.5 = (bf16[512,128]{1,0:T(8,128)(2,1)S(1)}, bf16[512,128]{1,0:T(8,128)(2,1)S(1)}, u32[]{:S(2)}, u32[]{:S(2)}) collective-permute-start(bf16[512,128]{1,0:T(8,128)(2,1)S(1)} %constant_dynamic-update-slice_fusion.refs_0_), channel_id=1, source_target_pairs={{0,32},{1,33},{2,34},{3,35},{4,36},{5,37},{6,38},{7,39},{8,40},{9,... | collective-permute-start | bytes 393224 | tf_op jit(solution)/shard_map/ppermute | solution.py:229
  15.6 9.3 %collective-permute-start.4 = (bf16[512,128]{1,0:T(8,128)(2,1)S(1)}, bf16[512,128]{1,0:T(8,128)(2,1)S(1)}, u32[]{:S(2)}, u32[]{:S(2)}) collective-permute-start(bf16[512,128]{1,0:T(8,128)(2,1)S(1)} %constant_dynamic-update-slice_fusion.refs_0_), channel_id=1, source_target_pairs={{0,112},{1,113},{2,114},{3,115},{4,116},{5,117},{6,118},{7,119},{8... | collective-permute-start | bytes 393224 | tf_op jit(solution)/shard_map/ppermute | solution.py:229
  19.2 7.1 %collective-permute-start.3 = (bf16[512,128]{1,0:T(8,128)(2,1)S(1)}, bf16[512,128]{1,0:T(8,128)(2,1)S(1)}, u32[]{:S(2)}, u32[]{:S(2)}) collective-permute-start(bf16[512,128]{1,0:T(8,128)(2,1)S(1)} %constant_dynamic-update-slice_fusion.refs_0_), channel_id=1, source_target_pairs={{0,16},{1,17},{2,18},{3,19},{4,20},{5,21},{6,22},{7,23},{8,24},{9,... | collective-permute-start | bytes 393224 | tf_op jit(solution)/shard_map/ppermute | solution.py:229
  23.1 23.6 %copy-start = (bf16[512,128]{1,0:T(8,128)(2,1)}, bf16[512,128]{1,0:T(8,128)(2,1)S(1)}, u32[]{:S(2)}) copy-start(bf16[512,128]{1,0:T(8,128)(2,1)S(1)} %collective-permute-done.6.refs_5_) | copy-start | bytes 393220
  24.9 21.8 %copy-start.1 = (bf16[512,128]{1,0:T(8,128)(2,1)}, bf16[512,128]{1,0:T(8,128)(2,1)S(1)}, u32[]{:S(2)}) copy-start(bf16[512,128]{1,0:T(8,128)(2,1)S(1)} %collective-permute-done.5.refs_2_) | copy-start | bytes 393220
  24.9 21.8 %copy-start.3 = (bf16[512,128]{1,0:T(8,128)(2,1)}, bf16[512,128]{1,0:T(8,128)(2,1)S(1)}, u32[]{:S(2)}) copy-start(bf16[512,128]{1,0:T(8,128)(2,1)S(1)} %collective-permute-done.4.refs_4_) | copy-start | bytes 393220
  26.4 20.4 %copy-start.4 = (bf16[512,128]{1,0:T(8,128)(2,1)}, bf16[512,128]{1,0:T(8,128)(2,1)S(1)}, u32[]{:S(2)}) copy-start(bf16[512,128]{1,0:T(8,128)(2,1)S(1)} %collective-permute-done.3.refs_1_) | copy-start | bytes 393220
  26.4 20.3 %all-to-all-start = ((bf16[16,256,128]{2,1,0:T(8,128)(2,1)}), bf16[16,256,128]{2,1,0:T(8,128)(2,1)S(1)}, u32[]{:S(2)}, u32[]{:S(2)}) async-start(bf16[16,256,128]{2,1,0:T(8,128)(2,1)} %split_q.1), calls=%async_computation | async-start | bytes 2097152 | tf_op jit(solution)/shard_map/all_to_all | solution.py:235
  34.7 11.5 %collective-permute-start.8 = (bf16[512,128]{1,0:T(8,128)(2,1)S(1)}, bf16[512,128]{1,0:T(8,128)(2,1)S(1)}, u32[]{:S(2)}, u32[]{:S(2)}) collective-permute-start(bf16[512,128]{1,0:T(8,128)(2,1)S(1)} %collective-permute-done.4.refs_4_), channel_id=1, source_target_pairs={{0,96},{1,97},{2,98},{3,99},{4,100},{5,101},{6,102},{7,103},{8,104... | collective-permute-start | bytes 393224 | tf_op jit(solution)/shard_map/ppermute | solution.py:229
  35.0 11.2 %collective-permute-start.7 = (bf16[512,128]{1,0:T(8,128)(2,1)S(1)}, bf16[512,128]{1,0:T(8,128)(2,1)S(1)}, u32[]{:S(2)}, u32[]{:S(2)}) collective-permute-start(bf16[512,128]{1,0:T(8,128)(2,1)S(1)} %collective-permute-done.3.refs_1_), channel_id=1, source_target_pairs={{0,32},{1,33},{2,34},{3,35},{4,36},{5,37},{6,38},{7,39},{8,40},{9,... | collective-permute-start | bytes 393224 | tf_op jit(solution)/shard_map/ppermute | solution.py:229
  37.7 6.3 %collective-permute-start.10 = (bf16[256,128]{1,0:T(8,128)(2,1)S(1)}, bf16[256,128]{1,0:T(8,128)(2,1)S(1)}, u32[]{:S(2)}, u32[]{:S(2)}) collective-permute-start(bf16[256,128]{1,0:T(8,128)(2,1)S(1)} %slice.17), channel_id=1, source_target_pairs={{0,96},{1,97},{2,98},{3,99},{4,100},{5,101},{6,102},{7,103},{8,104... | collective-permute-start | bytes 196616 | tf_op jit(solution)/shard_map/ppermute | solution.py:229
  39.3 6.9 %collective-permute-start.9 = (bf16[256,128]{1,0:T(8,128)(2,1)S(1)}, bf16[256,128]{1,0:T(8,128)(2,1)S(1)}, u32[]{:S(2)}, u32[]{:S(2)}) collective-permute-start(bf16[256,128]{1,0:T(8,128)(2,1)S(1)} %slice.16), channel_id=1, source_target_pairs={{0,32},{1,33},{2,34},{3,35},{4,36},{5,37},{6,38},{7,39},{8,40},{9,... | collective-permute-start | bytes 196616 | tf_op jit(solution)/shard_map/ppermute | solution.py:229
  44.0 13.3 %copy-start.7 = (bf16[256,128]{1,0:T(8,128)(2,1)}, bf16[256,128]{1,0:T(8,128)(2,1)S(1)}, u32[]{:S(2)}) copy-start(bf16[256,128]{1,0:T(8,128)(2,1)S(1)} %collective-permute-done.10.refs_8_) | copy-start | bytes 196612
  46.2 11.2 %copy-start.8 = (bf16[256,128]{1,0:T(8,128)(2,1)}, bf16[256,128]{1,0:T(8,128)(2,1)S(1)}, u32[]{:S(2)}) copy-start(bf16[256,128]{1,0:T(8,128)(2,1)S(1)} %collective-permute-done.9.refs_7_) | copy-start | bytes 196612
  46.2 11.2 %copy-start.5 = (bf16[512,128]{1,0:T(8,128)(2,1)}, bf16[512,128]{1,0:T(8,128)(2,1)S(1)}, u32[]{:S(2)}) copy-start(bf16[512,128]{1,0:T(8,128)(2,1)S(1)} %collective-permute-done.8.refs_6_) | copy-start | bytes 393220
  46.2 11.2 %copy-start.6 = (bf16[512,128]{1,0:T(8,128)(2,1)}, bf16[512,128]{1,0:T(8,128)(2,1)S(1)}, u32[]{:S(2)}) copy-start(bf16[512,128]{1,0:T(8,128)(2,1)S(1)} %collective-permute-done.7.refs_3_) | copy-start | bytes 393220
  57.4 8.7 %copy-start.10 = (s32[256]{0:T(256)S(1)}, s32[256]{0:T(256)}, u32[]{:S(2)}) copy-start(s32[256]{0:T(256)} %param.8) | copy-start | bytes 3076
  57.4 41.6 %all-to-all-start.1 = ((bf16[16,272,128]{2,1,0:T(8,128)(2,1)}), bf16[16,272,128]{2,1,0:T(8,128)(2,1)S(1)}, u32[]{:S(2)}, u32[]{:S(2)}) async-start(bf16[16,272,128]{2,1,0:T(8,128)(2,1)} %attention.1), calls=%async_computation.1 | async-start | bytes 2228224 | tf_op jit(solution)/shard_map/all_to_all | solution.py:235
  68.5 22.3 %collective-permute-start.11 = (bf16[64,256]{1,0:T(8,128)(2,1)}, bf16[64,256]{1,0:T(8,128)(2,1)S(1)}, u32[]{:S(2)}, u32[]{:S(2)}) collective-permute-start(bf16[64,256]{1,0:T(8,128)(2,1)} %get-tuple-element.34), channel_id=1, source_target_pairs={{0,0},{1,32},{2,64},{3,96},{4,4},{5,36},{6,68},{7,100},{8,8},{9,40... | collective-permute-start | bytes 98312 | tf_op jit(solution)/shard_map/ppermute | solution.py:229
  73.5 17.3 %collective-permute-start.12 = (bf16[64,256]{1,0:T(8,128)(2,1)}, bf16[64,256]{1,0:T(8,128)(2,1)S(1)}, u32[]{:S(2)}, u32[]{:S(2)}) collective-permute-start(bf16[64,256]{1,0:T(8,128)(2,1)} %get-tuple-element.35), channel_id=1, source_target_pairs={{0,4},{1,36},{2,68},{3,100},{4,0},{5,32},{6,64},{7,96},{8,12},{9,4... | collective-permute-start | bytes 98312 | tf_op jit(solution)/shard_map/ppermute | solution.py:229
  79.7 13.0 %collective-permute-start.13 = (bf16[64,256]{1,0:T(8,128)(2,1)}, bf16[64,256]{1,0:T(8,128)(2,1)S(1)}, u32[]{:S(2)}, u32[]{:S(2)}) collective-permute-start(bf16[64,256]{1,0:T(8,128)(2,1)} %get-tuple-element.36), channel_id=1, source_target_pairs={{0,8},{1,40},{2,72},{3,104},{4,12},{5,44},{6,76},{7,108},{8,0},{9,... | collective-permute-start | bytes 98312 | tf_op jit(solution)/shard_map/ppermute | solution.py:229
  85.3 12.5 %collective-permute-start.14 = (bf16[64,256]{1,0:T(8,128)(2,1)}, bf16[64,256]{1,0:T(8,128)(2,1)S(1)}, u32[]{:S(2)}, u32[]{:S(2)}) collective-permute-start(bf16[64,256]{1,0:T(8,128)(2,1)} %get-tuple-element.37), channel_id=1, source_target_pairs={{0,12},{1,44},{2,76},{3,108},{4,8},{5,40},{6,72},{7,104},{8,4},{9,... | collective-permute-start | bytes 98312 | tf_op jit(solution)/shard_map/ppermute | solution.py:229
  99.0 1.0 copy-start.9

commit v5 on v4

--- a/solution.py
+++ b/solution.py
@@ -34,7 +34,8 @@
 
 SMEM = pl.BlockSpec(memory_space=pltpu.SMEM)
 VMEM = pl.BlockSpec(memory_space=pltpu.VMEM)
-PARAMS = pltpu.CompilerParams(vmem_limit_bytes=40 * 1024 * 1024)
+PARAMS = pltpu.CompilerParams(vmem_limit_bytes=24 * 1024 * 1024)
+SMALL = pltpu.CompilerParams(vmem_limit_bytes=8 * 1024 * 1024)
 
 
 def split_kv_kernel(heads, kv_ref, *o_refs):
@@ -70,7 +71,7 @@
 
 def pick_kernel(*refs):
     own, r1, r2, r3, l1, l2, l3, r4, l4 = refs[:9]
-    o_refs = refs[9:]
+    o_ref = refs[9]
     place = lax.axis_index("blk")
     z, x = place // PLANE, lax.rem(place // NY, NX)
 
@@ -97,7 +98,7 @@
                 else:
                     at = (half * NX + k) * 8
                     rows.append(piece[at : at + 8])
-            o_refs[k][:, half * HEAD : (half + 1) * HEAD] = jnp.concatenate(rows, axis=0).astype(jnp.bfloat16)
+            o_ref[k, :, half * HEAD : (half + 1) * HEAD] = jnp.concatenate(rows, axis=0).astype(jnp.bfloat16)
 
 
 def attention_kernel(table, q_ref, kpos_ref, *refs):
@@ -239,25 +240,27 @@
         out_shape=(jax.ShapeDtypeStruct((128, HEAD), jnp.bfloat16),) * NY,
         in_specs=[SMEM, VMEM],
         out_specs=(VMEM,) * NY,
+        compiler_params=SMALL,
         name="split_kv",
     )(segment_head, rotated_key_value.reshape(128, KEY_VALUE_HEADS * HEAD))
     line = [kv[0]] + [move(kv[k], lambda a, b, c, k=k: index(a, b, c ^ k)) for k in range(1, NY)]
     own = jnp.concatenate(line, axis=0)
-    shift = lambda v, d: move(v, lambda a, b, c: index(a + d, b, c))
-    r1, l1 = shift(own, 1), shift(own, -1)
-    r2, l2 = shift(own, 2), shift(own, -2)
+    right = lambda v: move(v, lambda a, b, c: index(a + 1, b, c))
+    left = lambda v: move(v, lambda a, b, c: index(a - 1, b, c))
+    r1, l1 = right(own), left(own)
     q = pl.pallas_call(
         split_q_kernel,
         out_shape=jax.ShapeDtypeStruct((PLANE, 2 * ROWS, HEAD), jnp.bfloat16),
         in_specs=[SMEM, VMEM],
         out_specs=VMEM,
+        compiler_params=SMALL,
         name="split_q",
     )(segment_head, query.reshape(2 * BLOCK, QUERY_HEADS * HEAD))
-    q, _ = lax.optimization_barrier((q, (r1, l1, r2, l2)))
     q = exchange(q, planes).reshape(Q_BLOCKS, ROWS, HEAD)
-    r3, l3 = shift(r1, 2), shift(l1, -2)
+    r2, l2 = right(r1), left(l1)
+    r3, l3 = right(r2), left(l2)
     half = own.shape[0] // 2
-    r4, l4 = shift(r2[:half], 2), shift(l2[half:], -2)
+    r4, l4 = right(r3[:half]), left(l3[half:])
 
     ids = block_map.reshape(NZ, NX, NY, 2).transpose(1, 0, 2, 3).reshape(NX, KEY_BLOCKS)
     rank = ranks(ids)
@@ -277,6 +280,16 @@
     kpos = kpos.reshape(KEYS // CHUNK, CHUNK)
 
     pieces = (own, r1, r2, r3, l1, l2, l3, r4, l4)
+    picked = pl.pallas_call(
+        pick_kernel,
+        out_shape=jax.ShapeDtypeStruct((NX, KEY_BLOCKS, 2 * HEAD), jnp.bfloat16),
+        in_specs=[VMEM] * 9,
+        out_specs=VMEM,
+        cost_estimate=pl.CostEstimate(flops=20_000_000, bytes_accessed=1_200_000, transcendentals=0),
+        compiler_params=SMALL,
+        name="pick",
+    )(*pieces)
+    picked = move(picked, lambda a, b, c: index(2 * c + a % 2, b, a // 2))
     partial = pl.pallas_call(
         attention_kernel,
         out_shape=jax.ShapeDtypeStruct((PLANE, MESSAGE, HEAD), jnp.bfloat16),
@@ -293,19 +306,11 @@
         cost_estimate=pl.CostEstimate(flops=3_000_000_000, bytes_accessed=4_000_000, transcendentals=5_000_000),
         name="attention",
     )(table, q, kpos, *pieces)
+    partial, picked = lax.optimization_barrier((partial, picked))
     out = exchange(partial, planes)
 
-    pieces, _ = lax.optimization_barrier((pieces, partial))
-    picked = pl.pallas_call(
-        pick_kernel,
-        out_shape=(jax.ShapeDtypeStruct((KEY_BLOCKS, 2 * HEAD), jnp.bfloat16),) * NX,
-        in_specs=[VMEM] * 9,
-        out_specs=(VMEM,) * NX,
-        cost_estimate=pl.CostEstimate(flops=20_000_000, bytes_accessed=1_200_000, transcendentals=0),
-        name="pick",
-    )(*pieces)
     picked = jnp.concatenate(
-        [move(picked[k], lambda a, b, c, k=k: index(2 * c + a % 2, b ^ k, a // 2)) for k in range(NX)], axis=0
+        [picked[0]] + [move(picked[k], lambda a, b, c, k=k: index(a, b ^ k, c)) for k in range(1, NX)], axis=0
     )
     blocks = jnp.arange(BLOCKS, dtype=jnp.int32)
     stored = jnp.sum(jnp.where(block_map[None, :] == blocks[:, None], blocks[None, :], 0), axis=1, dtype=jnp.int32)
@@ -323,6 +328,7 @@
         out_shape=jax.ShapeDtypeStruct((2 * BLOCK, QUERY_HEADS * HEAD), jnp.bfloat16),
         in_specs=[SMEM] * 3 + [VMEM],
         out_specs=VMEM,
+        compiler_params=SMALL,
         name="combine",
     )(segment_head, my_blocks, lengths, out)
     return attended.reshape(1, 2 * BLOCK, QUERY_HEADS * HEAD), cache

time: 102 us -> 87.9 us (0.86)
  the two profiles are of different devices: /device:TPU:16 before, /device:TPU:8 now
where the time goes in v5:
time: 87.9 us; the launch traced here: 87.6 us
  starting transfers between devices  43.3 us (49%)
  waiting for transfers between devices  20.2 us (23%)
  Pallas kernels  16.6 us (19%)
  local copies, waits for them, and re-layouts  4.5 us (5%)
  between operations  1.55 us (2%)
  other arithmetic  1.27 us (1%)
    ppermute x15, starting transfers between devices, move(): lax.ppermute(value, 'blk', [(s, target(s // 16, s // 4 % 4, s % 4)) for s...  27.7 us
    ppermute x15, waiting for transfers between devices, move(): lax.ppermute(value, 'blk', [(s, target(s // 16, s // 4 % 4, s % 4)) for s...  20.2 us
    all_to_all x2, starting transfers between devices, exchange(): lax.all_to_all(value, 'blk', 0, 0, axis_index_groups=groups, tiled=True)  15.6 us
    pallas_call x1, Pallas kernels, body(): pl.pallas_call(attention_kernel, out_shape=jax.ShapeDtypeStruct((PLANE, M...  12 us
    unnamed x13, local copies, waits for them, and re-layouts  2.54 us
    pallas_call x1, Pallas kernels, body(): pl.pallas_call(combine_kernel, out_shape=jax.ShapeDtypeStruct((2 * BLOCK,...  2.08 us
  transfers between devices with their start and end apart: 17, of which 8 were waited for; matrix products, arithmetic and copies ran while one was open for 4% of the time, Pallas kernels for 16%

profile of v5, /device:TPU:8, one launch (start us, length us, event | category | flops | bytes accessed | tf_op | source)
XLA Modules:
  0.0 87.6 jit_solution(5949005683410619911)
XLA Ops:
  0.6 0.9 %copy-done.1 = bf16[1,2,64,512]{3,2,1,0:T(8,128)(2,1)S(1)} copy-done((bf16[1,2,64,512]{3,2,1,0:T(8,128)(2,1)S(1)}, bf16[1,2,64,512]{3,2,1,0:T(8,128)(2,1)}, u32[]{:S(2)}) %copy-start.1) | copy-done | bytes 131096
  1.5 0.7 copy-done.2
  2.2 0.6 split_kv.1
  2.8 2.3 %collective-permute-start = (bf16[128,128]{1,0:T(8,128)(2,1)S(1)}, bf16[128,128]{1,0:T(8,128)(2,1)S(1)}, u32[]{:S(2)}, u32[]{:S(2)}) collective-permute-start(bf16[128,128]{1,0:T(8,128)(2,1)S(1)} %get-tuple-element.9), channel_id=1, source_target_pairs={{0,1},{1,0},{2,3},{3,2},{4,5},{5,4},{6,7},{7,6},{8,9},{9,8},{10,11... | collective-permute-start | bytes 98312 | tf_op jit(solution)/shard_map/ppermute | solution.py:230
  5.0 0.9 collective-permute-start.1
  5.9 0.7 collective-permute-start.2
  6.6 0.9 %copy-done = bf16[1,64,2048]{2,1,0:T(8,128)(2,1)S(1)} copy-done((bf16[1,64,2048]{2,1,0:T(8,128)(2,1)S(1)}, bf16[1,64,2048]{2,1,0:T(8,128)(2,1)}, u32[]{:S(2)}) %copy-start) | copy-done | bytes 262168
  7.6 1.7 %split_q.1 = bf16[16,256,128]{2,1,0:T(8,128)(2,1)} custom-call(s32[4]{0:T(128)S(1)} %copy-done.2, bf16[64,2048]{1,0:T(8,128)(2,1)S(1)} %bitcast.25), custom_call_target="tpu_custom_call" | custom-call | tf_op jit(solution)/shard_map/split_q/pallas_call | solution.py:251
  9.2 8.3 %all-to-all-start = ((bf16[16,256,128]{2,1,0:T(8,128)(2,1)}), bf16[16,256,128]{2,1,0:T(8,128)(2,1)S(1)}, u32[]{:S(2)}, u32[]{:S(2)}) async-start(bf16[16,256,128]{2,1,0:T(8,128)(2,1)} %split_q.1), calls=%async_computation | async-start | bytes 2097152 | tf_op jit(solution)/shard_map/all_to_all | solution.py:236
  17.7 0.3 copy.12
  18.1 0.2 convert_reduce_fusion
  19.4 5.9 %collective-permute-start.6 = (bf16[512,128]{1,0:T(8,128)(2,1)S(1)}, bf16[512,128]{1,0:T(8,128)(2,1)S(1)}, u32[]{:S(2)}, u32[]{:S(2)}) collective-permute-start(bf16[512,128]{1,0:T(8,128)(2,1)S(1)} %constant_dynamic-update-slice_fusion.refs_0_), channel_id=1, source_target_pairs={{0,112},{1,113},{2,114},{3,115},{4,116},{5,117},{6,118},{7,119},{8... | collective-permute-start | bytes 393224 | tf_op jit(solution)/shard_map/ppermute | solution.py:230
  25.4 2.5 %collective-permute-done.6.refs_4_ = bf16[512,128]{1,0:T(8,128)(2,1)S(1)} collective-permute-done((bf16[512,128]{1,0:T(8,128)(2,1)S(1)}, bf16[512,128]{1,0:T(8,128)(2,1)S(1)}, u32[]{:S(2)}, u32[]{:S(2)}) %collective-permute-start.6) | collective-permute-done | bytes 131104 | tf_op jit(solution)/shard_map/ppermute | solution.py:230
  27.9 3.7 %collective-permute-start.7 = (bf16[512,128]{1,0:T(8,128)(2,1)S(1)}, bf16[512,128]{1,0:T(8,128)(2,1)S(1)}, u32[]{:S(2)}, u32[]{:S(2)}) collective-permute-start(bf16[512,128]{1,0:T(8,128)(2,1)S(1)} %collective-permute-done.6.refs_4_), channel_id=1, source_target_pairs={{0,112},{1,113},{2,114},{3,115},{4,116},{5,117},{6,118},{7,119},{8... | collective-permute-start | bytes 393224 | tf_op jit(solution)/shard_map/ppermute | solution.py:230
  31.9 2.1 %collective-permute-done.7.refs_5_ = bf16[512,128]{1,0:T(8,128)(2,1)S(1)} collective-permute-done((bf16[512,128]{1,0:T(8,128)(2,1)S(1)}, bf16[512,128]{1,0:T(8,128)(2,1)S(1)}, u32[]{:S(2)}, u32[]{:S(2)}) %collective-permute-start.7) | collective-permute-done | bytes 131104 | tf_op jit(solution)/shard_map/ppermute | solution.py:230
  34.0 3.7 %collective-permute-start.8 = (bf16[512,128]{1,0:T(8,128)(2,1)S(1)}, bf16[512,128]{1,0:T(8,128)(2,1)S(1)}, u32[]{:S(2)}, u32[]{:S(2)}) collective-permute-start(bf16[512,128]{1,0:T(8,128)(2,1)S(1)} %collective-permute-done.7.refs_5_), channel_id=1, source_target_pairs={{0,112},{1,113},{2,114},{3,115},{4,116},{5,117},{6,118},{7,119},{8... | collective-permute-start | bytes 393224 | tf_op jit(solution)/shard_map/ppermute | solution.py:230
  37.7 3.1 %collective-permute-done.8.refs_6_ = bf16[512,128]{1,0:T(8,128)(2,1)S(1)} collective-permute-done((bf16[512,128]{1,0:T(8,128)(2,1)S(1)}, bf16[512,128]{1,0:T(8,128)(2,1)S(1)}, u32[]{:S(2)}, u32[]{:S(2)}) %collective-permute-start.8) | collective-permute-done | bytes 131104 | tf_op jit(solution)/shard_map/ppermute | solution.py:230
  40.8 3.7 %collective-permute-start.10 = (bf16[256,128]{1,0:T(8,128)(2,1)S(1)}, bf16[256,128]{1,0:T(8,128)(2,1)S(1)}, u32[]{:S(2)}, u32[]{:S(2)}) collective-permute-start(bf16[256,128]{1,0:T(8,128)(2,1)S(1)} %slice.33), channel_id=1, source_target_pairs={{0,112},{1,113},{2,114},{3,115},{4,116},{5,117},{6,118},{7,119},{8... | collective-permute-start | bytes 196616 | tf_op jit(solution)/shard_map/ppermute | solution.py:230
  44.7 1.7 %collective-permute-done.10.refs_8_ = bf16[256,128]{1,0:T(8,128)(2,1)S(1)} collective-permute-done((bf16[256,128]{1,0:T(8,128)(2,1)S(1)}, bf16[256,128]{1,0:T(8,128)(2,1)S(1)}, u32[]{:S(2)}, u32[]{:S(2)}) %collective-permute-start.10) | collective-permute-done | bytes 65568 | tf_op jit(solution)/shard_map/ppermute | solution.py:230
  46.4 5.0 %collective-permute-done.9.refs_7_ = bf16[256,128]{1,0:T(8,128)(2,1)S(1)} collective-permute-done((bf16[256,128]{1,0:T(8,128)(2,1)S(1)}, bf16[256,128]{1,0:T(8,128)(2,1)S(1)}, u32[]{:S(2)}, u32[]{:S(2)}) %collective-permute-start.9) | collective-permute-done | bytes 65568 | tf_op jit(solution)/shard_map/ppermute | solution.py:230
  51.4 0.3 pick.1
  51.7 2.1 %collective-permute-start.11 = (bf16[4,64,256]{2,1,0:T(8,128)(2,1)S(1)}, bf16[4,64,256]{2,1,0:T(8,128)(2,1)S(1)}, u32[]{:S(2)}, u32[]{:S(2)}) collective-permute-start(bf16[4,64,256]{2,1,0:T(8,128)(2,1)S(1)} %pick.1), channel_id=1, source_target_pairs={{0,0},{1,32},{2,64},{3,96},{4,4},{5,36},{6,68},{7,100},{8,8},{9,40... | collective-permute-start | bytes 393224 | tf_op jit(solution)/shard_map/ppermute | solution.py:230
  53.8 12.0 %attention.1 = bf16[16,272,128]{2,1,0:T(8,128)(2,1)} custom-call(s32[144]{0:T(256)S(1)} %concatenate.9.table, bf16[32,128,128]{2,1,0:T(8,128)(2,1)S(1)} %bitcast.24, s32[8,256]{1,0:T(8,128)S(1)} %broadcast_add_fusion.kpos_ref, bf16[512,128]{1,0:T(8,128)(2,1)S(1)} %constant_dynamic-update-slice_fusion.refs_0_, ...), custom_call_target="tpu_custom_call" | custom-call | flops 3000000000 | bytes 4000000 | tf_op jit(solution)/shard_map/attention/pallas_call | solution.py:293
  65.8 7.3 %all-to-all-start.1 = ((bf16[16,272,128]{2,1,0:T(8,128)(2,1)}), bf16[16,272,128]{2,1,0:T(8,128)(2,1)S(1)}, u32[]{:S(2)}, u32[]{:S(2)}) async-start(bf16[16,272,128]{2,1,0:T(8,128)(2,1)} %attention.1), calls=%async_computation.1 | async-start | bytes 2228224 | tf_op jit(solution)/shard_map/all_to_all | solution.py:236
  73.9 1.6 %collective-permute-start.12 = (bf16[64,256]{1,0:T(8,128)(2,1)S(1)}, bf16[64,256]{1,0:T(8,128)(2,1)S(1)}, u32[]{:S(2)}, u32[]{:S(2)}) collective-permute-start(bf16[64,256]{1,0:T(8,128)(2,1)S(1)} %get-tuple-element.23), channel_id=1, source_target_pairs={{0,4},{1,5},{2,6},{3,7},{4,0},{5,1},{6,2},{7,3},{8,12},{9,13},{10,... | collective-permute-start | bytes 98312 | tf_op jit(solution)/shard_map/ppermute | solution.py:230
  75.5 2.7 %collective-permute-start.13 = (bf16[64,256]{1,0:T(8,128)(2,1)S(1)}, bf16[64,256]{1,0:T(8,128)(2,1)S(1)}, u32[]{:S(2)}, u32[]{:S(2)}) collective-permute-start(bf16[64,256]{1,0:T(8,128)(2,1)S(1)} %get-tuple-element.22), channel_id=1, source_target_pairs={{0,8},{1,9},{2,10},{3,11},{4,12},{5,13},{6,14},{7,15},{8,0},{9,1},... | collective-permute-start | bytes 98312 | tf_op jit(solution)/shard_map/ppermute | solution.py:230
  78.1 0.6 collective-permute-start.14
  78.8 3.8 %collective-permute-done.12 = bf16[64,256]{1,0:T(8,128)(2,1)S(1)} collective-permute-done((bf16[64,256]{1,0:T(8,128)(2,1)S(1)}, bf16[64,256]{1,0:T(8,128)(2,1)S(1)}, u32[]{:S(2)}, u32[]{:S(2)}) %collective-permute-start.12) | collective-permute-done | bytes 32800 | tf_op jit(solution)/shard_map/ppermute | solution.py:230
  82.6 1.9 %collective-permute-done.13 = bf16[64,256]{1,0:T(8,128)(2,1)S(1)} collective-permute-done((bf16[64,256]{1,0:T(8,128)(2,1)S(1)}, bf16[64,256]{1,0:T(8,128)(2,1)S(1)}, u32[]{:S(2)}, u32[]{:S(2)}) %collective-permute-start.13) | collective-permute-done | bytes 32800 | tf_op jit(solution)/shard_map/ppermute | solution.py:230
  84.5 0.3 convolution_convert_fusion
  84.8 0.8 copy.15
  85.6 2.1 %combine.1 = bf16[64,2048]{1,0:T(8,128)(2,1)} custom-call(s32[4]{0:T(128)S(1)} %copy-done.3, s32[2]{0:T(128)S(1)} %dynamic_slice.13.blocks, s32[1]{0:T(128)} %copy.19.length, bf16[16,272,128]{2,1,0:T(8,128)(2,1)S(1)} %all-to-all-done.1.m_ref), custom_call_target="tpu_custom_call" | custom-call | tf_op jit(solution)/shard_map/combine/pallas_call | solution.py:326
  (51 shorter events, 2.1 us)
Async XLA Ops:
  0.6 0.9 %copy-start.1 = (bf16[1,2,64,512]{3,2,1,0:T(8,128)(2,1)S(1)}, bf16[1,2,64,512]{3,2,1,0:T(8,128)(2,1)}, u32[]{:S(2)}) copy-start(bf16[1,2,64,512]{3,2,1,0:T(8,128)(2,1)} %param.6) | copy-start | bytes 393220
  1.5 0.7 copy-start.2
  2.8 16.6 %collective-permute-start = (bf16[128,128]{1,0:T(8,128)(2,1)S(1)}, bf16[128,128]{1,0:T(8,128)(2,1)S(1)}, u32[]{:S(2)}, u32[]{:S(2)}) collective-permute-start(bf16[128,128]{1,0:T(8,128)(2,1)S(1)} %get-tuple-element.9), channel_id=1, source_target_pairs={{0,1},{1,0},{2,3},{3,2},{4,5},{5,4},{6,7},{7,6},{8,9},{9,8},{10,11... | collective-permute-start | bytes 98312 | tf_op jit(solution)/shard_map/ppermute | solution.py:230
  5.0 14.3 %collective-permute-start.1 = (bf16[128,128]{1,0:T(8,128)(2,1)S(1)}, bf16[128,128]{1,0:T(8,128)(2,1)S(1)}, u32[]{:S(2)}, u32[]{:S(2)}) collective-permute-start(bf16[128,128]{1,0:T(8,128)(2,1)S(1)} %get-tuple-element.10), channel_id=1, source_target_pairs={{0,2},{1,3},{2,0},{3,1},{4,6},{5,7},{6,4},{7,5},{8,10},{9,11},{10,... | collective-permute-start | bytes 98312 | tf_op jit(solution)/shard_map/ppermute | solution.py:230
  5.9 13.5 %collective-permute-start.2 = (bf16[128,128]{1,0:T(8,128)(2,1)S(1)}, bf16[128,128]{1,0:T(8,128)(2,1)S(1)}, u32[]{:S(2)}, u32[]{:S(2)}) collective-permute-start(bf16[128,128]{1,0:T(8,128)(2,1)S(1)} %get-tuple-element.11), channel_id=1, source_target_pairs={{0,3},{1,2},{2,1},{3,0},{4,7},{5,6},{6,5},{7,4},{8,11},{9,10},{10,... | collective-permute-start | bytes 98312 | tf_op jit(solution)/shard_map/ppermute | solution.py:230
  6.6 0.9 %copy-start = (bf16[1,64,2048]{2,1,0:T(8,128)(2,1)S(1)}, bf16[1,64,2048]{2,1,0:T(8,128)(2,1)}, u32[]{:S(2)}) copy-start(bf16[1,64,2048]{2,1,0:T(8,128)(2,1)} %param.5) | copy-start | bytes 786436
  9.2 8.3 %copy-start.4 = (s32[256]{0:T(256)S(1)}, s32[256]{0:T(256)}, u32[]{:S(2)}) copy-start(s32[256]{0:T(256)} %param.8) | copy-start | bytes 3076
  9.2 44.6 %all-to-all-start = ((bf16[16,256,128]{2,1,0:T(8,128)(2,1)}), bf16[16,256,128]{2,1,0:T(8,128)(2,1)S(1)}, u32[]{:S(2)}, u32[]{:S(2)}) async-start(bf16[16,256,128]{2,1,0:T(8,128)(2,1)} %split_q.1), calls=%async_computation | async-start | bytes 2097152 | tf_op jit(solution)/shard_map/all_to_all | solution.py:236
  19.4 8.5 %collective-permute-start.6 = (bf16[512,128]{1,0:T(8,128)(2,1)S(1)}, bf16[512,128]{1,0:T(8,128)(2,1)S(1)}, u32[]{:S(2)}, u32[]{:S(2)}) collective-permute-start(bf16[512,128]{1,0:T(8,128)(2,1)S(1)} %constant_dynamic-update-slice_fusion.refs_0_), channel_id=1, source_target_pairs={{0,112},{1,113},{2,114},{3,115},{4,116},{5,117},{6,118},{7,119},{8... | collective-permute-start | bytes 393224 | tf_op jit(solution)/shard_map/ppermute | solution.py:230
  25.3 6.2 %collective-permute-start.3 = (bf16[512,128]{1,0:T(8,128)(2,1)S(1)}, bf16[512,128]{1,0:T(8,128)(2,1)S(1)}, u32[]{:S(2)}, u32[]{:S(2)}) collective-permute-start(bf16[512,128]{1,0:T(8,128)(2,1)S(1)} %constant_dynamic-update-slice_fusion.refs_0_), channel_id=1, source_target_pairs={{0,16},{1,17},{2,18},{3,19},{4,20},{5,21},{6,22},{7,23},{8,24},{9,... | collective-permute-start | bytes 393224 | tf_op jit(solution)/shard_map/ppermute | solution.py:230
  27.9 6.2 %collective-permute-start.7 = (bf16[512,128]{1,0:T(8,128)(2,1)S(1)}, bf16[512,128]{1,0:T(8,128)(2,1)S(1)}, u32[]{:S(2)}, u32[]{:S(2)}) collective-permute-start(bf16[512,128]{1,0:T(8,128)(2,1)S(1)} %collective-permute-done.6.refs_4_), channel_id=1, source_target_pairs={{0,112},{1,113},{2,114},{3,115},{4,116},{5,117},{6,118},{7,119},{8... | collective-permute-start | bytes 393224 | tf_op jit(solution)/shard_map/ppermute | solution.py:230
  31.5 6.2 %collective-permute-start.4 = (bf16[512,128]{1,0:T(8,128)(2,1)S(1)}, bf16[512,128]{1,0:T(8,128)(2,1)S(1)}, u32[]{:S(2)}, u32[]{:S(2)}) collective-permute-start(bf16[512,128]{1,0:T(8,128)(2,1)S(1)} %collective-permute-done.3.refs_1_), channel_id=1, source_target_pairs={{0,16},{1,17},{2,18},{3,19},{4,20},{5,21},{6,22},{7,23},{8,24},{9,... | collective-permute-start | bytes 393224 | tf_op jit(solution)/shard_map/ppermute | solution.py:230
  34.0 6.8 %collective-permute-start.8 = (bf16[512,128]{1,0:T(8,128)(2,1)S(1)}, bf16[512,128]{1,0:T(8,128)(2,1)S(1)}, u32[]{:S(2)}, u32[]{:S(2)}) collective-permute-start(bf16[512,128]{1,0:T(8,128)(2,1)S(1)} %collective-permute-done.7.refs_5_), channel_id=1, source_target_pairs={{0,112},{1,113},{2,114},{3,115},{4,116},{5,117},{6,118},{7,119},{8... | collective-permute-start | bytes 393224 | tf_op jit(solution)/shard_map/ppermute | solution.py:230
  37.7 6.9 %collective-permute-start.5 = (bf16[512,128]{1,0:T(8,128)(2,1)S(1)}, bf16[512,128]{1,0:T(8,128)(2,1)S(1)}, u32[]{:S(2)}, u32[]{:S(2)}) collective-permute-start(bf16[512,128]{1,0:T(8,128)(2,1)S(1)} %collective-permute-done.4.refs_2_), channel_id=1, source_target_pairs={{0,16},{1,17},{2,18},{3,19},{4,20},{5,21},{6,22},{7,23},{8,24},{9,... | collective-permute-start | bytes 393224 | tf_op jit(solution)/shard_map/ppermute | solution.py:230
  40.8 5.6 %collective-permute-start.10 = (bf16[256,128]{1,0:T(8,128)(2,1)S(1)}, bf16[256,128]{1,0:T(8,128)(2,1)S(1)}, u32[]{:S(2)}, u32[]{:S(2)}) collective-permute-start(bf16[256,128]{1,0:T(8,128)(2,1)S(1)} %slice.33), channel_id=1, source_target_pairs={{0,112},{1,113},{2,114},{3,115},{4,116},{5,117},{6,118},{7,119},{8... | collective-permute-start | bytes 196616 | tf_op jit(solution)/shard_map/ppermute | solution.py:230
  44.6 6.8 %collective-permute-start.9 = (bf16[256,128]{1,0:T(8,128)(2,1)S(1)}, bf16[256,128]{1,0:T(8,128)(2,1)S(1)}, u32[]{:S(2)}, u32[]{:S(2)}) collective-permute-start(bf16[256,128]{1,0:T(8,128)(2,1)S(1)} %slice.32), channel_id=1, source_target_pairs={{0,16},{1,17},{2,18},{3,19},{4,20},{5,21},{6,22},{7,23},{8,24},{9,... | collective-permute-start | bytes 196616 | tf_op jit(solution)/shard_map/ppermute | solution.py:230
  51.7 14.1 %collective-permute-start.11 = (bf16[4,64,256]{2,1,0:T(8,128)(2,1)S(1)}, bf16[4,64,256]{2,1,0:T(8,128)(2,1)S(1)}, u32[]{:S(2)}, u32[]{:S(2)}) collective-permute-start(bf16[4,64,256]{2,1,0:T(8,128)(2,1)S(1)} %pick.1), channel_id=1, source_target_pairs={{0,0},{1,32},{2,64},{3,96},{4,4},{5,36},{6,68},{7,100},{8,8},{9,40... | collective-permute-start | bytes 393224 | tf_op jit(solution)/shard_map/ppermute | solution.py:230
  65.8 19.8 %all-to-all-start.1 = ((bf16[16,272,128]{2,1,0:T(8,128)(2,1)}), bf16[16,272,128]{2,1,0:T(8,128)(2,1)S(1)}, u32[]{:S(2)}, u32[]{:S(2)}) async-start(bf16[16,272,128]{2,1,0:T(8,128)(2,1)} %attention.1), calls=%async_computation.1 | async-start | bytes 2228224 | tf_op jit(solution)/shard_map/all_to_all | solution.py:236
  73.0 12.5 %copy-start.3 = (s32[4]{0:T(128)S(1)}, s32[4]{0:T(128)}, u32[]{:S(2)}) copy-start(s32[4]{0:T(128)} %heads.5) | copy-start | bytes 52
  73.9 8.7 %collective-permute-start.12 = (bf16[64,256]{1,0:T(8,128)(2,1)S(1)}, bf16[64,256]{1,0:T(8,128)(2,1)S(1)}, u32[]{:S(2)}, u32[]{:S(2)}) collective-permute-start(bf16[64,256]{1,0:T(8,128)(2,1)S(1)} %get-tuple-element.23), channel_id=1, source_target_pairs={{0,4},{1,5},{2,6},{3,7},{4,0},{5,1},{6,2},{7,3},{8,12},{9,13},{10,... | collective-permute-start | bytes 98312 | tf_op jit(solution)/shard_map/ppermute | solution.py:230
  75.5 9.0 %collective-permute-start.13 = (bf16[64,256]{1,0:T(8,128)(2,1)S(1)}, bf16[64,256]{1,0:T(8,128)(2,1)S(1)}, u32[]{:S(2)}, u32[]{:S(2)}) collective-permute-start(bf16[64,256]{1,0:T(8,128)(2,1)S(1)} %get-tuple-element.22), channel_id=1, source_target_pairs={{0,8},{1,9},{2,10},{3,11},{4,12},{5,13},{6,14},{7,15},{8,0},{9,1},... | collective-permute-start | bytes 98312 | tf_op jit(solution)/shard_map/ppermute | solution.py:230
  78.1 6.3 %collective-permute-start.14 = (bf16[64,256]{1,0:T(8,128)(2,1)S(1)}, bf16[64,256]{1,0:T(8,128)(2,1)S(1)}, u32[]{:S(2)}, u32[]{:S(2)}) collective-permute-start(bf16[64,256]{1,0:T(8,128)(2,1)S(1)} %get-tuple-element.21), channel_id=1, source_target_pairs={{0,12},{1,13},{2,14},{3,15},{4,8},{5,9},{6,10},{7,11},{8,4},{9,5},... | collective-permute-start | bytes 98312 | tf_op jit(solution)/shard_map/ppermute | solution.py:230

commit v6 on v5

--- a/solution.py
+++ b/solution.py
@@ -44,14 +44,14 @@
         o_refs[k][...] = kv_ref[:, pl.ds(pl.multiple_of(heads[y ^ k] * HEAD, HEAD), HEAD)]
 
 
-def split_q_kernel(heads, q_ref, o_ref):
-    for y in range(NY):
+def split_q_kernel(heads, q_ref, *o_refs):
+    y = lax.rem(lax.axis_index("blk"), NY)
+    for k in range(NY):
         for g in range(GROUP):
-            column = pl.multiple_of((heads[y] * GROUP + g) * HEAD, HEAD)
+            column = pl.multiple_of((heads[y ^ k] * GROUP + g) * HEAD, HEAD)
             for j in range(2):
-                tile = q_ref[j * BLOCK : (j + 1) * BLOCK, pl.ds(column, HEAD)]
-                for x in range(NX):
-                    o_ref[x * NY + y, j * ROWS + g * BLOCK : j * ROWS + (g + 1) * BLOCK] = tile
+                rows = slice(j * ROWS + g * BLOCK, j * ROWS + (g + 1) * BLOCK)
+                o_refs[k][rows, :] = q_ref[j * BLOCK : (j + 1) * BLOCK, pl.ds(column, HEAD)]
 
 
 def arrange(table, pieces, k_scr, kt_scr, v_scr):
@@ -113,6 +113,7 @@
         kt_scr,
         v_scr,
     )
+    mine = 2 * lax.rem(lax.axis_index("blk"), PLANE)
     lane = lax.broadcasted_iota(jnp.int32, (ROWS, 128), 1)
     token = lax.broadcasted_iota(jnp.int32, (BLOCK, CHUNK), 0)
 
@@ -128,7 +129,7 @@
             stat[...] = jnp.where(lane == blocks[u] + Q_BLOCKS, total, old)
 
         def work(n):
-            q = jnp.concatenate([q_ref[blocks[u]] for u in range(JOINED)], axis=0)
+            q = jnp.concatenate([q_ref[blocks[u] ^ mine] for u in range(JOINED)], axis=0)
             tops = [None] * (JOINED * GROUP)
             for c in range(n):
                 start = pl.multiple_of((low + c) * CHUNK, CHUNK)
@@ -248,15 +249,19 @@
     right = lambda v: move(v, lambda a, b, c: index(a + 1, b, c))
     left = lambda v: move(v, lambda a, b, c: index(a - 1, b, c))
     r1, l1 = right(own), left(own)
-    q = pl.pallas_call(
+    qs = pl.pallas_call(
         split_q_kernel,
-        out_shape=jax.ShapeDtypeStruct((PLANE, 2 * ROWS, HEAD), jnp.bfloat16),
+        out_shape=(jax.ShapeDtypeStruct((2 * ROWS, HEAD), jnp.bfloat16),) * NY,
         in_specs=[SMEM, VMEM],
-        out_specs=VMEM,
+        out_specs=(VMEM,) * NY,
         compiler_params=SMALL,
         name="split_q",
     )(segment_head, query.reshape(2 * BLOCK, QUERY_HEADS * HEAD))
-    q = exchange(q, planes).reshape(Q_BLOCKS, ROWS, HEAD)
+    qs, _ = lax.optimization_barrier((qs, own))
+    q = [qs[0]] + [move(qs[k], lambda a, b, c, k=k: index(a, b, c ^ k)) for k in range(1, NY)]
+    q = jnp.concatenate(q, axis=0)
+    q = [q] + [move(q, lambda a, b, c, k=k: index(a, b ^ k, c)) for k in range(1, NX)]
+    q = jnp.concatenate(q, axis=0).reshape(Q_BLOCKS, ROWS, HEAD)
     r2, l2 = right(r1), left(l1)
     r3, l3 = right(r2), left(l2)
     half = own.shape[0] // 2

time: 87.9 us -> 91.3 us (1.039)
  starting transfers between devices: 43.3 us -> 47.6 us
  waiting for transfers between devices: 20.2 us -> 17.7 us
  local copies, waits for them, and re-layouts: 4.5 us -> 6.7 us
    ppermute x15 -> x21, starting transfers between devices: 27.7 us -> 41.5 us  [move(): lax.ppermute(value, 'blk', [(s, target(s // 16, s // 4 % 4, s % 4)) for s...]
    all_to_all x2 -> x1, starting transfers between devices: 15.6 us -> 6.08 us  [exchange(): lax.all_to_all(value, 'blk', 0, 0, axis_index_groups=groups, tiled=True)]
    ppermute x15 -> x21, waiting for transfers between devices: 20.2 us -> 17.7 us  [move(): lax.ppermute(value, 'blk', [(s, target(s // 16, s // 4 % 4, s % 4)) for s...]
    pallas_call x1, Pallas kernels: 1.67 us -> 0.62 us  [body(): pl.pallas_call(split_q_kernel, out_shape=(jax.ShapeDtypeStruct((2 * ROWS,...]
    unnamed x13 -> x20, local copies, waits for them, and re-layouts: 2.54 us -> 3.31 us
  transfers between devices with their start and end apart: 17 -> 22, of which waited for: 8 -> 8; matrix products, arithmetic and copies ran while one was open for 4% -> 6% of each run, Pallas kernels for 16% -> 14%
where the time goes in v6:
time: 91.3 us; the launch traced here: 91.2 us
  starting transfers between devices  47.6 us (52%)
  waiting for transfers between devices  17.7 us (19%)
  Pallas kernels  16.1 us (18%)
  local copies, waits for them, and re-layouts  6.7 us (7%)
  between operations  1.58 us (2%)
  other arithmetic  1.27 us (1%)
    ppermute x21, starting transfers between devices, move(): lax.ppermute(value, 'blk', [(s, target(s // 16, s // 4 % 4, s % 4)) for s...  41.5 us
    ppermute x21, waiting for transfers between devices, move(): lax.ppermute(value, 'blk', [(s, target(s // 16, s // 4 % 4, s % 4)) for s...  17.7 us
    pallas_call x1, Pallas kernels, body(): pl.pallas_call(attention_kernel, out_shape=jax.ShapeDtypeStruct((PLANE, M...  12.5 us
    all_to_all x1, starting transfers between devices, exchange(): lax.all_to_all(value, 'blk', 0, 0, axis_index_groups=groups, tiled=True)  6.08 us
    unnamed x20, local copies, waits for them, and re-layouts  3.31 us
    pallas_call x1, Pallas kernels, body(): pl.pallas_call(combine_kernel, out_shape=jax.ShapeDtypeStruct((2 * BLOCK,...  2.08 us
  transfers between devices with their start and end apart: 22, of which 8 were waited for; matrix products, arithmetic and copies ran while one was open for 6% of the time, Pallas kernels for 14%

profile of v6, /device:TPU:8, one launch (start us, length us, event | category | flops | bytes accessed | tf_op | source)
XLA Modules:
  0.0 91.2 jit_solution(16658428786182584569)
XLA Ops:
  0.6 0.9 copy-done.1
  1.5 0.7 copy-done.2
  2.8 2.3 %collective-permute-start = (bf16[128,128]{1,0:T(8,128)(2,1)S(1)}, bf16[128,128]{1,0:T(8,128)(2,1)S(1)}, u32[]{:S(2)}, u32[]{:S(2)}) collective-permute-start(bf16[128,128]{1,0:T(8,128)(2,1)S(1)} %get-tuple-element.21), channel_id=1, source_target_pairs={{0,1},{1,0},{2,3},{3,2},{4,5},{5,4},{6,7},{7,6},{8,9},{9,8},{10,11... | collective-permute-start | bytes 98312 | tf_op jit(solution)/shard_map/ppermute | solution.py:231
  5.0 0.9 collective-permute-start.1
  5.9 0.7 collective-permute-start.2
  6.6 0.8 reshape.143
  8.6 0.8 dynamic_slice.15
  10.2 0.9 %copy-done = bf16[1,64,2048]{2,1,0:T(8,128)(2,1)S(1)} copy-done((bf16[1,64,2048]{2,1,0:T(8,128)(2,1)S(1)}, bf16[1,64,2048]{2,1,0:T(8,128)(2,1)}, u32[]{:S(2)}) %copy-start) | copy-done | bytes 262168
  11.1 0.7 copy-done.3
  12.5 1.7 %collective-permute-start.9 = (bf16[512,128]{1,0:T(8,128)(2,1)S(1)}, bf16[512,128]{1,0:T(8,128)(2,1)S(1)}, u32[]{:S(2)}, u32[]{:S(2)}) collective-permute-start(bf16[512,128]{1,0:T(8,128)(2,1)S(1)} %constant_dynamic-update-slice_fusion.refs_0_), channel_id=1, source_target_pairs={{0,16},{1,17},{2,18},{3,19},{4,20},{5,21},{6,22},{7,23},{8,24},{9,... | collective-permute-start | bytes 393224 | tf_op jit(solution)/shard_map/ppermute | solution.py:231
  14.2 4.0 %collective-permute-start.12 = (bf16[512,128]{1,0:T(8,128)(2,1)S(1)}, bf16[512,128]{1,0:T(8,128)(2,1)S(1)}, u32[]{:S(2)}, u32[]{:S(2)}) collective-permute-start(bf16[512,128]{1,0:T(8,128)(2,1)S(1)} %constant_dynamic-update-slice_fusion.refs_0_), channel_id=1, source_target_pairs={{0,112},{1,113},{2,114},{3,115},{4,116},{5,117},{6,118},{7,119},{8... | collective-permute-start | bytes 393224 | tf_op jit(solution)/shard_map/ppermute | solution.py:231
  18.2 1.7 %collective-permute-start.3 = (bf16[256,128]{1,0:T(8,128)(2,1)S(1)}, bf16[256,128]{1,0:T(8,128)(2,1)S(1)}, u32[]{:S(2)}, u32[]{:S(2)}) collective-permute-start(bf16[256,128]{1,0:T(8,128)(2,1)S(1)} %get-tuple-element.25), channel_id=1, source_target_pairs={{0,1},{1,0},{2,3},{3,2},{4,5},{5,4},{6,7},{7,6},{8,9},{9,8},{10,11... | collective-permute-start | bytes 196616 | tf_op jit(solution)/shard_map/ppermute | solution.py:231
  19.9 1.8 %collective-permute-start.4 = (bf16[256,128]{1,0:T(8,128)(2,1)S(1)}, bf16[256,128]{1,0:T(8,128)(2,1)S(1)}, u32[]{:S(2)}, u32[]{:S(2)}) collective-permute-start(bf16[256,128]{1,0:T(8,128)(2,1)S(1)} %get-tuple-element.26), channel_id=1, source_target_pairs={{0,2},{1,3},{2,0},{3,1},{4,6},{5,7},{6,4},{7,5},{8,10},{9,11},{10,... | collective-permute-start | bytes 196616 | tf_op jit(solution)/shard_map/ppermute | solution.py:231
  22.5 3.2 %collective-permute-done.4 = bf16[256,128]{1,0:T(8,128)(2,1)S(1)} collective-permute-done((bf16[256,128]{1,0:T(8,128)(2,1)S(1)}, bf16[256,128]{1,0:T(8,128)(2,1)S(1)}, u32[]{:S(2)}, u32[]{:S(2)}) %collective-permute-start.4) | collective-permute-done | bytes 65568 | tf_op jit(solution)/shard_map/ppermute | solution.py:231
  25.7 0.6 collective-permute-done.5
  26.4 1.6 %collective-permute-start.6 = (bf16[1024,128]{1,0:T(8,128)(2,1)S(1)}, bf16[1024,128]{1,0:T(8,128)(2,1)S(1)}, u32[]{:S(2)}, u32[]{:S(2)}) collective-permute-start(bf16[1024,128]{1,0:T(8,128)(2,1)S(1)} %get-tuple-element.40), channel_id=1, source_target_pairs={{0,4},{1,5},{2,6},{3,7},{4,0},{5,1},{6,2},{7,3},{8,12},{9,13},{10,... | collective-permute-start | bytes 786440 | tf_op jit(solution)/shard_map/ppermute | solution.py:231
  28.0 2.7 %collective-permute-start.7 = (bf16[1024,128]{1,0:T(8,128)(2,1)S(1)}, bf16[1024,128]{1,0:T(8,128)(2,1)S(1)}, u32[]{:S(2)}, u32[]{:S(2)}) collective-permute-start(bf16[1024,128]{1,0:T(8,128)(2,1)S(1)} %get-tuple-element.40), channel_id=1, source_target_pairs={{0,8},{1,9},{2,10},{3,11},{4,12},{5,13},{6,14},{7,15},{8,0},{9,1},... | collective-permute-start | bytes 786440 | tf_op jit(solution)/shard_map/ppermute | solution.py:231
  30.7 3.2 %collective-permute-start.13 = (bf16[512,128]{1,0:T(8,128)(2,1)S(1)}, bf16[512,128]{1,0:T(8,128)(2,1)S(1)}, u32[]{:S(2)}, u32[]{:S(2)}) collective-permute-start(bf16[512,128]{1,0:T(8,128)(2,1)S(1)} %collective-permute-done.12.refs_4_), channel_id=1, source_target_pairs={{0,112},{1,113},{2,114},{3,115},{4,116},{5,117},{6,118},{7,119},{8... | collective-permute-start | bytes 393224 | tf_op jit(solution)/shard_map/ppermute | solution.py:231
  34.6 2.8 %collective-permute-done.10.refs_2_ = bf16[512,128]{1,0:T(8,128)(2,1)S(1)} collective-permute-done((bf16[512,128]{1,0:T(8,128)(2,1)S(1)}, bf16[512,128]{1,0:T(8,128)(2,1)S(1)}, u32[]{:S(2)}, u32[]{:S(2)}) %collective-permute-start.10) | collective-permute-done | bytes 131104 | tf_op jit(solution)/shard_map/ppermute | solution.py:231
  37.5 3.6 %collective-permute-start.14 = (bf16[512,128]{1,0:T(8,128)(2,1)S(1)}, bf16[512,128]{1,0:T(8,128)(2,1)S(1)}, u32[]{:S(2)}, u32[]{:S(2)}) collective-permute-start(bf16[512,128]{1,0:T(8,128)(2,1)S(1)} %collective-permute-done.13.refs_5_), channel_id=1, source_target_pairs={{0,112},{1,113},{2,114},{3,115},{4,116},{5,117},{6,118},{7,119},{8... | collective-permute-start | bytes 393224 | tf_op jit(solution)/shard_map/ppermute | solution.py:231
  41.1 3.2 %collective-permute-done.11.refs_3_ = bf16[512,128]{1,0:T(8,128)(2,1)S(1)} collective-permute-done((bf16[512,128]{1,0:T(8,128)(2,1)S(1)}, bf16[512,128]{1,0:T(8,128)(2,1)S(1)}, u32[]{:S(2)}, u32[]{:S(2)}) %collective-permute-start.11) | collective-permute-done | bytes 131104 | tf_op jit(solution)/shard_map/ppermute | solution.py:231
  44.4 3.5 %collective-permute-start.16 = (bf16[256,128]{1,0:T(8,128)(2,1)S(1)}, bf16[256,128]{1,0:T(8,128)(2,1)S(1)}, u32[]{:S(2)}, u32[]{:S(2)}) collective-permute-start(bf16[256,128]{1,0:T(8,128)(2,1)S(1)} %slice.33), channel_id=1, source_target_pairs={{0,112},{1,113},{2,114},{3,115},{4,116},{5,117},{6,118},{7,119},{8... | collective-permute-start | bytes 196616 | tf_op jit(solution)/shard_map/ppermute | solution.py:231
  47.9 1.9 %collective-permute-done.15.refs_7_ = bf16[256,128]{1,0:T(8,128)(2,1)S(1)} collective-permute-done((bf16[256,128]{1,0:T(8,128)(2,1)S(1)}, bf16[256,128]{1,0:T(8,128)(2,1)S(1)}, u32[]{:S(2)}, u32[]{:S(2)}) %collective-permute-start.15) | collective-permute-done | bytes 65568 | tf_op jit(solution)/shard_map/ppermute | solution.py:231
  50.1 7.9 %collective-permute-start.17 = (bf16[4,64,256]{2,1,0:T(8,128)(2,1)S(1)}, bf16[4,64,256]{2,1,0:T(8,128)(2,1)S(1)}, u32[]{:S(2)}, u32[]{:S(2)}) collective-permute-start(bf16[4,64,256]{2,1,0:T(8,128)(2,1)S(1)} %pick.1), channel_id=1, source_target_pairs={{0,0},{1,32},{2,64},{3,96},{4,4},{5,36},{6,68},{7,100},{8,8},{9,40... | collective-permute-start | bytes 393224 | tf_op jit(solution)/shard_map/ppermute | solution.py:231
  58.1 12.5 %attention.1 = bf16[16,272,128]{2,1,0:T(8,128)(2,1)} custom-call(s32[144]{0:T(256)S(1)} %concatenate.16.table, bf16[32,128,128]{2,1,0:T(8,128)(2,1)S(1)} %bitcast.26, s32[8,256]{1,0:T(8,128)S(1)} %broadcast_add_fusion.kpos_ref, bf16[512,128]{1,0:T(8,128)(2,1)S(1)} %constant_dynamic-update-slice_fusion.refs_0_, ...), custom_call_target="tpu_custom_call" | custom-call | flops 3000000000 | bytes 4000000 | tf_op jit(solution)/shard_map/attention/pallas_call | solution.py:298
  70.6 6.1 %all-to-all-start = ((bf16[16,272,128]{2,1,0:T(8,128)(2,1)}), bf16[16,272,128]{2,1,0:T(8,128)(2,1)S(1)}, u32[]{:S(2)}, u32[]{:S(2)}) async-start(bf16[16,272,128]{2,1,0:T(8,128)(2,1)} %attention.1), calls=%async_computation | async-start | bytes 2228224 | tf_op jit(solution)/shard_map/all_to_all | solution.py:237
  77.5 1.6 %collective-permute-start.18 = (bf16[64,256]{1,0:T(8,128)(2,1)S(1)}, bf16[64,256]{1,0:T(8,128)(2,1)S(1)}, u32[]{:S(2)}, u32[]{:S(2)}) collective-permute-start(bf16[64,256]{1,0:T(8,128)(2,1)S(1)} %get-tuple-element.39), channel_id=1, source_target_pairs={{0,4},{1,5},{2,6},{3,7},{4,0},{5,1},{6,2},{7,3},{8,12},{9,13},{10,... | collective-permute-start | bytes 98312 | tf_op jit(solution)/shard_map/ppermute | solution.py:231
  79.1 2.7 %collective-permute-start.19 = (bf16[64,256]{1,0:T(8,128)(2,1)S(1)}, bf16[64,256]{1,0:T(8,128)(2,1)S(1)}, u32[]{:S(2)}, u32[]{:S(2)}) collective-permute-start(bf16[64,256]{1,0:T(8,128)(2,1)S(1)} %get-tuple-element.38), channel_id=1, source_target_pairs={{0,8},{1,9},{2,10},{3,11},{4,12},{5,13},{6,14},{7,15},{8,0},{9,1},... | collective-permute-start | bytes 98312 | tf_op jit(solution)/shard_map/ppermute | solution.py:231
  82.4 3.8 %collective-permute-done.18 = bf16[64,256]{1,0:T(8,128)(2,1)S(1)} collective-permute-done((bf16[64,256]{1,0:T(8,128)(2,1)S(1)}, bf16[64,256]{1,0:T(8,128)(2,1)S(1)}, u32[]{:S(2)}, u32[]{:S(2)}) %collective-permute-start.18) | collective-permute-done | bytes 32800 | tf_op jit(solution)/shard_map/ppermute | solution.py:231
  86.2 1.8 %collective-permute-done.19 = bf16[64,256]{1,0:T(8,128)(2,1)S(1)} collective-permute-done((bf16[64,256]{1,0:T(8,128)(2,1)S(1)}, bf16[64,256]{1,0:T(8,128)(2,1)S(1)}, u32[]{:S(2)}, u32[]{:S(2)}) %collective-permute-start.19) | collective-permute-done | bytes 32800 | tf_op jit(solution)/shard_map/ppermute | solution.py:231
  88.4 0.8 copy.15
  89.2 2.1 %combine.1 = bf16[64,2048]{1,0:T(8,128)(2,1)} custom-call(s32[4]{0:T(128)S(1)} %copy-done.4, s32[2]{0:T(128)S(1)} %dynamic_slice.13.blocks, s32[1]{0:T(128)} %copy.28.length, bf16[16,272,128]{2,1,0:T(8,128)(2,1)S(1)} %all-to-all-done.m_ref), custom_call_target="tpu_custom_call" | custom-call | tf_op jit(solution)/shard_map/combine/pallas_call | solution.py:331
  (70 shorter events, 6.2 us)
Async XLA Ops:
  0.6 0.9 copy-start.1
  1.5 0.7 copy-start.2
  2.8 9.6 %collective-permute-start = (bf16[128,128]{1,0:T(8,128)(2,1)S(1)}, bf16[128,128]{1,0:T(8,128)(2,1)S(1)}, u32[]{:S(2)}, u32[]{:S(2)}) collective-permute-start(bf16[128,128]{1,0:T(8,128)(2,1)S(1)} %get-tuple-element.21), channel_id=1, source_target_pairs={{0,1},{1,0},{2,3},{3,2},{4,5},{5,4},{6,7},{7,6},{8,9},{9,8},{10,11... | collective-permute-start | bytes 98312 | tf_op jit(solution)/shard_map/ppermute | solution.py:231
  5.0 7.4 %collective-permute-start.1 = (bf16[128,128]{1,0:T(8,128)(2,1)S(1)}, bf16[128,128]{1,0:T(8,128)(2,1)S(1)}, u32[]{:S(2)}, u32[]{:S(2)}) collective-permute-start(bf16[128,128]{1,0:T(8,128)(2,1)S(1)} %get-tuple-element.22), channel_id=1, source_target_pairs={{0,2},{1,3},{2,0},{3,1},{4,6},{5,7},{6,4},{7,5},{8,10},{9,11},{10,... | collective-permute-start | bytes 98312 | tf_op jit(solution)/shard_map/ppermute | solution.py:231
  5.9 6.5 %collective-permute-start.2 = (bf16[128,128]{1,0:T(8,128)(2,1)S(1)}, bf16[128,128]{1,0:T(8,128)(2,1)S(1)}, u32[]{:S(2)}, u32[]{:S(2)}) collective-permute-start(bf16[128,128]{1,0:T(8,128)(2,1)S(1)} %get-tuple-element.23), channel_id=1, source_target_pairs={{0,3},{1,2},{2,1},{3,0},{4,7},{5,6},{6,5},{7,4},{8,11},{9,10},{10,... | collective-permute-start | bytes 98312 | tf_op jit(solution)/shard_map/ppermute | solution.py:231
  10.2 1.0 %copy-start = (bf16[1,64,2048]{2,1,0:T(8,128)(2,1)S(1)}, bf16[1,64,2048]{2,1,0:T(8,128)(2,1)}, u32[]{:S(2)}) copy-start(bf16[1,64,2048]{2,1,0:T(8,128)(2,1)} %param.5) | copy-start | bytes 786436
  11.1 0.7 copy-start.3
  12.5 18.2 %collective-permute-start.9 = (bf16[512,128]{1,0:T(8,128)(2,1)S(1)}, bf16[512,128]{1,0:T(8,128)(2,1)S(1)}, u32[]{:S(2)}, u32[]{:S(2)}) collective-permute-start(bf16[512,128]{1,0:T(8,128)(2,1)S(1)} %constant_dynamic-update-slice_fusion.refs_0_), channel_id=1, source_target_pairs={{0,16},{1,17},{2,18},{3,19},{4,20},{5,21},{6,22},{7,23},{8,24},{9,... | collective-permute-start | bytes 393224 | tf_op jit(solution)/shard_map/ppermute | solution.py:231
  14.2 16.5 %collective-permute-start.12 = (bf16[512,128]{1,0:T(8,128)(2,1)S(1)}, bf16[512,128]{1,0:T(8,128)(2,1)S(1)}, u32[]{:S(2)}, u32[]{:S(2)}) collective-permute-start(bf16[512,128]{1,0:T(8,128)(2,1)S(1)} %constant_dynamic-update-slice_fusion.refs_0_), channel_id=1, source_target_pairs={{0,112},{1,113},{2,114},{3,115},{4,116},{5,117},{6,118},{7,119},{8... | collective-permute-start | bytes 393224 | tf_op jit(solution)/shard_map/ppermute | solution.py:231
  18.2 4.3 %collective-permute-start.3 = (bf16[256,128]{1,0:T(8,128)(2,1)S(1)}, bf16[256,128]{1,0:T(8,128)(2,1)S(1)}, u32[]{:S(2)}, u32[]{:S(2)}) collective-permute-start(bf16[256,128]{1,0:T(8,128)(2,1)S(1)} %get-tuple-element.25), channel_id=1, source_target_pairs={{0,1},{1,0},{2,3},{3,2},{4,5},{5,4},{6,7},{7,6},{8,9},{9,8},{10,11... | collective-permute-start | bytes 196616 | tf_op jit(solution)/shard_map/ppermute | solution.py:231
  19.9 5.8 %collective-permute-start.4 = (bf16[256,128]{1,0:T(8,128)(2,1)S(1)}, bf16[256,128]{1,0:T(8,128)(2,1)S(1)}, u32[]{:S(2)}, u32[]{:S(2)}) collective-permute-start(bf16[256,128]{1,0:T(8,128)(2,1)S(1)} %get-tuple-element.26), channel_id=1, source_target_pairs={{0,2},{1,3},{2,0},{3,1},{4,6},{5,7},{6,4},{7,5},{8,10},{9,11},{10,... | collective-permute-start | bytes 196616 | tf_op jit(solution)/shard_map/ppermute | solution.py:231
  21.7 4.6 %collective-permute-start.5 = (bf16[256,128]{1,0:T(8,128)(2,1)S(1)}, bf16[256,128]{1,0:T(8,128)(2,1)S(1)}, u32[]{:S(2)}, u32[]{:S(2)}) collective-permute-start(bf16[256,128]{1,0:T(8,128)(2,1)S(1)} %get-tuple-element.27), channel_id=1, source_target_pairs={{0,3},{1,2},{2,1},{3,0},{4,7},{5,6},{6,5},{7,4},{8,11},{9,10},{10,... | collective-permute-start | bytes 196616 | tf_op jit(solution)/shard_map/ppermute | solution.py:231
  26.4 14.6 %collective-permute-start.6 = (bf16[1024,128]{1,0:T(8,128)(2,1)S(1)}, bf16[1024,128]{1,0:T(8,128)(2,1)S(1)}, u32[]{:S(2)}, u32[]{:S(2)}) collective-permute-start(bf16[1024,128]{1,0:T(8,128)(2,1)S(1)} %get-tuple-element.40), channel_id=1, source_target_pairs={{0,4},{1,5},{2,6},{3,7},{4,0},{5,1},{6,2},{7,3},{8,12},{9,13},{10,... | collective-permute-start | bytes 786440 | tf_op jit(solution)/shard_map/ppermute | solution.py:231
  28.0 13.1 %collective-permute-start.7 = (bf16[1024,128]{1,0:T(8,128)(2,1)S(1)}, bf16[1024,128]{1,0:T(8,128)(2,1)S(1)}, u32[]{:S(2)}, u32[]{:S(2)}) collective-permute-start(bf16[1024,128]{1,0:T(8,128)(2,1)S(1)} %get-tuple-element.40), channel_id=1, source_target_pairs={{0,8},{1,9},{2,10},{3,11},{4,12},{5,13},{6,14},{7,15},{8,0},{9,1},... | collective-permute-start | bytes 786440 | tf_op jit(solution)/shard_map/ppermute | solution.py:231
  30.7 6.8 %collective-permute-start.10 = (bf16[512,128]{1,0:T(8,128)(2,1)S(1)}, bf16[512,128]{1,0:T(8,128)(2,1)S(1)}, u32[]{:S(2)}, u32[]{:S(2)}) collective-permute-start(bf16[512,128]{1,0:T(8,128)(2,1)S(1)} %collective-permute-done.9.refs_1_), channel_id=1, source_target_pairs={{0,16},{1,17},{2,18},{3,19},{4,20},{5,21},{6,22},{7,23},{8,24},{9,... | collective-permute-start | bytes 393224 | tf_op jit(solution)/shard_map/ppermute | solution.py:231
  30.7 6.8 %collective-permute-start.13 = (bf16[512,128]{1,0:T(8,128)(2,1)S(1)}, bf16[512,128]{1,0:T(8,128)(2,1)S(1)}, u32[]{:S(2)}, u32[]{:S(2)}) collective-permute-start(bf16[512,128]{1,0:T(8,128)(2,1)S(1)} %collective-permute-done.12.refs_4_), channel_id=1, source_target_pairs={{0,112},{1,113},{2,114},{3,115},{4,116},{5,117},{6,118},{7,119},{8... | collective-permute-start | bytes 393224 | tf_op jit(solution)/shard_map/ppermute | solution.py:231
  34.0 13.9 %collective-permute-start.8 = (bf16[1024,128]{1,0:T(8,128)(2,1)S(1)}, bf16[1024,128]{1,0:T(8,128)(2,1)S(1)}, u32[]{:S(2)}, u32[]{:S(2)}) collective-permute-start(bf16[1024,128]{1,0:T(8,128)(2,1)S(1)} %get-tuple-element.40), channel_id=1, source_target_pairs={{0,12},{1,13},{2,14},{3,15},{4,8},{5,9},{6,10},{7,11},{8,4},{9,5},... | collective-permute-start | bytes 786440 | tf_op jit(solution)/shard_map/ppermute | solution.py:231
  37.5 6.9 %collective-permute-start.11 = (bf16[512,128]{1,0:T(8,128)(2,1)S(1)}, bf16[512,128]{1,0:T(8,128)(2,1)S(1)}, u32[]{:S(2)}, u32[]{:S(2)}) collective-permute-start(bf16[512,128]{1,0:T(8,128)(2,1)S(1)} %collective-permute-done.10.refs_2_), channel_id=1, source_target_pairs={{0,16},{1,17},{2,18},{3,19},{4,20},{5,21},{6,22},{7,23},{8,24},{9,... | collective-permute-start | bytes 393224 | tf_op jit(solution)/shard_map/ppermute | solution.py:231
  37.5 6.9 %collective-permute-start.14 = (bf16[512,128]{1,0:T(8,128)(2,1)S(1)}, bf16[512,128]{1,0:T(8,128)(2,1)S(1)}, u32[]{:S(2)}, u32[]{:S(2)}) collective-permute-start(bf16[512,128]{1,0:T(8,128)(2,1)S(1)} %collective-permute-done.13.refs_5_), channel_id=1, source_target_pairs={{0,112},{1,113},{2,114},{3,115},{4,116},{5,117},{6,118},{7,119},{8... | collective-permute-start | bytes 393224 | tf_op jit(solution)/shard_map/ppermute | solution.py:231
  44.3 5.5 %collective-permute-start.15 = (bf16[256,128]{1,0:T(8,128)(2,1)S(1)}, bf16[256,128]{1,0:T(8,128)(2,1)S(1)}, u32[]{:S(2)}, u32[]{:S(2)}) collective-permute-start(bf16[256,128]{1,0:T(8,128)(2,1)S(1)} %slice.32), channel_id=1, source_target_pairs={{0,16},{1,17},{2,18},{3,19},{4,20},{5,21},{6,22},{7,23},{8,24},{9,... | collective-permute-start | bytes 196616 | tf_op jit(solution)/shard_map/ppermute | solution.py:231
  44.4 5.4 %collective-permute-start.16 = (bf16[256,128]{1,0:T(8,128)(2,1)S(1)}, bf16[256,128]{1,0:T(8,128)(2,1)S(1)}, u32[]{:S(2)}, u32[]{:S(2)}) collective-permute-start(bf16[256,128]{1,0:T(8,128)(2,1)S(1)} %slice.33), channel_id=1, source_target_pairs={{0,112},{1,113},{2,114},{3,115},{4,116},{5,117},{6,118},{7,119},{8... | collective-permute-start | bytes 196616 | tf_op jit(solution)/shard_map/ppermute | solution.py:231
  50.1 20.4 %collective-permute-start.17 = (bf16[4,64,256]{2,1,0:T(8,128)(2,1)S(1)}, bf16[4,64,256]{2,1,0:T(8,128)(2,1)S(1)}, u32[]{:S(2)}, u32[]{:S(2)}) collective-permute-start(bf16[4,64,256]{2,1,0:T(8,128)(2,1)S(1)} %pick.1), channel_id=1, source_target_pairs={{0,0},{1,32},{2,64},{3,96},{4,4},{5,36},{6,68},{7,100},{8,8},{9,40... | collective-permute-start | bytes 393224 | tf_op jit(solution)/shard_map/ppermute | solution.py:231
  70.6 6.8 %copy-start.5 = (s32[256]{0:T(256)S(1)}, s32[256]{0:T(256)}, u32[]{:S(2)}) copy-start(s32[256]{0:T(256)} %param.8) | copy-start | bytes 3076
  70.6 18.6 %all-to-all-start = ((bf16[16,272,128]{2,1,0:T(8,128)(2,1)}), bf16[16,272,128]{2,1,0:T(8,128)(2,1)S(1)}, u32[]{:S(2)}, u32[]{:S(2)}) async-start(bf16[16,272,128]{2,1,0:T(8,128)(2,1)} %attention.1), calls=%async_computation | async-start | bytes 2228224 | tf_op jit(solution)/shard_map/all_to_all | solution.py:237
  76.6 12.5 %copy-start.4 = (s32[4]{0:T(128)S(1)}, s32[4]{0:T(128)}, u32[]{:S(2)}) copy-start(s32[4]{0:T(128)} %heads.5) | copy-start | bytes 52
  77.5 8.7 %collective-permute-start.18 = (bf16[64,256]{1,0:T(8,128)(2,1)S(1)}, bf16[64,256]{1,0:T(8,128)(2,1)S(1)}, u32[]{:S(2)}, u32[]{:S(2)}) collective-permute-start(bf16[64,256]{1,0:T(8,128)(2,1)S(1)} %get-tuple-element.39), channel_id=1, source_target_pairs={{0,4},{1,5},{2,6},{3,7},{4,0},{5,1},{6,2},{7,3},{8,12},{9,13},{10,... | collective-permute-start | bytes 98312 | tf_op jit(solution)/shard_map/ppermute | solution.py:231
  79.1 9.0 %collective-permute-start.19 = (bf16[64,256]{1,0:T(8,128)(2,1)S(1)}, bf16[64,256]{1,0:T(8,128)(2,1)S(1)}, u32[]{:S(2)}, u32[]{:S(2)}) collective-permute-start(bf16[64,256]{1,0:T(8,128)(2,1)S(1)} %get-tuple-element.38), channel_id=1, source_target_pairs={{0,8},{1,9},{2,10},{3,11},{4,12},{5,13},{6,14},{7,15},{8,0},{9,1},... | collective-permute-start | bytes 98312 | tf_op jit(solution)/shard_map/ppermute | solution.py:231
  81.8 6.3 %collective-permute-start.20 = (bf16[64,256]{1,0:T(8,128)(2,1)S(1)}, bf16[64,256]{1,0:T(8,128)(2,1)S(1)}, u32[]{:S(2)}, u32[]{:S(2)}) collective-permute-start(bf16[64,256]{1,0:T(8,128)(2,1)S(1)} %get-tuple-element.37), channel_id=1, source_target_pairs={{0,12},{1,13},{2,14},{3,15},{4,8},{5,9},{6,10},{7,11},{8,4},{9,5},... | collective-permute-start | bytes 98312 | tf_op jit(solution)/shard_map/ppermute | solution.py:231

commit v7 on v5

--- a/solution.py
+++ b/solution.py
@@ -69,36 +69,43 @@
         kt_scr[:, t * 128 : (t + 1) * 128] = k_scr[t * 128 : (t + 1) * 128, :].T
 
 
-def pick_kernel(*refs):
-    own, r1, r2, r3, l1, l2, l3, r4, l4 = refs[:9]
-    o_ref = refs[9]
+def pick_kernel(own, r1, r2, r3, l1, l2, l3, r4, l4, *o_refs):
     place = lax.axis_index("blk")
-    z, x = place // PLANE, lax.rem(place // NY, NX)
+    z, x, y = place // PLANE, lax.rem(place // NY, NX), lax.rem(place, NY)
 
     def select(lines, rows):
-        count = 2 * NX * lines * 2
-        out = lax.broadcasted_iota(jnp.int32, (count, rows), 0)
-        column = lax.broadcasted_iota(jnp.int32, (count, rows), 1)
-        half, k, line, j = out // (NX * lines * 2), out // (lines * 2) % NX, out // 2 % lines, out % 2
-        offset = lax.rem(z, 2) * 16 + (x ^ k) * NY + z // 2
+        blocks = 2 * lines
+        out = lax.broadcasted_iota(jnp.int32, (NY * NX * 2 * blocks, rows), 0)
+        column = lax.broadcasted_iota(jnp.int32, (NY * NX * 2 * blocks, rows), 1)
+        m, k, half, line, j = (
+            out // (NX * 2 * blocks),
+            out // (2 * blocks) % NX,
+            out // blocks % 2,
+            out // 2 % lines,
+            out % 2,
+        )
+        offset = lax.rem(z, 2) * 16 + (x ^ k) * NY + (y ^ m)
         wanted = line * 128 + half * 64 + j * BLOCK + offset
         return jnp.where(column == wanted, 1.0, 0.0).astype(jnp.bfloat16)
 
     whole, part = select(NY, 512), select(NY // 2, 256)
-    picked = [jnp.dot(whole, piece[...], preferred_element_type=jnp.float32) for piece in (own, l1, l2, l3)]
-    picked.append([jnp.dot(part, piece[...], preferred_element_type=jnp.float32) for piece in (r4, l4)])
-    picked += [jnp.dot(whole, piece[...], preferred_element_type=jnp.float32) for piece in (r3, r2, r1)]
-    for k in range(NX):
-        for half in range(2):
-            rows = []
-            for piece in picked:
-                if isinstance(piece, list):
-                    at = (half * NX + k) * 4
-                    rows += [piece[0][at : at + 4], piece[1][at : at + 4]]
-                else:
-                    at = (half * NX + k) * 8
-                    rows.append(piece[at : at + 8])
-            o_ref[k, :, half * HEAD : (half + 1) * HEAD] = jnp.concatenate(rows, axis=0).astype(jnp.bfloat16)
+    take = lambda matrix, piece: jnp.dot(matrix, piece[...], preferred_element_type=jnp.float32)
+    picked = [take(whole, piece) for piece in (own, l1, l2, l3)]
+    picked.append([take(part, piece) for piece in (r4, l4)])
+    picked += [take(whole, piece) for piece in (r3, r2, r1)]
+    for m in range(NY):
+        for k in range(NX):
+            for half in range(2):
+                rows = []
+                for piece in picked:
+                    if isinstance(piece, list):
+                        at = ((m * NX + k) * 2 + half) * 4
+                        rows += [piece[0][at : at + 4], piece[1][at : at + 4]]
+                    else:
+                        at = ((m * NX + k) * 2 + half) * 8
+                        rows.append(piece[at : at + 8])
+                rows = jnp.concatenate(rows, axis=0).astype(jnp.bfloat16)
+                o_refs[m][k, :, half * HEAD : (half + 1) * HEAD] = rows
 
 
 def attention_kernel(table, q_ref, kpos_ref, *refs):
@@ -282,14 +289,17 @@
     pieces = (own, r1, r2, r3, l1, l2, l3, r4, l4)
     picked = pl.pallas_call(
         pick_kernel,
-        out_shape=jax.ShapeDtypeStruct((NX, KEY_BLOCKS, 2 * HEAD), jnp.bfloat16),
+        out_shape=(jax.ShapeDtypeStruct((NX, KEY_BLOCKS, 2 * HEAD), jnp.bfloat16),) * NY,
         in_specs=[VMEM] * 9,
-        out_specs=VMEM,
-        cost_estimate=pl.CostEstimate(flops=20_000_000, bytes_accessed=1_200_000, transcendentals=0),
+        out_specs=(VMEM,) * NY,
+        cost_estimate=pl.CostEstimate(flops=80_000_000, bytes_accessed=1_500_000, transcendentals=0),
         compiler_params=SMALL,
         name="pick",
     )(*pieces)
-    picked = move(picked, lambda a, b, c: index(2 * c + a % 2, b, a // 2))
+    kept = [picked[0]]
+    for m in range(1, NY):
+        pairs = [(index(a, b, a // 2), index(a, b, a // 2 ^ m)) for a in range(NZ) for b in range(NX)]
+        kept.append(lax.ppermute(picked[m], "blk", pairs))
     partial = pl.pallas_call(
         attention_kernel,
         out_shape=jax.ShapeDtypeStruct((PLANE, MESSAGE, HEAD), jnp.bfloat16),
@@ -306,20 +316,21 @@
         cost_estimate=pl.CostEstimate(flops=3_000_000_000, bytes_accessed=4_000_000, transcendentals=5_000_000),
         name="attention",
     )(table, q, kpos, *pieces)
-    partial, picked = lax.optimization_barrier((partial, picked))
+    partial, kept = lax.optimization_barrier((partial, kept))
     out = exchange(partial, planes)
 
-    picked = jnp.concatenate(
-        [picked[0]] + [move(picked[k], lambda a, b, c, k=k: index(a, b ^ k, c)) for k in range(1, NX)], axis=0
+    hops = y ^ (z // 2)
+    kept = jnp.where(hops == 0, kept[0], jnp.where(hops == 1, kept[1], jnp.where(hops == 2, kept[2], kept[3])))
+    kept = jnp.concatenate(
+        [kept[0]] + [move(kept[k], lambda a, b, c, k=k: index(a, b ^ k, c)) for k in range(1, NX)], axis=0
     )
     blocks = jnp.arange(BLOCKS, dtype=jnp.int32)
     stored = jnp.sum(jnp.where(block_map[None, :] == blocks[:, None], blocks[None, :], 0), axis=1, dtype=jnp.int32)
-    from_z, from_y = 2 * y + z % 2, z // 2
-    row = ((stored // 8 % NX) ^ x) * KEY_BLOCKS + (stored // 32 - from_z) % NZ * 8
-    row = row + ((stored // 2 % NY) ^ from_y) * 2 + stored % 2
+    row = ((stored // 8 % NX) ^ x) * KEY_BLOCKS + (stored // 32 - z) % NZ * 8
+    row = row + ((stored // 2 % NY) ^ (z // 2)) * 2 + stored % 2
     position = blocks * BLOCK + place % BLOCK
     choose = (row[:, None] == blocks[None, :]) & (position < lengths[0])[:, None]
-    cache = jnp.dot(choose.astype(jnp.bfloat16), picked, preferred_element_type=jnp.float32).astype(jnp.bfloat16)
+    cache = jnp.dot(choose.astype(jnp.bfloat16), kept, preferred_element_type=jnp.float32).astype(jnp.bfloat16)
     cache = cache.reshape(BLOCKS, 2, HEAD).transpose(1, 0, 2)[None, :, None]
 
     my_blocks = lax.dynamic_slice_in_dim(block_map, 2 * place, 2)

time: 87.9 us -> 88.9 us (1.011)
  starting transfers between devices: 43.3 us -> 45.4 us
  waiting for transfers between devices: 20.2 us -> 18.8 us
    ppermute x0 -> x3, starting transfers between devices: none -> 2.81 us  [body(): kept.append(lax.ppermute(picked[m], 'blk', pairs))]
    ppermute x15 -> x14, starting transfers between devices: 27.7 us -> 25.6 us  [move(): lax.ppermute(value, 'blk', [(s, target(s // 16, s // 4 % 4, s % 4)) for s...]
    all_to_all x2, starting transfers between devices: 15.6 us -> 17 us  [exchange(): lax.all_to_all(value, 'blk', 0, 0, axis_index_groups=groups, tiled=True)]
    ppermute x15 -> x14, waiting for transfers between devices: 20.2 us -> 18.8 us  [move(): lax.ppermute(value, 'blk', [(s, target(s // 16, s // 4 % 4, s % 4)) for s...]
  transfers between devices with their start and end apart: 17 -> 19, of which waited for: 8 -> 8; matrix products, arithmetic and copies ran while one was open for 4% -> 4% of each run, Pallas kernels for 16% -> 16%
where the time goes in v7:
time: 88.9 us; the launch traced here: 88.7 us
  starting transfers between devices  45.4 us (51%)
  waiting for transfers between devices  18.8 us (21%)
  Pallas kernels  16.8 us (19%)
  local copies, waits for them, and re-layouts  4.5 us (5%)
  between operations  1.57 us (2%)
  other arithmetic  1.31 us (1%)
    ppermute x14, starting transfers between devices, move(): lax.ppermute(value, 'blk', [(s, target(s // 16, s // 4 % 4, s % 4)) for s...  25.6 us
    ppermute x14, waiting for transfers between devices, move(): lax.ppermute(value, 'blk', [(s, target(s // 16, s // 4 % 4, s % 4)) for s...  18.8 us
    all_to_all x2, starting transfers between devices, exchange(): lax.all_to_all(value, 'blk', 0, 0, axis_index_groups=groups, tiled=True)  17 us
    pallas_call x1, Pallas kernels, body(): pl.pallas_call(attention_kernel, out_shape=jax.ShapeDtypeStruct((PLANE, M...  11.7 us
    ppermute x3, starting transfers between devices, body(): kept.append(lax.ppermute(picked[m], 'blk', pairs))  2.81 us
    unnamed x13, local copies, waits for them, and re-layouts  2.54 us
    pallas_call x1, Pallas kernels, body(): pl.pallas_call(combine_kernel, out_shape=jax.ShapeDtypeStruct((2 * BLOCK,...  2.08 us
  transfers between devices with their start and end apart: 19, of which 8 were waited for; matrix products, arithmetic and copies ran while one was open for 4% of the time, Pallas kernels for 16%

profile of v7, /device:TPU:8, one launch (start us, length us, event | category | flops | bytes accessed | tf_op | source)
XLA Modules:
  0.0 88.7 jit_solution(192334511615804267)
XLA Ops:
  0.6 0.9 %copy-done.1 = bf16[1,2,64,512]{3,2,1,0:T(8,128)(2,1)S(1)} copy-done((bf16[1,2,64,512]{3,2,1,0:T(8,128)(2,1)S(1)}, bf16[1,2,64,512]{3,2,1,0:T(8,128)(2,1)}, u32[]{:S(2)}) %copy-start.1) | copy-done | bytes 131096
  1.5 0.7 copy-done.2
  2.2 0.6 split_kv.1
  2.8 2.3 %collective-permute-start = (bf16[128,128]{1,0:T(8,128)(2,1)S(1)}, bf16[128,128]{1,0:T(8,128)(2,1)S(1)}, u32[]{:S(2)}, u32[]{:S(2)}) collective-permute-start(bf16[128,128]{1,0:T(8,128)(2,1)S(1)} %get-tuple-element.16), channel_id=1, source_target_pairs={{0,1},{1,0},{2,3},{3,2},{4,5},{5,4},{6,7},{7,6},{8,9},{9,8},{10,11... | collective-permute-start | bytes 98312 | tf_op jit(solution)/shard_map/ppermute | solution.py:237
  5.0 0.9 collective-permute-start.1
  5.9 0.7 collective-permute-start.2
  6.6 0.9 %copy-done = bf16[1,64,2048]{2,1,0:T(8,128)(2,1)S(1)} copy-done((bf16[1,64,2048]{2,1,0:T(8,128)(2,1)S(1)}, bf16[1,64,2048]{2,1,0:T(8,128)(2,1)}, u32[]{:S(2)}) %copy-start) | copy-done | bytes 262168
  7.6 1.7 %split_q.1 = bf16[16,256,128]{2,1,0:T(8,128)(2,1)} custom-call(s32[4]{0:T(128)S(1)} %copy-done.2, bf16[64,2048]{1,0:T(8,128)(2,1)S(1)} %bitcast.25), custom_call_target="tpu_custom_call" | custom-call | tf_op jit(solution)/shard_map/split_q/pallas_call | solution.py:258
  9.2 8.3 %all-to-all-start = ((bf16[16,256,128]{2,1,0:T(8,128)(2,1)}), bf16[16,256,128]{2,1,0:T(8,128)(2,1)S(1)}, u32[]{:S(2)}, u32[]{:S(2)}) async-start(bf16[16,256,128]{2,1,0:T(8,128)(2,1)} %split_q.1), calls=%async_computation | async-start | bytes 2097152 | tf_op jit(solution)/shard_map/all_to_all | solution.py:243
  19.4 5.9 %collective-permute-start.6 = (bf16[512,128]{1,0:T(8,128)(2,1)S(1)}, bf16[512,128]{1,0:T(8,128)(2,1)S(1)}, u32[]{:S(2)}, u32[]{:S(2)}) collective-permute-start(bf16[512,128]{1,0:T(8,128)(2,1)S(1)} %constant_dynamic-update-slice_fusion.refs_0_.own), channel_id=1, source_target_pairs={{0,112},{1,113},{2,114},{3,115},{4,116},{5,117},{6,118},{7,119},{8... | collective-permute-start | bytes 393224 | tf_op jit(solution)/shard_map/ppermute | solution.py:237
  25.3 2.5 %collective-permute-done.6.refs_4_.l1 = bf16[512,128]{1,0:T(8,128)(2,1)S(1)} collective-permute-done((bf16[512,128]{1,0:T(8,128)(2,1)S(1)}, bf16[512,128]{1,0:T(8,128)(2,1)S(1)}, u32[]{:S(2)}, u32[]{:S(2)}) %collective-permute-start.6) | collective-permute-done | bytes 131104 | tf_op jit(solution)/shard_map/ppermute | solution.py:237
  27.9 3.7 %collective-permute-start.7 = (bf16[512,128]{1,0:T(8,128)(2,1)S(1)}, bf16[512,128]{1,0:T(8,128)(2,1)S(1)}, u32[]{:S(2)}, u32[]{:S(2)}) collective-permute-start(bf16[512,128]{1,0:T(8,128)(2,1)S(1)} %collective-permute-done.6.refs_4_.l1), channel_id=1, source_target_pairs={{0,112},{1,113},{2,114},{3,115},{4,116},{5,117},{6,118},{7,119},{8... | collective-permute-start | bytes 393224 | tf_op jit(solution)/shard_map/ppermute | solution.py:237
  31.9 2.1 %collective-permute-done.7.refs_5_.l2 = bf16[512,128]{1,0:T(8,128)(2,1)S(1)} collective-permute-done((bf16[512,128]{1,0:T(8,128)(2,1)S(1)}, bf16[512,128]{1,0:T(8,128)(2,1)S(1)}, u32[]{:S(2)}, u32[]{:S(2)}) %collective-permute-start.7) | collective-permute-done | bytes 131104 | tf_op jit(solution)/shard_map/ppermute | solution.py:237
  34.0 3.7 %collective-permute-start.8 = (bf16[512,128]{1,0:T(8,128)(2,1)S(1)}, bf16[512,128]{1,0:T(8,128)(2,1)S(1)}, u32[]{:S(2)}, u32[]{:S(2)}) collective-permute-start(bf16[512,128]{1,0:T(8,128)(2,1)S(1)} %collective-permute-done.7.refs_5_.l2), channel_id=1, source_target_pairs={{0,112},{1,113},{2,114},{3,115},{4,116},{5,117},{6,118},{7,119},{8... | collective-permute-start | bytes 393224 | tf_op jit(solution)/shard_map/ppermute | solution.py:237
  37.7 3.1 %collective-permute-done.8.refs_6_.l3 = bf16[512,128]{1,0:T(8,128)(2,1)S(1)} collective-permute-done((bf16[512,128]{1,0:T(8,128)(2,1)S(1)}, bf16[512,128]{1,0:T(8,128)(2,1)S(1)}, u32[]{:S(2)}, u32[]{:S(2)}) %collective-permute-start.8) | collective-permute-done | bytes 131104 | tf_op jit(solution)/shard_map/ppermute | solution.py:237
  40.8 3.7 %collective-permute-start.10 = (bf16[256,128]{1,0:T(8,128)(2,1)S(1)}, bf16[256,128]{1,0:T(8,128)(2,1)S(1)}, u32[]{:S(2)}, u32[]{:S(2)}) collective-permute-start(bf16[256,128]{1,0:T(8,128)(2,1)S(1)} %slice.33), channel_id=1, source_target_pairs={{0,112},{1,113},{2,114},{3,115},{4,116},{5,117},{6,118},{7,119},{8... | collective-permute-start | bytes 196616 | tf_op jit(solution)/shard_map/ppermute | solution.py:237
  44.7 1.7 %collective-permute-done.10.refs_8_.l4 = bf16[256,128]{1,0:T(8,128)(2,1)S(1)} collective-permute-done((bf16[256,128]{1,0:T(8,128)(2,1)S(1)}, bf16[256,128]{1,0:T(8,128)(2,1)S(1)}, u32[]{:S(2)}, u32[]{:S(2)}) %collective-permute-start.10) | collective-permute-done | bytes 65568 | tf_op jit(solution)/shard_map/ppermute | solution.py:237
  46.4 3.7 %collective-permute-done.9.refs_7_.r4 = bf16[256,128]{1,0:T(8,128)(2,1)S(1)} collective-permute-done((bf16[256,128]{1,0:T(8,128)(2,1)S(1)}, bf16[256,128]{1,0:T(8,128)(2,1)S(1)}, u32[]{:S(2)}, u32[]{:S(2)}) %collective-permute-start.9) | collective-permute-done | bytes 65568 | tf_op jit(solution)/shard_map/ppermute | solution.py:237
  50.1 0.7 pick.1
  50.8 1.3 %collective-permute-start.11 = (bf16[4,64,256]{2,1,0:T(8,128)(2,1)S(1)}, bf16[4,64,256]{2,1,0:T(8,128)(2,1)S(1)}, u32[]{:S(2)}, u32[]{:S(2)}) collective-permute-start(bf16[4,64,256]{2,1,0:T(8,128)(2,1)S(1)} %get-tuple-element.20), channel_id=1, source_target_pairs={{0,1},{4,5},{8,9},{12,13},{16,17},{20,21},{24,25},{28,29},{33,32},... | collective-permute-start | bytes 393224 | tf_op jit(solution)/shard_map/ppermute | solution.py:302
  52.1 0.7 collective-permute-start.12
  52.8 0.8 collective-permute-start.13
  53.7 11.7 %attention.1 = bf16[16,272,128]{2,1,0:T(8,128)(2,1)} custom-call(s32[144]{0:T(256)S(1)} %concatenate.9.table, bf16[32,128,128]{2,1,0:T(8,128)(2,1)S(1)} %bitcast.24, s32[8,256]{1,0:T(8,128)S(1)} %broadcast_add_fusion.kpos_ref, bf16[512,128]{1,0:T(8,128)(2,1)S(1)} %constant_dynamic-update-slice_fusion.refs_0_.own, ...), custom_call_target="tpu_custom_call" | custom-call | flops 3000000000 | bytes 4000000 | tf_op jit(solution)/shard_map/attention/pallas_call | solution.py:303
  65.4 8.7 %all-to-all-start.1 = ((bf16[16,272,128]{2,1,0:T(8,128)(2,1)}), bf16[16,272,128]{2,1,0:T(8,128)(2,1)S(1)}, u32[]{:S(2)}, u32[]{:S(2)}) async-start(bf16[16,272,128]{2,1,0:T(8,128)(2,1)} %attention.1), calls=%async_computation.1 | async-start | bytes 2228224 | tf_op jit(solution)/shard_map/all_to_all | solution.py:243
  75.0 1.6 %collective-permute-start.14 = (bf16[64,256]{1,0:T(8,128)(2,1)S(1)}, bf16[64,256]{1,0:T(8,128)(2,1)S(1)}, u32[]{:S(2)}, u32[]{:S(2)}) collective-permute-start(bf16[64,256]{1,0:T(8,128)(2,1)S(1)} %get-tuple-element.37), channel_id=1, source_target_pairs={{0,4},{1,5},{2,6},{3,7},{4,0},{5,1},{6,2},{7,3},{8,12},{9,13},{10,... | collective-permute-start | bytes 98312 | tf_op jit(solution)/shard_map/ppermute | solution.py:237
  76.6 2.7 %collective-permute-start.15 = (bf16[64,256]{1,0:T(8,128)(2,1)S(1)}, bf16[64,256]{1,0:T(8,128)(2,1)S(1)}, u32[]{:S(2)}, u32[]{:S(2)}) collective-permute-start(bf16[64,256]{1,0:T(8,128)(2,1)S(1)} %get-tuple-element.36), channel_id=1, source_target_pairs={{0,8},{1,9},{2,10},{3,11},{4,12},{5,13},{6,14},{7,15},{8,0},{9,1},... | collective-permute-start | bytes 98312 | tf_op jit(solution)/shard_map/ppermute | solution.py:237
  79.3 0.6 collective-permute-start.16
  79.9 3.8 %collective-permute-done.14 = bf16[64,256]{1,0:T(8,128)(2,1)S(1)} collective-permute-done((bf16[64,256]{1,0:T(8,128)(2,1)S(1)}, bf16[64,256]{1,0:T(8,128)(2,1)S(1)}, u32[]{:S(2)}, u32[]{:S(2)}) %collective-permute-start.14) | collective-permute-done | bytes 32800 | tf_op jit(solution)/shard_map/ppermute | solution.py:237
  83.7 1.9 %collective-permute-done.15 = bf16[64,256]{1,0:T(8,128)(2,1)S(1)} collective-permute-done((bf16[64,256]{1,0:T(8,128)(2,1)S(1)}, bf16[64,256]{1,0:T(8,128)(2,1)S(1)}, u32[]{:S(2)}, u32[]{:S(2)}) %collective-permute-start.15) | collective-permute-done | bytes 32800 | tf_op jit(solution)/shard_map/ppermute | solution.py:237
  85.6 0.3 convolution_convert_fusion
  85.9 0.8 copy.15
  86.7 2.1 %combine.1 = bf16[64,2048]{1,0:T(8,128)(2,1)} custom-call(s32[4]{0:T(128)S(1)} %copy-done.3, s32[2]{0:T(128)S(1)} %dynamic_slice.13.blocks, s32[1]{0:T(128)} %copy.19.length, bf16[16,272,128]{2,1,0:T(8,128)(2,1)S(1)} %all-to-all-done.1.m_ref), custom_call_target="tpu_custom_call" | custom-call | tf_op jit(solution)/shard_map/combine/pallas_call | solution.py:337
  (56 shorter events, 2.7 us)
Async XLA Ops:
  0.6 0.9 %copy-start.1 = (bf16[1,2,64,512]{3,2,1,0:T(8,128)(2,1)S(1)}, bf16[1,2,64,512]{3,2,1,0:T(8,128)(2,1)}, u32[]{:S(2)}) copy-start(bf16[1,2,64,512]{3,2,1,0:T(8,128)(2,1)} %param.6) | copy-start | bytes 393220
  1.5 0.7 copy-start.2
  2.8 16.5 %collective-permute-start = (bf16[128,128]{1,0:T(8,128)(2,1)S(1)}, bf16[128,128]{1,0:T(8,128)(2,1)S(1)}, u32[]{:S(2)}, u32[]{:S(2)}) collective-permute-start(bf16[128,128]{1,0:T(8,128)(2,1)S(1)} %get-tuple-element.16), channel_id=1, source_target_pairs={{0,1},{1,0},{2,3},{3,2},{4,5},{5,4},{6,7},{7,6},{8,9},{9,8},{10,11... | collective-permute-start | bytes 98312 | tf_op jit(solution)/shard_map/ppermute | solution.py:237
  5.0 14.3 %collective-permute-start.1 = (bf16[128,128]{1,0:T(8,128)(2,1)S(1)}, bf16[128,128]{1,0:T(8,128)(2,1)S(1)}, u32[]{:S(2)}, u32[]{:S(2)}) collective-permute-start(bf16[128,128]{1,0:T(8,128)(2,1)S(1)} %get-tuple-element.17), channel_id=1, source_target_pairs={{0,2},{1,3},{2,0},{3,1},{4,6},{5,7},{6,4},{7,5},{8,10},{9,11},{10,... | collective-permute-start | bytes 98312 | tf_op jit(solution)/shard_map/ppermute | solution.py:237
  5.9 13.5 %collective-permute-start.2 = (bf16[128,128]{1,0:T(8,128)(2,1)S(1)}, bf16[128,128]{1,0:T(8,128)(2,1)S(1)}, u32[]{:S(2)}, u32[]{:S(2)}) collective-permute-start(bf16[128,128]{1,0:T(8,128)(2,1)S(1)} %get-tuple-element.18), channel_id=1, source_target_pairs={{0,3},{1,2},{2,1},{3,0},{4,7},{5,6},{6,5},{7,4},{8,11},{9,10},{10,... | collective-permute-start | bytes 98312 | tf_op jit(solution)/shard_map/ppermute | solution.py:237
  6.6 0.9 %copy-start = (bf16[1,64,2048]{2,1,0:T(8,128)(2,1)S(1)}, bf16[1,64,2048]{2,1,0:T(8,128)(2,1)}, u32[]{:S(2)}) copy-start(bf16[1,64,2048]{2,1,0:T(8,128)(2,1)} %param.5) | copy-start | bytes 786436
  9.2 8.3 %copy-start.4 = (s32[256]{0:T(256)S(1)}, s32[256]{0:T(256)}, u32[]{:S(2)}) copy-start(s32[256]{0:T(256)} %param.8) | copy-start | bytes 3076
  9.2 44.4 %all-to-all-start = ((bf16[16,256,128]{2,1,0:T(8,128)(2,1)}), bf16[16,256,128]{2,1,0:T(8,128)(2,1)S(1)}, u32[]{:S(2)}, u32[]{:S(2)}) async-start(bf16[16,256,128]{2,1,0:T(8,128)(2,1)} %split_q.1), calls=%async_computation | async-start | bytes 2097152 | tf_op jit(solution)/shard_map/all_to_all | solution.py:243
  19.4 8.5 %collective-permute-start.6 = (bf16[512,128]{1,0:T(8,128)(2,1)S(1)}, bf16[512,128]{1,0:T(8,128)(2,1)S(1)}, u32[]{:S(2)}, u32[]{:S(2)}) collective-permute-start(bf16[512,128]{1,0:T(8,128)(2,1)S(1)} %constant_dynamic-update-slice_fusion.refs_0_.own), channel_id=1, source_target_pairs={{0,112},{1,113},{2,114},{3,115},{4,116},{5,117},{6,118},{7,119},{8... | collective-permute-start | bytes 393224 | tf_op jit(solution)/shard_map/ppermute | solution.py:237
  25.3 6.2 %collective-permute-start.3 = (bf16[512,128]{1,0:T(8,128)(2,1)S(1)}, bf16[512,128]{1,0:T(8,128)(2,1)S(1)}, u32[]{:S(2)}, u32[]{:S(2)}) collective-permute-start(bf16[512,128]{1,0:T(8,128)(2,1)S(1)} %constant_dynamic-update-slice_fusion.refs_0_.own), channel_id=1, source_target_pairs={{0,16},{1,17},{2,18},{3,19},{4,20},{5,21},{6,22},{7,23},{8,24},{9,... | collective-permute-start | bytes 393224 | tf_op jit(solution)/shard_map/ppermute | solution.py:237
  27.9 6.2 %collective-permute-start.7 = (bf16[512,128]{1,0:T(8,128)(2,1)S(1)}, bf16[512,128]{1,0:T(8,128)(2,1)S(1)}, u32[]{:S(2)}, u32[]{:S(2)}) collective-permute-start(bf16[512,128]{1,0:T(8,128)(2,1)S(1)} %collective-permute-done.6.refs_4_.l1), channel_id=1, source_target_pairs={{0,112},{1,113},{2,114},{3,115},{4,116},{5,117},{6,118},{7,119},{8... | collective-permute-start | bytes 393224 | tf_op jit(solution)/shard_map/ppermute | solution.py:237
  31.5 6.2 %collective-permute-start.4 = (bf16[512,128]{1,0:T(8,128)(2,1)S(1)}, bf16[512,128]{1,0:T(8,128)(2,1)S(1)}, u32[]{:S(2)}, u32[]{:S(2)}) collective-permute-start(bf16[512,128]{1,0:T(8,128)(2,1)S(1)} %collective-permute-done.3.refs_1_.r1), channel_id=1, source_target_pairs={{0,16},{1,17},{2,18},{3,19},{4,20},{5,21},{6,22},{7,23},{8,24},{9,... | collective-permute-start | bytes 393224 | tf_op jit(solution)/shard_map/ppermute | solution.py:237
  34.0 6.8 %collective-permute-start.8 = (bf16[512,128]{1,0:T(8,128)(2,1)S(1)}, bf16[512,128]{1,0:T(8,128)(2,1)S(1)}, u32[]{:S(2)}, u32[]{:S(2)}) collective-permute-start(bf16[512,128]{1,0:T(8,128)(2,1)S(1)} %collective-permute-done.7.refs_5_.l2), channel_id=1, source_target_pairs={{0,112},{1,113},{2,114},{3,115},{4,116},{5,117},{6,118},{7,119},{8... | collective-permute-start | bytes 393224 | tf_op jit(solution)/shard_map/ppermute | solution.py:237
  37.7 6.9 %collective-permute-start.5 = (bf16[512,128]{1,0:T(8,128)(2,1)S(1)}, bf16[512,128]{1,0:T(8,128)(2,1)S(1)}, u32[]{:S(2)}, u32[]{:S(2)}) collective-permute-start(bf16[512,128]{1,0:T(8,128)(2,1)S(1)} %collective-permute-done.4.refs_2_.r2), channel_id=1, source_target_pairs={{0,16},{1,17},{2,18},{3,19},{4,20},{5,21},{6,22},{7,23},{8,24},{9,... | collective-permute-start | bytes 393224 | tf_op jit(solution)/shard_map/ppermute | solution.py:237
  40.8 5.6 %collective-permute-start.10 = (bf16[256,128]{1,0:T(8,128)(2,1)S(1)}, bf16[256,128]{1,0:T(8,128)(2,1)S(1)}, u32[]{:S(2)}, u32[]{:S(2)}) collective-permute-start(bf16[256,128]{1,0:T(8,128)(2,1)S(1)} %slice.33), channel_id=1, source_target_pairs={{0,112},{1,113},{2,114},{3,115},{4,116},{5,117},{6,118},{7,119},{8... | collective-permute-start | bytes 196616 | tf_op jit(solution)/shard_map/ppermute | solution.py:237
  44.6 5.5 %collective-permute-start.9 = (bf16[256,128]{1,0:T(8,128)(2,1)S(1)}, bf16[256,128]{1,0:T(8,128)(2,1)S(1)}, u32[]{:S(2)}, u32[]{:S(2)}) collective-permute-start(bf16[256,128]{1,0:T(8,128)(2,1)S(1)} %slice.32), channel_id=1, source_target_pairs={{0,16},{1,17},{2,18},{3,19},{4,20},{5,21},{6,22},{7,23},{8,24},{9,... | collective-permute-start | bytes 196616 | tf_op jit(solution)/shard_map/ppermute | solution.py:237
  50.8 14.6 %collective-permute-start.11 = (bf16[4,64,256]{2,1,0:T(8,128)(2,1)S(1)}, bf16[4,64,256]{2,1,0:T(8,128)(2,1)S(1)}, u32[]{:S(2)}, u32[]{:S(2)}) collective-permute-start(bf16[4,64,256]{2,1,0:T(8,128)(2,1)S(1)} %get-tuple-element.20), channel_id=1, source_target_pairs={{0,1},{4,5},{8,9},{12,13},{16,17},{20,21},{24,25},{28,29},{33,32},... | collective-permute-start | bytes 393224 | tf_op jit(solution)/shard_map/ppermute | solution.py:302
  52.1 13.3 %collective-permute-start.12 = (bf16[4,64,256]{2,1,0:T(8,128)(2,1)S(1)}, bf16[4,64,256]{2,1,0:T(8,128)(2,1)S(1)}, u32[]{:S(2)}, u32[]{:S(2)}) collective-permute-start(bf16[4,64,256]{2,1,0:T(8,128)(2,1)S(1)} %get-tuple-element.21), channel_id=1, source_target_pairs={{0,2},{4,6},{8,10},{12,14},{16,18},{20,22},{24,26},{28,30},{33,35}... | collective-permute-start | bytes 393224 | tf_op jit(solution)/shard_map/ppermute | solution.py:302
  52.8 12.6 %collective-permute-start.13 = (bf16[4,64,256]{2,1,0:T(8,128)(2,1)S(1)}, bf16[4,64,256]{2,1,0:T(8,128)(2,1)S(1)}, u32[]{:S(2)}, u32[]{:S(2)}) collective-permute-start(bf16[4,64,256]{2,1,0:T(8,128)(2,1)S(1)} %get-tuple-element.22), channel_id=1, source_target_pairs={{0,3},{4,7},{8,11},{12,15},{16,19},{20,23},{24,27},{28,31},{33,34}... | collective-permute-start | bytes 393224 | tf_op jit(solution)/shard_map/ppermute | solution.py:302
  65.4 21.2 %all-to-all-start.1 = ((bf16[16,272,128]{2,1,0:T(8,128)(2,1)}), bf16[16,272,128]{2,1,0:T(8,128)(2,1)S(1)}, u32[]{:S(2)}, u32[]{:S(2)}) async-start(bf16[16,272,128]{2,1,0:T(8,128)(2,1)} %attention.1), calls=%async_computation.1 | async-start | bytes 2228224 | tf_op jit(solution)/shard_map/all_to_all | solution.py:243
  74.1 12.5 %copy-start.3 = (s32[4]{0:T(128)S(1)}, s32[4]{0:T(128)}, u32[]{:S(2)}) copy-start(s32[4]{0:T(128)} %heads.5) | copy-start | bytes 52
  75.0 8.7 %collective-permute-start.14 = (bf16[64,256]{1,0:T(8,128)(2,1)S(1)}, bf16[64,256]{1,0:T(8,128)(2,1)S(1)}, u32[]{:S(2)}, u32[]{:S(2)}) collective-permute-start(bf16[64,256]{1,0:T(8,128)(2,1)S(1)} %get-tuple-element.37), channel_id=1, source_target_pairs={{0,4},{1,5},{2,6},{3,7},{4,0},{5,1},{6,2},{7,3},{8,12},{9,13},{10,... | collective-permute-start | bytes 98312 | tf_op jit(solution)/shard_map/ppermute | solution.py:237
  76.6 9.0 %collective-permute-start.15 = (bf16[64,256]{1,0:T(8,128)(2,1)S(1)}, bf16[64,256]{1,0:T(8,128)(2,1)S(1)}, u32[]{:S(2)}, u32[]{:S(2)}) collective-permute-start(bf16[64,256]{1,0:T(8,128)(2,1)S(1)} %get-tuple-element.36), channel_id=1, source_target_pairs={{0,8},{1,9},{2,10},{3,11},{4,12},{5,13},{6,14},{7,15},{8,0},{9,1},... | collective-permute-start | bytes 98312 | tf_op jit(solution)/shard_map/ppermute | solution.py:237
  79.3 6.3 %collective-permute-start.16 = (bf16[64,256]{1,0:T(8,128)(2,1)S(1)}, bf16[64,256]{1,0:T(8,128)(2,1)S(1)}, u32[]{:S(2)}, u32[]{:S(2)}) collective-permute-start(bf16[64,256]{1,0:T(8,128)(2,1)S(1)} %get-tuple-element.35), channel_id=1, source_target_pairs={{0,12},{1,13},{2,14},{3,15},{4,8},{5,9},{6,10},{7,11},{8,4},{9,5},... | collective-permute-start | bytes 98312 | tf_op jit(solution)/shard_map/ppermute | solution.py:237

commit v8 on v7

--- a/solution.py
+++ b/solution.py
@@ -44,14 +44,14 @@
         o_refs[k][...] = kv_ref[:, pl.ds(pl.multiple_of(heads[y ^ k] * HEAD, HEAD), HEAD)]
 
 
-def split_q_kernel(heads, q_ref, o_ref):
-    for y in range(NY):
+def split_q_kernel(heads, q_ref, *o_refs):
+    y = lax.rem(lax.axis_index("blk"), NY)
+    for k in range(NY):
         for g in range(GROUP):
-            column = pl.multiple_of((heads[y] * GROUP + g) * HEAD, HEAD)
+            column = pl.multiple_of((heads[y ^ k] * GROUP + g) * HEAD, HEAD)
             for j in range(2):
-                tile = q_ref[j * BLOCK : (j + 1) * BLOCK, pl.ds(column, HEAD)]
-                for x in range(NX):
-                    o_ref[x * NY + y, j * ROWS + g * BLOCK : j * ROWS + (g + 1) * BLOCK] = tile
+                rows = slice(j * ROWS + g * BLOCK, j * ROWS + (g + 1) * BLOCK)
+                o_refs[k][rows, :] = q_ref[j * BLOCK : (j + 1) * BLOCK, pl.ds(column, HEAD)]
 
 
 def arrange(table, pieces, k_scr, kt_scr, v_scr):
@@ -120,6 +120,7 @@
         kt_scr,
         v_scr,
     )
+    mine = 2 * lax.rem(lax.axis_index("blk"), PLANE)
     lane = lax.broadcasted_iota(jnp.int32, (ROWS, 128), 1)
     token = lax.broadcasted_iota(jnp.int32, (BLOCK, CHUNK), 0)
 
@@ -135,7 +136,7 @@
             stat[...] = jnp.where(lane == blocks[u] + Q_BLOCKS, total, old)
 
         def work(n):
-            q = jnp.concatenate([q_ref[blocks[u]] for u in range(JOINED)], axis=0)
+            q = jnp.concatenate([q_ref[blocks[u] ^ mine] for u in range(JOINED)], axis=0)
             tops = [None] * (JOINED * GROUP)
             for c in range(n):
                 start = pl.multiple_of((low + c) * CHUNK, CHUNK)
@@ -255,16 +256,21 @@
     right = lambda v: move(v, lambda a, b, c: index(a + 1, b, c))
     left = lambda v: move(v, lambda a, b, c: index(a - 1, b, c))
     r1, l1 = right(own), left(own)
-    q = pl.pallas_call(
+    qs = pl.pallas_call(
         split_q_kernel,
-        out_shape=jax.ShapeDtypeStruct((PLANE, 2 * ROWS, HEAD), jnp.bfloat16),
+        out_shape=(jax.ShapeDtypeStruct((2 * ROWS, HEAD), jnp.bfloat16),) * NY,
         in_specs=[SMEM, VMEM],
-        out_specs=VMEM,
+        out_specs=(VMEM,) * NY,
         compiler_params=SMALL,
         name="split_q",
     )(segment_head, query.reshape(2 * BLOCK, QUERY_HEADS * HEAD))
-    q = exchange(q, planes).reshape(Q_BLOCKS, ROWS, HEAD)
+    qs, _ = lax.optimization_barrier((qs, own))
+    q = [qs[0]] + [move(qs[k], lambda a, b, c, k=k: index(a, b, c ^ k)) for k in range(1, NY)]
     r2, l2 = right(r1), left(l1)
+    q = jnp.concatenate(q, axis=0)
+    q, _ = lax.optimization_barrier((q, l2))
+    q = [q] + [move(q, lambda a, b, c, k=k: index(a, b ^ k, c)) for k in range(1, NX)]
+    q = jnp.concatenate(q, axis=0).reshape(Q_BLOCKS, ROWS, HEAD)
     r3, l3 = right(r2), left(l2)
     half = own.shape[0] // 2
     r4, l4 = right(r3[:half]), left(l3[half:])

time: 88.9 us -> 88.9 us (level)
  local copies, waits for them, and re-layouts: 4.5 us -> 6.53 us
  waiting for transfers between devices: 18.8 us -> 16.8 us
  Pallas kernels: 16.8 us -> 15.6 us
    ppermute x14 -> x20, starting transfers between devices: 25.6 us -> 34.1 us  [move(): lax.ppermute(value, 'blk', [(s, target(s // 16, s // 4 % 4, s % 4)) for s...]
    all_to_all x2 -> x1, starting transfers between devices: 17 us -> 9.03 us  [exchange(): lax.all_to_all(value, 'blk', 0, 0, axis_index_groups=groups, tiled=True)]
    ppermute x14 -> x20, waiting for transfers between devices: 18.8 us -> 16.8 us  [move(): lax.ppermute(value, 'blk', [(s, target(s // 16, s // 4 % 4, s % 4)) for s...]
    pallas_call x1, Pallas kernels: 1.66 us -> 0.62 us  [body(): pl.pallas_call(split_q_kernel, out_shape=(jax.ShapeDtypeStruct((2 * ROWS,...]
    unnamed x13 -> x15, local copies, waits for them, and re-layouts: 2.54 us -> 3.19 us
  transfers between devices with their start and end apart: 19 -> 24, of which waited for: 8 -> 8; matrix products, arithmetic and copies ran while one was open for 4% -> 6% of each run, Pallas kernels for 16% -> 15%
where the time goes in v8:
time: 88.9 us; the launch traced here: 88 us
  starting transfers between devices  45.8 us (52%)
  waiting for transfers between devices  16.8 us (19%)
  Pallas kernels  15.6 us (18%)
  local copies, waits for them, and re-layouts  6.53 us (7%)
  between operations  1.59 us (2%)
  other arithmetic  1.38 us (2%)
    ppermute x20, starting transfers between devices, move(): lax.ppermute(value, 'blk', [(s, target(s // 16, s // 4 % 4, s % 4)) for s...  34.1 us
    ppermute x20, waiting for transfers between devices, move(): lax.ppermute(value, 'blk', [(s, target(s // 16, s // 4 % 4, s % 4)) for s...  16.8 us
    pallas_call x1, Pallas kernels, body(): pl.pallas_call(attention_kernel, out_shape=jax.ShapeDtypeStruct((PLANE, M...  11.6 us
    all_to_all x1, starting transfers between devices, exchange(): lax.all_to_all(value, 'blk', 0, 0, axis_index_groups=groups, tiled=True)  9.03 us
    unnamed x15, local copies, waits for them, and re-layouts  3.19 us
    ppermute x3, starting transfers between devices, body(): kept.append(lax.ppermute(picked[m], 'blk', pairs))  2.63 us
    pallas_call x1, Pallas kernels, body(): pl.pallas_call(combine_kernel, out_shape=jax.ShapeDtypeStruct((2 * BLOCK,...  2.08 us
  transfers between devices with their start and end apart: 24, of which 8 were waited for; matrix products, arithmetic and copies ran while one was open for 6% of the time, Pallas kernels for 15%

profile of v8, /device:TPU:8, one launch (start us, length us, event | category | flops | bytes accessed | tf_op | source)
XLA Modules:
  0.0 88.0 jit_solution(13762428753686475938)
XLA Ops:
  0.6 0.9 %copy-done.1 = bf16[1,2,64,512]{3,2,1,0:T(8,128)(2,1)S(1)} copy-done((bf16[1,2,64,512]{3,2,1,0:T(8,128)(2,1)S(1)}, bf16[1,2,64,512]{3,2,1,0:T(8,128)(2,1)}, u32[]{:S(2)}) %copy-start.1) | copy-done | bytes 131096
  2.8 2.3 %collective-permute-start = (bf16[128,128]{1,0:T(8,128)(2,1)S(1)}, bf16[128,128]{1,0:T(8,128)(2,1)S(1)}, u32[]{:S(2)}, u32[]{:S(2)}) collective-permute-start(bf16[128,128]{1,0:T(8,128)(2,1)S(1)} %get-tuple-element.29), channel_id=1, source_target_pairs={{0,1},{1,0},{2,3},{3,2},{4,5},{5,4},{6,7},{7,6},{8,9},{9,8},{10,11... | collective-permute-start | bytes 98312 | tf_op jit(solution)/shard_map/ppermute | solution.py:238
  5.0 0.9 collective-permute-start.1
  5.9 0.7 collective-permute-start.2
  6.6 0.8 reshape.143
  8.6 0.8 dynamic_slice.15
  9.6 0.9 %collective-permute-done.1 = bf16[128,128]{1,0:T(8,128)(2,1)S(1)} collective-permute-done((bf16[128,128]{1,0:T(8,128)(2,1)S(1)}, bf16[128,128]{1,0:T(8,128)(2,1)S(1)}, u32[]{:S(2)}, u32[]{:S(2)}) %collective-permute-start.1) | collective-permute-done | bytes 32800 | tf_op jit(solution)/shard_map/ppermute | solution.py:238
  10.5 5.2 %collective-permute-start.6 = (bf16[512,128]{1,0:T(8,128)(2,1)S(1)}, bf16[512,128]{1,0:T(8,128)(2,1)S(1)}, u32[]{:S(2)}, u32[]{:S(2)}) collective-permute-start(bf16[512,128]{1,0:T(8,128)(2,1)S(1)} %constant_dynamic-update-slice_fusion.refs_0_.own), channel_id=1, source_target_pairs={{0,112},{1,113},{2,114},{3,115},{4,116},{5,117},{6,118},{7,119},{8... | collective-permute-start | bytes 393224 | tf_op jit(solution)/shard_map/ppermute | solution.py:238
  15.8 0.9 %copy-done = bf16[1,64,2048]{2,1,0:T(8,128)(2,1)S(1)} copy-done((bf16[1,64,2048]{2,1,0:T(8,128)(2,1)S(1)}, bf16[1,64,2048]{2,1,0:T(8,128)(2,1)}, u32[]{:S(2)}) %copy-start) | copy-done | bytes 262168
  18.3 3.2 %collective-permute-start.3 = (bf16[256,128]{1,0:T(8,128)(2,1)S(1)}, bf16[256,128]{1,0:T(8,128)(2,1)S(1)}, u32[]{:S(2)}, u32[]{:S(2)}) collective-permute-start(bf16[256,128]{1,0:T(8,128)(2,1)S(1)} %get-tuple-element.33), channel_id=1, source_target_pairs={{0,1},{1,0},{2,3},{3,2},{4,5},{5,4},{6,7},{7,6},{8,9},{9,8},{10,11... | collective-permute-start | bytes 196616 | tf_op jit(solution)/shard_map/ppermute | solution.py:238
  21.6 1.4 %collective-permute-start.5 = (bf16[256,128]{1,0:T(8,128)(2,1)S(1)}, bf16[256,128]{1,0:T(8,128)(2,1)S(1)}, u32[]{:S(2)}, u32[]{:S(2)}) collective-permute-start(bf16[256,128]{1,0:T(8,128)(2,1)S(1)} %get-tuple-element.35), channel_id=1, source_target_pairs={{0,3},{1,2},{2,1},{3,0},{4,7},{5,6},{6,5},{7,4},{8,11},{9,10},{10,... | collective-permute-start | bytes 196616 | tf_op jit(solution)/shard_map/ppermute | solution.py:238
  23.1 3.2 %collective-permute-start.7 = (bf16[512,128]{1,0:T(8,128)(2,1)S(1)}, bf16[512,128]{1,0:T(8,128)(2,1)S(1)}, u32[]{:S(2)}, u32[]{:S(2)}) collective-permute-start(bf16[512,128]{1,0:T(8,128)(2,1)S(1)} %collective-permute-done.6.refs_4_.l1), channel_id=1, source_target_pairs={{0,112},{1,113},{2,114},{3,115},{4,116},{5,117},{6,118},{7,119},{8... | collective-permute-start | bytes 393224 | tf_op jit(solution)/shard_map/ppermute | solution.py:238
  26.5 0.7 collective-permute-done.4
  27.3 1.5 %collective-permute-done.7.refs_5_.l2 = bf16[512,128]{1,0:T(8,128)(2,1)S(1)} collective-permute-done((bf16[512,128]{1,0:T(8,128)(2,1)S(1)}, bf16[512,128]{1,0:T(8,128)(2,1)S(1)}, u32[]{:S(2)}, u32[]{:S(2)}) %collective-permute-start.7) | collective-permute-done | bytes 131104 | tf_op jit(solution)/shard_map/ppermute | solution.py:238
  28.8 2.8 %collective-permute-start.10 = (bf16[1024,128]{1,0:T(8,128)(2,1)S(1)}, bf16[1024,128]{1,0:T(8,128)(2,1)S(1)}, u32[]{:S(2)}, u32[]{:S(2)}) collective-permute-start(bf16[1024,128]{1,0:T(8,128)(2,1)S(1)} %pad_maximum_fusion.1), channel_id=1, source_target_pairs={{0,12},{1,13},{2,14},{3,15},{4,8},{5,9},{6,10},{7,11},{8,4},{9,5},... | collective-permute-start | bytes 786440 | tf_op jit(solution)/shard_map/ppermute | solution.py:238
  31.8 1.7 %collective-permute-start.9 = (bf16[1024,128]{1,0:T(8,128)(2,1)S(1)}, bf16[1024,128]{1,0:T(8,128)(2,1)S(1)}, u32[]{:S(2)}, u32[]{:S(2)}) collective-permute-start(bf16[1024,128]{1,0:T(8,128)(2,1)S(1)} %pad_maximum_fusion.1), channel_id=1, source_target_pairs={{0,8},{1,9},{2,10},{3,11},{4,12},{5,13},{6,14},{7,15},{8,0},{9,1},... | collective-permute-start | bytes 786440 | tf_op jit(solution)/shard_map/ppermute | solution.py:238
  33.5 3.7 %collective-permute-start.14 = (bf16[512,128]{1,0:T(8,128)(2,1)S(1)}, bf16[512,128]{1,0:T(8,128)(2,1)S(1)}, u32[]{:S(2)}, u32[]{:S(2)}) collective-permute-start(bf16[512,128]{1,0:T(8,128)(2,1)S(1)} %collective-permute-done.7.refs_5_.l2), channel_id=1, source_target_pairs={{0,112},{1,113},{2,114},{3,115},{4,116},{5,117},{6,118},{7,119},{8... | collective-permute-start | bytes 393224 | tf_op jit(solution)/shard_map/ppermute | solution.py:238
  37.2 2.5 %collective-permute-done.14.refs_6_.l3 = bf16[512,128]{1,0:T(8,128)(2,1)S(1)} collective-permute-done((bf16[512,128]{1,0:T(8,128)(2,1)S(1)}, bf16[512,128]{1,0:T(8,128)(2,1)S(1)}, u32[]{:S(2)}, u32[]{:S(2)}) %collective-permute-start.14) | collective-permute-done | bytes 131104 | tf_op jit(solution)/shard_map/ppermute | solution.py:238
  39.7 3.7 %collective-permute-start.16 = (bf16[256,128]{1,0:T(8,128)(2,1)S(1)}, bf16[256,128]{1,0:T(8,128)(2,1)S(1)}, u32[]{:S(2)}, u32[]{:S(2)}) collective-permute-start(bf16[256,128]{1,0:T(8,128)(2,1)S(1)} %slice.33), channel_id=1, source_target_pairs={{0,112},{1,113},{2,114},{3,115},{4,116},{5,117},{6,118},{7,119},{8... | collective-permute-start | bytes 196616 | tf_op jit(solution)/shard_map/ppermute | solution.py:238
  43.8 1.5 %collective-permute-done.16.refs_8_.l4 = bf16[256,128]{1,0:T(8,128)(2,1)S(1)} collective-permute-done((bf16[256,128]{1,0:T(8,128)(2,1)S(1)}, bf16[256,128]{1,0:T(8,128)(2,1)S(1)}, u32[]{:S(2)}, u32[]{:S(2)}) %collective-permute-start.16) | collective-permute-done | bytes 65568 | tf_op jit(solution)/shard_map/ppermute | solution.py:238
  45.3 3.8 %collective-permute-done.15.refs_7_.r4 = bf16[256,128]{1,0:T(8,128)(2,1)S(1)} collective-permute-done((bf16[256,128]{1,0:T(8,128)(2,1)S(1)}, bf16[256,128]{1,0:T(8,128)(2,1)S(1)}, u32[]{:S(2)}, u32[]{:S(2)}) %collective-permute-start.15) | collective-permute-done | bytes 65568 | tf_op jit(solution)/shard_map/ppermute | solution.py:238
  49.2 0.7 pick.1
  49.9 1.3 %collective-permute-start.17 = (bf16[4,64,256]{2,1,0:T(8,128)(2,1)S(1)}, bf16[4,64,256]{2,1,0:T(8,128)(2,1)S(1)}, u32[]{:S(2)}, u32[]{:S(2)}) collective-permute-start(bf16[4,64,256]{2,1,0:T(8,128)(2,1)S(1)} %get-tuple-element.38), channel_id=1, source_target_pairs={{0,1},{4,5},{8,9},{12,13},{16,17},{20,21},{24,25},{28,29},{33,32},... | collective-permute-start | bytes 393224 | tf_op jit(solution)/shard_map/ppermute | solution.py:308
  51.2 0.7 collective-permute-start.18
  52.7 11.6 %attention.1 = bf16[16,272,128]{2,1,0:T(8,128)(2,1)} custom-call(s32[144]{0:T(256)S(1)} %concatenate.15.table, bf16[32,128,128]{2,1,0:T(8,128)(2,1)S(1)} %bitcast.24, s32[8,256]{1,0:T(8,128)S(1)} %broadcast_add_fusion.kpos_ref, bf16[512,128]{1,0:T(8,128)(2,1)S(1)} %constant_dynamic-update-slice_fusion.refs_0_.own, ...), custom_call_target="tpu_custom_call" | custom-call | flops 3000000000 | bytes 4000000 | tf_op jit(solution)/shard_map/attention/pallas_call | solution.py:309
  64.3 9.0 %all-to-all-start = ((bf16[16,272,128]{2,1,0:T(8,128)(2,1)}), bf16[16,272,128]{2,1,0:T(8,128)(2,1)S(1)}, u32[]{:S(2)}, u32[]{:S(2)}) async-start(bf16[16,272,128]{2,1,0:T(8,128)(2,1)} %attention.1), calls=%async_computation | async-start | bytes 2228224 | tf_op jit(solution)/shard_map/all_to_all | solution.py:244
  74.3 1.6 %collective-permute-start.20 = (bf16[64,256]{1,0:T(8,128)(2,1)S(1)}, bf16[64,256]{1,0:T(8,128)(2,1)S(1)}, u32[]{:S(2)}, u32[]{:S(2)}) collective-permute-start(bf16[64,256]{1,0:T(8,128)(2,1)S(1)} %get-tuple-element.55), channel_id=1, source_target_pairs={{0,4},{1,5},{2,6},{3,7},{4,0},{5,1},{6,2},{7,3},{8,12},{9,13},{10,... | collective-permute-start | bytes 98312 | tf_op jit(solution)/shard_map/ppermute | solution.py:238
  75.8 2.7 %collective-permute-start.21 = (bf16[64,256]{1,0:T(8,128)(2,1)S(1)}, bf16[64,256]{1,0:T(8,128)(2,1)S(1)}, u32[]{:S(2)}, u32[]{:S(2)}) collective-permute-start(bf16[64,256]{1,0:T(8,128)(2,1)S(1)} %get-tuple-element.54), channel_id=1, source_target_pairs={{0,8},{1,9},{2,10},{3,11},{4,12},{5,13},{6,14},{7,15},{8,0},{9,1},... | collective-permute-start | bytes 98312 | tf_op jit(solution)/shard_map/ppermute | solution.py:238
  79.1 3.8 %collective-permute-done.20 = bf16[64,256]{1,0:T(8,128)(2,1)S(1)} collective-permute-done((bf16[64,256]{1,0:T(8,128)(2,1)S(1)}, bf16[64,256]{1,0:T(8,128)(2,1)S(1)}, u32[]{:S(2)}, u32[]{:S(2)}) %collective-permute-start.20) | collective-permute-done | bytes 32800 | tf_op jit(solution)/shard_map/ppermute | solution.py:238
  82.9 1.9 %collective-permute-done.21 = bf16[64,256]{1,0:T(8,128)(2,1)S(1)} collective-permute-done((bf16[64,256]{1,0:T(8,128)(2,1)S(1)}, bf16[64,256]{1,0:T(8,128)(2,1)S(1)}, u32[]{:S(2)}, u32[]{:S(2)}) %collective-permute-start.21) | collective-permute-done | bytes 32800 | tf_op jit(solution)/shard_map/ppermute | solution.py:238
  85.1 0.8 copy.15
  85.9 2.1 %combine.1 = bf16[64,2048]{1,0:T(8,128)(2,1)} custom-call(s32[4]{0:T(128)S(1)} %copy-done.4, s32[2]{0:T(128)S(1)} %dynamic_slice.13.blocks, s32[1]{0:T(128)} %copy.19.length, bf16[16,272,128]{2,1,0:T(8,128)(2,1)S(1)} %all-to-all-done.m_ref), custom_call_target="tpu_custom_call" | custom-call | tf_op jit(solution)/shard_map/combine/pallas_call | solution.py:343
  (70 shorter events, 7.0 us)
Async XLA Ops:
  0.6 0.9 %copy-start.1 = (bf16[1,2,64,512]{3,2,1,0:T(8,128)(2,1)S(1)}, bf16[1,2,64,512]{3,2,1,0:T(8,128)(2,1)}, u32[]{:S(2)}) copy-start(bf16[1,2,64,512]{3,2,1,0:T(8,128)(2,1)} %param.6) | copy-start | bytes 393220
  1.5 0.7 copy-start.2
  2.8 6.8 %collective-permute-start = (bf16[128,128]{1,0:T(8,128)(2,1)S(1)}, bf16[128,128]{1,0:T(8,128)(2,1)S(1)}, u32[]{:S(2)}, u32[]{:S(2)}) collective-permute-start(bf16[128,128]{1,0:T(8,128)(2,1)S(1)} %get-tuple-element.29), channel_id=1, source_target_pairs={{0,1},{1,0},{2,3},{3,2},{4,5},{5,4},{6,7},{7,6},{8,9},{9,8},{10,11... | collective-permute-start | bytes 98312 | tf_op jit(solution)/shard_map/ppermute | solution.py:238
  5.0 5.4 %collective-permute-start.1 = (bf16[128,128]{1,0:T(8,128)(2,1)S(1)}, bf16[128,128]{1,0:T(8,128)(2,1)S(1)}, u32[]{:S(2)}, u32[]{:S(2)}) collective-permute-start(bf16[128,128]{1,0:T(8,128)(2,1)S(1)} %get-tuple-element.30), channel_id=1, source_target_pairs={{0,2},{1,3},{2,0},{3,1},{4,6},{5,7},{6,4},{7,5},{8,10},{9,11},{10,... | collective-permute-start | bytes 98312 | tf_op jit(solution)/shard_map/ppermute | solution.py:238
  5.9 4.6 %collective-permute-start.2 = (bf16[128,128]{1,0:T(8,128)(2,1)S(1)}, bf16[128,128]{1,0:T(8,128)(2,1)S(1)}, u32[]{:S(2)}, u32[]{:S(2)}) collective-permute-start(bf16[128,128]{1,0:T(8,128)(2,1)S(1)} %get-tuple-element.31), channel_id=1, source_target_pairs={{0,3},{1,2},{2,1},{3,0},{4,7},{5,6},{6,5},{7,4},{8,11},{9,10},{10,... | collective-permute-start | bytes 98312 | tf_op jit(solution)/shard_map/ppermute | solution.py:238
  10.5 12.6 %collective-permute-start.6 = (bf16[512,128]{1,0:T(8,128)(2,1)S(1)}, bf16[512,128]{1,0:T(8,128)(2,1)S(1)}, u32[]{:S(2)}, u32[]{:S(2)}) collective-permute-start(bf16[512,128]{1,0:T(8,128)(2,1)S(1)} %constant_dynamic-update-slice_fusion.refs_0_.own), channel_id=1, source_target_pairs={{0,112},{1,113},{2,114},{3,115},{4,116},{5,117},{6,118},{7,119},{8... | collective-permute-start | bytes 393224 | tf_op jit(solution)/shard_map/ppermute | solution.py:238
  15.7 10.6 %collective-permute-start.11 = (bf16[512,128]{1,0:T(8,128)(2,1)S(1)}, bf16[512,128]{1,0:T(8,128)(2,1)S(1)}, u32[]{:S(2)}, u32[]{:S(2)}) collective-permute-start(bf16[512,128]{1,0:T(8,128)(2,1)S(1)} %constant_dynamic-update-slice_fusion.refs_0_.own), channel_id=1, source_target_pairs={{0,16},{1,17},{2,18},{3,19},{4,20},{5,21},{6,22},{7,23},{8,24},{9,... | collective-permute-start | bytes 393224 | tf_op jit(solution)/shard_map/ppermute | solution.py:238
  15.8 1.0 %copy-start = (bf16[1,64,2048]{2,1,0:T(8,128)(2,1)S(1)}, bf16[1,64,2048]{2,1,0:T(8,128)(2,1)}, u32[]{:S(2)}) copy-start(bf16[1,64,2048]{2,1,0:T(8,128)(2,1)} %param.5) | copy-start | bytes 786436
  16.8 0.7 copy-start.3
  18.3 8.2 %collective-permute-start.3 = (bf16[256,128]{1,0:T(8,128)(2,1)S(1)}, bf16[256,128]{1,0:T(8,128)(2,1)S(1)}, u32[]{:S(2)}, u32[]{:S(2)}) collective-permute-start(bf16[256,128]{1,0:T(8,128)(2,1)S(1)} %get-tuple-element.33), channel_id=1, source_target_pairs={{0,1},{1,0},{2,3},{3,2},{4,5},{5,4},{6,7},{7,6},{8,9},{9,8},{10,11... | collective-permute-start | bytes 196616 | tf_op jit(solution)/shard_map/ppermute | solution.py:238
  21.5 5.8 %collective-permute-start.4 = (bf16[256,128]{1,0:T(8,128)(2,1)S(1)}, bf16[256,128]{1,0:T(8,128)(2,1)S(1)}, u32[]{:S(2)}, u32[]{:S(2)}) collective-permute-start(bf16[256,128]{1,0:T(8,128)(2,1)S(1)} %get-tuple-element.34), channel_id=1, source_target_pairs={{0,2},{1,3},{2,0},{3,1},{4,6},{5,7},{6,4},{7,5},{8,10},{9,11},{10,... | collective-permute-start | bytes 196616 | tf_op jit(solution)/shard_map/ppermute | solution.py:238
  21.6 5.7 %collective-permute-start.5 = (bf16[256,128]{1,0:T(8,128)(2,1)S(1)}, bf16[256,128]{1,0:T(8,128)(2,1)S(1)}, u32[]{:S(2)}, u32[]{:S(2)}) collective-permute-start(bf16[256,128]{1,0:T(8,128)(2,1)S(1)} %get-tuple-element.35), channel_id=1, source_target_pairs={{0,3},{1,2},{2,1},{3,0},{4,7},{5,6},{6,5},{7,4},{8,11},{9,10},{10,... | collective-permute-start | bytes 196616 | tf_op jit(solution)/shard_map/ppermute | solution.py:238
  23.1 5.8 %collective-permute-start.7 = (bf16[512,128]{1,0:T(8,128)(2,1)S(1)}, bf16[512,128]{1,0:T(8,128)(2,1)S(1)}, u32[]{:S(2)}, u32[]{:S(2)}) collective-permute-start(bf16[512,128]{1,0:T(8,128)(2,1)S(1)} %collective-permute-done.6.refs_4_.l1), channel_id=1, source_target_pairs={{0,112},{1,113},{2,114},{3,115},{4,116},{5,117},{6,118},{7,119},{8... | collective-permute-start | bytes 393224 | tf_op jit(solution)/shard_map/ppermute | solution.py:238
  26.3 10.9 %collective-permute-start.12 = (bf16[512,128]{1,0:T(8,128)(2,1)S(1)}, bf16[512,128]{1,0:T(8,128)(2,1)S(1)}, u32[]{:S(2)}, u32[]{:S(2)}) collective-permute-start(bf16[512,128]{1,0:T(8,128)(2,1)S(1)} %collective-permute-done.11.refs_1_.r1), channel_id=1, source_target_pairs={{0,16},{1,17},{2,18},{3,19},{4,20},{5,21},{6,22},{7,23},{8,24},{9,... | collective-permute-start | bytes 393224 | tf_op jit(solution)/shard_map/ppermute | solution.py:238
  28.8 23.1 %collective-permute-start.10 = (bf16[1024,128]{1,0:T(8,128)(2,1)S(1)}, bf16[1024,128]{1,0:T(8,128)(2,1)S(1)}, u32[]{:S(2)}, u32[]{:S(2)}) collective-permute-start(bf16[1024,128]{1,0:T(8,128)(2,1)S(1)} %pad_maximum_fusion.1), channel_id=1, source_target_pairs={{0,12},{1,13},{2,14},{3,15},{4,8},{5,9},{6,10},{7,11},{8,4},{9,5},... | collective-permute-start | bytes 786440 | tf_op jit(solution)/shard_map/ppermute | solution.py:238
  31.6 21.0 %collective-permute-start.8 = (bf16[1024,128]{1,0:T(8,128)(2,1)S(1)}, bf16[1024,128]{1,0:T(8,128)(2,1)S(1)}, u32[]{:S(2)}, u32[]{:S(2)}) collective-permute-start(bf16[1024,128]{1,0:T(8,128)(2,1)S(1)} %pad_maximum_fusion.1), channel_id=1, source_target_pairs={{0,4},{1,5},{2,6},{3,7},{4,0},{5,1},{6,2},{7,3},{8,12},{9,13},{10,... | collective-permute-start | bytes 786440 | tf_op jit(solution)/shard_map/ppermute | solution.py:238
  31.8 20.8 %collective-permute-start.9 = (bf16[1024,128]{1,0:T(8,128)(2,1)S(1)}, bf16[1024,128]{1,0:T(8,128)(2,1)S(1)}, u32[]{:S(2)}, u32[]{:S(2)}) collective-permute-start(bf16[1024,128]{1,0:T(8,128)(2,1)S(1)} %pad_maximum_fusion.1), channel_id=1, source_target_pairs={{0,8},{1,9},{2,10},{3,11},{4,12},{5,13},{6,14},{7,15},{8,0},{9,1},... | collective-permute-start | bytes 786440 | tf_op jit(solution)/shard_map/ppermute | solution.py:238
  33.5 6.2 %collective-permute-start.14 = (bf16[512,128]{1,0:T(8,128)(2,1)S(1)}, bf16[512,128]{1,0:T(8,128)(2,1)S(1)}, u32[]{:S(2)}, u32[]{:S(2)}) collective-permute-start(bf16[512,128]{1,0:T(8,128)(2,1)S(1)} %collective-permute-done.7.refs_5_.l2), channel_id=1, source_target_pairs={{0,112},{1,113},{2,114},{3,115},{4,116},{5,117},{6,118},{7,119},{8... | collective-permute-start | bytes 393224 | tf_op jit(solution)/shard_map/ppermute | solution.py:238
  37.2 6.3 %collective-permute-start.13 = (bf16[512,128]{1,0:T(8,128)(2,1)S(1)}, bf16[512,128]{1,0:T(8,128)(2,1)S(1)}, u32[]{:S(2)}, u32[]{:S(2)}) collective-permute-start(bf16[512,128]{1,0:T(8,128)(2,1)S(1)} %collective-permute-done.12.refs_2_.r2), channel_id=1, source_target_pairs={{0,16},{1,17},{2,18},{3,19},{4,20},{5,21},{6,22},{7,23},{8,24},{9,... | collective-permute-start | bytes 393224 | tf_op jit(solution)/shard_map/ppermute | solution.py:238
  39.7 5.6 %collective-permute-start.16 = (bf16[256,128]{1,0:T(8,128)(2,1)S(1)}, bf16[256,128]{1,0:T(8,128)(2,1)S(1)}, u32[]{:S(2)}, u32[]{:S(2)}) collective-permute-start(bf16[256,128]{1,0:T(8,128)(2,1)S(1)} %slice.33), channel_id=1, source_target_pairs={{0,112},{1,113},{2,114},{3,115},{4,116},{5,117},{6,118},{7,119},{8... | collective-permute-start | bytes 196616 | tf_op jit(solution)/shard_map/ppermute | solution.py:238
  43.4 5.7 %collective-permute-start.15 = (bf16[256,128]{1,0:T(8,128)(2,1)S(1)}, bf16[256,128]{1,0:T(8,128)(2,1)S(1)}, u32[]{:S(2)}, u32[]{:S(2)}) collective-permute-start(bf16[256,128]{1,0:T(8,128)(2,1)S(1)} %slice.32), channel_id=1, source_target_pairs={{0,16},{1,17},{2,18},{3,19},{4,20},{5,21},{6,22},{7,23},{8,24},{9,... | collective-permute-start | bytes 196616 | tf_op jit(solution)/shard_map/ppermute | solution.py:238
  49.9 14.4 %collective-permute-start.17 = (bf16[4,64,256]{2,1,0:T(8,128)(2,1)S(1)}, bf16[4,64,256]{2,1,0:T(8,128)(2,1)S(1)}, u32[]{:S(2)}, u32[]{:S(2)}) collective-permute-start(bf16[4,64,256]{2,1,0:T(8,128)(2,1)S(1)} %get-tuple-element.38), channel_id=1, source_target_pairs={{0,1},{4,5},{8,9},{12,13},{16,17},{20,21},{24,25},{28,29},{33,32},... | collective-permute-start | bytes 393224 | tf_op jit(solution)/shard_map/ppermute | solution.py:308
  51.2 13.1 %collective-permute-start.18 = (bf16[4,64,256]{2,1,0:T(8,128)(2,1)S(1)}, bf16[4,64,256]{2,1,0:T(8,128)(2,1)S(1)}, u32[]{:S(2)}, u32[]{:S(2)}) collective-permute-start(bf16[4,64,256]{2,1,0:T(8,128)(2,1)S(1)} %get-tuple-element.39), channel_id=1, source_target_pairs={{0,2},{4,6},{8,10},{12,14},{16,18},{20,22},{24,26},{28,30},{33,35}... | collective-permute-start | bytes 393224 | tf_op jit(solution)/shard_map/ppermute | solution.py:308
  51.9 12.4 %collective-permute-start.19 = (bf16[4,64,256]{2,1,0:T(8,128)(2,1)S(1)}, bf16[4,64,256]{2,1,0:T(8,128)(2,1)S(1)}, u32[]{:S(2)}, u32[]{:S(2)}) collective-permute-start(bf16[4,64,256]{2,1,0:T(8,128)(2,1)S(1)} %get-tuple-element.40), channel_id=1, source_target_pairs={{0,3},{4,7},{8,11},{12,15},{16,19},{20,23},{24,27},{28,31},{33,34}... | collective-permute-start | bytes 393224 | tf_op jit(solution)/shard_map/ppermute | solution.py:308
  64.3 9.0 %copy-start.5 = (s32[256]{0:T(256)S(1)}, s32[256]{0:T(256)}, u32[]{:S(2)}) copy-start(s32[256]{0:T(256)} %param.8) | copy-start | bytes 3076
  64.3 21.6 %all-to-all-start = ((bf16[16,272,128]{2,1,0:T(8,128)(2,1)}), bf16[16,272,128]{2,1,0:T(8,128)(2,1)S(1)}, u32[]{:S(2)}, u32[]{:S(2)}) async-start(bf16[16,272,128]{2,1,0:T(8,128)(2,1)} %attention.1), calls=%async_computation | async-start | bytes 2228224 | tf_op jit(solution)/shard_map/all_to_all | solution.py:244
  73.3 12.6 %copy-start.4 = (s32[4]{0:T(128)S(1)}, s32[4]{0:T(128)}, u32[]{:S(2)}) copy-start(s32[4]{0:T(128)} %heads.5) | copy-start | bytes 52
  74.3 8.7 %collective-permute-start.20 = (bf16[64,256]{1,0:T(8,128)(2,1)S(1)}, bf16[64,256]{1,0:T(8,128)(2,1)S(1)}, u32[]{:S(2)}, u32[]{:S(2)}) collective-permute-start(bf16[64,256]{1,0:T(8,128)(2,1)S(1)} %get-tuple-element.55), channel_id=1, source_target_pairs={{0,4},{1,5},{2,6},{3,7},{4,0},{5,1},{6,2},{7,3},{8,12},{9,13},{10,... | collective-permute-start | bytes 98312 | tf_op jit(solution)/shard_map/ppermute | solution.py:238
  75.8 9.0 %collective-permute-start.21 = (bf16[64,256]{1,0:T(8,128)(2,1)S(1)}, bf16[64,256]{1,0:T(8,128)(2,1)S(1)}, u32[]{:S(2)}, u32[]{:S(2)}) collective-permute-start(bf16[64,256]{1,0:T(8,128)(2,1)S(1)} %get-tuple-element.54), channel_id=1, source_target_pairs={{0,8},{1,9},{2,10},{3,11},{4,12},{5,13},{6,14},{7,15},{8,0},{9,1},... | collective-permute-start | bytes 98312 | tf_op jit(solution)/shard_map/ppermute | solution.py:238
  78.6 6.3 %collective-permute-start.22 = (bf16[64,256]{1,0:T(8,128)(2,1)S(1)}, bf16[64,256]{1,0:T(8,128)(2,1)S(1)}, u32[]{:S(2)}, u32[]{:S(2)}) collective-permute-start(bf16[64,256]{1,0:T(8,128)(2,1)S(1)} %get-tuple-element.53), channel_id=1, source_target_pairs={{0,12},{1,13},{2,14},{3,15},{4,8},{5,9},{6,10},{7,11},{8,4},{9,5},... | collective-permute-start | bytes 98312 | tf_op jit(solution)/shard_map/ppermute | solution.py:238

commit v9 on v3

--- a/solution.py
+++ b/solution.py
@@ -24,7 +24,8 @@
 JOINED = 4
 CHUNK_BLOCKS = 8
 CHUNK = CHUNK_BLOCKS * BLOCK
-MESSAGE = 2 * ROWS + 16
+PARTIAL = 2 * ROWS + 16
+MESSAGE = PARTIAL + 2 * KEY_BLOCKS
 SCALE = HEAD**-0.5 * 1.4426950408889634
 NEG = -1e30
 AT_ORDER = KEY_BLOCKS
@@ -34,7 +35,8 @@
 
 SMEM = pl.BlockSpec(memory_space=pltpu.SMEM)
 VMEM = pl.BlockSpec(memory_space=pltpu.VMEM)
-PARAMS = pltpu.CompilerParams(vmem_limit_bytes=40 * 1024 * 1024)
+PARAMS = pltpu.CompilerParams(vmem_limit_bytes=24 * 1024 * 1024)
+SMALL = pltpu.CompilerParams(vmem_limit_bytes=8 * 1024 * 1024)
 
 
 def split_kv_kernel(heads, kv_ref, *o_refs):
@@ -53,7 +55,7 @@
                     o_ref[x * NY + y, j * ROWS + g * BLOCK : j * ROWS + (g + 1) * BLOCK] = tile
 
 
-def arrange(table, pieces, k_scr, kt_scr, v_scr, pick_ref):
+def arrange(table, pieces, k_scr, kt_scr, v_scr):
     place = lax.axis_index("blk")
     z, y = place // PLANE, lax.rem(place, NY)
     v_scr[:, HEAD:] = jnp.ones((KEYS, HEAD), jnp.bfloat16)
@@ -66,23 +68,34 @@
                 v_scr[pl.ds(row, BLOCK), :HEAD] = piece[at * 128 + 64 + j * BLOCK : at * 128 + 64 + (j + 1) * BLOCK, :]
     for t in range(KEYS // 128):
         kt_scr[:, t * 128 : (t + 1) * 128] = k_scr[t * 128 : (t + 1) * 128, :].T
+
+
+def pick(k_scr, v_scr, o_ref):
+    place = lax.axis_index("blk")
+    z, y = place // PLANE, lax.rem(place, NY)
     some = 16
-    offset = lax.rem(z, 2) * 16 + z // 2
-    line = lax.broadcasted_iota(jnp.int32, (NX * some, some * BLOCK), 0)
-    column = lax.broadcasted_iota(jnp.int32, (NX * some, some * BLOCK), 1)
-    wanted = (line % some) * BLOCK + offset + (line // some) * NY
-    select = jnp.where(column == wanted, 1.0, 0.0).astype(jnp.bfloat16)
-    for c in range(KEY_BLOCKS // some):
-        rows = slice(c * some * BLOCK, (c + 1) * some * BLOCK)
-        k = jnp.dot(select, k_scr[rows, :], preferred_element_type=jnp.float32).astype(jnp.bfloat16)
-        v = jnp.dot(select, v_scr[rows, :HEAD], preferred_element_type=jnp.float32).astype(jnp.bfloat16)
-        for x in range(NX):
-            pick_ref[x, c * some : (c + 1) * some, :HEAD] = k[x * some : (x + 1) * some]
-            pick_ref[x, c * some : (c + 1) * some, HEAD:] = v[x * some : (x + 1) * some]
+
+    @pl.when(y == z // 2)
+    def _():
+        line = lax.broadcasted_iota(jnp.int32, (PLANE * some, some * BLOCK), 0)
+        column = lax.broadcasted_iota(jnp.int32, (PLANE * some, some * BLOCK), 1)
+        wanted = (line % some) * BLOCK + lax.rem(z, 2) * PLANE + line // some
+        select = jnp.where(column == wanted, 1.0, 0.0).astype(jnp.bfloat16)
+        for c in range(KEY_BLOCKS // some):
+            rows = slice(c * some * BLOCK, (c + 1) * some * BLOCK)
+            for at, scr in ((PARTIAL, k_scr), (PARTIAL + KEY_BLOCKS, v_scr)):
+                values = jnp.dot(select, scr[rows, :HEAD], preferred_element_type=jnp.float32).astype(jnp.bfloat16)
+                for d in range(PLANE):
+                    o_ref[d, at + c * some : at + (c + 1) * some, :] = values[d * some : (d + 1) * some]
+
+    @pl.when(y != z // 2)
+    def _():
+        for d in range(PLANE):
+            o_ref[d, PARTIAL:, :] = jnp.zeros((2 * KEY_BLOCKS, HEAD), jnp.bfloat16)
 
 
 def attention_kernel(table, q_ref, kpos_ref, *refs):
-    pieces, (o_ref, pick_ref, k_scr, kt_scr, v_scr, s_scr, stat) = refs[:9], refs[9:]
+    pieces, (o_ref, k_scr, kt_scr, v_scr, s_scr, stat) = refs[:9], refs[9:]
     own, r1, r2, r3, l1, l2, l3, r4, l4 = pieces
     every, first, last = range(NY), range(NY // 2), range(NY // 2, NY)
     arrange(
@@ -92,8 +105,8 @@
         k_scr,
         kt_scr,
         v_scr,
-        pick_ref,
     )
+    pick(k_scr, v_scr, o_ref)
     lane = lax.broadcasted_iota(jnp.int32, (ROWS, 128), 1)
     token = lax.broadcasted_iota(jnp.int32, (BLOCK, CHUNK), 0)
 
@@ -158,13 +171,19 @@
         second = (value - first).astype(jnp.bfloat16).astype(jnp.float32)
         third = value - first - second
         rows = jnp.concatenate([first, second, third, jnp.zeros_like(first)], axis=0)
-        o_ref[d, 2 * ROWS :, :] = rows.astype(jnp.bfloat16)
-
-
-def combine_kernel(heads, blocks, length, m_ref, o_ref):
+        o_ref[d, 2 * ROWS : PARTIAL, :] = rows.astype(jnp.bfloat16)
+
+
+def combine_kernel(heads, blocks, length, choose_ref, m_ref, o_ref, cache_ref):
+    keeper = lax.axis_index("blk") // (2 * PLANE)
+    for half in range(2):
+        rows = slice(PARTIAL + half * KEY_BLOCKS, PARTIAL + (half + 1) * KEY_BLOCKS)
+        found = jnp.concatenate([m_ref[x * NY + keeper, rows, :] for x in range(NX)], axis=0)
+        cache = jnp.dot(choose_ref[...], found, preferred_element_type=jnp.float32)
+        cache_ref[half] = cache.astype(jnp.bfloat16)
     values = []
     for d in range(PLANE):
-        rows = m_ref[d, 2 * ROWS :, :].astype(jnp.float32)
+        rows = m_ref[d, 2 * ROWS : PARTIAL, :].astype(jnp.float32)
         values.append(rows[0:4] + rows[4:8] + rows[8:12])
     weights = [None] * PLANE
     for y in range(NY):
@@ -221,6 +240,7 @@
         out_shape=(jax.ShapeDtypeStruct((128, HEAD), jnp.bfloat16),) * NY,
         in_specs=[SMEM, VMEM],
         out_specs=(VMEM,) * NY,
+        compiler_params=SMALL,
         name="split_kv",
     )(segment_head, rotated_key_value.reshape(128, KEY_VALUE_HEADS * HEAD))
     line = [kv[0]] + [move(kv[k], lambda a, b, c, k=k: index(a, b, c ^ k)) for k in range(1, NY)]
@@ -233,13 +253,15 @@
         out_shape=jax.ShapeDtypeStruct((PLANE, 2 * ROWS, HEAD), jnp.bfloat16),
         in_specs=[SMEM, VMEM],
         out_specs=VMEM,
+        compiler_params=SMALL,
         name="split_q",
     )(segment_head, query.reshape(2 * BLOCK, QUERY_HEADS * HEAD))
     q = exchange(q, planes).reshape(Q_BLOCKS, ROWS, HEAD)
     r2, l2 = right(r1), left(l1)
     r3, l3 = right(r2), left(l2)
     half = own.shape[0] // 2
-    r4, l4 = right(r3[:half]), left(l3[half:])
+    r4 = move(r2[:half], lambda a, b, c: index(a + 2, b, c))
+    l4 = move(l2[half:], lambda a, b, c: index(a - 2, b, c))
 
     ids = block_map.reshape(NZ, NX, NY, 2).transpose(1, 0, 2, 3).reshape(NX, KEY_BLOCKS)
     rank = ranks(ids)
@@ -258,14 +280,12 @@
     kpos = mine[:, None] * BLOCK + jnp.arange(BLOCK, dtype=jnp.int32)[None, :]
     kpos = kpos.reshape(KEYS // CHUNK, CHUNK)
 
-    out, pick = pl.pallas_call(
+    pieces = (own, r1, r2, r3, l1, l2, l3, r4, l4)
+    partial = pl.pallas_call(
         attention_kernel,
-        out_shape=(
-            jax.ShapeDtypeStruct((PLANE, MESSAGE, HEAD), jnp.bfloat16),
-            jax.ShapeDtypeStruct((NX, KEY_BLOCKS, 2 * HEAD), jnp.bfloat16),
-        ),
+        out_shape=jax.ShapeDtypeStruct((PLANE, MESSAGE, HEAD), jnp.bfloat16),
         in_specs=[SMEM] + [VMEM] * 11,
-        out_specs=(VMEM, VMEM),
+        out_specs=VMEM,
         scratch_shapes=[
             pltpu.VMEM((KEYS, HEAD), jnp.bfloat16),
             pltpu.VMEM((HEAD, KEYS), jnp.bfloat16),
@@ -276,27 +296,26 @@
         compiler_params=PARAMS,
         cost_estimate=pl.CostEstimate(flops=3_000_000_000, bytes_accessed=4_000_000, transcendentals=5_000_000),
         name="attention",
-    )(table, q, kpos, own, r1, r2, r3, l1, l2, l3, r4, l4)
-    out = exchange(out, planes)
-    offset = (z % 2) * 16 + z // 2
-
-    pick = exchange(pick, x_groups).reshape(BLOCKS, 2 * HEAD)
+    )(table, q, kpos, *pieces)
+    out = exchange(partial, planes)
+
     blocks = jnp.arange(BLOCKS, dtype=jnp.int32)
-    position = blocks * BLOCK + offset + 4 * x
+    position = blocks * BLOCK + place % BLOCK
     choose = (ordered.reshape(1, BLOCKS) == blocks[:, None]) & (position < lengths[0])[:, None]
-    cache = jnp.dot(choose.astype(jnp.bfloat16), pick, preferred_element_type=jnp.float32).astype(jnp.bfloat16)
-    cache = move(cache, lambda a, b, c: index(2 * c + a % 2, b, a // 2))
-    cache = cache.reshape(BLOCKS, 2, HEAD).transpose(1, 0, 2)[None, :, None]
-
+    choose = choose.astype(jnp.bfloat16)
     my_blocks = lax.dynamic_slice_in_dim(block_map, 2 * place, 2)
-    attended = pl.pallas_call(
+    attended, cache = pl.pallas_call(
         combine_kernel,
-        out_shape=jax.ShapeDtypeStruct((2 * BLOCK, QUERY_HEADS * HEAD), jnp.bfloat16),
-        in_specs=[SMEM] * 3 + [VMEM],
-        out_specs=VMEM,
+        out_shape=(
+            jax.ShapeDtypeStruct((2 * BLOCK, QUERY_HEADS * HEAD), jnp.bfloat16),
+            jax.ShapeDtypeStruct((2, BLOCKS, HEAD), jnp.bfloat16),
+        ),
+        in_specs=[SMEM] * 3 + [VMEM] * 2,
+        out_specs=(VMEM, VMEM),
+        compiler_params=SMALL,
         name="combine",
-    )(segment_head, my_blocks, lengths, out)
-    return attended.reshape(1, 2 * BLOCK, QUERY_HEADS * HEAD), cache
+    )(segment_head, my_blocks, lengths, choose, out)
+    return attended.reshape(1, 2 * BLOCK, QUERY_HEADS * HEAD), cache[None, :, None]
 
 
 def solution(mesh):

time: 95 us -> 87.8 us (0.924)
  the two profiles are of different devices: /device:TPU:16 before, /device:TPU:8 now
where the time goes in v9:
time: 87.8 us; the launch traced here: 87.3 us
  starting transfers between devices  34.9 us (40%)
  waiting for transfers between devices  28.8 us (33%)
  Pallas kernels  17 us (19%)
  local copies, waits for them, and re-layouts  3.81 us (4%)
  between operations  1.46 us (2%)
  other arithmetic  1.23 us (1%)
    ppermute x11, starting transfers between devices, move(): lax.ppermute(value, 'blk', [(s, target(s // 16, s // 4 % 4, s % 4)) for s...  19.7 us
    all_to_all x2, waiting for transfers between devices, exchange(): lax.all_to_all(value, 'blk', 0, 0, axis_index_groups=groups, tiled=True)  17 us
    all_to_all x2, starting transfers between devices, exchange(): lax.all_to_all(value, 'blk', 0, 0, axis_index_groups=groups, tiled=True)  15.3 us
    pallas_call x1, Pallas kernels, body(): pl.pallas_call(attention_kernel, out_shape=jax.ShapeDtypeStruct((PLANE, M...  12.7 us
    ppermute x11, waiting for transfers between devices, move(): lax.ppermute(value, 'blk', [(s, target(s // 16, s // 4 % 4, s % 4)) for s...  11.9 us
    unnamed x13, local copies, waits for them, and re-layouts  2.54 us
    pallas_call x1, Pallas kernels, body(): pl.pallas_call(combine_kernel, out_shape=(jax.ShapeDtypeStruct((2 * BLOCK...  2.1 us
  transfers between devices with their start and end apart: 13, of which 5 were waited for; matrix products, arithmetic and copies ran while one was open for 3% of the time, Pallas kernels for 2%

profile of v9, /device:TPU:8, one launch (start us, length us, event | category | flops | bytes accessed | tf_op | source)
XLA Modules:
  0.0 87.3 jit_solution(1583618154244073892)
XLA Ops:
  0.6 0.9 %copy-done.1 = bf16[1,2,64,512]{3,2,1,0:T(8,128)(2,1)S(1)} copy-done((bf16[1,2,64,512]{3,2,1,0:T(8,128)(2,1)S(1)}, bf16[1,2,64,512]{3,2,1,0:T(8,128)(2,1)}, u32[]{:S(2)}) %copy-start.1) | copy-done | bytes 131096
  1.5 0.7 copy-done.2
  2.2 0.6 split_kv.1
  2.8 2.3 %collective-permute-start = (bf16[128,128]{1,0:T(8,128)(2,1)S(1)}, bf16[128,128]{1,0:T(8,128)(2,1)S(1)}, u32[]{:S(2)}, u32[]{:S(2)}) collective-permute-start(bf16[128,128]{1,0:T(8,128)(2,1)S(1)} %get-tuple-element.9), channel_id=1, source_target_pairs={{0,1},{1,0},{2,3},{3,2},{4,5},{5,4},{6,7},{7,6},{8,9},{9,8},{10,11... | collective-permute-start | bytes 98312 | tf_op jit(solution)/shard_map/ppermute | solution.py:230
  5.0 0.9 collective-permute-start.1
  5.9 0.7 collective-permute-start.2
  6.6 0.9 %copy-done = bf16[1,64,2048]{2,1,0:T(8,128)(2,1)S(1)} copy-done((bf16[1,64,2048]{2,1,0:T(8,128)(2,1)S(1)}, bf16[1,64,2048]{2,1,0:T(8,128)(2,1)}, u32[]{:S(2)}) %copy-start) | copy-done | bytes 262168
  7.6 1.7 %split_q.1 = bf16[16,256,128]{2,1,0:T(8,128)(2,1)} custom-call(s32[4]{0:T(128)S(1)} %copy-done.2, bf16[64,2048]{1,0:T(8,128)(2,1)S(1)} %bitcast.16), custom_call_target="tpu_custom_call" | custom-call | tf_op jit(solution)/shard_map/split_q/pallas_call | solution.py:251
  9.2 8.2 %all-to-all-start = ((bf16[16,256,128]{2,1,0:T(8,128)(2,1)}), bf16[16,256,128]{2,1,0:T(8,128)(2,1)S(1)}, u32[]{:S(2)}, u32[]{:S(2)}) async-start(bf16[16,256,128]{2,1,0:T(8,128)(2,1)} %split_q.1), calls=%async_computation | async-start | bytes 2097152 | tf_op jit(solution)/shard_map/all_to_all | solution.py:236
  17.4 0.2 reshape.51
  17.6 0.3 copy.12
  18.0 0.2 convert_reduce_fusion
  18.2 0.2 select_reduce_fusion
  18.4 0.2 convert_reduce_fusion.1
  18.6 0.1 select_reduce_fusion.1
  19.3 5.9 %collective-permute-start.6 = (bf16[512,128]{1,0:T(8,128)(2,1)S(1)}, bf16[512,128]{1,0:T(8,128)(2,1)S(1)}, u32[]{:S(2)}, u32[]{:S(2)}) collective-permute-start(bf16[512,128]{1,0:T(8,128)(2,1)S(1)} %constant_dynamic-update-slice_fusion.refs_0_), channel_id=1, source_target_pairs={{0,112},{1,113},{2,114},{3,115},{4,116},{5,117},{6,118},{7,119},{8... | collective-permute-start | bytes 393224 | tf_op jit(solution)/shard_map/ppermute | solution.py:230
  25.2 2.5 %collective-permute-done.6.refs_4_ = bf16[512,128]{1,0:T(8,128)(2,1)S(1)} collective-permute-done((bf16[512,128]{1,0:T(8,128)(2,1)S(1)}, bf16[512,128]{1,0:T(8,128)(2,1)S(1)}, u32[]{:S(2)}, u32[]{:S(2)}) %collective-permute-start.6) | collective-permute-done | bytes 131104 | tf_op jit(solution)/shard_map/ppermute | solution.py:230
  27.7 3.7 %collective-permute-start.7 = (bf16[512,128]{1,0:T(8,128)(2,1)S(1)}, bf16[512,128]{1,0:T(8,128)(2,1)S(1)}, u32[]{:S(2)}, u32[]{:S(2)}) collective-permute-start(bf16[512,128]{1,0:T(8,128)(2,1)S(1)} %collective-permute-done.6.refs_4_), channel_id=1, source_target_pairs={{0,112},{1,113},{2,114},{3,115},{4,116},{5,117},{6,118},{7,119},{8... | collective-permute-start | bytes 393224 | tf_op jit(solution)/shard_map/ppermute | solution.py:230
  31.4 0.2 slice_reduce_fusion
  31.6 0.2 convert_reduce_fusion.2
  31.8 5.8 %collective-permute-done.4.refs_2_ = bf16[512,128]{1,0:T(8,128)(2,1)S(1)} collective-permute-done((bf16[512,128]{1,0:T(8,128)(2,1)S(1)}, bf16[512,128]{1,0:T(8,128)(2,1)S(1)}, u32[]{:S(2)}, u32[]{:S(2)}) %collective-permute-start.4) | collective-permute-done | bytes 131104 | tf_op jit(solution)/shard_map/ppermute | solution.py:230
  37.6 3.2 %collective-permute-start.8 = (bf16[512,128]{1,0:T(8,128)(2,1)S(1)}, bf16[512,128]{1,0:T(8,128)(2,1)S(1)}, u32[]{:S(2)}, u32[]{:S(2)}) collective-permute-start(bf16[512,128]{1,0:T(8,128)(2,1)S(1)} %collective-permute-done.7.refs_5_), channel_id=1, source_target_pairs={{0,112},{1,113},{2,114},{3,115},{4,116},{5,117},{6,118},{7,119},{8... | collective-permute-start | bytes 393224 | tf_op jit(solution)/shard_map/ppermute | solution.py:230
  40.8 0.1 collective-permute-start.10
  40.9 2.9 %collective-permute-start.9 = (bf16[256,128]{1,0:T(8,128)(2,1)S(1)}, bf16[256,128]{1,0:T(8,128)(2,1)S(1)}, u32[]{:S(2)}, u32[]{:S(2)}) collective-permute-start(bf16[256,128]{1,0:T(8,128)(2,1)S(1)} %slice.16), channel_id=1, source_target_pairs={{0,32},{1,33},{2,34},{3,35},{4,36},{5,37},{6,38},{7,39},{8,40},{9,... | collective-permute-start | bytes 196616 | tf_op jit(solution)/shard_map/ppermute | solution.py:230
  43.9 2.1 %collective-permute-done.10.refs_8_ = bf16[256,128]{1,0:T(8,128)(2,1)S(1)} collective-permute-done((bf16[256,128]{1,0:T(8,128)(2,1)S(1)}, bf16[256,128]{1,0:T(8,128)(2,1)S(1)}, u32[]{:S(2)}, u32[]{:S(2)}) %collective-permute-start.10) | collective-permute-done | bytes 65568 | tf_op jit(solution)/shard_map/ppermute | solution.py:230
  46.1 1.4 %collective-permute-done.9.refs_7_ = bf16[256,128]{1,0:T(8,128)(2,1)S(1)} collective-permute-done((bf16[256,128]{1,0:T(8,128)(2,1)S(1)}, bf16[256,128]{1,0:T(8,128)(2,1)S(1)}, u32[]{:S(2)}, u32[]{:S(2)}) %collective-permute-start.9) | collective-permute-done | bytes 65568 | tf_op jit(solution)/shard_map/ppermute | solution.py:230
  47.5 12.7 %attention.1 = bf16[16,400,128]{2,1,0:T(8,128)(2,1)} custom-call(s32[144]{0:T(256)S(1)} %concatenate.6.table, bf16[32,128,128]{2,1,0:T(8,128)(2,1)S(1)} %bitcast.15, s32[8,256]{1,0:T(8,128)S(1)} %broadcast_add_fusion.kpos_ref, bf16[512,128]{1,0:T(8,128)(2,1)S(1)} %constant_dynamic-update-slice_fusion.refs_0_, ...), custom_call_target="tpu_custom_call" | custom-call | flops 3000000000 | bytes 4000000 | tf_op jit(solution)/shard_map/attention/pallas_call | solution.py:284
  60.2 7.1 %all-to-all-start.1 = ((bf16[16,400,128]{2,1,0:T(8,128)(2,1)}), bf16[16,400,128]{2,1,0:T(8,128)(2,1)S(1)}, u32[]{:S(2)}, u32[]{:S(2)}) async-start(bf16[16,400,128]{2,1,0:T(8,128)(2,1)} %attention.1), calls=%async_computation.1 | async-start | bytes 3276800 | tf_op jit(solution)/shard_map/all_to_all | solution.py:236
  67.3 0.1 eq.26
  68.1 0.1 fusion.1.choose_ref
  68.2 17.0 %all-to-all-done.1.m_ref = bf16[16,400,128]{2,1,0:T(8,128)(2,1)S(1)} async-done(((bf16[16,400,128]{2,1,0:T(8,128)(2,1)}), bf16[16,400,128]{2,1,0:T(8,128)(2,1)S(1)}, u32[]{:S(2)}, u32[]{:S(2)}) %all-to-all-start.1) | async-done | bytes 1638432 | tf_op jit(solution)/shard_map/all_to_all | solution.py:236
  85.2 2.1 %combine.1 = (bf16[64,2048]{1,0:T(8,128)(2,1)}, bf16[2,256,128]{2,1,0:T(8,128)(2,1)}) custom-call(s32[4]{0:T(128)S(1)} %copy-done.3, s32[2]{0:T(128)S(1)} %dynamic_slice.13.blocks, s32[1]{0:T(128)} %copy.19.length, bf16[256,256]{1,0:T(8,128)(2,1)S(1)} %fusion.1.choose_ref, bf16[16,400,128]{2,1,0:T(8,128)(2,1)S(1)} %all-to-all-done.1.m_ref), custom_call_target="tpu_custom_call" | custom-call | tf_op jit(solution)/shard_map/combine/pallas_call | solution.py:307
  (39 shorter events, 0.8 us)
Async XLA Ops:
  0.6 0.9 %copy-start.1 = (bf16[1,2,64,512]{3,2,1,0:T(8,128)(2,1)S(1)}, bf16[1,2,64,512]{3,2,1,0:T(8,128)(2,1)}, u32[]{:S(2)}) copy-start(bf16[1,2,64,512]{3,2,1,0:T(8,128)(2,1)} %param.6) | copy-start | bytes 393220
  1.5 0.7 copy-start.2
  2.8 16.4 %collective-permute-start = (bf16[128,128]{1,0:T(8,128)(2,1)S(1)}, bf16[128,128]{1,0:T(8,128)(2,1)S(1)}, u32[]{:S(2)}, u32[]{:S(2)}) collective-permute-start(bf16[128,128]{1,0:T(8,128)(2,1)S(1)} %get-tuple-element.9), channel_id=1, source_target_pairs={{0,1},{1,0},{2,3},{3,2},{4,5},{5,4},{6,7},{7,6},{8,9},{9,8},{10,11... | collective-permute-start | bytes 98312 | tf_op jit(solution)/shard_map/ppermute | solution.py:230
  5.0 14.2 %collective-permute-start.1 = (bf16[128,128]{1,0:T(8,128)(2,1)S(1)}, bf16[128,128]{1,0:T(8,128)(2,1)S(1)}, u32[]{:S(2)}, u32[]{:S(2)}) collective-permute-start(bf16[128,128]{1,0:T(8,128)(2,1)S(1)} %get-tuple-element.10), channel_id=1, source_target_pairs={{0,2},{1,3},{2,0},{3,1},{4,6},{5,7},{6,4},{7,5},{8,10},{9,11},{10,... | collective-permute-start | bytes 98312 | tf_op jit(solution)/shard_map/ppermute | solution.py:230
  5.9 13.3 %collective-permute-start.2 = (bf16[128,128]{1,0:T(8,128)(2,1)S(1)}, bf16[128,128]{1,0:T(8,128)(2,1)S(1)}, u32[]{:S(2)}, u32[]{:S(2)}) collective-permute-start(bf16[128,128]{1,0:T(8,128)(2,1)S(1)} %get-tuple-element.11), channel_id=1, source_target_pairs={{0,3},{1,2},{2,1},{3,0},{4,7},{5,6},{6,5},{7,4},{8,11},{9,10},{10,... | collective-permute-start | bytes 98312 | tf_op jit(solution)/shard_map/ppermute | solution.py:230
  6.6 0.9 %copy-start = (bf16[1,64,2048]{2,1,0:T(8,128)(2,1)S(1)}, bf16[1,64,2048]{2,1,0:T(8,128)(2,1)}, u32[]{:S(2)}) copy-start(bf16[1,64,2048]{2,1,0:T(8,128)(2,1)} %param.5) | copy-start | bytes 786436
  7.6 9.8 %copy-start.4 = (s32[256]{0:T(256)S(1)}, s32[256]{0:T(256)}, u32[]{:S(2)}) copy-start(s32[256]{0:T(256)} %param.8) | copy-start | bytes 3076
  9.2 38.3 %all-to-all-start = ((bf16[16,256,128]{2,1,0:T(8,128)(2,1)}), bf16[16,256,128]{2,1,0:T(8,128)(2,1)S(1)}, u32[]{:S(2)}, u32[]{:S(2)}) async-start(bf16[16,256,128]{2,1,0:T(8,128)(2,1)} %split_q.1), calls=%async_computation | async-start | bytes 2097152 | tf_op jit(solution)/shard_map/all_to_all | solution.py:236
  19.3 8.5 %collective-permute-start.6 = (bf16[512,128]{1,0:T(8,128)(2,1)S(1)}, bf16[512,128]{1,0:T(8,128)(2,1)S(1)}, u32[]{:S(2)}, u32[]{:S(2)}) collective-permute-start(bf16[512,128]{1,0:T(8,128)(2,1)S(1)} %constant_dynamic-update-slice_fusion.refs_0_), channel_id=1, source_target_pairs={{0,112},{1,113},{2,114},{3,115},{4,116},{5,117},{6,118},{7,119},{8... | collective-permute-start | bytes 393224 | tf_op jit(solution)/shard_map/ppermute | solution.py:230
  25.2 6.2 %collective-permute-start.3 = (bf16[512,128]{1,0:T(8,128)(2,1)S(1)}, bf16[512,128]{1,0:T(8,128)(2,1)S(1)}, u32[]{:S(2)}, u32[]{:S(2)}) collective-permute-start(bf16[512,128]{1,0:T(8,128)(2,1)S(1)} %constant_dynamic-update-slice_fusion.refs_0_), channel_id=1, source_target_pairs={{0,16},{1,17},{2,18},{3,19},{4,20},{5,21},{6,22},{7,23},{8,24},{9,... | collective-permute-start | bytes 393224 | tf_op jit(solution)/shard_map/ppermute | solution.py:230
  27.7 9.8 %collective-permute-start.7 = (bf16[512,128]{1,0:T(8,128)(2,1)S(1)}, bf16[512,128]{1,0:T(8,128)(2,1)S(1)}, u32[]{:S(2)}, u32[]{:S(2)}) collective-permute-start(bf16[512,128]{1,0:T(8,128)(2,1)S(1)} %collective-permute-done.6.refs_4_), channel_id=1, source_target_pairs={{0,112},{1,113},{2,114},{3,115},{4,116},{5,117},{6,118},{7,119},{8... | collective-permute-start | bytes 393224 | tf_op jit(solution)/shard_map/ppermute | solution.py:230
  31.4 6.2 %collective-permute-start.4 = (bf16[512,128]{1,0:T(8,128)(2,1)S(1)}, bf16[512,128]{1,0:T(8,128)(2,1)S(1)}, u32[]{:S(2)}, u32[]{:S(2)}) collective-permute-start(bf16[512,128]{1,0:T(8,128)(2,1)S(1)} %collective-permute-done.3.refs_1_), channel_id=1, source_target_pairs={{0,16},{1,17},{2,18},{3,19},{4,20},{5,21},{6,22},{7,23},{8,24},{9,... | collective-permute-start | bytes 393224 | tf_op jit(solution)/shard_map/ppermute | solution.py:230
  37.6 9.9 %collective-permute-start.5 = (bf16[512,128]{1,0:T(8,128)(2,1)S(1)}, bf16[512,128]{1,0:T(8,128)(2,1)S(1)}, u32[]{:S(2)}, u32[]{:S(2)}) collective-permute-start(bf16[512,128]{1,0:T(8,128)(2,1)S(1)} %collective-permute-done.4.refs_2_), channel_id=1, source_target_pairs={{0,16},{1,17},{2,18},{3,19},{4,20},{5,21},{6,22},{7,23},{8,24},{9,... | collective-permute-start | bytes 393224 | tf_op jit(solution)/shard_map/ppermute | solution.py:230
  37.6 9.9 %collective-permute-start.8 = (bf16[512,128]{1,0:T(8,128)(2,1)S(1)}, bf16[512,128]{1,0:T(8,128)(2,1)S(1)}, u32[]{:S(2)}, u32[]{:S(2)}) collective-permute-start(bf16[512,128]{1,0:T(8,128)(2,1)S(1)} %collective-permute-done.7.refs_5_), channel_id=1, source_target_pairs={{0,112},{1,113},{2,114},{3,115},{4,116},{5,117},{6,118},{7,119},{8... | collective-permute-start | bytes 393224 | tf_op jit(solution)/shard_map/ppermute | solution.py:230
  40.8 5.2 %collective-permute-start.10 = (bf16[256,128]{1,0:T(8,128)(2,1)S(1)}, bf16[256,128]{1,0:T(8,128)(2,1)S(1)}, u32[]{:S(2)}, u32[]{:S(2)}) collective-permute-start(bf16[256,128]{1,0:T(8,128)(2,1)S(1)} %slice.17), channel_id=1, source_target_pairs={{0,96},{1,97},{2,98},{3,99},{4,100},{5,101},{6,102},{7,103},{8,104... | collective-permute-start | bytes 196616 | tf_op jit(solution)/shard_map/ppermute | solution.py:230
  40.9 6.6 %collective-permute-start.9 = (bf16[256,128]{1,0:T(8,128)(2,1)S(1)}, bf16[256,128]{1,0:T(8,128)(2,1)S(1)}, u32[]{:S(2)}, u32[]{:S(2)}) collective-permute-start(bf16[256,128]{1,0:T(8,128)(2,1)S(1)} %slice.16), channel_id=1, source_target_pairs={{0,32},{1,33},{2,34},{3,35},{4,36},{5,37},{6,38},{7,39},{8,40},{9,... | collective-permute-start | bytes 196616 | tf_op jit(solution)/shard_map/ppermute | solution.py:230
  60.2 25.0 %copy-start.3 = (s32[4]{0:T(128)S(1)}, s32[4]{0:T(128)}, u32[]{:S(2)}) copy-start(s32[4]{0:T(128)} %heads.5) | copy-start | bytes 52
  60.2 25.0 %all-to-all-start.1 = ((bf16[16,400,128]{2,1,0:T(8,128)(2,1)}), bf16[16,400,128]{2,1,0:T(8,128)(2,1)S(1)}, u32[]{:S(2)}, u32[]{:S(2)}) async-start(bf16[16,400,128]{2,1,0:T(8,128)(2,1)} %attention.1), calls=%async_computation.1 | async-start | bytes 3276800 | tf_op jit(solution)/shard_map/all_to_all | solution.py:236

commit v10 on v9

--- a/solution.py
+++ b/solution.py
@@ -24,7 +24,8 @@
 JOINED = 4
 CHUNK_BLOCKS = 8
 CHUNK = CHUNK_BLOCKS * BLOCK
-PARTIAL = 2 * ROWS + 16
+HALF = Q_BLOCKS // 2
+PARTIAL = ROWS + 16
 MESSAGE = PARTIAL + 2 * KEY_BLOCKS
 SCALE = HEAD**-0.5 * 1.4426950408889634
 NEG = -1e30
@@ -94,8 +95,8 @@
             o_ref[d, PARTIAL:, :] = jnp.zeros((2 * KEY_BLOCKS, HEAD), jnp.bfloat16)
 
 
-def attention_kernel(table, q_ref, kpos_ref, *refs):
-    pieces, (o_ref, k_scr, kt_scr, v_scr, s_scr, stat) = refs[:9], refs[9:]
+def low_kernel(table, q_ref, kpos_ref, *refs):
+    pieces, (o_ref, kt_ref, v_ref, k_scr, s_scr, stat) = refs[:9], refs[9:]
     own, r1, r2, r3, l1, l2, l3, r4, l4 = pieces
     every, first, last = range(NY), range(NY // 2), range(NY // 2, NY)
     arrange(
@@ -103,10 +104,18 @@
         [(own, 0, every), (l1, 1, every), (l2, 2, every), (l3, 3, every), (r4, 4, first), (l4, 4, last)]
         + [(r3, 5, every), (r2, 6, every), (r1, 7, every)],
         k_scr,
-        kt_scr,
-        v_scr,
+        kt_ref,
+        v_ref,
     )
-    pick(k_scr, v_scr, o_ref)
+    pick(k_scr, v_ref, o_ref)
+    attend(0, KEYS // CHUNK // 2, table, q_ref, kpos_ref, kt_ref, v_ref, o_ref, s_scr, stat)
+
+
+def high_kernel(table, q_ref, kpos_ref, kt_ref, v_ref, o_ref, s_scr, stat):
+    attend(HALF // JOINED, KEYS // CHUNK, table, q_ref, kpos_ref, kt_ref, v_ref, o_ref, s_scr, stat)
+
+
+def attend(first_group, most, table, q_ref, kpos_ref, kt_ref, v_ref, o_ref, s_scr, stat):
     lane = lax.broadcasted_iota(jnp.int32, (ROWS, 128), 1)
     token = lax.broadcasted_iota(jnp.int32, (BLOCK, CHUNK), 0)
 
@@ -116,17 +125,17 @@
         ids = [table[AT_ID + i * JOINED + u] for u in range(JOINED)]
 
         def finish(u, out, total, top):
-            place = pl.ds(pl.multiple_of(blocks[u] % 2 * ROWS, ROWS), ROWS)
-            o_ref[blocks[u] // 2, place, :] = out.astype(jnp.bfloat16)
-            old = jnp.where(lane == blocks[u], top, stat[...])
-            stat[...] = jnp.where(lane == blocks[u] + Q_BLOCKS, total, old)
+            target = blocks[u] // 2
+            o_ref[target, :ROWS, :] = out.astype(jnp.bfloat16)
+            old = jnp.where(lane == target, top, stat[...])
+            stat[...] = jnp.where(lane == target + PLANE, total, old)
 
         def work(n):
             q = jnp.concatenate([q_ref[blocks[u]] for u in range(JOINED)], axis=0)
             tops = [None] * (JOINED * GROUP)
             for c in range(n):
                 start = pl.multiple_of((low + c) * CHUNK, CHUNK)
-                s = jnp.dot(q, kt_scr[:, pl.ds(start, CHUNK)], preferred_element_type=jnp.float32)
+                s = jnp.dot(q, kt_ref[:, pl.ds(start, CHUNK)], preferred_element_type=jnp.float32)
                 kpos = kpos_ref[pl.ds(low + c, 1), :]
                 for u in range(JOINED):
                     distance = (ids[u] * BLOCK + token) - kpos
@@ -144,7 +153,7 @@
             for c in range(n):
                 start = pl.multiple_of((low + c) * CHUNK, CHUNK)
                 p = jnp.exp2(s_scr[c] * SCALE - twice).astype(jnp.bfloat16)
-                part = jnp.dot(p, v_scr[pl.ds(start, CHUNK), :], preferred_element_type=jnp.float32)
+                part = jnp.dot(p, v_ref[pl.ds(start, CHUNK), :], preferred_element_type=jnp.float32)
                 acc = part if acc is None else acc + part
             for u in range(JOINED):
                 rows = slice(u * ROWS, (u + 1) * ROWS)
@@ -156,58 +165,73 @@
             for u in range(JOINED):
                 finish(u, nothing, nothing, nothing + NEG)
 
-        for n in range(1, KEYS // CHUNK + 1):
+        for n in range(1, most + 1):
             pl.when(high - low == n)(functools.partial(work, n))
         return carry
 
     stat[...] = jnp.zeros((ROWS, 128), jnp.float32)
-    lax.fori_loop(0, Q_BLOCKS // JOINED, one_group, 0)
+    lax.fori_loop(first_group, first_group + HALF // JOINED, one_group, 0)
     turned = stat[...].T
     for d in range(PLANE):
-        value = jnp.concatenate(
-            [turned[2 * d : 2 * d + 2], turned[Q_BLOCKS + 2 * d : Q_BLOCKS + 2 * d + 2]], axis=0
-        )
+        value = jnp.concatenate([turned[d : d + 1], turned[PLANE + d : PLANE + d + 1]], axis=0)
         first = value.astype(jnp.bfloat16).astype(jnp.float32)
         second = (value - first).astype(jnp.bfloat16).astype(jnp.float32)
         third = value - first - second
-        rows = jnp.concatenate([first, second, third, jnp.zeros_like(first)], axis=0)
-        o_ref[d, 2 * ROWS : PARTIAL, :] = rows.astype(jnp.bfloat16)
-
-
-def combine_kernel(heads, blocks, length, choose_ref, m_ref, o_ref, cache_ref):
+        rows = jnp.concatenate([first, second, third, jnp.zeros((10, 128), jnp.float32)], axis=0)
+        o_ref[d, ROWS:PARTIAL, :] = rows.astype(jnp.bfloat16)
+
+
+def merge(heads, block, length, m_ref, store):
+    values = []
+    for d in range(PLANE):
+        rows = m_ref[d, ROWS:PARTIAL, :].astype(jnp.float32)
+        values.append(rows[0:2] + rows[2:4] + rows[4:6])
+    weights = [None] * PLANE
+    for y in range(NY):
+        sources = [x * NY + y for x in range(NX)]
+        top = values[sources[0]][0:1]
+        for d in sources[1:]:
+            top = jnp.maximum(top, values[d][0:1])
+        parts = [jnp.exp2(values[d][0:1] - top) * values[d][1:2] for d in sources]
+        total = parts[0] + parts[1] + parts[2] + parts[3]
+        for d, part in zip(sources, parts):
+            weights[d] = part / total
+    matrix = jnp.concatenate(weights + [jnp.zeros((128 - PLANE, 128), jnp.float32)], axis=0).T
+    token = lax.broadcasted_iota(jnp.int32, (ROWS, HEAD), 0) % BLOCK
+    for y in range(NY):
+        out = jnp.zeros((ROWS, HEAD), jnp.float32)
+        for x in range(NX):
+            d = x * NY + y
+            out += matrix[:, d : d + 1] * m_ref[d, :ROWS, :].astype(jnp.float32)
+        out = jnp.where(block * BLOCK + token < length[0], out, 0.0).astype(jnp.bfloat16)
+        for g in range(GROUP):
+            column = pl.multiple_of((heads[y] * GROUP + g) * HEAD, HEAD)
+            store(pl.ds(column, HEAD), out[g * BLOCK : (g + 1) * BLOCK])
+
+
+def combine_low_kernel(heads, blocks, length, choose_ref, m_ref, o_ref, cache_ref):
     keeper = lax.axis_index("blk") // (2 * PLANE)
     for half in range(2):
         rows = slice(PARTIAL + half * KEY_BLOCKS, PARTIAL + (half + 1) * KEY_BLOCKS)
         found = jnp.concatenate([m_ref[x * NY + keeper, rows, :] for x in range(NX)], axis=0)
         cache = jnp.dot(choose_ref[...], found, preferred_element_type=jnp.float32)
         cache_ref[half] = cache.astype(jnp.bfloat16)
-    values = []
-    for d in range(PLANE):
-        rows = m_ref[d, 2 * ROWS : PARTIAL, :].astype(jnp.float32)
-        values.append(rows[0:4] + rows[4:8] + rows[8:12])
-    weights = [None] * PLANE
-    for y in range(NY):
-        sources = [x * NY + y for x in range(NX)]
-        top = values[sources[0]][0:2]
-        for d in sources[1:]:
-            top = jnp.maximum(top, values[d][0:2])
-        parts = [jnp.exp2(values[d][0:2] - top) * values[d][2:4] for d in sources]
-        total = parts[0] + parts[1] + parts[2] + parts[3]
-        for d, part in zip(sources, parts):
-            weights[d] = part / total
-    matrix = jnp.concatenate(weights + [jnp.zeros((128 - Q_BLOCKS, 128), jnp.float32)], axis=0).T
-    token = lax.broadcasted_iota(jnp.int32, (ROWS, HEAD), 0) % BLOCK
-    for y in range(NY):
-        for j in range(2):
-            out = jnp.zeros((ROWS, HEAD), jnp.float32)
-            for x in range(NX):
-                d = x * NY + y
-                weight = matrix[:, 2 * d + j : 2 * d + j + 1]
-                out += weight * m_ref[d, j * ROWS : (j + 1) * ROWS, :].astype(jnp.float32)
-            out = jnp.where(blocks[j] * BLOCK + token < length[0], out, 0.0).astype(jnp.bfloat16)
-            for g in range(GROUP):
-                column = pl.multiple_of((heads[y] * GROUP + g) * HEAD, HEAD)
-                o_ref[j * BLOCK : (j + 1) * BLOCK, pl.ds(column, HEAD)] = out[g * BLOCK : (g + 1) * BLOCK]
+
+    def store(columns, value):
+        o_ref[:, columns] = value
+
+    merge(heads, jnp.minimum(blocks[0], blocks[1]), length, m_ref, store)
+
+
+def combine_high_kernel(heads, blocks, length, low_ref, m_ref, o_ref):
+    second = jnp.where(blocks[0] < blocks[1], 1, 0)
+    rows = pl.ds(pl.multiple_of(second * BLOCK, BLOCK), BLOCK)
+    o_ref[pl.ds(pl.multiple_of((1 - second) * BLOCK, BLOCK), BLOCK), :] = low_ref[...]
+
+    def store(columns, value):
+        o_ref[rows, columns] = value
+
+    merge(heads, jnp.maximum(blocks[0], blocks[1]), length, m_ref, store)
 
 
 def ranks(ids):
@@ -281,40 +305,64 @@
     kpos = kpos.reshape(KEYS // CHUNK, CHUNK)
 
     pieces = (own, r1, r2, r3, l1, l2, l3, r4, l4)
-    partial = pl.pallas_call(
-        attention_kernel,
-        out_shape=jax.ShapeDtypeStruct((PLANE, MESSAGE, HEAD), jnp.bfloat16),
+    low, kt, v = pl.pallas_call(
+        low_kernel,
+        out_shape=(
+            jax.ShapeDtypeStruct((PLANE, MESSAGE, HEAD), jnp.bfloat16),
+            jax.ShapeDtypeStruct((HEAD, KEYS), jnp.bfloat16),
+            jax.ShapeDtypeStruct((KEYS, 2 * HEAD), jnp.bfloat16),
+        ),
         in_specs=[SMEM] + [VMEM] * 11,
+        out_specs=(VMEM,) * 3,
+        scratch_shapes=[
+            pltpu.VMEM((KEYS, HEAD), jnp.bfloat16),
+            pltpu.VMEM((KEYS // CHUNK // 2, JOINED * ROWS, CHUNK), jnp.float32),
+            pltpu.VMEM((ROWS, 128), jnp.float32),
+        ],
+        compiler_params=PARAMS,
+        cost_estimate=pl.CostEstimate(flops=1_000_000_000, bytes_accessed=4_000_000, transcendentals=2_000_000),
+        name="low",
+    )(table, q, kpos, *pieces)
+    low = exchange(low, planes)
+    high = pl.pallas_call(
+        high_kernel,
+        out_shape=jax.ShapeDtypeStruct((PLANE, PARTIAL, HEAD), jnp.bfloat16),
+        in_specs=[SMEM] + [VMEM] * 4,
         out_specs=VMEM,
         scratch_shapes=[
-            pltpu.VMEM((KEYS, HEAD), jnp.bfloat16),
-            pltpu.VMEM((HEAD, KEYS), jnp.bfloat16),
-            pltpu.VMEM((KEYS, 2 * HEAD), jnp.bfloat16),
             pltpu.VMEM((KEYS // CHUNK, JOINED * ROWS, CHUNK), jnp.float32),
             pltpu.VMEM((ROWS, 128), jnp.float32),
         ],
         compiler_params=PARAMS,
-        cost_estimate=pl.CostEstimate(flops=3_000_000_000, bytes_accessed=4_000_000, transcendentals=5_000_000),
-        name="attention",
-    )(table, q, kpos, *pieces)
-    out = exchange(partial, planes)
+        cost_estimate=pl.CostEstimate(flops=2_000_000_000, bytes_accessed=3_000_000, transcendentals=3_000_000),
+        name="high",
+    )(table, q, kpos, kt, v)
+    high = exchange(high, planes)
 
     blocks = jnp.arange(BLOCKS, dtype=jnp.int32)
     position = blocks * BLOCK + place % BLOCK
     choose = (ordered.reshape(1, BLOCKS) == blocks[:, None]) & (position < lengths[0])[:, None]
     choose = choose.astype(jnp.bfloat16)
     my_blocks = lax.dynamic_slice_in_dim(block_map, 2 * place, 2)
-    attended, cache = pl.pallas_call(
-        combine_kernel,
+    low, cache = pl.pallas_call(
+        combine_low_kernel,
         out_shape=(
-            jax.ShapeDtypeStruct((2 * BLOCK, QUERY_HEADS * HEAD), jnp.bfloat16),
+            jax.ShapeDtypeStruct((BLOCK, QUERY_HEADS * HEAD), jnp.bfloat16),
             jax.ShapeDtypeStruct((2, BLOCKS, HEAD), jnp.bfloat16),
         ),
         in_specs=[SMEM] * 3 + [VMEM] * 2,
         out_specs=(VMEM, VMEM),
         compiler_params=SMALL,
-        name="combine",
-    )(segment_head, my_blocks, lengths, choose, out)
+        name="combine_low",
+    )(segment_head, my_blocks, lengths, choose, low)
+    attended = pl.pallas_call(
+        combine_high_kernel,
+        out_shape=jax.ShapeDtypeStruct((2 * BLOCK, QUERY_HEADS * HEAD), jnp.bfloat16),
+        in_specs=[SMEM] * 3 + [VMEM] * 2,
+        out_specs=VMEM,
+        compiler_params=SMALL,
+        name="combine_high",
+    )(segment_head, my_blocks, lengths, low, high)
     return attended.reshape(1, 2 * BLOCK, QUERY_HEADS * HEAD), cache[None, :, None]
 
 

time: 87.8 us -> 90.5 us (1.031)
  waiting for transfers between devices: 28.8 us -> 22.2 us
  starting transfers between devices: 34.9 us -> 40.3 us
  local copies, waits for them, and re-layouts: 3.81 us -> 5.65 us
  Pallas kernels: 17 us -> 18.4 us
    all_to_all x2 -> x3, waiting for transfers between devices: 17 us -> 10.3 us  [exchange(): lax.all_to_all(value, 'blk', 0, 0, axis_index_groups=groups, tiled=True)]
    all_to_all x2 -> x3, starting transfers between devices: 15.3 us -> 20.6 us  [exchange(): lax.all_to_all(value, 'blk', 0, 0, axis_index_groups=groups, tiled=True)]
    unnamed x13 -> x17, local copies, waits for them, and re-layouts: 2.54 us -> 4.38 us
    pallas_call x2 -> x4, Pallas kernels: 14.8 us -> 16.2 us  [the longest x1 7.17 us: body(): pl.pallas_call(high_kernel, out_shape=jax.ShapeDtypeStruct((PLANE, PARTIA...]
  transfers between devices with their start and end apart: 13 -> 14, of which waited for: 5 -> 6; matrix products, arithmetic and copies ran while one was open for 3% -> 3% of each run, Pallas kernels for 2% -> 12%
where the time goes in v10:
time: 90.5 us; the launch traced here: 89.2 us
  starting transfers between devices  40.3 us (45%)
  waiting for transfers between devices  22.2 us (25%)
  Pallas kernels  18.4 us (20%)
  local copies, waits for them, and re-layouts  5.65 us (6%)
  between operations  1.48 us (2%)
  other arithmetic  1.24 us (1%)
    all_to_all x3, starting transfers between devices, exchange(): lax.all_to_all(value, 'blk', 0, 0, axis_index_groups=groups, tiled=True)  20.6 us
    ppermute x11, starting transfers between devices, move(): lax.ppermute(value, 'blk', [(s, target(s // 16, s // 4 % 4, s % 4)) for s...  19.7 us
    ppermute x11, waiting for transfers between devices, move(): lax.ppermute(value, 'blk', [(s, target(s // 16, s // 4 % 4, s % 4)) for s...  11.9 us
    all_to_all x3, waiting for transfers between devices, exchange(): lax.all_to_all(value, 'blk', 0, 0, axis_index_groups=groups, tiled=True)  10.3 us
    pallas_call x1, Pallas kernels, body(): pl.pallas_call(high_kernel, out_shape=jax.ShapeDtypeStruct((PLANE, PARTIA...  7.17 us
    pallas_call x1, Pallas kernels, body(): pl.pallas_call(low_kernel, out_shape=(jax.ShapeDtypeStruct((PLANE, MESSAG...  5.54 us
    unnamed x17, local copies, waits for them, and re-layouts  4.38 us
  transfers between devices with their start and end apart: 14, of which 6 were waited for; matrix products, arithmetic and copies ran while one was open for 3% of the time, Pallas kernels for 12%

profile of v10, /device:TPU:8, one launch (start us, length us, event | category | flops | bytes accessed | tf_op | source)
XLA Modules:
  0.0 89.2 jit_solution(13860574624227854062)
XLA Ops:
  0.6 0.9 %copy-done.1 = bf16[1,2,64,512]{3,2,1,0:T(8,128)(2,1)S(1)} copy-done((bf16[1,2,64,512]{3,2,1,0:T(8,128)(2,1)S(1)}, bf16[1,2,64,512]{3,2,1,0:T(8,128)(2,1)}, u32[]{:S(2)}) %copy-start.1) | copy-done | bytes 131096
  1.5 0.7 copy-done.2
  2.2 0.6 split_kv.1
  2.8 2.3 %collective-permute-start = (bf16[128,128]{1,0:T(8,128)(2,1)S(1)}, bf16[128,128]{1,0:T(8,128)(2,1)S(1)}, u32[]{:S(2)}, u32[]{:S(2)}) collective-permute-start(bf16[128,128]{1,0:T(8,128)(2,1)S(1)} %get-tuple-element.12), channel_id=1, source_target_pairs={{0,1},{1,0},{2,3},{3,2},{4,5},{5,4},{6,7},{7,6},{8,9},{9,8},{10,11... | collective-permute-start | bytes 98312 | tf_op jit(solution)/shard_map/ppermute | solution.py:254
  5.0 0.9 collective-permute-start.1
  5.9 0.7 collective-permute-start.2
  6.6 0.9 %copy-done = bf16[1,64,2048]{2,1,0:T(8,128)(2,1)S(1)} copy-done((bf16[1,64,2048]{2,1,0:T(8,128)(2,1)S(1)}, bf16[1,64,2048]{2,1,0:T(8,128)(2,1)}, u32[]{:S(2)}) %copy-start) | copy-done | bytes 262168
  7.6 1.7 %split_q.1 = bf16[16,256,128]{2,1,0:T(8,128)(2,1)} custom-call(s32[4]{0:T(128)S(1)} %copy-done.2, bf16[64,2048]{1,0:T(8,128)(2,1)S(1)} %bitcast.17), custom_call_target="tpu_custom_call" | custom-call | tf_op jit(solution)/shard_map/split_q/pallas_call | solution.py:275
  9.2 8.3 %all-to-all-start = ((bf16[16,256,128]{2,1,0:T(8,128)(2,1)}), bf16[16,256,128]{2,1,0:T(8,128)(2,1)S(1)}, u32[]{:S(2)}, u32[]{:S(2)}) async-start(bf16[16,256,128]{2,1,0:T(8,128)(2,1)} %split_q.1), calls=%async_computation | async-start | bytes 2097152 | tf_op jit(solution)/shard_map/all_to_all | solution.py:260
  17.7 0.3 copy.12
  18.1 0.2 convert_reduce_fusion
  18.6 0.2 convert_reduce_fusion.1
  19.4 5.9 %collective-permute-start.6 = (bf16[512,128]{1,0:T(8,128)(2,1)S(1)}, bf16[512,128]{1,0:T(8,128)(2,1)S(1)}, u32[]{:S(2)}, u32[]{:S(2)}) collective-permute-start(bf16[512,128]{1,0:T(8,128)(2,1)S(1)} %constant_dynamic-update-slice_fusion.refs_0_), channel_id=1, source_target_pairs={{0,112},{1,113},{2,114},{3,115},{4,116},{5,117},{6,118},{7,119},{8... | collective-permute-start | bytes 393224 | tf_op jit(solution)/shard_map/ppermute | solution.py:254
  25.3 2.5 %collective-permute-done.6.refs_4_ = bf16[512,128]{1,0:T(8,128)(2,1)S(1)} collective-permute-done((bf16[512,128]{1,0:T(8,128)(2,1)S(1)}, bf16[512,128]{1,0:T(8,128)(2,1)S(1)}, u32[]{:S(2)}, u32[]{:S(2)}) %collective-permute-start.6) | collective-permute-done | bytes 131104 | tf_op jit(solution)/shard_map/ppermute | solution.py:254
  27.8 3.7 %collective-permute-start.7 = (bf16[512,128]{1,0:T(8,128)(2,1)S(1)}, bf16[512,128]{1,0:T(8,128)(2,1)S(1)}, u32[]{:S(2)}, u32[]{:S(2)}) collective-permute-start(bf16[512,128]{1,0:T(8,128)(2,1)S(1)} %collective-permute-done.6.refs_4_), channel_id=1, source_target_pairs={{0,112},{1,113},{2,114},{3,115},{4,116},{5,117},{6,118},{7,119},{8... | collective-permute-start | bytes 393224 | tf_op jit(solution)/shard_map/ppermute | solution.py:254
  31.5 0.2 slice_reduce_fusion
  31.7 0.2 convert_reduce_fusion.2
  31.9 5.8 %collective-permute-done.4.refs_2_ = bf16[512,128]{1,0:T(8,128)(2,1)S(1)} collective-permute-done((bf16[512,128]{1,0:T(8,128)(2,1)S(1)}, bf16[512,128]{1,0:T(8,128)(2,1)S(1)}, u32[]{:S(2)}, u32[]{:S(2)}) %collective-permute-start.4) | collective-permute-done | bytes 131104 | tf_op jit(solution)/shard_map/ppermute | solution.py:254
  37.7 3.2 %collective-permute-start.8 = (bf16[512,128]{1,0:T(8,128)(2,1)S(1)}, bf16[512,128]{1,0:T(8,128)(2,1)S(1)}, u32[]{:S(2)}, u32[]{:S(2)}) collective-permute-start(bf16[512,128]{1,0:T(8,128)(2,1)S(1)} %collective-permute-done.7.refs_5_), channel_id=1, source_target_pairs={{0,112},{1,113},{2,114},{3,115},{4,116},{5,117},{6,118},{7,119},{8... | collective-permute-start | bytes 393224 | tf_op jit(solution)/shard_map/ppermute | solution.py:254
  41.1 2.9 %collective-permute-start.9 = (bf16[256,128]{1,0:T(8,128)(2,1)S(1)}, bf16[256,128]{1,0:T(8,128)(2,1)S(1)}, u32[]{:S(2)}, u32[]{:S(2)}) collective-permute-start(bf16[256,128]{1,0:T(8,128)(2,1)S(1)} %slice.16), channel_id=1, source_target_pairs={{0,32},{1,33},{2,34},{3,35},{4,36},{5,37},{6,38},{7,39},{8,40},{9,... | collective-permute-start | bytes 196616 | tf_op jit(solution)/shard_map/ppermute | solution.py:254
  44.0 2.1 %collective-permute-done.10.refs_8_ = bf16[256,128]{1,0:T(8,128)(2,1)S(1)} collective-permute-done((bf16[256,128]{1,0:T(8,128)(2,1)S(1)}, bf16[256,128]{1,0:T(8,128)(2,1)S(1)}, u32[]{:S(2)}, u32[]{:S(2)}) %collective-permute-start.10) | collective-permute-done | bytes 65568 | tf_op jit(solution)/shard_map/ppermute | solution.py:254
  46.2 1.4 %collective-permute-done.9.refs_7_ = bf16[256,128]{1,0:T(8,128)(2,1)S(1)} collective-permute-done((bf16[256,128]{1,0:T(8,128)(2,1)S(1)}, bf16[256,128]{1,0:T(8,128)(2,1)S(1)}, u32[]{:S(2)}, u32[]{:S(2)}) %collective-permute-start.9) | collective-permute-done | bytes 65568 | tf_op jit(solution)/shard_map/ppermute | solution.py:254
  47.6 5.5 %low.1 = (bf16[16,272,128]{2,1,0:T(8,128)(2,1)}, bf16[128,2048]{1,0:T(8,128)(2,1)S(1)}, bf16[2048,256]{1,0:T(8,128)(2,1)S(1)}) custom-call(s32[144]{0:T(256)S(1)} %concatenate.6.table, bf16[32,128,128]{2,1,0:T(8,128)(2,1)S(1)} %bitcast.15, s32[8,256]{1,0:T(8,128)S(1)} %broadcast_add_fusion.kpos_ref, ...), custom_call_target="tpu_custom_call" | custom-call | flops 1000000000 | bytes 4000000 | tf_op jit(solution)/shard_map/low/pallas_call | solution.py:308
  53.2 0.8 copy-done.4
  54.0 7.5 %all-to-all-start.1 = ((bf16[16,272,128]{2,1,0:T(8,128)(2,1)}), bf16[16,272,128]{2,1,0:T(8,128)(2,1)S(1)}, u32[]{:S(2)}, u32[]{:S(2)}) async-start(bf16[16,272,128]{2,1,0:T(8,128)(2,1)} %get-tuple-element.15), calls=%async_computation.1 | async-start | bytes 2228224 | tf_op jit(solution)/shard_map/all_to_all | solution.py:260
  61.4 1.0 %copy-done.5 = bf16[128,2048]{1,0:T(8,128)(2,1)S(1)} copy-done((bf16[128,2048]{1,0:T(8,128)(2,1)S(1)}, bf16[128,2048]{1,0:T(8,128)(2,1)}, u32[]{:S(2)}) %copy-start.5) | copy-done | bytes 524312
  62.5 7.2 %high.1 = bf16[16,144,128]{2,1,0:T(8,128)(2,1)} custom-call(s32[144]{0:T(256)S(1)} %concatenate.6.table, bf16[32,128,128]{2,1,0:T(8,128)(2,1)S(1)} %bitcast.16, s32[8,256]{1,0:T(8,128)S(1)} %broadcast_add_fusion.kpos_ref, bf16[128,2048]{1,0:T(8,128)(2,1)S(1)} %copy-done.5, bf16[2048,256]{1,0:T(8,128)(2,1)S(1)} %get-tuple-element.18.v_ref), custom_call_target="tpu_custom_call" | custom-call | flops 2000000000 | bytes 3000000 | tf_op jit(solution)/shard_map/high/pallas_call | solution.py:327
  69.6 3.8 %all-to-all-done.1.m_ref = bf16[16,272,128]{2,1,0:T(8,128)(2,1)S(1)} async-done(((bf16[16,272,128]{2,1,0:T(8,128)(2,1)}), bf16[16,272,128]{2,1,0:T(8,128)(2,1)S(1)}, u32[]{:S(2)}, u32[]{:S(2)}) %all-to-all-start.1) | async-done | bytes 1114144 | tf_op jit(solution)/shard_map/all_to_all | solution.py:260
  73.4 4.8 %all-to-all-start.2 = ((bf16[16,144,128]{2,1,0:T(8,128)(2,1)}), bf16[16,144,128]{2,1,0:T(8,128)(2,1)S(1)}, u32[]{:S(2)}, u32[]{:S(2)}) async-start(bf16[16,144,128]{2,1,0:T(8,128)(2,1)} %high.1), calls=%async_computation.2 | async-start | bytes 1179648 | tf_op jit(solution)/shard_map/all_to_all | solution.py:260
  79.2 1.7 %combine_low.1 = (bf16[32,2048]{1,0:T(8,128)(2,1)S(1)}, bf16[2,256,128]{2,1,0:T(8,128)(2,1)}) custom-call(s32[4]{0:T(128)S(1)} %copy-done.3, s32[2]{0:T(128)S(1)} %dynamic_slice.13.blocks, s32[1]{0:T(128)} %copy.19.length, bf16[256,256]{1,0:T(8,128)(2,1)S(1)} %fusion.1.choose_ref, bf16[16,272,128]{2,1,0:T(8,128)(2,1)S(1)} %all-to-all-done.1.m_ref), custom_call_target="tpu_custom_call" | custom-call | tf_op jit(solution)/shard_map/combine_low/pallas_call | solution.py:347
  80.9 6.5 %all-to-all-done.2.m_ref = bf16[16,144,128]{2,1,0:T(8,128)(2,1)S(1)} async-done(((bf16[16,144,128]{2,1,0:T(8,128)(2,1)}), bf16[16,144,128]{2,1,0:T(8,128)(2,1)S(1)}, u32[]{:S(2)}, u32[]{:S(2)}) %all-to-all-start.2) | async-done | bytes 589856 | tf_op jit(solution)/shard_map/all_to_all | solution.py:260
  87.4 1.8 %combine_high.1 = bf16[64,2048]{1,0:T(8,128)(2,1)} custom-call(s32[4]{0:T(128)S(1)} %copy-done.3, s32[2]{0:T(128)S(1)} %dynamic_slice.13.blocks, s32[1]{0:T(128)} %copy.19.length, bf16[32,2048]{1,0:T(8,128)(2,1)S(1)} %get-tuple-element.16.low_ref, bf16[16,144,128]{2,1,0:T(8,128)(2,1)S(1)} %all-to-all-done.2.m_ref), custom_call_target="tpu_custom_call" | custom-call | tf_op jit(solution)/shard_map/combine_high/pallas_call | solution.py:358
  (47 shorter events, 1.5 us)
Async XLA Ops:
  0.6 0.9 %copy-start.1 = (bf16[1,2,64,512]{3,2,1,0:T(8,128)(2,1)S(1)}, bf16[1,2,64,512]{3,2,1,0:T(8,128)(2,1)}, u32[]{:S(2)}) copy-start(bf16[1,2,64,512]{3,2,1,0:T(8,128)(2,1)} %param.6) | copy-start | bytes 393220
  1.5 0.7 copy-start.2
  2.8 16.5 %collective-permute-start = (bf16[128,128]{1,0:T(8,128)(2,1)S(1)}, bf16[128,128]{1,0:T(8,128)(2,1)S(1)}, u32[]{:S(2)}, u32[]{:S(2)}) collective-permute-start(bf16[128,128]{1,0:T(8,128)(2,1)S(1)} %get-tuple-element.12), channel_id=1, source_target_pairs={{0,1},{1,0},{2,3},{3,2},{4,5},{5,4},{6,7},{7,6},{8,9},{9,8},{10,11... | collective-permute-start | bytes 98312 | tf_op jit(solution)/shard_map/ppermute | solution.py:254
  5.0 14.3 %collective-permute-start.1 = (bf16[128,128]{1,0:T(8,128)(2,1)S(1)}, bf16[128,128]{1,0:T(8,128)(2,1)S(1)}, u32[]{:S(2)}, u32[]{:S(2)}) collective-permute-start(bf16[128,128]{1,0:T(8,128)(2,1)S(1)} %get-tuple-element.13), channel_id=1, source_target_pairs={{0,2},{1,3},{2,0},{3,1},{4,6},{5,7},{6,4},{7,5},{8,10},{9,11},{10,... | collective-permute-start | bytes 98312 | tf_op jit(solution)/shard_map/ppermute | solution.py:254
  5.9 13.5 %collective-permute-start.2 = (bf16[128,128]{1,0:T(8,128)(2,1)S(1)}, bf16[128,128]{1,0:T(8,128)(2,1)S(1)}, u32[]{:S(2)}, u32[]{:S(2)}) collective-permute-start(bf16[128,128]{1,0:T(8,128)(2,1)S(1)} %get-tuple-element.14), channel_id=1, source_target_pairs={{0,3},{1,2},{2,1},{3,0},{4,7},{5,6},{6,5},{7,4},{8,11},{9,10},{10,... | collective-permute-start | bytes 98312 | tf_op jit(solution)/shard_map/ppermute | solution.py:254
  6.6 0.9 %copy-start = (bf16[1,64,2048]{2,1,0:T(8,128)(2,1)S(1)}, bf16[1,64,2048]{2,1,0:T(8,128)(2,1)}, u32[]{:S(2)}) copy-start(bf16[1,64,2048]{2,1,0:T(8,128)(2,1)} %param.5) | copy-start | bytes 786436
  9.2 8.3 %copy-start.6 = (s32[256]{0:T(256)S(1)}, s32[256]{0:T(256)}, u32[]{:S(2)}) copy-start(s32[256]{0:T(256)} %param.8) | copy-start | bytes 3076
  9.2 38.4 %all-to-all-start = ((bf16[16,256,128]{2,1,0:T(8,128)(2,1)}), bf16[16,256,128]{2,1,0:T(8,128)(2,1)S(1)}, u32[]{:S(2)}, u32[]{:S(2)}) async-start(bf16[16,256,128]{2,1,0:T(8,128)(2,1)} %split_q.1), calls=%async_computation | async-start | bytes 2097152 | tf_op jit(solution)/shard_map/all_to_all | solution.py:260
  19.4 8.5 %collective-permute-start.6 = (bf16[512,128]{1,0:T(8,128)(2,1)S(1)}, bf16[512,128]{1,0:T(8,128)(2,1)S(1)}, u32[]{:S(2)}, u32[]{:S(2)}) collective-permute-start(bf16[512,128]{1,0:T(8,128)(2,1)S(1)} %constant_dynamic-update-slice_fusion.refs_0_), channel_id=1, source_target_pairs={{0,112},{1,113},{2,114},{3,115},{4,116},{5,117},{6,118},{7,119},{8... | collective-permute-start | bytes 393224 | tf_op jit(solution)/shard_map/ppermute | solution.py:254
  25.3 6.2 %collective-permute-start.3 = (bf16[512,128]{1,0:T(8,128)(2,1)S(1)}, bf16[512,128]{1,0:T(8,128)(2,1)S(1)}, u32[]{:S(2)}, u32[]{:S(2)}) collective-permute-start(bf16[512,128]{1,0:T(8,128)(2,1)S(1)} %constant_dynamic-update-slice_fusion.refs_0_), channel_id=1, source_target_pairs={{0,16},{1,17},{2,18},{3,19},{4,20},{5,21},{6,22},{7,23},{8,24},{9,... | collective-permute-start | bytes 393224 | tf_op jit(solution)/shard_map/ppermute | solution.py:254
  27.8 9.8 %collective-permute-start.7 = (bf16[512,128]{1,0:T(8,128)(2,1)S(1)}, bf16[512,128]{1,0:T(8,128)(2,1)S(1)}, u32[]{:S(2)}, u32[]{:S(2)}) collective-permute-start(bf16[512,128]{1,0:T(8,128)(2,1)S(1)} %collective-permute-done.6.refs_4_), channel_id=1, source_target_pairs={{0,112},{1,113},{2,114},{3,115},{4,116},{5,117},{6,118},{7,119},{8... | collective-permute-start | bytes 393224 | tf_op jit(solution)/shard_map/ppermute | solution.py:254
  31.5 6.2 %collective-permute-start.4 = (bf16[512,128]{1,0:T(8,128)(2,1)S(1)}, bf16[512,128]{1,0:T(8,128)(2,1)S(1)}, u32[]{:S(2)}, u32[]{:S(2)}) collective-permute-start(bf16[512,128]{1,0:T(8,128)(2,1)S(1)} %collective-permute-done.3.refs_1_), channel_id=1, source_target_pairs={{0,16},{1,17},{2,18},{3,19},{4,20},{5,21},{6,22},{7,23},{8,24},{9,... | collective-permute-start | bytes 393224 | tf_op jit(solution)/shard_map/ppermute | solution.py:254
  37.7 9.9 %collective-permute-start.5 = (bf16[512,128]{1,0:T(8,128)(2,1)S(1)}, bf16[512,128]{1,0:T(8,128)(2,1)S(1)}, u32[]{:S(2)}, u32[]{:S(2)}) collective-permute-start(bf16[512,128]{1,0:T(8,128)(2,1)S(1)} %collective-permute-done.4.refs_2_), channel_id=1, source_target_pairs={{0,16},{1,17},{2,18},{3,19},{4,20},{5,21},{6,22},{7,23},{8,24},{9,... | collective-permute-start | bytes 393224 | tf_op jit(solution)/shard_map/ppermute | solution.py:254
  37.7 9.9 %collective-permute-start.8 = (bf16[512,128]{1,0:T(8,128)(2,1)S(1)}, bf16[512,128]{1,0:T(8,128)(2,1)S(1)}, u32[]{:S(2)}, u32[]{:S(2)}) collective-permute-start(bf16[512,128]{1,0:T(8,128)(2,1)S(1)} %collective-permute-done.7.refs_5_), channel_id=1, source_target_pairs={{0,112},{1,113},{2,114},{3,115},{4,116},{5,117},{6,118},{7,119},{8... | collective-permute-start | bytes 393224 | tf_op jit(solution)/shard_map/ppermute | solution.py:254
  41.0 5.2 %collective-permute-start.10 = (bf16[256,128]{1,0:T(8,128)(2,1)S(1)}, bf16[256,128]{1,0:T(8,128)(2,1)S(1)}, u32[]{:S(2)}, u32[]{:S(2)}) collective-permute-start(bf16[256,128]{1,0:T(8,128)(2,1)S(1)} %slice.17), channel_id=1, source_target_pairs={{0,96},{1,97},{2,98},{3,99},{4,100},{5,101},{6,102},{7,103},{8,104... | collective-permute-start | bytes 196616 | tf_op jit(solution)/shard_map/ppermute | solution.py:254
  41.1 6.6 %collective-permute-start.9 = (bf16[256,128]{1,0:T(8,128)(2,1)S(1)}, bf16[256,128]{1,0:T(8,128)(2,1)S(1)}, u32[]{:S(2)}, u32[]{:S(2)}) collective-permute-start(bf16[256,128]{1,0:T(8,128)(2,1)S(1)} %slice.16), channel_id=1, source_target_pairs={{0,32},{1,33},{2,34},{3,35},{4,36},{5,37},{6,38},{7,39},{8,40},{9,... | collective-permute-start | bytes 196616 | tf_op jit(solution)/shard_map/ppermute | solution.py:254
  53.2 0.8 copy-start.4
  54.0 19.5 %all-to-all-start.1 = ((bf16[16,272,128]{2,1,0:T(8,128)(2,1)}), bf16[16,272,128]{2,1,0:T(8,128)(2,1)S(1)}, u32[]{:S(2)}, u32[]{:S(2)}) async-start(bf16[16,272,128]{2,1,0:T(8,128)(2,1)} %get-tuple-element.15), calls=%async_computation.1 | async-start | bytes 2228224 | tf_op jit(solution)/shard_map/all_to_all | solution.py:260
  61.4 1.0 %copy-start.5 = (bf16[128,2048]{1,0:T(8,128)(2,1)S(1)}, bf16[128,2048]{1,0:T(8,128)(2,1)}, u32[]{:S(2)}) copy-start(bf16[128,2048]{1,0:T(8,128)(2,1)} %copy-done.4) | copy-start | bytes 1572868
  69.6 9.6 %copy-start.3 = (s32[4]{0:T(128)S(1)}, s32[4]{0:T(128)}, u32[]{:S(2)}) copy-start(s32[4]{0:T(128)} %heads.7) | copy-start | bytes 52
  73.4 14.0 %all-to-all-start.2 = ((bf16[16,144,128]{2,1,0:T(8,128)(2,1)}), bf16[16,144,128]{2,1,0:T(8,128)(2,1)S(1)}, u32[]{:S(2)}, u32[]{:S(2)}) async-start(bf16[16,144,128]{2,1,0:T(8,128)(2,1)} %high.1), calls=%async_computation.2 | async-start | bytes 1179648 | tf_op jit(solution)/shard_map/all_to_all | solution.py:260

commit v11 on v5

--- a/solution.py
+++ b/solution.py
@@ -240,7 +240,6 @@
         out_shape=(jax.ShapeDtypeStruct((128, HEAD), jnp.bfloat16),) * NY,
         in_specs=[SMEM, VMEM],
         out_specs=(VMEM,) * NY,
-        compiler_params=SMALL,
         name="split_kv",
     )(segment_head, rotated_key_value.reshape(128, KEY_VALUE_HEADS * HEAD))
     line = [kv[0]] + [move(kv[k], lambda a, b, c, k=k: index(a, b, c ^ k)) for k in range(1, NY)]
@@ -260,7 +259,8 @@
     r2, l2 = right(r1), left(l1)
     r3, l3 = right(r2), left(l2)
     half = own.shape[0] // 2
-    r4, l4 = right(r3[:half]), left(l3[half:])
+    r4 = move(r2[:half], lambda a, b, c: index(a + 2, b, c))
+    l4 = move(l2[half:], lambda a, b, c: index(a - 2, b, c))
 
     ids = block_map.reshape(NZ, NX, NY, 2).transpose(1, 0, 2, 3).reshape(NX, KEY_BLOCKS)
     rank = ranks(ids)

time: 87.9 us -> 86.5 us (0.984)
  waiting for transfers between devices: 20.2 us -> 17.6 us
  starting transfers between devices: 43.3 us -> 44.6 us
  local copies, waits for them, and re-layouts: 4.5 us -> 3.61 us
    ppermute x15, waiting for transfers between devices: 20.2 us -> 17.6 us  [move(): lax.ppermute(value, 'blk', [(s, target(s // 16, s // 4 % 4, s % 4)) for s...]
    all_to_all x2, starting transfers between devices: 15.6 us -> 17.2 us  [exchange(): lax.all_to_all(value, 'blk', 0, 0, axis_index_groups=groups, tiled=True)]
    pallas_call x1, Pallas kernels: 0.58 us -> 1.59 us  [body(): pl.pallas_call(split_kv_kernel, out_shape=(jax.ShapeDtypeStruct((128, HEA...]
    unnamed x13, local copies, waits for them, and re-layouts: 2.54 us -> 1.64 us
  transfers between devices with their start and end apart: 17 -> 17, of which waited for: 8 -> 6; matrix products, arithmetic and copies ran while one was open for 4% -> 4% of each run, Pallas kernels for 16% -> 16%
where the time goes in v11:
time: 86.5 us; the launch traced here: 86.2 us
  starting transfers between devices  44.6 us (52%)
  waiting for transfers between devices  17.6 us (20%)
  Pallas kernels  17.3 us (20%)
  local copies, waits for them, and re-layouts  3.61 us (4%)
  between operations  1.54 us (2%)
  other arithmetic  1.27 us (1%)
    ppermute x15, starting transfers between devices, move(): lax.ppermute(value, 'blk', [(s, target(s // 16, s // 4 % 4, s % 4)) for s...  27.4 us
    ppermute x15, waiting for transfers between devices, move(): lax.ppermute(value, 'blk', [(s, target(s // 16, s // 4 % 4, s % 4)) for s...  17.6 us
    all_to_all x2, starting transfers between devices, exchange(): lax.all_to_all(value, 'blk', 0, 0, axis_index_groups=groups, tiled=True)  17.2 us
    pallas_call x1, Pallas kernels, body(): pl.pallas_call(attention_kernel, out_shape=jax.ShapeDtypeStruct((PLANE, M...  11.6 us
    pallas_call x1, Pallas kernels, body(): pl.pallas_call(combine_kernel, out_shape=jax.ShapeDtypeStruct((2 * BLOCK,...  2.08 us
  transfers between devices with their start and end apart: 17, of which 6 were waited for; matrix products, arithmetic and copies ran while one was open for 4% of the time, Pallas kernels for 16%

profile of v11, /device:TPU:8, one launch (start us, length us, event | category | flops | bytes accessed | tf_op | source)
XLA Modules:
  0.0 86.2 jit_solution(2964931815973105477)
XLA Ops:
  0.6 1.6 %split_kv.1 = (bf16[128,128]{1,0:T(8,128)(2,1)}, bf16[128,128]{1,0:T(8,128)(2,1)}, bf16[128,128]{1,0:T(8,128)(2,1)}, bf16[128,128]{1,0:T(8,128)(2,1)}) custom-call(s32[4]{0:T(128)} %heads.5, bf16[128,512]{1,0:T(8,128)(2,1)} %bitcast.29), custom_call_target="tpu_custom_call" | custom-call | tf_op jit(solution)/shard_map/split_kv/pallas_call | solution.py:238
  2.2 2.2 %collective-permute-start = (bf16[128,128]{1,0:T(8,128)(2,1)}, bf16[128,128]{1,0:T(8,128)(2,1)S(1)}, u32[]{:S(2)}, u32[]{:S(2)}) collective-permute-start(bf16[128,128]{1,0:T(8,128)(2,1)} %get-tuple-element.9), channel_id=1, source_target_pairs={{0,1},{1,0},{2,3},{3,2},{4,5},{5,4},{6,7},{7,6},{8,9},{9,8},{10,11... | collective-permute-start | bytes 98312 | tf_op jit(solution)/shard_map/ppermute | solution.py:230
  4.4 0.9 collective-permute-start.1
  5.3 0.6 collective-permute-start.2
  5.9 0.9 %copy-done = bf16[1,64,2048]{2,1,0:T(8,128)(2,1)S(1)} copy-done((bf16[1,64,2048]{2,1,0:T(8,128)(2,1)S(1)}, bf16[1,64,2048]{2,1,0:T(8,128)(2,1)}, u32[]{:S(2)}) %copy-start) | copy-done | bytes 262168
  6.8 0.7 copy-done.1
  7.5 1.7 %split_q.1 = bf16[16,256,128]{2,1,0:T(8,128)(2,1)} custom-call(s32[4]{0:T(128)S(1)} %copy-done.1, bf16[64,2048]{1,0:T(8,128)(2,1)S(1)} %bitcast.25), custom_call_target="tpu_custom_call" | custom-call | tf_op jit(solution)/shard_map/split_q/pallas_call | solution.py:250
  9.2 8.4 %all-to-all-start = ((bf16[16,256,128]{2,1,0:T(8,128)(2,1)}), bf16[16,256,128]{2,1,0:T(8,128)(2,1)S(1)}, u32[]{:S(2)}, u32[]{:S(2)}) async-start(bf16[16,256,128]{2,1,0:T(8,128)(2,1)} %split_q.1), calls=%async_computation | async-start | bytes 2097152 | tf_op jit(solution)/shard_map/all_to_all | solution.py:236
  17.7 0.3 copy.12
  18.1 0.2 convert_reduce_fusion
  19.4 5.9 %collective-permute-start.6 = (bf16[512,128]{1,0:T(8,128)(2,1)S(1)}, bf16[512,128]{1,0:T(8,128)(2,1)S(1)}, u32[]{:S(2)}, u32[]{:S(2)}) collective-permute-start(bf16[512,128]{1,0:T(8,128)(2,1)S(1)} %constant_dynamic-update-slice_fusion.refs_0_), channel_id=1, source_target_pairs={{0,112},{1,113},{2,114},{3,115},{4,116},{5,117},{6,118},{7,119},{8... | collective-permute-start | bytes 393224 | tf_op jit(solution)/shard_map/ppermute | solution.py:230
  25.4 2.5 %collective-permute-done.6.refs_4_ = bf16[512,128]{1,0:T(8,128)(2,1)S(1)} collective-permute-done((bf16[512,128]{1,0:T(8,128)(2,1)S(1)}, bf16[512,128]{1,0:T(8,128)(2,1)S(1)}, u32[]{:S(2)}, u32[]{:S(2)}) %collective-permute-start.6) | collective-permute-done | bytes 131104 | tf_op jit(solution)/shard_map/ppermute | solution.py:230
  27.9 3.7 %collective-permute-start.7 = (bf16[512,128]{1,0:T(8,128)(2,1)S(1)}, bf16[512,128]{1,0:T(8,128)(2,1)S(1)}, u32[]{:S(2)}, u32[]{:S(2)}) collective-permute-start(bf16[512,128]{1,0:T(8,128)(2,1)S(1)} %collective-permute-done.6.refs_4_), channel_id=1, source_target_pairs={{0,112},{1,113},{2,114},{3,115},{4,116},{5,117},{6,118},{7,119},{8... | collective-permute-start | bytes 393224 | tf_op jit(solution)/shard_map/ppermute | solution.py:230
  31.6 0.2 slice_reduce_fusion
  31.7 0.2 convert_reduce_fusion.2
  32.0 5.8 %collective-permute-done.4.refs_2_ = bf16[512,128]{1,0:T(8,128)(2,1)S(1)} collective-permute-done((bf16[512,128]{1,0:T(8,128)(2,1)S(1)}, bf16[512,128]{1,0:T(8,128)(2,1)S(1)}, u32[]{:S(2)}, u32[]{:S(2)}) %collective-permute-start.4) | collective-permute-done | bytes 131104 | tf_op jit(solution)/shard_map/ppermute | solution.py:230
  37.7 3.2 %collective-permute-start.8 = (bf16[512,128]{1,0:T(8,128)(2,1)S(1)}, bf16[512,128]{1,0:T(8,128)(2,1)S(1)}, u32[]{:S(2)}, u32[]{:S(2)}) collective-permute-start(bf16[512,128]{1,0:T(8,128)(2,1)S(1)} %collective-permute-done.7.refs_5_), channel_id=1, source_target_pairs={{0,112},{1,113},{2,114},{3,115},{4,116},{5,117},{6,118},{7,119},{8... | collective-permute-start | bytes 393224 | tf_op jit(solution)/shard_map/ppermute | solution.py:230
  41.1 2.9 %collective-permute-start.9 = (bf16[256,128]{1,0:T(8,128)(2,1)S(1)}, bf16[256,128]{1,0:T(8,128)(2,1)S(1)}, u32[]{:S(2)}, u32[]{:S(2)}) collective-permute-start(bf16[256,128]{1,0:T(8,128)(2,1)S(1)} %slice.32), channel_id=1, source_target_pairs={{0,32},{1,33},{2,34},{3,35},{4,36},{5,37},{6,38},{7,39},{8,40},{9,... | collective-permute-start | bytes 196616 | tf_op jit(solution)/shard_map/ppermute | solution.py:230
  44.1 2.1 %collective-permute-done.10.refs_8_ = bf16[256,128]{1,0:T(8,128)(2,1)S(1)} collective-permute-done((bf16[256,128]{1,0:T(8,128)(2,1)S(1)}, bf16[256,128]{1,0:T(8,128)(2,1)S(1)}, u32[]{:S(2)}, u32[]{:S(2)}) %collective-permute-start.10) | collective-permute-done | bytes 65568 | tf_op jit(solution)/shard_map/ppermute | solution.py:230
  46.2 1.4 %collective-permute-done.9.refs_7_ = bf16[256,128]{1,0:T(8,128)(2,1)S(1)} collective-permute-done((bf16[256,128]{1,0:T(8,128)(2,1)S(1)}, bf16[256,128]{1,0:T(8,128)(2,1)S(1)}, u32[]{:S(2)}, u32[]{:S(2)}) %collective-permute-start.9) | collective-permute-done | bytes 65568 | tf_op jit(solution)/shard_map/ppermute | solution.py:230
  47.7 0.3 pick.1
  48.0 3.2 %collective-permute-start.11 = (bf16[4,64,256]{2,1,0:T(8,128)(2,1)S(1)}, bf16[4,64,256]{2,1,0:T(8,128)(2,1)S(1)}, u32[]{:S(2)}, u32[]{:S(2)}) collective-permute-start(bf16[4,64,256]{2,1,0:T(8,128)(2,1)S(1)} %pick.1), channel_id=1, source_target_pairs={{0,0},{1,32},{2,64},{3,96},{4,4},{5,36},{6,68},{7,100},{8,8},{9,40... | collective-permute-start | bytes 393224 | tf_op jit(solution)/shard_map/ppermute | solution.py:230
  51.2 11.6 %attention.1 = bf16[16,272,128]{2,1,0:T(8,128)(2,1)} custom-call(s32[144]{0:T(256)S(1)} %concatenate.9.table, bf16[32,128,128]{2,1,0:T(8,128)(2,1)S(1)} %bitcast.24, s32[8,256]{1,0:T(8,128)S(1)} %broadcast_add_fusion.kpos_ref, bf16[512,128]{1,0:T(8,128)(2,1)S(1)} %constant_dynamic-update-slice_fusion.refs_0_, ...), custom_call_target="tpu_custom_call" | custom-call | flops 3000000000 | bytes 4000000 | tf_op jit(solution)/shard_map/attention/pallas_call | solution.py:293
  62.8 8.8 %all-to-all-start.1 = ((bf16[16,272,128]{2,1,0:T(8,128)(2,1)}), bf16[16,272,128]{2,1,0:T(8,128)(2,1)S(1)}, u32[]{:S(2)}, u32[]{:S(2)}) async-start(bf16[16,272,128]{2,1,0:T(8,128)(2,1)} %attention.1), calls=%async_computation.1 | async-start | bytes 2228224 | tf_op jit(solution)/shard_map/all_to_all | solution.py:236
  72.4 1.6 %collective-permute-start.12 = (bf16[64,256]{1,0:T(8,128)(2,1)S(1)}, bf16[64,256]{1,0:T(8,128)(2,1)S(1)}, u32[]{:S(2)}, u32[]{:S(2)}) collective-permute-start(bf16[64,256]{1,0:T(8,128)(2,1)S(1)} %get-tuple-element.23), channel_id=1, source_target_pairs={{0,4},{1,5},{2,6},{3,7},{4,0},{5,1},{6,2},{7,3},{8,12},{9,13},{10,... | collective-permute-start | bytes 98312 | tf_op jit(solution)/shard_map/ppermute | solution.py:230
  74.0 2.7 %collective-permute-start.13 = (bf16[64,256]{1,0:T(8,128)(2,1)S(1)}, bf16[64,256]{1,0:T(8,128)(2,1)S(1)}, u32[]{:S(2)}, u32[]{:S(2)}) collective-permute-start(bf16[64,256]{1,0:T(8,128)(2,1)S(1)} %get-tuple-element.22), channel_id=1, source_target_pairs={{0,8},{1,9},{2,10},{3,11},{4,12},{5,13},{6,14},{7,15},{8,0},{9,1},... | collective-permute-start | bytes 98312 | tf_op jit(solution)/shard_map/ppermute | solution.py:230
  76.7 0.6 collective-permute-start.14
  77.3 3.8 %collective-permute-done.12 = bf16[64,256]{1,0:T(8,128)(2,1)S(1)} collective-permute-done((bf16[64,256]{1,0:T(8,128)(2,1)S(1)}, bf16[64,256]{1,0:T(8,128)(2,1)S(1)}, u32[]{:S(2)}, u32[]{:S(2)}) %collective-permute-start.12) | collective-permute-done | bytes 32800 | tf_op jit(solution)/shard_map/ppermute | solution.py:230
  81.1 1.9 %collective-permute-done.13 = bf16[64,256]{1,0:T(8,128)(2,1)S(1)} collective-permute-done((bf16[64,256]{1,0:T(8,128)(2,1)S(1)}, bf16[64,256]{1,0:T(8,128)(2,1)S(1)}, u32[]{:S(2)}, u32[]{:S(2)}) %collective-permute-start.13) | collective-permute-done | bytes 32800 | tf_op jit(solution)/shard_map/ppermute | solution.py:230
  83.0 0.3 convolution_convert_fusion
  83.3 0.8 copy.15
  84.1 2.1 %combine.1 = bf16[64,2048]{1,0:T(8,128)(2,1)} custom-call(s32[4]{0:T(128)S(1)} %copy-done.2, s32[2]{0:T(128)S(1)} %dynamic_slice.13.blocks, s32[1]{0:T(128)} %copy.19.length, bf16[16,272,128]{2,1,0:T(8,128)(2,1)S(1)} %all-to-all-done.1.m_ref), custom_call_target="tpu_custom_call" | custom-call | tf_op jit(solution)/shard_map/combine/pallas_call | solution.py:326
  (51 shorter events, 1.7 us)
Async XLA Ops:
  2.2 17.1 %collective-permute-start = (bf16[128,128]{1,0:T(8,128)(2,1)}, bf16[128,128]{1,0:T(8,128)(2,1)S(1)}, u32[]{:S(2)}, u32[]{:S(2)}) collective-permute-start(bf16[128,128]{1,0:T(8,128)(2,1)} %get-tuple-element.9), channel_id=1, source_target_pairs={{0,1},{1,0},{2,3},{3,2},{4,5},{5,4},{6,7},{7,6},{8,9},{9,8},{10,11... | collective-permute-start | bytes 98312 | tf_op jit(solution)/shard_map/ppermute | solution.py:230
  4.4 15.0 %collective-permute-start.1 = (bf16[128,128]{1,0:T(8,128)(2,1)}, bf16[128,128]{1,0:T(8,128)(2,1)S(1)}, u32[]{:S(2)}, u32[]{:S(2)}) collective-permute-start(bf16[128,128]{1,0:T(8,128)(2,1)} %get-tuple-element.10), channel_id=1, source_target_pairs={{0,2},{1,3},{2,0},{3,1},{4,6},{5,7},{6,4},{7,5},{8,10},{9,11},{10,... | collective-permute-start | bytes 98312 | tf_op jit(solution)/shard_map/ppermute | solution.py:230
  5.3 14.2 %collective-permute-start.2 = (bf16[128,128]{1,0:T(8,128)(2,1)}, bf16[128,128]{1,0:T(8,128)(2,1)S(1)}, u32[]{:S(2)}, u32[]{:S(2)}) collective-permute-start(bf16[128,128]{1,0:T(8,128)(2,1)} %get-tuple-element.11), channel_id=1, source_target_pairs={{0,3},{1,2},{2,1},{3,0},{4,7},{5,6},{6,5},{7,4},{8,11},{9,10},{10,... | collective-permute-start | bytes 98312 | tf_op jit(solution)/shard_map/ppermute | solution.py:230
  5.9 0.9 %copy-start = (bf16[1,64,2048]{2,1,0:T(8,128)(2,1)S(1)}, bf16[1,64,2048]{2,1,0:T(8,128)(2,1)}, u32[]{:S(2)}) copy-start(bf16[1,64,2048]{2,1,0:T(8,128)(2,1)} %param.5) | copy-start | bytes 786436
  6.8 0.7 copy-start.1
  9.2 8.4 %copy-start.4 = (s32[256]{0:T(256)S(1)}, s32[256]{0:T(256)}, u32[]{:S(2)}) copy-start(s32[256]{0:T(256)} %param.8) | copy-start | bytes 3076
  9.2 9.6 %copy-start.3 = (bf16[128,128]{1,0:T(8,128)(2,1)S(1)}, bf16[128,128]{1,0:T(8,128)(2,1)}, u32[]{:S(2)}) copy-start(bf16[128,128]{1,0:T(8,128)(2,1)} %get-tuple-element.8) | copy-start | bytes 98308
  9.2 42.0 %all-to-all-start = ((bf16[16,256,128]{2,1,0:T(8,128)(2,1)}), bf16[16,256,128]{2,1,0:T(8,128)(2,1)S(1)}, u32[]{:S(2)}, u32[]{:S(2)}) async-start(bf16[16,256,128]{2,1,0:T(8,128)(2,1)} %split_q.1), calls=%async_computation | async-start | bytes 2097152 | tf_op jit(solution)/shard_map/all_to_all | solution.py:236
  19.4 8.5 %collective-permute-start.6 = (bf16[512,128]{1,0:T(8,128)(2,1)S(1)}, bf16[512,128]{1,0:T(8,128)(2,1)S(1)}, u32[]{:S(2)}, u32[]{:S(2)}) collective-permute-start(bf16[512,128]{1,0:T(8,128)(2,1)S(1)} %constant_dynamic-update-slice_fusion.refs_0_), channel_id=1, source_target_pairs={{0,112},{1,113},{2,114},{3,115},{4,116},{5,117},{6,118},{7,119},{8... | collective-permute-start | bytes 393224 | tf_op jit(solution)/shard_map/ppermute | solution.py:230
  25.4 6.2 %collective-permute-start.3 = (bf16[512,128]{1,0:T(8,128)(2,1)S(1)}, bf16[512,128]{1,0:T(8,128)(2,1)S(1)}, u32[]{:S(2)}, u32[]{:S(2)}) collective-permute-start(bf16[512,128]{1,0:T(8,128)(2,1)S(1)} %constant_dynamic-update-slice_fusion.refs_0_), channel_id=1, source_target_pairs={{0,16},{1,17},{2,18},{3,19},{4,20},{5,21},{6,22},{7,23},{8,24},{9,... | collective-permute-start | bytes 393224 | tf_op jit(solution)/shard_map/ppermute | solution.py:230
  27.9 9.8 %collective-permute-start.7 = (bf16[512,128]{1,0:T(8,128)(2,1)S(1)}, bf16[512,128]{1,0:T(8,128)(2,1)S(1)}, u32[]{:S(2)}, u32[]{:S(2)}) collective-permute-start(bf16[512,128]{1,0:T(8,128)(2,1)S(1)} %collective-permute-done.6.refs_4_), channel_id=1, source_target_pairs={{0,112},{1,113},{2,114},{3,115},{4,116},{5,117},{6,118},{7,119},{8... | collective-permute-start | bytes 393224 | tf_op jit(solution)/shard_map/ppermute | solution.py:230
  31.6 6.2 %collective-permute-start.4 = (bf16[512,128]{1,0:T(8,128)(2,1)S(1)}, bf16[512,128]{1,0:T(8,128)(2,1)S(1)}, u32[]{:S(2)}, u32[]{:S(2)}) collective-permute-start(bf16[512,128]{1,0:T(8,128)(2,1)S(1)} %collective-permute-done.3.refs_1_), channel_id=1, source_target_pairs={{0,16},{1,17},{2,18},{3,19},{4,20},{5,21},{6,22},{7,23},{8,24},{9,... | collective-permute-start | bytes 393224 | tf_op jit(solution)/shard_map/ppermute | solution.py:230
  37.7 9.9 %collective-permute-start.5 = (bf16[512,128]{1,0:T(8,128)(2,1)S(1)}, bf16[512,128]{1,0:T(8,128)(2,1)S(1)}, u32[]{:S(2)}, u32[]{:S(2)}) collective-permute-start(bf16[512,128]{1,0:T(8,128)(2,1)S(1)} %collective-permute-done.4.refs_2_), channel_id=1, source_target_pairs={{0,16},{1,17},{2,18},{3,19},{4,20},{5,21},{6,22},{7,23},{8,24},{9,... | collective-permute-start | bytes 393224 | tf_op jit(solution)/shard_map/ppermute | solution.py:230
  37.7 9.9 %collective-permute-start.8 = (bf16[512,128]{1,0:T(8,128)(2,1)S(1)}, bf16[512,128]{1,0:T(8,128)(2,1)S(1)}, u32[]{:S(2)}, u32[]{:S(2)}) collective-permute-start(bf16[512,128]{1,0:T(8,128)(2,1)S(1)} %collective-permute-done.7.refs_5_), channel_id=1, source_target_pairs={{0,112},{1,113},{2,114},{3,115},{4,116},{5,117},{6,118},{7,119},{8... | collective-permute-start | bytes 393224 | tf_op jit(solution)/shard_map/ppermute | solution.py:230
  41.0 5.2 %collective-permute-start.10 = (bf16[256,128]{1,0:T(8,128)(2,1)S(1)}, bf16[256,128]{1,0:T(8,128)(2,1)S(1)}, u32[]{:S(2)}, u32[]{:S(2)}) collective-permute-start(bf16[256,128]{1,0:T(8,128)(2,1)S(1)} %slice.33), channel_id=1, source_target_pairs={{0,96},{1,97},{2,98},{3,99},{4,100},{5,101},{6,102},{7,103},{8,104... | collective-permute-start | bytes 196616 | tf_op jit(solution)/shard_map/ppermute | solution.py:230
  41.1 6.6 %collective-permute-start.9 = (bf16[256,128]{1,0:T(8,128)(2,1)S(1)}, bf16[256,128]{1,0:T(8,128)(2,1)S(1)}, u32[]{:S(2)}, u32[]{:S(2)}) collective-permute-start(bf16[256,128]{1,0:T(8,128)(2,1)S(1)} %slice.32), channel_id=1, source_target_pairs={{0,32},{1,33},{2,34},{3,35},{4,36},{5,37},{6,38},{7,39},{8,40},{9,... | collective-permute-start | bytes 196616 | tf_op jit(solution)/shard_map/ppermute | solution.py:230
  48.0 14.8 %collective-permute-start.11 = (bf16[4,64,256]{2,1,0:T(8,128)(2,1)S(1)}, bf16[4,64,256]{2,1,0:T(8,128)(2,1)S(1)}, u32[]{:S(2)}, u32[]{:S(2)}) collective-permute-start(bf16[4,64,256]{2,1,0:T(8,128)(2,1)S(1)} %pick.1), channel_id=1, source_target_pairs={{0,0},{1,32},{2,64},{3,96},{4,4},{5,36},{6,68},{7,100},{8,8},{9,40... | collective-permute-start | bytes 393224 | tf_op jit(solution)/shard_map/ppermute | solution.py:230
  62.8 21.3 %all-to-all-start.1 = ((bf16[16,272,128]{2,1,0:T(8,128)(2,1)}), bf16[16,272,128]{2,1,0:T(8,128)(2,1)S(1)}, u32[]{:S(2)}, u32[]{:S(2)}) async-start(bf16[16,272,128]{2,1,0:T(8,128)(2,1)} %attention.1), calls=%async_computation.1 | async-start | bytes 2228224 | tf_op jit(solution)/shard_map/all_to_all | solution.py:236
  71.6 12.5 %copy-start.2 = (s32[4]{0:T(128)S(1)}, s32[4]{0:T(128)}, u32[]{:S(2)}) copy-start(s32[4]{0:T(128)} %heads.5) | copy-start | bytes 52
  72.4 8.7 %collective-permute-start.12 = (bf16[64,256]{1,0:T(8,128)(2,1)S(1)}, bf16[64,256]{1,0:T(8,128)(2,1)S(1)}, u32[]{:S(2)}, u32[]{:S(2)}) collective-permute-start(bf16[64,256]{1,0:T(8,128)(2,1)S(1)} %get-tuple-element.23), channel_id=1, source_target_pairs={{0,4},{1,5},{2,6},{3,7},{4,0},{5,1},{6,2},{7,3},{8,12},{9,13},{10,... | collective-permute-start | bytes 98312 | tf_op jit(solution)/shard_map/ppermute | solution.py:230
  74.0 9.0 %collective-permute-start.13 = (bf16[64,256]{1,0:T(8,128)(2,1)S(1)}, bf16[64,256]{1,0:T(8,128)(2,1)S(1)}, u32[]{:S(2)}, u32[]{:S(2)}) collective-permute-start(bf16[64,256]{1,0:T(8,128)(2,1)S(1)} %get-tuple-element.22), channel_id=1, source_target_pairs={{0,8},{1,9},{2,10},{3,11},{4,12},{5,13},{6,14},{7,15},{8,0},{9,1},... | collective-permute-start | bytes 98312 | tf_op jit(solution)/shard_map/ppermute | solution.py:230
  76.7 6.3 %collective-permute-start.14 = (bf16[64,256]{1,0:T(8,128)(2,1)S(1)}, bf16[64,256]{1,0:T(8,128)(2,1)S(1)}, u32[]{:S(2)}, u32[]{:S(2)}) collective-permute-start(bf16[64,256]{1,0:T(8,128)(2,1)S(1)} %get-tuple-element.21), channel_id=1, source_target_pairs={{0,12},{1,13},{2,14},{3,15},{4,8},{5,9},{6,10},{7,11},{8,4},{9,5},... | collective-permute-start | bytes 98312 | tf_op jit(solution)/shard_map/ppermute | solution.py:230

commit v12 on v11

--- a/solution.py
+++ b/solution.py
@@ -180,7 +180,11 @@
         o_ref[d, 2 * ROWS :, :] = rows.astype(jnp.bfloat16)
 
 
-def combine_kernel(heads, blocks, length, m_ref, o_ref):
+def combine_kernel(heads, blocks, length, choose_ref, k0_ref, k1_ref, k2_ref, k3_ref, m_ref, o_ref, cache_ref):
+    found = jnp.concatenate([k0_ref[0], k1_ref[...], k2_ref[...], k3_ref[...]], axis=0)
+    for half in range(2):
+        cache = jnp.dot(choose_ref[...], found[:, half * HEAD : (half + 1) * HEAD], preferred_element_type=jnp.float32)
+        cache_ref[half] = cache.astype(jnp.bfloat16)
     values = []
     for d in range(PLANE):
         rows = m_ref[d, 2 * ROWS :, :].astype(jnp.float32)
@@ -309,9 +313,7 @@
     partial, picked = lax.optimization_barrier((partial, picked))
     out = exchange(partial, planes)
 
-    picked = jnp.concatenate(
-        [picked[0]] + [move(picked[k], lambda a, b, c, k=k: index(a, b ^ k, c)) for k in range(1, NX)], axis=0
-    )
+    kept = [move(picked[k], lambda a, b, c, k=k: index(a, b ^ k, c)) for k in range(1, NX)]
     blocks = jnp.arange(BLOCKS, dtype=jnp.int32)
     stored = jnp.sum(jnp.where(block_map[None, :] == blocks[:, None], blocks[None, :], 0), axis=1, dtype=jnp.int32)
     from_z, from_y = 2 * y + z % 2, z // 2
@@ -319,19 +321,20 @@
     row = row + ((stored // 2 % NY) ^ from_y) * 2 + stored % 2
     position = blocks * BLOCK + place % BLOCK
     choose = (row[:, None] == blocks[None, :]) & (position < lengths[0])[:, None]
-    cache = jnp.dot(choose.astype(jnp.bfloat16), picked, preferred_element_type=jnp.float32).astype(jnp.bfloat16)
-    cache = cache.reshape(BLOCKS, 2, HEAD).transpose(1, 0, 2)[None, :, None]
-
+    choose = choose.astype(jnp.bfloat16)
     my_blocks = lax.dynamic_slice_in_dim(block_map, 2 * place, 2)
-    attended = pl.pallas_call(
+    attended, cache = pl.pallas_call(
         combine_kernel,
-        out_shape=jax.ShapeDtypeStruct((2 * BLOCK, QUERY_HEADS * HEAD), jnp.bfloat16),
-        in_specs=[SMEM] * 3 + [VMEM],
-        out_specs=VMEM,
+        out_shape=(
+            jax.ShapeDtypeStruct((2 * BLOCK, QUERY_HEADS * HEAD), jnp.bfloat16),
+            jax.ShapeDtypeStruct((2, BLOCKS, HEAD), jnp.bfloat16),
+        ),
+        in_specs=[SMEM] * 3 + [VMEM] * 6,
+        out_specs=(VMEM, VMEM),
         compiler_params=SMALL,
         name="combine",
-    )(segment_head, my_blocks, lengths, out)
-    return attended.reshape(1, 2 * BLOCK, QUERY_HEADS * HEAD), cache
+    )(segment_head, my_blocks, lengths, choose, picked, *kept, out)
+    return attended.reshape(1, 2 * BLOCK, QUERY_HEADS * HEAD), cache[None, :, None]
 
 
 def solution(mesh):

time: 86.5 us -> 86.1 us (level)
  transfers between devices with their start and end apart: 17 -> 17, of which waited for: 6 -> 7; matrix products, arithmetic and copies ran while one was open for 4% -> 3% of each run, Pallas kernels for 16% -> 17%
where the time goes in v12:
time: 86.1 us; the launch traced here: 85.5 us
  starting transfers between devices  43.9 us (51%)
  waiting for transfers between devices  18 us (21%)
  Pallas kernels  17.8 us (21%)
  local copies, waits for them, and re-layouts  2.85 us (3%)
  between operations  1.52 us (2%)
  other arithmetic  1.4 us (2%)
    ppermute x15, starting transfers between devices, move(): lax.ppermute(value, 'blk', [(s, target(s // 16, s // 4 % 4, s % 4)) for s...  27.4 us
    ppermute x15, waiting for transfers between devices, move(): lax.ppermute(value, 'blk', [(s, target(s // 16, s // 4 % 4, s % 4)) for s...  17.4 us
    all_to_all x2, starting transfers between devices, exchange(): lax.all_to_all(value, 'blk', 0, 0, axis_index_groups=groups, tiled=True)  16.4 us
    pallas_call x1, Pallas kernels, body(): pl.pallas_call(attention_kernel, out_shape=jax.ShapeDtypeStruct((PLANE, M...  12.1 us
    pallas_call x1, Pallas kernels, body(): pl.pallas_call(combine_kernel, out_shape=(jax.ShapeDtypeStruct((2 * BLOCK...  2.1 us
  transfers between devices with their start and end apart: 17, of which 7 were waited for; matrix products, arithmetic and copies ran while one was open for 3% of the time, Pallas kernels for 17%

profile of v12, /device:TPU:8, one launch (start us, length us, event | category | flops | bytes accessed | tf_op | source)
XLA Modules:
  0.0 85.5 jit_solution(123466408260076808)
XLA Ops:
  0.6 1.6 %split_kv.1 = (bf16[128,128]{1,0:T(8,128)(2,1)}, bf16[128,128]{1,0:T(8,128)(2,1)}, bf16[128,128]{1,0:T(8,128)(2,1)}, bf16[128,128]{1,0:T(8,128)(2,1)}) custom-call(s32[4]{0:T(128)} %heads.5, bf16[128,512]{1,0:T(8,128)(2,1)} %bitcast.25), custom_call_target="tpu_custom_call" | custom-call | tf_op jit(solution)/shard_map/split_kv/pallas_call | solution.py:242
  2.2 2.2 %collective-permute-start = (bf16[128,128]{1,0:T(8,128)(2,1)}, bf16[128,128]{1,0:T(8,128)(2,1)S(1)}, u32[]{:S(2)}, u32[]{:S(2)}) collective-permute-start(bf16[128,128]{1,0:T(8,128)(2,1)} %get-tuple-element.11), channel_id=1, source_target_pairs={{0,1},{1,0},{2,3},{3,2},{4,5},{5,4},{6,7},{7,6},{8,9},{9,8},{10,11... | collective-permute-start | bytes 98312 | tf_op jit(solution)/shard_map/ppermute | solution.py:234
  4.4 0.9 collective-permute-start.1
  5.3 0.6 collective-permute-start.2
  5.9 0.9 %copy-done = bf16[1,64,2048]{2,1,0:T(8,128)(2,1)S(1)} copy-done((bf16[1,64,2048]{2,1,0:T(8,128)(2,1)S(1)}, bf16[1,64,2048]{2,1,0:T(8,128)(2,1)}, u32[]{:S(2)}) %copy-start) | copy-done | bytes 262168
  6.8 0.7 copy-done.1
  7.5 1.7 %split_q.1 = bf16[16,256,128]{2,1,0:T(8,128)(2,1)} custom-call(s32[4]{0:T(128)S(1)} %copy-done.1, bf16[64,2048]{1,0:T(8,128)(2,1)S(1)} %bitcast.22), custom_call_target="tpu_custom_call" | custom-call | tf_op jit(solution)/shard_map/split_q/pallas_call | solution.py:254
  9.2 8.4 %all-to-all-start = ((bf16[16,256,128]{2,1,0:T(8,128)(2,1)}), bf16[16,256,128]{2,1,0:T(8,128)(2,1)S(1)}, u32[]{:S(2)}, u32[]{:S(2)}) async-start(bf16[16,256,128]{2,1,0:T(8,128)(2,1)} %split_q.1), calls=%async_computation | async-start | bytes 2097152 | tf_op jit(solution)/shard_map/all_to_all | solution.py:240
  17.7 0.3 copy.12
  18.1 0.2 convert_reduce_fusion
  18.6 0.2 convert_reduce_fusion.1
  19.4 5.9 %collective-permute-start.6 = (bf16[512,128]{1,0:T(8,128)(2,1)S(1)}, bf16[512,128]{1,0:T(8,128)(2,1)S(1)}, u32[]{:S(2)}, u32[]{:S(2)}) collective-permute-start(bf16[512,128]{1,0:T(8,128)(2,1)S(1)} %constant_dynamic-update-slice_fusion.refs_0_), channel_id=1, source_target_pairs={{0,112},{1,113},{2,114},{3,115},{4,116},{5,117},{6,118},{7,119},{8... | collective-permute-start | bytes 393224 | tf_op jit(solution)/shard_map/ppermute | solution.py:234
  25.4 2.5 %collective-permute-done.6.refs_4_ = bf16[512,128]{1,0:T(8,128)(2,1)S(1)} collective-permute-done((bf16[512,128]{1,0:T(8,128)(2,1)S(1)}, bf16[512,128]{1,0:T(8,128)(2,1)S(1)}, u32[]{:S(2)}, u32[]{:S(2)}) %collective-permute-start.6) | collective-permute-done | bytes 131104 | tf_op jit(solution)/shard_map/ppermute | solution.py:234
  27.9 3.7 %collective-permute-start.7 = (bf16[512,128]{1,0:T(8,128)(2,1)S(1)}, bf16[512,128]{1,0:T(8,128)(2,1)S(1)}, u32[]{:S(2)}, u32[]{:S(2)}) collective-permute-start(bf16[512,128]{1,0:T(8,128)(2,1)S(1)} %collective-permute-done.6.refs_4_), channel_id=1, source_target_pairs={{0,112},{1,113},{2,114},{3,115},{4,116},{5,117},{6,118},{7,119},{8... | collective-permute-start | bytes 393224 | tf_op jit(solution)/shard_map/ppermute | solution.py:234
  31.6 0.2 slice_reduce_fusion
  31.7 0.2 convert_reduce_fusion.2
  32.0 5.8 %collective-permute-done.4.refs_2_ = bf16[512,128]{1,0:T(8,128)(2,1)S(1)} collective-permute-done((bf16[512,128]{1,0:T(8,128)(2,1)S(1)}, bf16[512,128]{1,0:T(8,128)(2,1)S(1)}, u32[]{:S(2)}, u32[]{:S(2)}) %collective-permute-start.4) | collective-permute-done | bytes 131104 | tf_op jit(solution)/shard_map/ppermute | solution.py:234
  37.7 3.2 %collective-permute-start.8 = (bf16[512,128]{1,0:T(8,128)(2,1)S(1)}, bf16[512,128]{1,0:T(8,128)(2,1)S(1)}, u32[]{:S(2)}, u32[]{:S(2)}) collective-permute-start(bf16[512,128]{1,0:T(8,128)(2,1)S(1)} %collective-permute-done.7.refs_5_), channel_id=1, source_target_pairs={{0,112},{1,113},{2,114},{3,115},{4,116},{5,117},{6,118},{7,119},{8... | collective-permute-start | bytes 393224 | tf_op jit(solution)/shard_map/ppermute | solution.py:234
  41.1 2.9 %collective-permute-start.9 = (bf16[256,128]{1,0:T(8,128)(2,1)S(1)}, bf16[256,128]{1,0:T(8,128)(2,1)S(1)}, u32[]{:S(2)}, u32[]{:S(2)}) collective-permute-start(bf16[256,128]{1,0:T(8,128)(2,1)S(1)} %slice.28), channel_id=1, source_target_pairs={{0,32},{1,33},{2,34},{3,35},{4,36},{5,37},{6,38},{7,39},{8,40},{9,... | collective-permute-start | bytes 196616 | tf_op jit(solution)/shard_map/ppermute | solution.py:234
  44.1 2.1 %collective-permute-done.10.refs_8_ = bf16[256,128]{1,0:T(8,128)(2,1)S(1)} collective-permute-done((bf16[256,128]{1,0:T(8,128)(2,1)S(1)}, bf16[256,128]{1,0:T(8,128)(2,1)S(1)}, u32[]{:S(2)}, u32[]{:S(2)}) %collective-permute-start.10) | collective-permute-done | bytes 65568 | tf_op jit(solution)/shard_map/ppermute | solution.py:234
  46.2 1.4 %collective-permute-done.9.refs_7_ = bf16[256,128]{1,0:T(8,128)(2,1)S(1)} collective-permute-done((bf16[256,128]{1,0:T(8,128)(2,1)S(1)}, bf16[256,128]{1,0:T(8,128)(2,1)S(1)}, u32[]{:S(2)}, u32[]{:S(2)}) %collective-permute-start.9) | collective-permute-done | bytes 65568 | tf_op jit(solution)/shard_map/ppermute | solution.py:234
  47.7 0.3 pick.1
  48.0 3.2 %collective-permute-start.11 = (bf16[4,64,256]{2,1,0:T(8,128)(2,1)S(1)}, bf16[4,64,256]{2,1,0:T(8,128)(2,1)S(1)}, u32[]{:S(2)}, u32[]{:S(2)}) collective-permute-start(bf16[4,64,256]{2,1,0:T(8,128)(2,1)S(1)} %pick.1), channel_id=1, source_target_pairs={{0,0},{1,32},{2,64},{3,96},{4,4},{5,36},{6,68},{7,100},{8,8},{9,40... | collective-permute-start | bytes 393224 | tf_op jit(solution)/shard_map/ppermute | solution.py:234
  51.2 12.1 %attention.1 = bf16[16,272,128]{2,1,0:T(8,128)(2,1)} custom-call(s32[144]{0:T(256)S(1)} %concatenate.6.table, bf16[32,128,128]{2,1,0:T(8,128)(2,1)S(1)} %bitcast.21, s32[8,256]{1,0:T(8,128)S(1)} %broadcast_add_fusion.kpos_ref, bf16[512,128]{1,0:T(8,128)(2,1)S(1)} %constant_dynamic-update-slice_fusion.refs_0_, ...), custom_call_target="tpu_custom_call" | custom-call | flops 3000000000 | bytes 4000000 | tf_op jit(solution)/shard_map/attention/pallas_call | solution.py:297
  63.3 8.1 %all-to-all-start.1 = ((bf16[16,272,128]{2,1,0:T(8,128)(2,1)}), bf16[16,272,128]{2,1,0:T(8,128)(2,1)S(1)}, u32[]{:S(2)}, u32[]{:S(2)}) async-start(bf16[16,272,128]{2,1,0:T(8,128)(2,1)} %attention.1), calls=%async_computation.1 | async-start | bytes 2228224 | tf_op jit(solution)/shard_map/all_to_all | solution.py:240
  72.2 1.6 %collective-permute-start.12 = (bf16[64,256]{1,0:T(8,128)(2,1)S(1)}, bf16[64,256]{1,0:T(8,128)(2,1)S(1)}, u32[]{:S(2)}, u32[]{:S(2)}) collective-permute-start(bf16[64,256]{1,0:T(8,128)(2,1)S(1)} %get-tuple-element.32), channel_id=1, source_target_pairs={{0,4},{1,5},{2,6},{3,7},{4,0},{5,1},{6,2},{7,3},{8,12},{9,13},{10,... | collective-permute-start | bytes 98312 | tf_op jit(solution)/shard_map/ppermute | solution.py:234
  73.7 2.7 %collective-permute-start.13 = (bf16[64,256]{1,0:T(8,128)(2,1)S(1)}, bf16[64,256]{1,0:T(8,128)(2,1)S(1)}, u32[]{:S(2)}, u32[]{:S(2)}) collective-permute-start(bf16[64,256]{1,0:T(8,128)(2,1)S(1)} %get-tuple-element.31), channel_id=1, source_target_pairs={{0,8},{1,9},{2,10},{3,11},{4,12},{5,13},{6,14},{7,15},{8,0},{9,1},... | collective-permute-start | bytes 98312 | tf_op jit(solution)/shard_map/ppermute | solution.py:234
  76.4 0.6 collective-permute-start.14
  77.2 3.7 %collective-permute-done.12.k1_ref = bf16[64,256]{1,0:T(8,128)(2,1)S(1)} collective-permute-done((bf16[64,256]{1,0:T(8,128)(2,1)S(1)}, bf16[64,256]{1,0:T(8,128)(2,1)S(1)}, u32[]{:S(2)}, u32[]{:S(2)}) %collective-permute-start.12) | collective-permute-done | bytes 32800 | tf_op jit(solution)/shard_map/ppermute | solution.py:234
  80.9 1.9 %collective-permute-done.13.k2_ref = bf16[64,256]{1,0:T(8,128)(2,1)S(1)} collective-permute-done((bf16[64,256]{1,0:T(8,128)(2,1)S(1)}, bf16[64,256]{1,0:T(8,128)(2,1)S(1)}, u32[]{:S(2)}, u32[]{:S(2)}) %collective-permute-start.13) | collective-permute-done | bytes 32800 | tf_op jit(solution)/shard_map/ppermute | solution.py:234
  82.8 0.6 all-to-all-done.1.m_ref
  83.4 2.1 %combine.1 = (bf16[64,2048]{1,0:T(8,128)(2,1)}, bf16[2,256,128]{2,1,0:T(8,128)(2,1)}) custom-call(s32[4]{0:T(128)S(1)} %copy-done.2, s32[2]{0:T(128)S(1)} %dynamic_slice.13.blocks, s32[1]{0:T(128)} %copy.19.length, bf16[256,256]{1,0:T(8,128)(2,1)S(1)} %fusion.1.choose_ref, bf16[4,64,256]{2,1,0:T(8,128)(2,1)S(1)} %collective-permute-done.11.k0_ref, ...), custom_call_target="tpu_custom_call" | custom-call | tf_op jit(solution)/shard_map/combine/pallas_call | solution.py:326
  (50 shorter events, 1.6 us)
Async XLA Ops:
  2.2 17.1 %collective-permute-start = (bf16[128,128]{1,0:T(8,128)(2,1)}, bf16[128,128]{1,0:T(8,128)(2,1)S(1)}, u32[]{:S(2)}, u32[]{:S(2)}) collective-permute-start(bf16[128,128]{1,0:T(8,128)(2,1)} %get-tuple-element.11), channel_id=1, source_target_pairs={{0,1},{1,0},{2,3},{3,2},{4,5},{5,4},{6,7},{7,6},{8,9},{9,8},{10,11... | collective-permute-start | bytes 98312 | tf_op jit(solution)/shard_map/ppermute | solution.py:234
  4.4 15.0 %collective-permute-start.1 = (bf16[128,128]{1,0:T(8,128)(2,1)}, bf16[128,128]{1,0:T(8,128)(2,1)S(1)}, u32[]{:S(2)}, u32[]{:S(2)}) collective-permute-start(bf16[128,128]{1,0:T(8,128)(2,1)} %get-tuple-element.12), channel_id=1, source_target_pairs={{0,2},{1,3},{2,0},{3,1},{4,6},{5,7},{6,4},{7,5},{8,10},{9,11},{10,... | collective-permute-start | bytes 98312 | tf_op jit(solution)/shard_map/ppermute | solution.py:234
  5.3 14.2 %collective-permute-start.2 = (bf16[128,128]{1,0:T(8,128)(2,1)}, bf16[128,128]{1,0:T(8,128)(2,1)S(1)}, u32[]{:S(2)}, u32[]{:S(2)}) collective-permute-start(bf16[128,128]{1,0:T(8,128)(2,1)} %get-tuple-element.13), channel_id=1, source_target_pairs={{0,3},{1,2},{2,1},{3,0},{4,7},{5,6},{6,5},{7,4},{8,11},{9,10},{10,... | collective-permute-start | bytes 98312 | tf_op jit(solution)/shard_map/ppermute | solution.py:234
  5.9 0.9 %copy-start = (bf16[1,64,2048]{2,1,0:T(8,128)(2,1)S(1)}, bf16[1,64,2048]{2,1,0:T(8,128)(2,1)}, u32[]{:S(2)}) copy-start(bf16[1,64,2048]{2,1,0:T(8,128)(2,1)} %param.5) | copy-start | bytes 786436
  6.8 0.7 copy-start.1
  9.2 8.4 %copy-start.4 = (s32[256]{0:T(256)S(1)}, s32[256]{0:T(256)}, u32[]{:S(2)}) copy-start(s32[256]{0:T(256)} %param.8) | copy-start | bytes 3076
  9.2 9.6 %copy-start.3 = (bf16[128,128]{1,0:T(8,128)(2,1)S(1)}, bf16[128,128]{1,0:T(8,128)(2,1)}, u32[]{:S(2)}) copy-start(bf16[128,128]{1,0:T(8,128)(2,1)} %get-tuple-element.10) | copy-start | bytes 98308
  9.2 42.0 %all-to-all-start = ((bf16[16,256,128]{2,1,0:T(8,128)(2,1)}), bf16[16,256,128]{2,1,0:T(8,128)(2,1)S(1)}, u32[]{:S(2)}, u32[]{:S(2)}) async-start(bf16[16,256,128]{2,1,0:T(8,128)(2,1)} %split_q.1), calls=%async_computation | async-start | bytes 2097152 | tf_op jit(solution)/shard_map/all_to_all | solution.py:240
  19.4 8.5 %collective-permute-start.6 = (bf16[512,128]{1,0:T(8,128)(2,1)S(1)}, bf16[512,128]{1,0:T(8,128)(2,1)S(1)}, u32[]{:S(2)}, u32[]{:S(2)}) collective-permute-start(bf16[512,128]{1,0:T(8,128)(2,1)S(1)} %constant_dynamic-update-slice_fusion.refs_0_), channel_id=1, source_target_pairs={{0,112},{1,113},{2,114},{3,115},{4,116},{5,117},{6,118},{7,119},{8... | collective-permute-start | bytes 393224 | tf_op jit(solution)/shard_map/ppermute | solution.py:234
  25.4 6.2 %collective-permute-start.3 = (bf16[512,128]{1,0:T(8,128)(2,1)S(1)}, bf16[512,128]{1,0:T(8,128)(2,1)S(1)}, u32[]{:S(2)}, u32[]{:S(2)}) collective-permute-start(bf16[512,128]{1,0:T(8,128)(2,1)S(1)} %constant_dynamic-update-slice_fusion.refs_0_), channel_id=1, source_target_pairs={{0,16},{1,17},{2,18},{3,19},{4,20},{5,21},{6,22},{7,23},{8,24},{9,... | collective-permute-start | bytes 393224 | tf_op jit(solution)/shard_map/ppermute | solution.py:234
  27.9 9.8 %collective-permute-start.7 = (bf16[512,128]{1,0:T(8,128)(2,1)S(1)}, bf16[512,128]{1,0:T(8,128)(2,1)S(1)}, u32[]{:S(2)}, u32[]{:S(2)}) collective-permute-start(bf16[512,128]{1,0:T(8,128)(2,1)S(1)} %collective-permute-done.6.refs_4_), channel_id=1, source_target_pairs={{0,112},{1,113},{2,114},{3,115},{4,116},{5,117},{6,118},{7,119},{8... | collective-permute-start | bytes 393224 | tf_op jit(solution)/shard_map/ppermute | solution.py:234
  31.6 6.2 %collective-permute-start.4 = (bf16[512,128]{1,0:T(8,128)(2,1)S(1)}, bf16[512,128]{1,0:T(8,128)(2,1)S(1)}, u32[]{:S(2)}, u32[]{:S(2)}) collective-permute-start(bf16[512,128]{1,0:T(8,128)(2,1)S(1)} %collective-permute-done.3.refs_1_), channel_id=1, source_target_pairs={{0,16},{1,17},{2,18},{3,19},{4,20},{5,21},{6,22},{7,23},{8,24},{9,... | collective-permute-start | bytes 393224 | tf_op jit(solution)/shard_map/ppermute | solution.py:234
  37.7 9.9 %collective-permute-start.5 = (bf16[512,128]{1,0:T(8,128)(2,1)S(1)}, bf16[512,128]{1,0:T(8,128)(2,1)S(1)}, u32[]{:S(2)}, u32[]{:S(2)}) collective-permute-start(bf16[512,128]{1,0:T(8,128)(2,1)S(1)} %collective-permute-done.4.refs_2_), channel_id=1, source_target_pairs={{0,16},{1,17},{2,18},{3,19},{4,20},{5,21},{6,22},{7,23},{8,24},{9,... | collective-permute-start | bytes 393224 | tf_op jit(solution)/shard_map/ppermute | solution.py:234
  37.7 9.9 %collective-permute-start.8 = (bf16[512,128]{1,0:T(8,128)(2,1)S(1)}, bf16[512,128]{1,0:T(8,128)(2,1)S(1)}, u32[]{:S(2)}, u32[]{:S(2)}) collective-permute-start(bf16[512,128]{1,0:T(8,128)(2,1)S(1)} %collective-permute-done.7.refs_5_), channel_id=1, source_target_pairs={{0,112},{1,113},{2,114},{3,115},{4,116},{5,117},{6,118},{7,119},{8... | collective-permute-start | bytes 393224 | tf_op jit(solution)/shard_map/ppermute | solution.py:234
  41.0 5.2 %collective-permute-start.10 = (bf16[256,128]{1,0:T(8,128)(2,1)S(1)}, bf16[256,128]{1,0:T(8,128)(2,1)S(1)}, u32[]{:S(2)}, u32[]{:S(2)}) collective-permute-start(bf16[256,128]{1,0:T(8,128)(2,1)S(1)} %slice.29), channel_id=1, source_target_pairs={{0,96},{1,97},{2,98},{3,99},{4,100},{5,101},{6,102},{7,103},{8,104... | collective-permute-start | bytes 196616 | tf_op jit(solution)/shard_map/ppermute | solution.py:234
  41.1 6.6 %collective-permute-start.9 = (bf16[256,128]{1,0:T(8,128)(2,1)S(1)}, bf16[256,128]{1,0:T(8,128)(2,1)S(1)}, u32[]{:S(2)}, u32[]{:S(2)}) collective-permute-start(bf16[256,128]{1,0:T(8,128)(2,1)S(1)} %slice.28), channel_id=1, source_target_pairs={{0,32},{1,33},{2,34},{3,35},{4,36},{5,37},{6,38},{7,39},{8,40},{9,... | collective-permute-start | bytes 196616 | tf_op jit(solution)/shard_map/ppermute | solution.py:234
  48.0 15.3 %collective-permute-start.11 = (bf16[4,64,256]{2,1,0:T(8,128)(2,1)S(1)}, bf16[4,64,256]{2,1,0:T(8,128)(2,1)S(1)}, u32[]{:S(2)}, u32[]{:S(2)}) collective-permute-start(bf16[4,64,256]{2,1,0:T(8,128)(2,1)S(1)} %pick.1), channel_id=1, source_target_pairs={{0,0},{1,32},{2,64},{3,96},{4,4},{5,36},{6,68},{7,100},{8,8},{9,40... | collective-permute-start | bytes 393224 | tf_op jit(solution)/shard_map/ppermute | solution.py:234
  63.3 20.1 %copy-start.2 = (s32[4]{0:T(128)S(1)}, s32[4]{0:T(128)}, u32[]{:S(2)}) copy-start(s32[4]{0:T(128)} %heads.5) | copy-start | bytes 52
  63.3 20.1 %all-to-all-start.1 = ((bf16[16,272,128]{2,1,0:T(8,128)(2,1)}), bf16[16,272,128]{2,1,0:T(8,128)(2,1)S(1)}, u32[]{:S(2)}, u32[]{:S(2)}) async-start(bf16[16,272,128]{2,1,0:T(8,128)(2,1)} %attention.1), calls=%async_computation.1 | async-start | bytes 2228224 | tf_op jit(solution)/shard_map/all_to_all | solution.py:240
  72.2 8.7 %collective-permute-start.12 = (bf16[64,256]{1,0:T(8,128)(2,1)S(1)}, bf16[64,256]{1,0:T(8,128)(2,1)S(1)}, u32[]{:S(2)}, u32[]{:S(2)}) collective-permute-start(bf16[64,256]{1,0:T(8,128)(2,1)S(1)} %get-tuple-element.32), channel_id=1, source_target_pairs={{0,4},{1,5},{2,6},{3,7},{4,0},{5,1},{6,2},{7,3},{8,12},{9,13},{10,... | collective-permute-start | bytes 98312 | tf_op jit(solution)/shard_map/ppermute | solution.py:234
  73.7 9.0 %collective-permute-start.13 = (bf16[64,256]{1,0:T(8,128)(2,1)S(1)}, bf16[64,256]{1,0:T(8,128)(2,1)S(1)}, u32[]{:S(2)}, u32[]{:S(2)}) collective-permute-start(bf16[64,256]{1,0:T(8,128)(2,1)S(1)} %get-tuple-element.31), channel_id=1, source_target_pairs={{0,8},{1,9},{2,10},{3,11},{4,12},{5,13},{6,14},{7,15},{8,0},{9,1},... | collective-permute-start | bytes 98312 | tf_op jit(solution)/shard_map/ppermute | solution.py:234
  76.4 6.3 %collective-permute-start.14 = (bf16[64,256]{1,0:T(8,128)(2,1)S(1)}, bf16[64,256]{1,0:T(8,128)(2,1)S(1)}, u32[]{:S(2)}, u32[]{:S(2)}) collective-permute-start(bf16[64,256]{1,0:T(8,128)(2,1)S(1)} %get-tuple-element.30), channel_id=1, source_target_pairs={{0,12},{1,13},{2,14},{3,15},{4,8},{5,9},{6,10},{7,11},{8,4},{9,5},... | collective-permute-start | bytes 98312 | tf_op jit(solution)/shard_map/ppermute | solution.py:234

commit v13 on v12

--- a/solution.py
+++ b/solution.py
@@ -266,6 +266,8 @@
     r4 = move(r2[:half], lambda a, b, c: index(a + 2, b, c))
     l4 = move(l2[half:], lambda a, b, c: index(a - 2, b, c))
 
+    block_map, _ = lax.optimization_barrier((block_map, l1))
+
     ids = block_map.reshape(NZ, NX, NY, 2).transpose(1, 0, 2, 3).reshape(NX, KEY_BLOCKS)
     rank = ranks(ids)
     ordered = placed(ids, rank)

time: 86.1 us -> 86.5 us (level)
  the two profiles are of different devices: /device:TPU:8 before, /device:TPU:32 now
where the time goes in v13:
time: 86.5 us; the launch traced here: 86.1 us
  starting transfers between devices  41.1 us (48%)
  waiting for transfers between devices  22 us (25%)
  Pallas kernels  16.5 us (19%)
  local copies, waits for them, and re-layouts  3.61 us (4%)
  between operations  1.5 us (2%)
  other arithmetic  1.41 us (2%)
    ppermute x15, starting transfers between devices, move(): lax.ppermute(value, 'blk', [(s, target(s // 16, s // 4 % 4, s % 4)) for s...  25.9 us
    ppermute x15, waiting for transfers between devices, move(): lax.ppermute(value, 'blk', [(s, target(s // 16, s // 4 % 4, s % 4)) for s...  20.6 us
    all_to_all x2, starting transfers between devices, exchange(): lax.all_to_all(value, 'blk', 0, 0, axis_index_groups=groups, tiled=True)  15.2 us
    pallas_call x1, Pallas kernels, body(): pl.pallas_call(attention_kernel, out_shape=jax.ShapeDtypeStruct((PLANE, M...  10.8 us
    unnamed x11, local copies, waits for them, and re-layouts  2.39 us
    pallas_call x1, Pallas kernels, body(): pl.pallas_call(combine_kernel, out_shape=(jax.ShapeDtypeStruct((2 * BLOCK...  2.1 us
  transfers between devices with their start and end apart: 17, of which 10 were waited for; matrix products, arithmetic and copies ran while one was open for 4% of the time, Pallas kernels for 15%

profile of v13, /device:TPU:32, one launch (start us, length us, event | category | flops | bytes accessed | tf_op | source)
XLA Modules:
  0.0 86.1 jit_solution(13021997414039159794)
XLA Ops:
  0.6 1.6 %split_kv.1 = (bf16[128,128]{1,0:T(8,128)(2,1)}, bf16[128,128]{1,0:T(8,128)(2,1)}, bf16[128,128]{1,0:T(8,128)(2,1)}, bf16[128,128]{1,0:T(8,128)(2,1)}) custom-call(s32[4]{0:T(128)} %heads.5, bf16[128,512]{1,0:T(8,128)(2,1)} %bitcast.25), custom_call_target="tpu_custom_call" | custom-call | tf_op jit(solution)/shard_map/split_kv/pallas_call | solution.py:242
  2.2 1.6 %collective-permute-start = (bf16[128,128]{1,0:T(8,128)(2,1)}, bf16[128,128]{1,0:T(8,128)(2,1)S(1)}, u32[]{:S(2)}, u32[]{:S(2)}) collective-permute-start(bf16[128,128]{1,0:T(8,128)(2,1)} %get-tuple-element.12), channel_id=1, source_target_pairs={{0,1},{1,0},{2,3},{3,2},{4,5},{5,4},{6,7},{7,6},{8,9},{9,8},{10,11... | collective-permute-start | bytes 98312 | tf_op jit(solution)/shard_map/ppermute | solution.py:234
  3.8 2.9 %collective-permute-start.1 = (bf16[128,128]{1,0:T(8,128)(2,1)}, bf16[128,128]{1,0:T(8,128)(2,1)S(1)}, u32[]{:S(2)}, u32[]{:S(2)}) collective-permute-start(bf16[128,128]{1,0:T(8,128)(2,1)} %get-tuple-element.13), channel_id=1, source_target_pairs={{0,2},{1,3},{2,0},{3,1},{4,6},{5,7},{6,4},{7,5},{8,10},{9,11},{10,... | collective-permute-start | bytes 98312 | tf_op jit(solution)/shard_map/ppermute | solution.py:234
  6.7 0.2 collective-permute-start.2
  6.9 0.8 constant_dynamic-update-slice_fusion.3
  7.7 1.7 %collective-permute-done.1 = bf16[128,128]{1,0:T(8,128)(2,1)S(1)} collective-permute-done((bf16[128,128]{1,0:T(8,128)(2,1)}, bf16[128,128]{1,0:T(8,128)(2,1)S(1)}, u32[]{:S(2)}, u32[]{:S(2)}) %collective-permute-start.1) | collective-permute-done | bytes 32800 | tf_op jit(solution)/shard_map/ppermute | solution.py:234
  9.4 2.6 %collective-permute-done.2 = bf16[128,128]{1,0:T(8,128)(2,1)S(1)} collective-permute-done((bf16[128,128]{1,0:T(8,128)(2,1)}, bf16[128,128]{1,0:T(8,128)(2,1)S(1)}, u32[]{:S(2)}, u32[]{:S(2)}) %collective-permute-start.2) | collective-permute-done | bytes 32800 | tf_op jit(solution)/shard_map/ppermute | solution.py:234
  12.2 0.9 %copy-done = bf16[1,64,2048]{2,1,0:T(8,128)(2,1)S(1)} copy-done((bf16[1,64,2048]{2,1,0:T(8,128)(2,1)S(1)}, bf16[1,64,2048]{2,1,0:T(8,128)(2,1)}, u32[]{:S(2)}) %copy-start) | copy-done | bytes 262168
  13.1 0.7 copy-done.1
  13.8 1.7 %split_q.1 = bf16[16,256,128]{2,1,0:T(8,128)(2,1)} custom-call(s32[4]{0:T(128)S(1)} %copy-done.1, bf16[64,2048]{1,0:T(8,128)(2,1)S(1)} %bitcast.22), custom_call_target="tpu_custom_call" | custom-call | tf_op jit(solution)/shard_map/split_q/pallas_call | solution.py:254
  15.4 4.5 %all-to-all-start = ((bf16[16,256,128]{2,1,0:T(8,128)(2,1)}), bf16[16,256,128]{2,1,0:T(8,128)(2,1)S(1)}, u32[]{:S(2)}, u32[]{:S(2)}) async-start(bf16[16,256,128]{2,1,0:T(8,128)(2,1)} %split_q.1), calls=%async_computation | async-start | bytes 2097152 | tf_op jit(solution)/shard_map/all_to_all | solution.py:240
  20.1 2.0 %collective-permute-start.4 = (bf16[512,128]{1,0:T(8,128)(2,1)S(1)}, bf16[512,128]{1,0:T(8,128)(2,1)S(1)}, u32[]{:S(2)}, u32[]{:S(2)}) collective-permute-start(bf16[512,128]{1,0:T(8,128)(2,1)S(1)} %constant_dynamic-update-slice_fusion.refs_0_), channel_id=1, source_target_pairs={{0,16},{1,17},{2,18},{3,19},{4,20},{5,21},{6,22},{7,23},{8,24},{9,... | collective-permute-start | bytes 393224 | tf_op jit(solution)/shard_map/ppermute | solution.py:234
  22.2 0.3 copy.12
  22.6 0.2 convert_reduce_fusion
  23.7 4.0 %collective-permute-start.7 = (bf16[512,128]{1,0:T(8,128)(2,1)S(1)}, bf16[512,128]{1,0:T(8,128)(2,1)S(1)}, u32[]{:S(2)}, u32[]{:S(2)}) collective-permute-start(bf16[512,128]{1,0:T(8,128)(2,1)S(1)} %collective-permute-done.3.refs_4_), channel_id=1, source_target_pairs={{0,112},{1,113},{2,114},{3,115},{4,116},{5,117},{6,118},{7,119},{8... | collective-permute-start | bytes 393224 | tf_op jit(solution)/shard_map/ppermute | solution.py:234
  27.7 1.2 %collective-permute-done.4.refs_1_ = bf16[512,128]{1,0:T(8,128)(2,1)S(1)} collective-permute-done((bf16[512,128]{1,0:T(8,128)(2,1)S(1)}, bf16[512,128]{1,0:T(8,128)(2,1)S(1)}, u32[]{:S(2)}, u32[]{:S(2)}) %collective-permute-start.4) | collective-permute-done | bytes 131104 | tf_op jit(solution)/shard_map/ppermute | solution.py:234
  29.4 0.9 %collective-permute-done.7.refs_5_ = bf16[512,128]{1,0:T(8,128)(2,1)S(1)} collective-permute-done((bf16[512,128]{1,0:T(8,128)(2,1)S(1)}, bf16[512,128]{1,0:T(8,128)(2,1)S(1)}, u32[]{:S(2)}, u32[]{:S(2)}) %collective-permute-start.7) | collective-permute-done | bytes 131104 | tf_op jit(solution)/shard_map/ppermute | solution.py:234
  30.2 3.2 %collective-permute-start.8 = (bf16[512,128]{1,0:T(8,128)(2,1)S(1)}, bf16[512,128]{1,0:T(8,128)(2,1)S(1)}, u32[]{:S(2)}, u32[]{:S(2)}) collective-permute-start(bf16[512,128]{1,0:T(8,128)(2,1)S(1)} %collective-permute-done.7.refs_5_), channel_id=1, source_target_pairs={{0,112},{1,113},{2,114},{3,115},{4,116},{5,117},{6,118},{7,119},{8... | collective-permute-start | bytes 393224 | tf_op jit(solution)/shard_map/ppermute | solution.py:234
  33.4 1.9 %collective-permute-done.5.refs_2_ = bf16[512,128]{1,0:T(8,128)(2,1)S(1)} collective-permute-done((bf16[512,128]{1,0:T(8,128)(2,1)S(1)}, bf16[512,128]{1,0:T(8,128)(2,1)S(1)}, u32[]{:S(2)}, u32[]{:S(2)}) %collective-permute-start.5) | collective-permute-done | bytes 131104 | tf_op jit(solution)/shard_map/ppermute | solution.py:234
  35.4 6.3 %collective-permute-start.10 = (bf16[256,128]{1,0:T(8,128)(2,1)S(1)}, bf16[256,128]{1,0:T(8,128)(2,1)S(1)}, u32[]{:S(2)}, u32[]{:S(2)}) collective-permute-start(bf16[256,128]{1,0:T(8,128)(2,1)S(1)} %slice.29), channel_id=1, source_target_pairs={{0,96},{1,97},{2,98},{3,99},{4,100},{5,101},{6,102},{7,103},{8,104... | collective-permute-start | bytes 196616 | tf_op jit(solution)/shard_map/ppermute | solution.py:234
  41.8 1.8 %collective-permute-done.10.refs_8_ = bf16[256,128]{1,0:T(8,128)(2,1)S(1)} collective-permute-done((bf16[256,128]{1,0:T(8,128)(2,1)S(1)}, bf16[256,128]{1,0:T(8,128)(2,1)S(1)}, u32[]{:S(2)}, u32[]{:S(2)}) %collective-permute-start.10) | collective-permute-done | bytes 65568 | tf_op jit(solution)/shard_map/ppermute | solution.py:234
  43.6 4.5 %collective-permute-done.9.refs_7_ = bf16[256,128]{1,0:T(8,128)(2,1)S(1)} collective-permute-done((bf16[256,128]{1,0:T(8,128)(2,1)S(1)}, bf16[256,128]{1,0:T(8,128)(2,1)S(1)}, u32[]{:S(2)}, u32[]{:S(2)}) %collective-permute-start.9) | collective-permute-done | bytes 65568 | tf_op jit(solution)/shard_map/ppermute | solution.py:234
  48.1 0.3 pick.1
  48.4 0.8 collective-permute-start.11
  49.3 10.8 %attention.1 = bf16[16,272,128]{2,1,0:T(8,128)(2,1)} custom-call(s32[144]{0:T(256)S(1)} %concatenate.7.table, bf16[32,128,128]{2,1,0:T(8,128)(2,1)S(1)} %bitcast.21, s32[8,256]{1,0:T(8,128)S(1)} %broadcast_add_fusion.kpos_ref, bf16[512,128]{1,0:T(8,128)(2,1)S(1)} %constant_dynamic-update-slice_fusion.refs_0_, ...), custom_call_target="tpu_custom_call" | custom-call | flops 3000000000 | bytes 4000000 | tf_op jit(solution)/shard_map/attention/pallas_call | solution.py:299
  60.1 10.6 %all-to-all-start.1 = ((bf16[16,272,128]{2,1,0:T(8,128)(2,1)}), bf16[16,272,128]{2,1,0:T(8,128)(2,1)S(1)}, u32[]{:S(2)}, u32[]{:S(2)}) async-start(bf16[16,272,128]{2,1,0:T(8,128)(2,1)} %attention.1), calls=%async_computation.1 | async-start | bytes 2228224 | tf_op jit(solution)/shard_map/all_to_all | solution.py:240
  71.6 2.0 %collective-permute-start.12 = (bf16[64,256]{1,0:T(8,128)(2,1)S(1)}, bf16[64,256]{1,0:T(8,128)(2,1)S(1)}, u32[]{:S(2)}, u32[]{:S(2)}) collective-permute-start(bf16[64,256]{1,0:T(8,128)(2,1)S(1)} %get-tuple-element.34), channel_id=1, source_target_pairs={{0,4},{1,5},{2,6},{3,7},{4,0},{5,1},{6,2},{7,3},{8,12},{9,13},{10,... | collective-permute-start | bytes 98312 | tf_op jit(solution)/shard_map/ppermute | solution.py:234
  73.6 2.7 %collective-permute-start.13 = (bf16[64,256]{1,0:T(8,128)(2,1)S(1)}, bf16[64,256]{1,0:T(8,128)(2,1)S(1)}, u32[]{:S(2)}, u32[]{:S(2)}) collective-permute-start(bf16[64,256]{1,0:T(8,128)(2,1)S(1)} %get-tuple-element.33), channel_id=1, source_target_pairs={{0,8},{1,9},{2,10},{3,11},{4,12},{5,13},{6,14},{7,15},{8,0},{9,1},... | collective-permute-start | bytes 98312 | tf_op jit(solution)/shard_map/ppermute | solution.py:234
  76.6 4.1 %collective-permute-done.12.k1_ref = bf16[64,256]{1,0:T(8,128)(2,1)S(1)} collective-permute-done((bf16[64,256]{1,0:T(8,128)(2,1)S(1)}, bf16[64,256]{1,0:T(8,128)(2,1)S(1)}, u32[]{:S(2)}, u32[]{:S(2)}) %collective-permute-start.12) | collective-permute-done | bytes 32800 | tf_op jit(solution)/shard_map/ppermute | solution.py:234
  80.8 1.9 %collective-permute-done.13.k2_ref = bf16[64,256]{1,0:T(8,128)(2,1)S(1)} collective-permute-done((bf16[64,256]{1,0:T(8,128)(2,1)S(1)}, bf16[64,256]{1,0:T(8,128)(2,1)S(1)}, u32[]{:S(2)}, u32[]{:S(2)}) %collective-permute-start.13) | collective-permute-done | bytes 32800 | tf_op jit(solution)/shard_map/ppermute | solution.py:234
  82.6 1.4 %all-to-all-done.1.m_ref = bf16[16,272,128]{2,1,0:T(8,128)(2,1)S(1)} async-done(((bf16[16,272,128]{2,1,0:T(8,128)(2,1)}), bf16[16,272,128]{2,1,0:T(8,128)(2,1)S(1)}, u32[]{:S(2)}, u32[]{:S(2)}) %all-to-all-start.1) | async-done | bytes 1114144 | tf_op jit(solution)/shard_map/all_to_all | solution.py:240
  84.0 2.1 %combine.1 = (bf16[64,2048]{1,0:T(8,128)(2,1)}, bf16[2,256,128]{2,1,0:T(8,128)(2,1)}) custom-call(s32[4]{0:T(128)S(1)} %copy-done.2, s32[2]{0:T(128)S(1)} %dynamic_slice.13.blocks, s32[1]{0:T(128)} %copy.19.length, bf16[256,256]{1,0:T(8,128)(2,1)S(1)} %fusion.1.choose_ref, bf16[4,64,256]{2,1,0:T(8,128)(2,1)S(1)} %collective-permute-done.11.k0_ref, ...), custom_call_target="tpu_custom_call" | custom-call | tf_op jit(solution)/shard_map/combine/pallas_call | solution.py:328
  (48 shorter events, 2.4 us)
Async XLA Ops:
  2.2 5.5 %collective-permute-start = (bf16[128,128]{1,0:T(8,128)(2,1)}, bf16[128,128]{1,0:T(8,128)(2,1)S(1)}, u32[]{:S(2)}, u32[]{:S(2)}) collective-permute-start(bf16[128,128]{1,0:T(8,128)(2,1)} %get-tuple-element.12), channel_id=1, source_target_pairs={{0,1},{1,0},{2,3},{3,2},{4,5},{5,4},{6,7},{7,6},{8,9},{9,8},{10,11... | collective-permute-start | bytes 98312 | tf_op jit(solution)/shard_map/ppermute | solution.py:234
  3.8 5.6 %collective-permute-start.1 = (bf16[128,128]{1,0:T(8,128)(2,1)}, bf16[128,128]{1,0:T(8,128)(2,1)S(1)}, u32[]{:S(2)}, u32[]{:S(2)}) collective-permute-start(bf16[128,128]{1,0:T(8,128)(2,1)} %get-tuple-element.13), channel_id=1, source_target_pairs={{0,2},{1,3},{2,0},{3,1},{4,6},{5,7},{6,4},{7,5},{8,10},{9,11},{10,... | collective-permute-start | bytes 98312 | tf_op jit(solution)/shard_map/ppermute | solution.py:234
  6.7 5.3 %collective-permute-start.2 = (bf16[128,128]{1,0:T(8,128)(2,1)}, bf16[128,128]{1,0:T(8,128)(2,1)S(1)}, u32[]{:S(2)}, u32[]{:S(2)}) collective-permute-start(bf16[128,128]{1,0:T(8,128)(2,1)} %get-tuple-element.14), channel_id=1, source_target_pairs={{0,3},{1,2},{2,1},{3,0},{4,7},{5,6},{6,5},{7,4},{8,11},{9,10},{10,... | collective-permute-start | bytes 98312 | tf_op jit(solution)/shard_map/ppermute | solution.py:234
  12.0 10.0 %collective-permute-start.3 = (bf16[512,128]{1,0:T(8,128)(2,1)S(1)}, bf16[512,128]{1,0:T(8,128)(2,1)S(1)}, u32[]{:S(2)}, u32[]{:S(2)}) collective-permute-start(bf16[512,128]{1,0:T(8,128)(2,1)S(1)} %constant_dynamic-update-slice_fusion.refs_0_), channel_id=1, source_target_pairs={{0,112},{1,113},{2,114},{3,115},{4,116},{5,117},{6,118},{7,119},{8... | collective-permute-start | bytes 393224 | tf_op jit(solution)/shard_map/ppermute | solution.py:234
  12.2 0.9 %copy-start = (bf16[1,64,2048]{2,1,0:T(8,128)(2,1)S(1)}, bf16[1,64,2048]{2,1,0:T(8,128)(2,1)}, u32[]{:S(2)}) copy-start(bf16[1,64,2048]{2,1,0:T(8,128)(2,1)} %param.5) | copy-start | bytes 786436
  13.1 0.7 copy-start.1
  15.4 6.6 %copy-start.3 = (s32[256]{0:T(256)S(1)}, s32[256]{0:T(256)}, u32[]{:S(2)}) copy-start(s32[256]{0:T(256)} %param.8) | copy-start | bytes 3076
  15.4 33.8 %all-to-all-start = ((bf16[16,256,128]{2,1,0:T(8,128)(2,1)}), bf16[16,256,128]{2,1,0:T(8,128)(2,1)S(1)}, u32[]{:S(2)}, u32[]{:S(2)}) async-start(bf16[16,256,128]{2,1,0:T(8,128)(2,1)} %split_q.1), calls=%async_computation | async-start | bytes 2097152 | tf_op jit(solution)/shard_map/all_to_all | solution.py:240
  20.1 8.8 %collective-permute-start.4 = (bf16[512,128]{1,0:T(8,128)(2,1)S(1)}, bf16[512,128]{1,0:T(8,128)(2,1)S(1)}, u32[]{:S(2)}, u32[]{:S(2)}) collective-permute-start(bf16[512,128]{1,0:T(8,128)(2,1)S(1)} %constant_dynamic-update-slice_fusion.refs_0_), channel_id=1, source_target_pairs={{0,16},{1,17},{2,18},{3,19},{4,20},{5,21},{6,22},{7,23},{8,24},{9,... | collective-permute-start | bytes 393224 | tf_op jit(solution)/shard_map/ppermute | solution.py:234
  23.7 6.5 %collective-permute-start.7 = (bf16[512,128]{1,0:T(8,128)(2,1)S(1)}, bf16[512,128]{1,0:T(8,128)(2,1)S(1)}, u32[]{:S(2)}, u32[]{:S(2)}) collective-permute-start(bf16[512,128]{1,0:T(8,128)(2,1)S(1)} %collective-permute-done.3.refs_4_), channel_id=1, source_target_pairs={{0,112},{1,113},{2,114},{3,115},{4,116},{5,117},{6,118},{7,119},{8... | collective-permute-start | bytes 393224 | tf_op jit(solution)/shard_map/ppermute | solution.py:234
  28.9 6.4 %collective-permute-start.5 = (bf16[512,128]{1,0:T(8,128)(2,1)S(1)}, bf16[512,128]{1,0:T(8,128)(2,1)S(1)}, u32[]{:S(2)}, u32[]{:S(2)}) collective-permute-start(bf16[512,128]{1,0:T(8,128)(2,1)S(1)} %collective-permute-done.4.refs_1_), channel_id=1, source_target_pairs={{0,16},{1,17},{2,18},{3,19},{4,20},{5,21},{6,22},{7,23},{8,24},{9,... | collective-permute-start | bytes 393224 | tf_op jit(solution)/shard_map/ppermute | solution.py:234
  30.2 17.8 %collective-permute-start.8 = (bf16[512,128]{1,0:T(8,128)(2,1)S(1)}, bf16[512,128]{1,0:T(8,128)(2,1)S(1)}, u32[]{:S(2)}, u32[]{:S(2)}) collective-permute-start(bf16[512,128]{1,0:T(8,128)(2,1)S(1)} %collective-permute-done.7.refs_5_), channel_id=1, source_target_pairs={{0,112},{1,113},{2,114},{3,115},{4,116},{5,117},{6,118},{7,119},{8... | collective-permute-start | bytes 393224 | tf_op jit(solution)/shard_map/ppermute | solution.py:234
  35.3 12.7 %collective-permute-start.6 = (bf16[512,128]{1,0:T(8,128)(2,1)S(1)}, bf16[512,128]{1,0:T(8,128)(2,1)S(1)}, u32[]{:S(2)}, u32[]{:S(2)}) collective-permute-start(bf16[512,128]{1,0:T(8,128)(2,1)S(1)} %collective-permute-done.5.refs_2_), channel_id=1, source_target_pairs={{0,16},{1,17},{2,18},{3,19},{4,20},{5,21},{6,22},{7,23},{8,24},{9,... | collective-permute-start | bytes 393224 | tf_op jit(solution)/shard_map/ppermute | solution.py:234
  35.4 8.2 %collective-permute-start.10 = (bf16[256,128]{1,0:T(8,128)(2,1)S(1)}, bf16[256,128]{1,0:T(8,128)(2,1)S(1)}, u32[]{:S(2)}, u32[]{:S(2)}) collective-permute-start(bf16[256,128]{1,0:T(8,128)(2,1)S(1)} %slice.29), channel_id=1, source_target_pairs={{0,96},{1,97},{2,98},{3,99},{4,100},{5,101},{6,102},{7,103},{8,104... | collective-permute-start | bytes 196616 | tf_op jit(solution)/shard_map/ppermute | solution.py:234
  41.7 6.4 %collective-permute-start.9 = (bf16[256,128]{1,0:T(8,128)(2,1)S(1)}, bf16[256,128]{1,0:T(8,128)(2,1)S(1)}, u32[]{:S(2)}, u32[]{:S(2)}) collective-permute-start(bf16[256,128]{1,0:T(8,128)(2,1)S(1)} %slice.28), channel_id=1, source_target_pairs={{0,32},{1,33},{2,34},{3,35},{4,36},{5,37},{6,38},{7,39},{8,40},{9,... | collective-permute-start | bytes 196616 | tf_op jit(solution)/shard_map/ppermute | solution.py:234
  48.4 11.7 %collective-permute-start.11 = (bf16[4,64,256]{2,1,0:T(8,128)(2,1)S(1)}, bf16[4,64,256]{2,1,0:T(8,128)(2,1)S(1)}, u32[]{:S(2)}, u32[]{:S(2)}) collective-permute-start(bf16[4,64,256]{2,1,0:T(8,128)(2,1)S(1)} %pick.1), channel_id=1, source_target_pairs={{0,0},{1,32},{2,64},{3,96},{4,4},{5,36},{6,68},{7,100},{8,8},{9,40... | collective-permute-start | bytes 393224 | tf_op jit(solution)/shard_map/ppermute | solution.py:234
  60.1 23.9 %copy-start.2 = (s32[4]{0:T(128)S(1)}, s32[4]{0:T(128)}, u32[]{:S(2)}) copy-start(s32[4]{0:T(128)} %heads.5) | copy-start | bytes 52
  60.1 23.9 %all-to-all-start.1 = ((bf16[16,272,128]{2,1,0:T(8,128)(2,1)}), bf16[16,272,128]{2,1,0:T(8,128)(2,1)S(1)}, u32[]{:S(2)}, u32[]{:S(2)}) async-start(bf16[16,272,128]{2,1,0:T(8,128)(2,1)} %attention.1), calls=%async_computation.1 | async-start | bytes 2228224 | tf_op jit(solution)/shard_map/all_to_all | solution.py:240
  71.6 9.2 %collective-permute-start.12 = (bf16[64,256]{1,0:T(8,128)(2,1)S(1)}, bf16[64,256]{1,0:T(8,128)(2,1)S(1)}, u32[]{:S(2)}, u32[]{:S(2)}) collective-permute-start(bf16[64,256]{1,0:T(8,128)(2,1)S(1)} %get-tuple-element.34), channel_id=1, source_target_pairs={{0,4},{1,5},{2,6},{3,7},{4,0},{5,1},{6,2},{7,3},{8,12},{9,13},{10,... | collective-permute-start | bytes 98312 | tf_op jit(solution)/shard_map/ppermute | solution.py:234
  73.6 9.0 %collective-permute-start.13 = (bf16[64,256]{1,0:T(8,128)(2,1)S(1)}, bf16[64,256]{1,0:T(8,128)(2,1)S(1)}, u32[]{:S(2)}, u32[]{:S(2)}) collective-permute-start(bf16[64,256]{1,0:T(8,128)(2,1)S(1)} %get-tuple-element.33), channel_id=1, source_target_pairs={{0,8},{1,9},{2,10},{3,11},{4,12},{5,13},{6,14},{7,15},{8,0},{9,1},... | collective-permute-start | bytes 98312 | tf_op jit(solution)/shard_map/ppermute | solution.py:234
  76.2 6.4 %collective-permute-start.14 = (bf16[64,256]{1,0:T(8,128)(2,1)S(1)}, bf16[64,256]{1,0:T(8,128)(2,1)S(1)}, u32[]{:S(2)}, u32[]{:S(2)}) collective-permute-start(bf16[64,256]{1,0:T(8,128)(2,1)S(1)} %get-tuple-element.32), channel_id=1, source_target_pairs={{0,12},{1,13},{2,14},{3,15},{4,8},{5,9},{6,10},{7,11},{8,4},{9,5},... | collective-permute-start | bytes 98312 | tf_op jit(solution)/shard_map/ppermute | solution.py:234

commit v14 on v12

--- a/solution.py
+++ b/solution.py
@@ -266,6 +266,8 @@
     r4 = move(r2[:half], lambda a, b, c: index(a + 2, b, c))
     l4 = move(l2[half:], lambda a, b, c: index(a - 2, b, c))
 
+    block_map, _ = lax.optimization_barrier((block_map, own))
+
     ids = block_map.reshape(NZ, NX, NY, 2).transpose(1, 0, 2, 3).reshape(NX, KEY_BLOCKS)
     rank = ranks(ids)
     ordered = placed(ids, rank)

time: 86.1 us -> 84.7 us (0.984)
  waiting for transfers between devices: 18 us -> 16.4 us
  Pallas kernels: 17.8 us -> 16.8 us
  starting transfers between devices: 43.9 us -> 44.9 us
    ppermute x15, waiting for transfers between devices: 17.4 us -> 15.8 us  [move(): lax.ppermute(value, 'blk', [(s, target(s // 16, s // 4 % 4, s % 4)) for s...]
    all_to_all x2, starting transfers between devices: 16.4 us -> 17.5 us  [exchange(): lax.all_to_all(value, 'blk', 0, 0, axis_index_groups=groups, tiled=True)]
    pallas_call x1, Pallas kernels: 12.1 us -> 11.1 us  [body(): pl.pallas_call(attention_kernel, out_shape=jax.ShapeDtypeStruct((PLANE, M...]
  transfers between devices with their start and end apart: 17 -> 17, of which waited for: 7 -> 7; matrix products, arithmetic and copies ran while one was open for 3% -> 3% of each run, Pallas kernels for 17% -> 16%
where the time goes in v14:
time: 84.7 us; the launch traced here: 83.9 us
  starting transfers between devices  44.9 us (53%)
  Pallas kernels  16.8 us (20%)
  waiting for transfers between devices  16.4 us (19%)
  local copies, waits for them, and re-layouts  2.85 us (3%)
  between operations  1.49 us (2%)
  other arithmetic  1.41 us (2%)
    ppermute x15, starting transfers between devices, move(): lax.ppermute(value, 'blk', [(s, target(s // 16, s // 4 % 4, s % 4)) for s...  27.4 us
    all_to_all x2, starting transfers between devices, exchange(): lax.all_to_all(value, 'blk', 0, 0, axis_index_groups=groups, tiled=True)  17.5 us
    ppermute x15, waiting for transfers between devices, move(): lax.ppermute(value, 'blk', [(s, target(s // 16, s // 4 % 4, s % 4)) for s...  15.8 us
    pallas_call x1, Pallas kernels, body(): pl.pallas_call(attention_kernel, out_shape=jax.ShapeDtypeStruct((PLANE, M...  11.1 us
    pallas_call x1, Pallas kernels, body(): pl.pallas_call(combine_kernel, out_shape=(jax.ShapeDtypeStruct((2 * BLOCK...  2.1 us
  transfers between devices with their start and end apart: 17, of which 7 were waited for; matrix products, arithmetic and copies ran while one was open for 3% of the time, Pallas kernels for 16%

profile of v14, /device:TPU:8, one launch (start us, length us, event | category | flops | bytes accessed | tf_op | source)
XLA Modules:
  0.0 83.9 jit_solution(11601122364058784024)
XLA Ops:
  0.6 1.6 %split_kv.1 = (bf16[128,128]{1,0:T(8,128)(2,1)}, bf16[128,128]{1,0:T(8,128)(2,1)}, bf16[128,128]{1,0:T(8,128)(2,1)}, bf16[128,128]{1,0:T(8,128)(2,1)}) custom-call(s32[4]{0:T(128)} %heads.5, bf16[128,512]{1,0:T(8,128)(2,1)} %bitcast.25), custom_call_target="tpu_custom_call" | custom-call | tf_op jit(solution)/shard_map/split_kv/pallas_call | solution.py:242
  2.2 2.2 %collective-permute-start = (bf16[128,128]{1,0:T(8,128)(2,1)}, bf16[128,128]{1,0:T(8,128)(2,1)S(1)}, u32[]{:S(2)}, u32[]{:S(2)}) collective-permute-start(bf16[128,128]{1,0:T(8,128)(2,1)} %get-tuple-element.12), channel_id=1, source_target_pairs={{0,1},{1,0},{2,3},{3,2},{4,5},{5,4},{6,7},{7,6},{8,9},{9,8},{10,11... | collective-permute-start | bytes 98312 | tf_op jit(solution)/shard_map/ppermute | solution.py:234
  4.4 0.9 %collective-permute-start.1 = (bf16[128,128]{1,0:T(8,128)(2,1)}, bf16[128,128]{1,0:T(8,128)(2,1)S(1)}, u32[]{:S(2)}, u32[]{:S(2)}) collective-permute-start(bf16[128,128]{1,0:T(8,128)(2,1)} %get-tuple-element.13), channel_id=1, source_target_pairs={{0,2},{1,3},{2,0},{3,1},{4,6},{5,7},{6,4},{7,5},{8,10},{9,11},{10,... | collective-permute-start | bytes 98312 | tf_op jit(solution)/shard_map/ppermute | solution.py:234
  5.3 0.6 collective-permute-start.2
  5.9 0.9 %copy-done = bf16[1,64,2048]{2,1,0:T(8,128)(2,1)S(1)} copy-done((bf16[1,64,2048]{2,1,0:T(8,128)(2,1)S(1)}, bf16[1,64,2048]{2,1,0:T(8,128)(2,1)}, u32[]{:S(2)}) %copy-start) | copy-done | bytes 262168
  6.8 0.7 copy-done.1
  7.5 1.7 %split_q.1 = bf16[16,256,128]{2,1,0:T(8,128)(2,1)} custom-call(s32[4]{0:T(128)S(1)} %copy-done.1, bf16[64,2048]{1,0:T(8,128)(2,1)S(1)} %bitcast.22), custom_call_target="tpu_custom_call" | custom-call | tf_op jit(solution)/shard_map/split_q/pallas_call | solution.py:254
  9.2 8.4 %all-to-all-start = ((bf16[16,256,128]{2,1,0:T(8,128)(2,1)}), bf16[16,256,128]{2,1,0:T(8,128)(2,1)S(1)}, u32[]{:S(2)}, u32[]{:S(2)}) async-start(bf16[16,256,128]{2,1,0:T(8,128)(2,1)} %split_q.1), calls=%async_computation | async-start | bytes 2097152 | tf_op jit(solution)/shard_map/all_to_all | solution.py:240
  17.8 5.9 %collective-permute-start.6 = (bf16[512,128]{1,0:T(8,128)(2,1)S(1)}, bf16[512,128]{1,0:T(8,128)(2,1)S(1)}, u32[]{:S(2)}, u32[]{:S(2)}) collective-permute-start(bf16[512,128]{1,0:T(8,128)(2,1)S(1)} %constant_dynamic-update-slice_fusion.refs_0_), channel_id=1, source_target_pairs={{0,112},{1,113},{2,114},{3,115},{4,116},{5,117},{6,118},{7,119},{8... | collective-permute-start | bytes 393224 | tf_op jit(solution)/shard_map/ppermute | solution.py:234
  23.9 0.3 copy.12
  24.2 0.2 convert_reduce_fusion
  25.0 0.2 convert_reduce_fusion.1
  25.4 0.8 %collective-permute-done.6.refs_4_ = bf16[512,128]{1,0:T(8,128)(2,1)S(1)} collective-permute-done((bf16[512,128]{1,0:T(8,128)(2,1)S(1)}, bf16[512,128]{1,0:T(8,128)(2,1)S(1)}, u32[]{:S(2)}, u32[]{:S(2)}) %collective-permute-start.6) | collective-permute-done | bytes 131104 | tf_op jit(solution)/shard_map/ppermute | solution.py:234
  26.2 3.7 %collective-permute-start.7 = (bf16[512,128]{1,0:T(8,128)(2,1)S(1)}, bf16[512,128]{1,0:T(8,128)(2,1)S(1)}, u32[]{:S(2)}, u32[]{:S(2)}) collective-permute-start(bf16[512,128]{1,0:T(8,128)(2,1)S(1)} %collective-permute-done.6.refs_4_), channel_id=1, source_target_pairs={{0,112},{1,113},{2,114},{3,115},{4,116},{5,117},{6,118},{7,119},{8... | collective-permute-start | bytes 393224 | tf_op jit(solution)/shard_map/ppermute | solution.py:234
  29.9 0.2 slice_reduce_fusion
  30.1 0.2 convert_reduce_fusion.2
  30.3 5.8 %collective-permute-done.4.refs_2_ = bf16[512,128]{1,0:T(8,128)(2,1)S(1)} collective-permute-done((bf16[512,128]{1,0:T(8,128)(2,1)S(1)}, bf16[512,128]{1,0:T(8,128)(2,1)S(1)}, u32[]{:S(2)}, u32[]{:S(2)}) %collective-permute-start.4) | collective-permute-done | bytes 131104 | tf_op jit(solution)/shard_map/ppermute | solution.py:234
  36.1 3.2 %collective-permute-start.8 = (bf16[512,128]{1,0:T(8,128)(2,1)S(1)}, bf16[512,128]{1,0:T(8,128)(2,1)S(1)}, u32[]{:S(2)}, u32[]{:S(2)}) collective-permute-start(bf16[512,128]{1,0:T(8,128)(2,1)S(1)} %collective-permute-done.7.refs_5_), channel_id=1, source_target_pairs={{0,112},{1,113},{2,114},{3,115},{4,116},{5,117},{6,118},{7,119},{8... | collective-permute-start | bytes 393224 | tf_op jit(solution)/shard_map/ppermute | solution.py:234
  39.4 2.9 %collective-permute-start.9 = (bf16[256,128]{1,0:T(8,128)(2,1)S(1)}, bf16[256,128]{1,0:T(8,128)(2,1)S(1)}, u32[]{:S(2)}, u32[]{:S(2)}) collective-permute-start(bf16[256,128]{1,0:T(8,128)(2,1)S(1)} %slice.28), channel_id=1, source_target_pairs={{0,32},{1,33},{2,34},{3,35},{4,36},{5,37},{6,38},{7,39},{8,40},{9,... | collective-permute-start | bytes 196616 | tf_op jit(solution)/shard_map/ppermute | solution.py:234
  42.4 2.1 %collective-permute-done.10.refs_8_ = bf16[256,128]{1,0:T(8,128)(2,1)S(1)} collective-permute-done((bf16[256,128]{1,0:T(8,128)(2,1)S(1)}, bf16[256,128]{1,0:T(8,128)(2,1)S(1)}, u32[]{:S(2)}, u32[]{:S(2)}) %collective-permute-start.10) | collective-permute-done | bytes 65568 | tf_op jit(solution)/shard_map/ppermute | solution.py:234
  44.6 1.4 %collective-permute-done.9.refs_7_ = bf16[256,128]{1,0:T(8,128)(2,1)S(1)} collective-permute-done((bf16[256,128]{1,0:T(8,128)(2,1)S(1)}, bf16[256,128]{1,0:T(8,128)(2,1)S(1)}, u32[]{:S(2)}, u32[]{:S(2)}) %collective-permute-start.9) | collective-permute-done | bytes 65568 | tf_op jit(solution)/shard_map/ppermute | solution.py:234
  46.0 0.3 pick.1
  46.3 3.2 %collective-permute-start.11 = (bf16[4,64,256]{2,1,0:T(8,128)(2,1)S(1)}, bf16[4,64,256]{2,1,0:T(8,128)(2,1)S(1)}, u32[]{:S(2)}, u32[]{:S(2)}) collective-permute-start(bf16[4,64,256]{2,1,0:T(8,128)(2,1)S(1)} %pick.1), channel_id=1, source_target_pairs={{0,0},{1,32},{2,64},{3,96},{4,4},{5,36},{6,68},{7,100},{8,8},{9,40... | collective-permute-start | bytes 393224 | tf_op jit(solution)/shard_map/ppermute | solution.py:234
  49.5 11.1 %attention.1 = bf16[16,272,128]{2,1,0:T(8,128)(2,1)} custom-call(s32[144]{0:T(256)S(1)} %concatenate.7.table, bf16[32,128,128]{2,1,0:T(8,128)(2,1)S(1)} %bitcast.21, s32[8,256]{1,0:T(8,128)S(1)} %broadcast_add_fusion.kpos_ref, bf16[512,128]{1,0:T(8,128)(2,1)S(1)} %constant_dynamic-update-slice_fusion.refs_0_, ...), custom_call_target="tpu_custom_call" | custom-call | flops 3000000000 | bytes 4000000 | tf_op jit(solution)/shard_map/attention/pallas_call | solution.py:299
  60.6 9.1 %all-to-all-start.1 = ((bf16[16,272,128]{2,1,0:T(8,128)(2,1)}), bf16[16,272,128]{2,1,0:T(8,128)(2,1)S(1)}, u32[]{:S(2)}, u32[]{:S(2)}) async-start(bf16[16,272,128]{2,1,0:T(8,128)(2,1)} %attention.1), calls=%async_computation.1 | async-start | bytes 2228224 | tf_op jit(solution)/shard_map/all_to_all | solution.py:240
  70.5 1.6 %collective-permute-start.12 = (bf16[64,256]{1,0:T(8,128)(2,1)S(1)}, bf16[64,256]{1,0:T(8,128)(2,1)S(1)}, u32[]{:S(2)}, u32[]{:S(2)}) collective-permute-start(bf16[64,256]{1,0:T(8,128)(2,1)S(1)} %get-tuple-element.34), channel_id=1, source_target_pairs={{0,4},{1,5},{2,6},{3,7},{4,0},{5,1},{6,2},{7,3},{8,12},{9,13},{10,... | collective-permute-start | bytes 98312 | tf_op jit(solution)/shard_map/ppermute | solution.py:234
  72.1 2.7 %collective-permute-start.13 = (bf16[64,256]{1,0:T(8,128)(2,1)S(1)}, bf16[64,256]{1,0:T(8,128)(2,1)S(1)}, u32[]{:S(2)}, u32[]{:S(2)}) collective-permute-start(bf16[64,256]{1,0:T(8,128)(2,1)S(1)} %get-tuple-element.33), channel_id=1, source_target_pairs={{0,8},{1,9},{2,10},{3,11},{4,12},{5,13},{6,14},{7,15},{8,0},{9,1},... | collective-permute-start | bytes 98312 | tf_op jit(solution)/shard_map/ppermute | solution.py:234
  74.8 0.6 collective-permute-start.14
  75.5 3.7 %collective-permute-done.12.k1_ref = bf16[64,256]{1,0:T(8,128)(2,1)S(1)} collective-permute-done((bf16[64,256]{1,0:T(8,128)(2,1)S(1)}, bf16[64,256]{1,0:T(8,128)(2,1)S(1)}, u32[]{:S(2)}, u32[]{:S(2)}) %collective-permute-start.12) | collective-permute-done | bytes 32800 | tf_op jit(solution)/shard_map/ppermute | solution.py:234
  79.3 1.9 %collective-permute-done.13.k2_ref = bf16[64,256]{1,0:T(8,128)(2,1)S(1)} collective-permute-done((bf16[64,256]{1,0:T(8,128)(2,1)S(1)}, bf16[64,256]{1,0:T(8,128)(2,1)S(1)}, u32[]{:S(2)}, u32[]{:S(2)}) %collective-permute-start.13) | collective-permute-done | bytes 32800 | tf_op jit(solution)/shard_map/ppermute | solution.py:234
  81.1 0.6 all-to-all-done.1.m_ref
  81.8 2.1 %combine.1 = (bf16[64,2048]{1,0:T(8,128)(2,1)}, bf16[2,256,128]{2,1,0:T(8,128)(2,1)}) custom-call(s32[4]{0:T(128)S(1)} %copy-done.2, s32[2]{0:T(128)S(1)} %dynamic_slice.13.blocks, s32[1]{0:T(128)} %copy.19.length, bf16[256,256]{1,0:T(8,128)(2,1)S(1)} %fusion.1.choose_ref, bf16[4,64,256]{2,1,0:T(8,128)(2,1)S(1)} %collective-permute-done.11.k0_ref, ...), custom_call_target="tpu_custom_call" | custom-call | tf_op jit(solution)/shard_map/combine/pallas_call | solution.py:328
  (50 shorter events, 1.7 us)
Async XLA Ops:
  2.2 15.5 %collective-permute-start = (bf16[128,128]{1,0:T(8,128)(2,1)}, bf16[128,128]{1,0:T(8,128)(2,1)S(1)}, u32[]{:S(2)}, u32[]{:S(2)}) collective-permute-start(bf16[128,128]{1,0:T(8,128)(2,1)} %get-tuple-element.12), channel_id=1, source_target_pairs={{0,1},{1,0},{2,3},{3,2},{4,5},{5,4},{6,7},{7,6},{8,9},{9,8},{10,11... | collective-permute-start | bytes 98312 | tf_op jit(solution)/shard_map/ppermute | solution.py:234
  4.4 13.3 %collective-permute-start.1 = (bf16[128,128]{1,0:T(8,128)(2,1)}, bf16[128,128]{1,0:T(8,128)(2,1)S(1)}, u32[]{:S(2)}, u32[]{:S(2)}) collective-permute-start(bf16[128,128]{1,0:T(8,128)(2,1)} %get-tuple-element.13), channel_id=1, source_target_pairs={{0,2},{1,3},{2,0},{3,1},{4,6},{5,7},{6,4},{7,5},{8,10},{9,11},{10,... | collective-permute-start | bytes 98312 | tf_op jit(solution)/shard_map/ppermute | solution.py:234
  5.3 12.5 %collective-permute-start.2 = (bf16[128,128]{1,0:T(8,128)(2,1)}, bf16[128,128]{1,0:T(8,128)(2,1)S(1)}, u32[]{:S(2)}, u32[]{:S(2)}) collective-permute-start(bf16[128,128]{1,0:T(8,128)(2,1)} %get-tuple-element.14), channel_id=1, source_target_pairs={{0,3},{1,2},{2,1},{3,0},{4,7},{5,6},{6,5},{7,4},{8,11},{9,10},{10,... | collective-permute-start | bytes 98312 | tf_op jit(solution)/shard_map/ppermute | solution.py:234
  5.9 0.9 %copy-start = (bf16[1,64,2048]{2,1,0:T(8,128)(2,1)S(1)}, bf16[1,64,2048]{2,1,0:T(8,128)(2,1)}, u32[]{:S(2)}) copy-start(bf16[1,64,2048]{2,1,0:T(8,128)(2,1)} %param.5) | copy-start | bytes 786436
  6.8 0.7 copy-start.1
  9.2 8.4 %copy-start.3 = (bf16[128,128]{1,0:T(8,128)(2,1)S(1)}, bf16[128,128]{1,0:T(8,128)(2,1)}, u32[]{:S(2)}) copy-start(bf16[128,128]{1,0:T(8,128)(2,1)} %get-tuple-element.11) | copy-start | bytes 98308
  9.2 14.5 %copy-start.4 = (s32[256]{0:T(256)S(1)}, s32[256]{0:T(256)}, u32[]{:S(2)}) copy-start(s32[256]{0:T(256)} %param.8) | copy-start | bytes 3076
  9.2 40.3 %all-to-all-start = ((bf16[16,256,128]{2,1,0:T(8,128)(2,1)}), bf16[16,256,128]{2,1,0:T(8,128)(2,1)S(1)}, u32[]{:S(2)}, u32[]{:S(2)}) async-start(bf16[16,256,128]{2,1,0:T(8,128)(2,1)} %split_q.1), calls=%async_computation | async-start | bytes 2097152 | tf_op jit(solution)/shard_map/all_to_all | solution.py:240
  17.8 8.5 %collective-permute-start.6 = (bf16[512,128]{1,0:T(8,128)(2,1)S(1)}, bf16[512,128]{1,0:T(8,128)(2,1)S(1)}, u32[]{:S(2)}, u32[]{:S(2)}) collective-permute-start(bf16[512,128]{1,0:T(8,128)(2,1)S(1)} %constant_dynamic-update-slice_fusion.refs_0_), channel_id=1, source_target_pairs={{0,112},{1,113},{2,114},{3,115},{4,116},{5,117},{6,118},{7,119},{8... | collective-permute-start | bytes 393224 | tf_op jit(solution)/shard_map/ppermute | solution.py:234
  23.7 6.2 %collective-permute-start.3 = (bf16[512,128]{1,0:T(8,128)(2,1)S(1)}, bf16[512,128]{1,0:T(8,128)(2,1)S(1)}, u32[]{:S(2)}, u32[]{:S(2)}) collective-permute-start(bf16[512,128]{1,0:T(8,128)(2,1)S(1)} %constant_dynamic-update-slice_fusion.refs_0_), channel_id=1, source_target_pairs={{0,16},{1,17},{2,18},{3,19},{4,20},{5,21},{6,22},{7,23},{8,24},{9,... | collective-permute-start | bytes 393224 | tf_op jit(solution)/shard_map/ppermute | solution.py:234
  26.2 9.8 %collective-permute-start.7 = (bf16[512,128]{1,0:T(8,128)(2,1)S(1)}, bf16[512,128]{1,0:T(8,128)(2,1)S(1)}, u32[]{:S(2)}, u32[]{:S(2)}) collective-permute-start(bf16[512,128]{1,0:T(8,128)(2,1)S(1)} %collective-permute-done.6.refs_4_), channel_id=1, source_target_pairs={{0,112},{1,113},{2,114},{3,115},{4,116},{5,117},{6,118},{7,119},{8... | collective-permute-start | bytes 393224 | tf_op jit(solution)/shard_map/ppermute | solution.py:234
  29.9 6.2 %collective-permute-start.4 = (bf16[512,128]{1,0:T(8,128)(2,1)S(1)}, bf16[512,128]{1,0:T(8,128)(2,1)S(1)}, u32[]{:S(2)}, u32[]{:S(2)}) collective-permute-start(bf16[512,128]{1,0:T(8,128)(2,1)S(1)} %collective-permute-done.3.refs_1_), channel_id=1, source_target_pairs={{0,16},{1,17},{2,18},{3,19},{4,20},{5,21},{6,22},{7,23},{8,24},{9,... | collective-permute-start | bytes 393224 | tf_op jit(solution)/shard_map/ppermute | solution.py:234
  36.1 9.9 %collective-permute-start.5 = (bf16[512,128]{1,0:T(8,128)(2,1)S(1)}, bf16[512,128]{1,0:T(8,128)(2,1)S(1)}, u32[]{:S(2)}, u32[]{:S(2)}) collective-permute-start(bf16[512,128]{1,0:T(8,128)(2,1)S(1)} %collective-permute-done.4.refs_2_), channel_id=1, source_target_pairs={{0,16},{1,17},{2,18},{3,19},{4,20},{5,21},{6,22},{7,23},{8,24},{9,... | collective-permute-start | bytes 393224 | tf_op jit(solution)/shard_map/ppermute | solution.py:234
  36.1 9.9 %collective-permute-start.8 = (bf16[512,128]{1,0:T(8,128)(2,1)S(1)}, bf16[512,128]{1,0:T(8,128)(2,1)S(1)}, u32[]{:S(2)}, u32[]{:S(2)}) collective-permute-start(bf16[512,128]{1,0:T(8,128)(2,1)S(1)} %collective-permute-done.7.refs_5_), channel_id=1, source_target_pairs={{0,112},{1,113},{2,114},{3,115},{4,116},{5,117},{6,118},{7,119},{8... | collective-permute-start | bytes 393224 | tf_op jit(solution)/shard_map/ppermute | solution.py:234
  39.3 5.2 %collective-permute-start.10 = (bf16[256,128]{1,0:T(8,128)(2,1)S(1)}, bf16[256,128]{1,0:T(8,128)(2,1)S(1)}, u32[]{:S(2)}, u32[]{:S(2)}) collective-permute-start(bf16[256,128]{1,0:T(8,128)(2,1)S(1)} %slice.29), channel_id=1, source_target_pairs={{0,96},{1,97},{2,98},{3,99},{4,100},{5,101},{6,102},{7,103},{8,104... | collective-permute-start | bytes 196616 | tf_op jit(solution)/shard_map/ppermute | solution.py:234
  39.4 6.6 %collective-permute-start.9 = (bf16[256,128]{1,0:T(8,128)(2,1)S(1)}, bf16[256,128]{1,0:T(8,128)(2,1)S(1)}, u32[]{:S(2)}, u32[]{:S(2)}) collective-permute-start(bf16[256,128]{1,0:T(8,128)(2,1)S(1)} %slice.28), channel_id=1, source_target_pairs={{0,32},{1,33},{2,34},{3,35},{4,36},{5,37},{6,38},{7,39},{8,40},{9,... | collective-permute-start | bytes 196616 | tf_op jit(solution)/shard_map/ppermute | solution.py:234
  46.3 14.3 %collective-permute-start.11 = (bf16[4,64,256]{2,1,0:T(8,128)(2,1)S(1)}, bf16[4,64,256]{2,1,0:T(8,128)(2,1)S(1)}, u32[]{:S(2)}, u32[]{:S(2)}) collective-permute-start(bf16[4,64,256]{2,1,0:T(8,128)(2,1)S(1)} %pick.1), channel_id=1, source_target_pairs={{0,0},{1,32},{2,64},{3,96},{4,4},{5,36},{6,68},{7,100},{8,8},{9,40... | collective-permute-start | bytes 393224 | tf_op jit(solution)/shard_map/ppermute | solution.py:234
  60.6 21.2 %copy-start.2 = (s32[4]{0:T(128)S(1)}, s32[4]{0:T(128)}, u32[]{:S(2)}) copy-start(s32[4]{0:T(128)} %heads.5) | copy-start | bytes 52
  60.6 21.2 %all-to-all-start.1 = ((bf16[16,272,128]{2,1,0:T(8,128)(2,1)}), bf16[16,272,128]{2,1,0:T(8,128)(2,1)S(1)}, u32[]{:S(2)}, u32[]{:S(2)}) async-start(bf16[16,272,128]{2,1,0:T(8,128)(2,1)} %attention.1), calls=%async_computation.1 | async-start | bytes 2228224 | tf_op jit(solution)/shard_map/all_to_all | solution.py:240
  70.5 8.7 %collective-permute-start.12 = (bf16[64,256]{1,0:T(8,128)(2,1)S(1)}, bf16[64,256]{1,0:T(8,128)(2,1)S(1)}, u32[]{:S(2)}, u32[]{:S(2)}) collective-permute-start(bf16[64,256]{1,0:T(8,128)(2,1)S(1)} %get-tuple-element.34), channel_id=1, source_target_pairs={{0,4},{1,5},{2,6},{3,7},{4,0},{5,1},{6,2},{7,3},{8,12},{9,13},{10,... | collective-permute-start | bytes 98312 | tf_op jit(solution)/shard_map/ppermute | solution.py:234
  72.1 9.0 %collective-permute-start.13 = (bf16[64,256]{1,0:T(8,128)(2,1)S(1)}, bf16[64,256]{1,0:T(8,128)(2,1)S(1)}, u32[]{:S(2)}, u32[]{:S(2)}) collective-permute-start(bf16[64,256]{1,0:T(8,128)(2,1)S(1)} %get-tuple-element.33), channel_id=1, source_target_pairs={{0,8},{1,9},{2,10},{3,11},{4,12},{5,13},{6,14},{7,15},{8,0},{9,1},... | collective-permute-start | bytes 98312 | tf_op jit(solution)/shard_map/ppermute | solution.py:234
  74.8 6.4 %collective-permute-start.14 = (bf16[64,256]{1,0:T(8,128)(2,1)S(1)}, bf16[64,256]{1,0:T(8,128)(2,1)S(1)}, u32[]{:S(2)}, u32[]{:S(2)}) collective-permute-start(bf16[64,256]{1,0:T(8,128)(2,1)S(1)} %get-tuple-element.32), channel_id=1, source_target_pairs={{0,12},{1,13},{2,14},{3,15},{4,8},{5,9},{6,10},{7,11},{8,4},{9,5},... | collective-permute-start | bytes 98312 | tf_op jit(solution)/shard_map/ppermute | solution.py:234
